TPU v7x, 32 devices: a whole 2x2x4 slice. The times are simulated.
32 devices in a mesh: outer: 8 (over z, core), inner: 4 (over y, x).
Axes of the slice: x: 2, y: 2, z: 4, core: 2. Of those that a mesh axis runs over, the one named last changes fastest.
Arguments:
- right_side: float32 [128, 128, 512], P('outer', 'inner'), may hold values from -6 to 6
- coefficient: float32 [128, 128, 512], P('outer', 'inner'), may hold values from 0.1 to 10
Outputs:
- fine_field: float32 [128, 128, 512], P('outer', 'inner')
- middle_field: float32 [64, 64, 256], P('outer', 'inner')
- coarse_field: float32 [32, 32, 128], P('outer', 'inner')
- coarse_residual: float32 [32, 32, 128], P('outer', 'inner')
All inputs are finite; a program needn't handle non-finite values.
Results may differ from a plain program's by a relative error of at most 0.0003.
Values sent between devices are 32-bit elements; how exact they have to be, the bound alone decides.
No kernel may reach another device: no remote copies, remote signals or barrier semaphores. Data moves between devices by JAX's collectives and lax.ppermute only.
A program may use at most 192 MiB of HBM per device.

v0:
```python
import jax
import jax.numpy as jnp
from jax import lax
from jax.sharding import PartitionSpec as P

NU = 2
LEVELS = 3


NEIGHBOUR_CUTS = (
    (slice(0, -2), slice(1, -1), slice(1, -1)),
    (slice(2, None), slice(1, -1), slice(1, -1)),
    (slice(1, -1), slice(0, -2), slice(1, -1)),
    (slice(1, -1), slice(2, None), slice(1, -1)),
    (slice(1, -1), slice(1, -1), slice(0, -2)),
    (slice(1, -1), slice(1, -1), slice(2, None)),
)
CENTRE_CUT = (slice(1, -1), slice(1, -1), slice(1, -1))


def extended(x, sides, width):
    for axis, dim in sides:
        size, length = (lax.axis_size(axis), x.shape[dim])
        up = [(i, (i + 1) % size) for i in range(size - 1)]
        down = [(j, i) for i, j in up]
        last = lax.slice_in_dim(x, length - width, length, axis=dim)
        initial = lax.slice_in_dim(x, 0, width, axis=dim)
        before = lax.ppermute(last, axis, up)
        after = lax.ppermute(initial, axis, down)
        x = jnp.concatenate([before, x, after], axis=dim)
    return x


def pad_last(values):
    return jnp.pad(values, ((0, 0), (0, 0), (1, 1)))


def pad_along(values, dimension):
    widths = [(0, 0), (0, 0), (0, 0)]
    widths[dimension] = (1, 1)
    return jnp.pad(values, widths)


def diagonal_of(padded_coefficient):
    wider = pad_last(padded_coefficient)
    centre = wider[CENTRE_CUT]
    total = wider[NEIGHBOUR_CUTS[0]]
    for neighbour_cut in NEIGHBOUR_CUTS[1:]:
        total = total + wider[neighbour_cut]
    return 3.0 * centre + 0.5 * total


def neighbour_term(padded_coefficient, padded_solution):
    wide_k = pad_last(padded_coefficient)
    wide_u = pad_last(padded_solution)
    centre = wide_k[CENTRE_CUT]
    value_total = wide_u[NEIGHBOUR_CUTS[0]]
    weighted_total = wide_k[NEIGHBOUR_CUTS[0]] * wide_u[NEIGHBOUR_CUTS[0]]
    for neighbour_cut in NEIGHBOUR_CUTS[1:]:
        value_total = value_total + wide_u[neighbour_cut]
        weighted_total = weighted_total + wide_k[neighbour_cut] * wide_u[neighbour_cut]
    return 0.5 * (centre * value_total + weighted_total)


def parity_mask(grid_shape):
    total = (
        lax.broadcasted_iota(jnp.int32, grid_shape, 0)
        + lax.broadcasted_iota(jnp.int32, grid_shape, 1)
        + lax.broadcasted_iota(jnp.int32, grid_shape, 2)
    )
    return total % 2 == 0


def restrict_padded(padded, dimension):
    moved = jnp.moveaxis(padded, dimension, 0)
    half_count = (moved.shape[0] - 2) // 2
    middle = moved[1:-1].reshape((half_count, 2) + moved.shape[1:])
    earlier = moved[0:-2:2]
    later = moved[3::2]
    coarse = (3.0 * (middle[:, 0] + middle[:, 1]) + (earlier + later)) * 0.125
    return jnp.moveaxis(coarse, 0, dimension)


def block_mean(values):
    grid_shape = values.shape
    blocks = values.reshape((grid_shape[0] // 2, 2, grid_shape[1] // 2, 2, grid_shape[2] // 2, 2))
    return jnp.sum(blocks, axis=(1, 3, 5)) * 0.125


def extend(stacked, margin_width):
    return extended(stacked, (("outer", 1), ("inner", 2)), margin_width)


def body(right_side, coefficient):
    source = right_side
    conductivity = coefficient
    fields = []
    residual = source
    for level_index in range(LEVELS):
        solution = jnp.zeros_like(source)
        near_k = extend(conductivity[None], 1)[0]
        diagonal = diagonal_of(near_k)
        red_cells = parity_mask(source.shape)
        for sweep_index in range(NU):
            for colour in (red_cells, jnp.logical_not(red_cells)):
                grown = extend(solution[None], 1)[0]
                term = neighbour_term(near_k, grown)
                solution = jnp.where(colour, (source + term) / diagonal, solution)
        grown = extend(solution[None], 1)[0]
        term = neighbour_term(near_k, grown)
        residual = source - (diagonal * solution - term)
        fields.append(solution)
        if level_index + 1 < LEVELS:
            residual_wide = extend(residual[None], 1)[0]
            coarse = restrict_padded(residual_wide, 0)
            coarse = restrict_padded(coarse, 1)
            coarse = restrict_padded(pad_along(coarse, 2), 2)
            source = 4.0 * coarse
            conductivity = block_mean(conductivity)
    return (fields[0], fields[1], fields[2], residual)


def solution(mesh):
    return jax.shard_map(
        body,
        mesh=mesh,
        in_specs=(P("outer", "inner", None), P("outer", "inner", None)),
        out_specs=(
            P("outer", "inner", None),
            P("outer", "inner", None),
            P("outer", "inner", None),
            P("outer", "inner", None),
        ),
        check_vma=False,
    )
```

profile of v0, /device:TPU:1, one launch (start us, length us, event | category | flops | bytes accessed | tf_op | source)
XLA Modules:
  0.0 431.6 jit_solution(4333586716194823612)
XLA Ops:
  1.5 4.6 %collective-permute-start = (f32[1,1,32,512]{3,2,1,0:T(8,128)S(1)}, f32[1,1,32,512]{3,2,1,0:T(8,128)S(1)}, u32[]{:S(2)}, u32[]{:S(2)}) collective-permute-start(f32[1,1,32,512]{3,2,1,0:T(8,128)S(1)} %get-tuple-element.44), channel_id=1, source_target_pairs={{0,4},{4,8},{8,12},{12,16},{16,20},{20,24},{24,28},{1,5},{5,9},{9,... | collective-permute-start | bytes 196616 | tf_op jit(solution)/shard_map/ppermute | solution.py:28
  8.1 3.8 collective-permute-start.4
  19.5 4.0 collective-permute-start.6
  25.2 3.7 collective-permute-done.7
  29.1 3.4 divide_select_fusion.3
  32.5 5.4 %collective-permute-start.8 = (f32[1,1,32,512]{3,2,1,0:T(8,128)S(1)}, f32[1,1,32,512]{3,2,1,0:T(8,128)S(1)}, u32[]{:S(2)}, u32[]{:S(2)}) collective-permute-start(f32[1,1,32,512]{3,2,1,0:T(8,128)S(1)} %get-tuple-element.42), channel_id=1, source_target_pairs={{0,4},{4,8},{8,12},{12,16},{16,20},{20,24},{24,28},{1,5},{5,9},{9,... | collective-permute-start | bytes 196616 | tf_op jit(solution)/shard_map/ppermute | solution.py:28
  39.8 3.6 collective-permute-done.9
  43.5 4.5 %collective-permute-start.10 = (f32[1,18,1,512]{3,2,1,0:T(1,128)S(1)}, f32[1,18,1,512]{3,2,1,0:T(1,128)S(1)}, u32[]{:S(2)}, u32[]{:S(2)}) collective-permute-start(f32[1,18,1,512]{3,2,1,0:T(1,128)S(1)} %get-tuple-element.28), channel_id=1, source_target_pairs={{0,1},{1,2},{2,3},{4,5},{5,6},{6,7},{8,9},{9,10},{10,11},{12,13},{... | collective-permute-start | bytes 110600 | tf_op jit(solution)/shard_map/ppermute | solution.py:28
  49.4 3.4 collective-permute-done.11
  53.0 3.4 divide_select_fusion.2
  56.5 3.3 collective-permute-start.12
  61.7 3.6 collective-permute-done.13
  73.6 69.1 %reshape.76 = f32[8,2,16,2,256,2]{5,4,3,2,1,0:T(8,128)} reshape(f32[16,32,512]{2,1,0:T(8,128)} %param.3) | data formatting | bytes 2097152 | tf_op jit(solution)/shard_map/reshape | solution.py:86
  142.8 20.8 %reduce_sum.18 = f32[8,16,256]{2,1,0:T(8,128)S(1)} reduce(f32[8,2,16,2,256,2]{5,4,3,2,1,0:T(8,128)} %reshape.76, f32[]{:T(128)} %constant.24.clone.1), dimensions={1,3,5}, to_apply=%region_0.1 | reduce | flops 229376 | bytes 1179652 | tf_op jit(solution)/shard_map/reduce_sum | solution.py:87
  165.1 3.4 divide_select_fusion.1
  168.6 3.4 collective-permute-start.16
  173.9 3.6 collective-permute-done.17
  177.6 4.3 collective-permute-start.18
  187.8 3.4 divide_select_fusion
  191.2 3.4 collective-permute-start.20
  196.6 4.3 collective-permute-start.30
  202.3 4.1 collective-permute-start.22
  207.9 4.9 %collective-permute-start.34 = (f32[1,10,1,256]{3,2,1,0:T(1,128)S(1)}, f32[1,10,1,256]{3,2,1,0:T(1,128)S(1)}, u32[]{:S(2)}, u32[]{:S(2)}) collective-permute-start(f32[1,10,1,256]{3,2,1,0:T(1,128)S(1)} %get-tuple-element.64), channel_id=1, source_target_pairs={{0,1},{1,2},{2,3},{4,5},{5,6},{6,7},{8,9},{9,10},{10,11},{12,13},{... | collective-permute-start | bytes 30728 | tf_op jit(solution)/shard_map/ppermute | solution.py:28
  217.4 4.8 %collective-permute-start.24 = (f32[1,1,32,512]{3,2,1,0:T(8,128)S(1)}, f32[1,1,32,512]{3,2,1,0:T(8,128)S(1)}, u32[]{:S(2)}, u32[]{:S(2)}) collective-permute-start(f32[1,1,32,512]{3,2,1,0:T(8,128)S(1)} %get-tuple-element.34), channel_id=1, source_target_pairs={{0,4},{4,8},{8,12},{12,16},{16,20},{20,24},{24,28},{1,5},{5,9},{9,... | collective-permute-start | bytes 196616 | tf_op jit(solution)/shard_map/ppermute | solution.py:28
  224.2 3.6 collective-permute-done.25
  227.8 5.2 %collective-permute-start.26 = (f32[1,18,1,512]{3,2,1,0:T(1,128)S(1)}, f32[1,18,1,512]{3,2,1,0:T(1,128)S(1)}, u32[]{:S(2)}, u32[]{:S(2)}) collective-permute-start(f32[1,18,1,512]{3,2,1,0:T(1,128)S(1)} %get-tuple-element.20), channel_id=1, source_target_pairs={{0,1},{1,2},{2,3},{4,5},{5,6},{6,7},{8,9},{9,10},{10,11},{12,13},{... | collective-permute-start | bytes 110600 | tf_op jit(solution)/shard_map/ppermute | solution.py:28
  234.4 4.5 %collective-permute-done.27 = f32[1,18,1,512]{3,2,1,0:T(1,128)S(1)} collective-permute-done((f32[1,18,1,512]{3,2,1,0:T(1,128)S(1)}, f32[1,18,1,512]{3,2,1,0:T(1,128)S(1)}, u32[]{:S(2)}, u32[]{:S(2)}) %collective-permute-start.27) | collective-permute-done | bytes 36896 | tf_op jit(solution)/shard_map/ppermute | solution.py:29
  241.0 4.5 %slice.993 = f32[256,8,16]{0,2,1:T(8,128)S(1)} slice(f32[514,8,16]{0,2,1:T(8,128)S(1)} %pad_bitcast_fusion), slice={[0:512:2], [0:8:1], [0:16:1]} | slice | bytes 262144 | tf_op jit(solution)/shard_map/slice | solution.py:78
  245.5 4.5 %slice.994 = f32[256,8,16]{0,2,1:T(8,128)S(1)} slice(f32[514,8,16]{0,2,1:T(8,128)S(1)} %pad_bitcast_fusion), slice={[3:514:2], [0:8:1], [0:16:1]} | slice | bytes 262144 | tf_op jit(solution)/shard_map/slice | solution.py:79
  259.5 3.1 collective-permute-done.37
  262.6 4.5 %collective-permute-start.38 = (f32[1,10,1,256]{3,2,1,0:T(1,128)S(1)}, f32[1,10,1,256]{3,2,1,0:T(1,128)S(1)}, u32[]{:S(2)}, u32[]{:S(2)}) collective-permute-start(f32[1,10,1,256]{3,2,1,0:T(1,128)S(1)} %get-tuple-element.60), channel_id=1, source_target_pairs={{0,1},{1,2},{2,3},{4,5},{5,6},{6,7},{8,9},{9,10},{10,11},{12,13},{... | collective-permute-start | bytes 30728 | tf_op jit(solution)/shard_map/ppermute | solution.py:28
  271.9 3.4 collective-permute-start.40
  277.2 3.1 collective-permute-done.41
  288.8 9.8 %mul.655 = f32[4,2,8,2,128,2]{5,4,3,2,1,0:T(8,128)} reshape(f32[8,16,256]{2,1,0:T(8,128)S(1)} %get-tuple-element.70) | data formatting | bytes 262144 | tf_op jit(solution)/shard_map/mul | solution.py:87
  298.6 4.0 reduce_sum.19
  303.0 3.5 collective-permute-start.44
  311.5 4.3 collective-permute-start.46
  321.8 3.5 collective-permute-start.48
  327.2 4.3 collective-permute-start.58
  332.8 4.1 collective-permute-start.50
  338.3 4.9 %collective-permute-start.62 = (f32[1,6,1,128]{3,2,1,0:T(1,128)S(1)}, f32[1,6,1,128]{3,2,1,0:T(1,128)S(1)}, u32[]{:S(2)}, u32[]{:S(2)}) collective-permute-start(f32[1,6,1,128]{3,2,1,0:T(1,128)S(1)} %get-tuple-element.92), channel_id=1, source_target_pairs={{0,1},{1,2},{2,3},{4,5},{5,6},{6,7},{8,9},{9,10},{10,11},{12,13},{... | collective-permute-start | bytes 9224 | tf_op jit(solution)/shard_map/ppermute | solution.py:28
  344.8 4.8 %collective-permute-start.52 = (f32[1,1,16,256]{3,2,1,0:T(8,128)S(1)}, f32[1,1,16,256]{3,2,1,0:T(8,128)S(1)}, u32[]{:S(2)}, u32[]{:S(2)}) collective-permute-start(f32[1,1,16,256]{3,2,1,0:T(8,128)S(1)} %get-tuple-element.66), channel_id=1, source_target_pairs={{0,4},{4,8},{8,12},{12,16},{16,20},{20,24},{24,28},{1,5},{5,9},{9,... | collective-permute-start | bytes 49160 | tf_op jit(solution)/shard_map/ppermute | solution.py:28
  354.6 5.2 %collective-permute-start.54 = (f32[1,10,1,256]{3,2,1,0:T(1,128)S(1)}, f32[1,10,1,256]{3,2,1,0:T(1,128)S(1)}, u32[]{:S(2)}, u32[]{:S(2)}) collective-permute-start(f32[1,10,1,256]{3,2,1,0:T(1,128)S(1)} %get-tuple-element.52), channel_id=1, source_target_pairs={{0,1},{1,2},{2,3},{4,5},{5,6},{6,7},{8,9},{9,10},{10,11},{12,13},{... | collective-permute-start | bytes 30728 | tf_op jit(solution)/shard_map/ppermute | solution.py:28
  361.2 4.2 collective-permute-done.55
  376.0 4.5 %collective-permute-start.66 = (f32[1,6,1,128]{3,2,1,0:T(1,128)S(1)}, f32[1,6,1,128]{3,2,1,0:T(1,128)S(1)}, u32[]{:S(2)}, u32[]{:S(2)}) collective-permute-start(f32[1,6,1,128]{3,2,1,0:T(1,128)S(1)} %get-tuple-element.88), channel_id=1, source_target_pairs={{0,1},{1,2},{2,3},{4,5},{5,6},{6,7},{8,9},{9,10},{10,11},{12,13},{... | collective-permute-start | bytes 9224 | tf_op jit(solution)/shard_map/ppermute | solution.py:28
  385.0 3.4 collective-permute-start.68
  400.4 3.4 collective-permute-start.72
  415.7 3.4 collective-permute-start.76
  (244 shorter events, 149.6 us)
Async XLA Ops:
  1.5 12.3 %collective-permute-start = (f32[1,1,32,512]{3,2,1,0:T(8,128)S(1)}, f32[1,1,32,512]{3,2,1,0:T(8,128)S(1)}, u32[]{:S(2)}, u32[]{:S(2)}) collective-permute-start(f32[1,1,32,512]{3,2,1,0:T(8,128)S(1)} %get-tuple-element.44), channel_id=1, source_target_pairs={{0,4},{4,8},{8,12},{12,16},{16,20},{20,24},{24,28},{1,5},{5,9},{9,... | collective-permute-start | bytes 196616 | tf_op jit(solution)/shard_map/ppermute | solution.py:28
  6.1 7.7 %collective-permute-start.1 = (f32[1,1,32,512]{3,2,1,0:T(8,128)S(1)}, f32[1,1,32,512]{3,2,1,0:T(8,128)S(1)}, u32[]{:S(2)}, u32[]{:S(2)}) collective-permute-start(f32[1,1,32,512]{3,2,1,0:T(8,128)S(1)} %get-tuple-element.45), channel_id=1, source_target_pairs={{4,0},{8,4},{12,8},{16,12},{20,16},{24,20},{28,24},{5,1},{9,5},{13... | collective-permute-start | bytes 196616 | tf_op jit(solution)/shard_map/ppermute | solution.py:29
  8.1 11.3 %collective-permute-start.4 = (f32[1,1,32,512]{3,2,1,0:T(8,128)S(1)}, f32[1,1,32,512]{3,2,1,0:T(8,128)S(1)}, u32[]{:S(2)}, u32[]{:S(2)}) collective-permute-start(f32[1,1,32,512]{3,2,1,0:T(8,128)S(1)} %broadcast.116), channel_id=1, source_target_pairs={{0,4},{4,8},{8,12},{12,16},{16,20},{20,24},{24,28},{1,5},{5,9},{9,... | collective-permute-start | bytes 196616 | tf_op jit(solution)/shard_map/ppermute | solution.py:28
  11.8 7.5 %collective-permute-start.5 = (f32[1,1,32,512]{3,2,1,0:T(8,128)S(1)}, f32[1,1,32,512]{3,2,1,0:T(8,128)S(1)}, u32[]{:S(2)}, u32[]{:S(2)}) collective-permute-start(f32[1,1,32,512]{3,2,1,0:T(8,128)S(1)} %broadcast.116), channel_id=1, source_target_pairs={{4,0},{8,4},{12,8},{16,12},{20,16},{24,20},{28,24},{5,1},{9,5},{13... | collective-permute-start | bytes 196616 | tf_op jit(solution)/shard_map/ppermute | solution.py:29
  14.9 9.9 %collective-permute-start.2 = (f32[1,18,1,512]{3,2,1,0:T(1,128)S(1)}, f32[1,18,1,512]{3,2,1,0:T(1,128)S(1)}, u32[]{:S(2)}, u32[]{:S(2)}) collective-permute-start(f32[1,18,1,512]{3,2,1,0:T(1,128)S(1)} %get-tuple-element.30), channel_id=1, source_target_pairs={{0,1},{1,2},{2,3},{4,5},{5,6},{6,7},{8,9},{9,10},{10,11},{12,13},{... | collective-permute-start | bytes 110600 | tf_op jit(solution)/shard_map/ppermute | solution.py:28
  18.0 6.8 %collective-permute-start.3 = (f32[1,18,1,512]{3,2,1,0:T(1,128)S(1)}, f32[1,18,1,512]{3,2,1,0:T(1,128)S(1)}, u32[]{:S(2)}, u32[]{:S(2)}) collective-permute-start(f32[1,18,1,512]{3,2,1,0:T(1,128)S(1)} %get-tuple-element.31), channel_id=1, source_target_pairs={{1,0},{2,1},{3,2},{5,4},{6,5},{7,6},{9,8},{10,9},{11,10},{13,12},{... | collective-permute-start | bytes 110600 | tf_op jit(solution)/shard_map/ppermute | solution.py:29
  19.5 5.6 %collective-permute-start.6 = (f32[1,18,1,512]{3,2,1,0:T(1,128)S(1)}, f32[1,18,1,512]{3,2,1,0:T(1,128)S(1)}, u32[]{:S(2)}, u32[]{:S(2)}) collective-permute-start(f32[1,18,1,512]{3,2,1,0:T(1,128)S(1)} %get-tuple-element.32), channel_id=1, source_target_pairs={{0,1},{1,2},{2,3},{4,5},{5,6},{6,7},{8,9},{9,10},{10,11},{12,13},{... | collective-permute-start | bytes 110600 | tf_op jit(solution)/shard_map/ppermute | solution.py:28
  32.5 7.3 %collective-permute-start.8 = (f32[1,1,32,512]{3,2,1,0:T(8,128)S(1)}, f32[1,1,32,512]{3,2,1,0:T(8,128)S(1)}, u32[]{:S(2)}, u32[]{:S(2)}) collective-permute-start(f32[1,1,32,512]{3,2,1,0:T(8,128)S(1)} %get-tuple-element.42), channel_id=1, source_target_pairs={{0,4},{4,8},{8,12},{12,16},{16,20},{20,24},{24,28},{1,5},{5,9},{9,... | collective-permute-start | bytes 196616 | tf_op jit(solution)/shard_map/ppermute | solution.py:28
  43.5 5.8 %collective-permute-start.10 = (f32[1,18,1,512]{3,2,1,0:T(1,128)S(1)}, f32[1,18,1,512]{3,2,1,0:T(1,128)S(1)}, u32[]{:S(2)}, u32[]{:S(2)}) collective-permute-start(f32[1,18,1,512]{3,2,1,0:T(1,128)S(1)} %get-tuple-element.28), channel_id=1, source_target_pairs={{0,1},{1,2},{2,3},{4,5},{5,6},{6,7},{8,9},{9,10},{10,11},{12,13},{... | collective-permute-start | bytes 110600 | tf_op jit(solution)/shard_map/ppermute | solution.py:28
  65.4 98.1 %collective-permute-start.14 = (f32[1,18,1,512]{3,2,1,0:T(1,128)S(1)}, f32[1,18,1,512]{3,2,1,0:T(1,128)S(1)}, u32[]{:S(2)}, u32[]{:S(2)}) collective-permute-start(f32[1,18,1,512]{3,2,1,0:T(1,128)S(1)} %get-tuple-element.26), channel_id=1, source_target_pairs={{0,1},{1,2},{2,3},{4,5},{5,6},{6,7},{8,9},{9,10},{10,11},{12,13},{... | collective-permute-start | bytes 110600 | tf_op jit(solution)/shard_map/ppermute | solution.py:28
  68.0 95.6 %collective-permute-start.15 = (f32[1,18,1,512]{3,2,1,0:T(1,128)S(1)}, f32[1,18,1,512]{3,2,1,0:T(1,128)S(1)}, u32[]{:S(2)}, u32[]{:S(2)}) collective-permute-start(f32[1,18,1,512]{3,2,1,0:T(1,128)S(1)} %get-tuple-element.27), channel_id=1, source_target_pairs={{1,0},{2,1},{3,2},{5,4},{6,5},{7,6},{9,8},{10,9},{11,10},{13,12},{... | collective-permute-start | bytes 110600 | tf_op jit(solution)/shard_map/ppermute | solution.py:29
  69.3 137.1 %collective-permute-start.32 = (f32[1,1,16,256]{3,2,1,0:T(8,128)S(1)}, f32[1,1,16,256]{3,2,1,0:T(8,128)S(1)}, u32[]{:S(2)}, u32[]{:S(2)}) collective-permute-start(f32[1,1,16,256]{3,2,1,0:T(8,128)S(1)} %broadcast.119), channel_id=1, source_target_pairs={{0,4},{4,8},{8,12},{12,16},{16,20},{20,24},{24,28},{1,5},{5,9},{9,... | collective-permute-start | bytes 49160 | tf_op jit(solution)/shard_map/ppermute | solution.py:28
  71.4 136.4 %collective-permute-start.33 = (f32[1,1,16,256]{3,2,1,0:T(8,128)S(1)}, f32[1,1,16,256]{3,2,1,0:T(8,128)S(1)}, u32[]{:S(2)}, u32[]{:S(2)}) collective-permute-start(f32[1,1,16,256]{3,2,1,0:T(8,128)S(1)} %broadcast.119), channel_id=1, source_target_pairs={{4,0},{8,4},{12,8},{16,12},{20,16},{24,20},{28,24},{5,1},{9,5},{13... | collective-permute-start | bytes 49160 | tf_op jit(solution)/shard_map/ppermute | solution.py:29
  177.6 7.7 %collective-permute-start.18 = (f32[1,18,1,512]{3,2,1,0:T(1,128)S(1)}, f32[1,18,1,512]{3,2,1,0:T(1,128)S(1)}, u32[]{:S(2)}, u32[]{:S(2)}) collective-permute-start(f32[1,18,1,512]{3,2,1,0:T(1,128)S(1)} %get-tuple-element.24), channel_id=1, source_target_pairs={{0,1},{1,2},{2,3},{4,5},{5,6},{6,7},{8,9},{9,10},{10,11},{12,13},{... | collective-permute-start | bytes 110600 | tf_op jit(solution)/shard_map/ppermute | solution.py:28
  181.9 5.7 %collective-permute-start.19 = (f32[1,18,1,512]{3,2,1,0:T(1,128)S(1)}, f32[1,18,1,512]{3,2,1,0:T(1,128)S(1)}, u32[]{:S(2)}, u32[]{:S(2)}) collective-permute-start(f32[1,18,1,512]{3,2,1,0:T(1,128)S(1)} %get-tuple-element.25), channel_id=1, source_target_pairs={{1,0},{2,1},{3,2},{5,4},{6,5},{7,6},{9,8},{10,9},{11,10},{13,12},{... | collective-permute-start | bytes 110600 | tf_op jit(solution)/shard_map/ppermute | solution.py:29
  183.2 11.5 %collective-permute-start.28 = (f32[1,1,16,256]{3,2,1,0:T(8,128)S(1)}, f32[1,1,16,256]{3,2,1,0:T(8,128)S(1)}, u32[]{:S(2)}, u32[]{:S(2)}) collective-permute-start(f32[1,1,16,256]{3,2,1,0:T(8,128)S(1)} %get-tuple-element.78), channel_id=1, source_target_pairs={{0,4},{4,8},{8,12},{12,16},{16,20},{20,24},{24,28},{1,5},{5,9},{9,... | collective-permute-start | bytes 49160 | tf_op jit(solution)/shard_map/ppermute | solution.py:28
  185.4 11.2 %collective-permute-start.29 = (f32[1,1,16,256]{3,2,1,0:T(8,128)S(1)}, f32[1,1,16,256]{3,2,1,0:T(8,128)S(1)}, u32[]{:S(2)}, u32[]{:S(2)}) collective-permute-start(f32[1,1,16,256]{3,2,1,0:T(8,128)S(1)} %get-tuple-element.79), channel_id=1, source_target_pairs={{4,0},{8,4},{12,8},{16,12},{20,16},{24,20},{28,24},{5,1},{9,5},{13... | collective-permute-start | bytes 49160 | tf_op jit(solution)/shard_map/ppermute | solution.py:29
  191.2 9.6 %collective-permute-start.20 = (f32[1,1,32,512]{3,2,1,0:T(8,128)S(1)}, f32[1,1,32,512]{3,2,1,0:T(8,128)S(1)}, u32[]{:S(2)}, u32[]{:S(2)}) collective-permute-start(f32[1,1,32,512]{3,2,1,0:T(8,128)S(1)} %get-tuple-element.36), channel_id=1, source_target_pairs={{0,4},{4,8},{8,12},{12,16},{16,20},{20,24},{24,28},{1,5},{5,9},{9,... | collective-permute-start | bytes 196616 | tf_op jit(solution)/shard_map/ppermute | solution.py:28
  194.7 7.6 %collective-permute-start.21 = (f32[1,1,32,512]{3,2,1,0:T(8,128)S(1)}, f32[1,1,32,512]{3,2,1,0:T(8,128)S(1)}, u32[]{:S(2)}, u32[]{:S(2)}) collective-permute-start(f32[1,1,32,512]{3,2,1,0:T(8,128)S(1)} %get-tuple-element.37), channel_id=1, source_target_pairs={{4,0},{8,4},{12,8},{16,12},{20,16},{24,20},{28,24},{5,1},{9,5},{13... | collective-permute-start | bytes 196616 | tf_op jit(solution)/shard_map/ppermute | solution.py:29
  196.6 25.6 %collective-permute-start.30 = (f32[1,10,1,256]{3,2,1,0:T(1,128)S(1)}, f32[1,10,1,256]{3,2,1,0:T(1,128)S(1)}, u32[]{:S(2)}, u32[]{:S(2)}) collective-permute-start(f32[1,10,1,256]{3,2,1,0:T(1,128)S(1)} %get-tuple-element.62), channel_id=1, source_target_pairs={{0,1},{1,2},{2,3},{4,5},{5,6},{6,7},{8,9},{9,10},{10,11},{12,13},{... | collective-permute-start | bytes 30728 | tf_op jit(solution)/shard_map/ppermute | solution.py:28
  200.9 23.2 %collective-permute-start.31 = (f32[1,10,1,256]{3,2,1,0:T(1,128)S(1)}, f32[1,10,1,256]{3,2,1,0:T(1,128)S(1)}, u32[]{:S(2)}, u32[]{:S(2)}) collective-permute-start(f32[1,10,1,256]{3,2,1,0:T(1,128)S(1)} %get-tuple-element.63), channel_id=1, source_target_pairs={{1,0},{2,1},{3,2},{5,4},{6,5},{7,6},{9,8},{10,9},{11,10},{13,12},{... | collective-permute-start | bytes 30728 | tf_op jit(solution)/shard_map/ppermute | solution.py:29
  202.3 10.5 %collective-permute-start.22 = (f32[1,18,1,512]{3,2,1,0:T(1,128)S(1)}, f32[1,18,1,512]{3,2,1,0:T(1,128)S(1)}, u32[]{:S(2)}, u32[]{:S(2)}) collective-permute-start(f32[1,18,1,512]{3,2,1,0:T(1,128)S(1)} %get-tuple-element.22), channel_id=1, source_target_pairs={{0,1},{1,2},{2,3},{4,5},{5,6},{6,7},{8,9},{9,10},{10,11},{12,13},{... | collective-permute-start | bytes 110600 | tf_op jit(solution)/shard_map/ppermute | solution.py:28
  206.4 7.7 %collective-permute-start.23 = (f32[1,18,1,512]{3,2,1,0:T(1,128)S(1)}, f32[1,18,1,512]{3,2,1,0:T(1,128)S(1)}, u32[]{:S(2)}, u32[]{:S(2)}) collective-permute-start(f32[1,18,1,512]{3,2,1,0:T(1,128)S(1)} %get-tuple-element.23), channel_id=1, source_target_pairs={{1,0},{2,1},{3,2},{5,4},{6,5},{7,6},{9,8},{10,9},{11,10},{13,12},{... | collective-permute-start | bytes 110600 | tf_op jit(solution)/shard_map/ppermute | solution.py:29
  207.9 26.4 %collective-permute-start.34 = (f32[1,10,1,256]{3,2,1,0:T(1,128)S(1)}, f32[1,10,1,256]{3,2,1,0:T(1,128)S(1)}, u32[]{:S(2)}, u32[]{:S(2)}) collective-permute-start(f32[1,10,1,256]{3,2,1,0:T(1,128)S(1)} %get-tuple-element.64), channel_id=1, source_target_pairs={{0,1},{1,2},{2,3},{4,5},{5,6},{6,7},{8,9},{9,10},{10,11},{12,13},{... | collective-permute-start | bytes 30728 | tf_op jit(solution)/shard_map/ppermute | solution.py:28
  212.8 21.5 %collective-permute-start.35 = (f32[1,10,1,256]{3,2,1,0:T(1,128)S(1)}, f32[1,10,1,256]{3,2,1,0:T(1,128)S(1)}, u32[]{:S(2)}, u32[]{:S(2)}) collective-permute-start(f32[1,10,1,256]{3,2,1,0:T(1,128)S(1)} %get-tuple-element.65), channel_id=1, source_target_pairs={{1,0},{2,1},{3,2},{5,4},{6,5},{7,6},{9,8},{10,9},{11,10},{13,12},{... | collective-permute-start | bytes 30728 | tf_op jit(solution)/shard_map/ppermute | solution.py:29
  217.4 6.8 %collective-permute-start.24 = (f32[1,1,32,512]{3,2,1,0:T(8,128)S(1)}, f32[1,1,32,512]{3,2,1,0:T(8,128)S(1)}, u32[]{:S(2)}, u32[]{:S(2)}) collective-permute-start(f32[1,1,32,512]{3,2,1,0:T(8,128)S(1)} %get-tuple-element.34), channel_id=1, source_target_pairs={{0,4},{4,8},{8,12},{12,16},{16,20},{20,24},{24,28},{1,5},{5,9},{9,... | collective-permute-start | bytes 196616 | tf_op jit(solution)/shard_map/ppermute | solution.py:28
  227.8 6.5 %collective-permute-start.26 = (f32[1,18,1,512]{3,2,1,0:T(1,128)S(1)}, f32[1,18,1,512]{3,2,1,0:T(1,128)S(1)}, u32[]{:S(2)}, u32[]{:S(2)}) collective-permute-start(f32[1,18,1,512]{3,2,1,0:T(1,128)S(1)} %get-tuple-element.20), channel_id=1, source_target_pairs={{0,1},{1,2},{2,3},{4,5},{5,6},{6,7},{8,9},{9,10},{10,11},{12,13},{... | collective-permute-start | bytes 110600 | tf_op jit(solution)/shard_map/ppermute | solution.py:28
  233.0 5.9 %collective-permute-start.27 = (f32[1,18,1,512]{3,2,1,0:T(1,128)S(1)}, f32[1,18,1,512]{3,2,1,0:T(1,128)S(1)}, u32[]{:S(2)}, u32[]{:S(2)}) collective-permute-start(f32[1,18,1,512]{3,2,1,0:T(1,128)S(1)} %get-tuple-element.21), channel_id=1, source_target_pairs={{1,0},{2,1},{3,2},{5,4},{6,5},{7,6},{9,8},{10,9},{11,10},{13,12},{... | collective-permute-start | bytes 110600 | tf_op jit(solution)/shard_map/ppermute | solution.py:29
  262.6 5.8 %collective-permute-start.38 = (f32[1,10,1,256]{3,2,1,0:T(1,128)S(1)}, f32[1,10,1,256]{3,2,1,0:T(1,128)S(1)}, u32[]{:S(2)}, u32[]{:S(2)}) collective-permute-start(f32[1,10,1,256]{3,2,1,0:T(1,128)S(1)} %get-tuple-element.60), channel_id=1, source_target_pairs={{0,1},{1,2},{2,3},{4,5},{5,6},{6,7},{8,9},{9,10},{10,11},{12,13},{... | collective-permute-start | bytes 30728 | tf_op jit(solution)/shard_map/ppermute | solution.py:28
  280.4 22.2 %collective-permute-start.42 = (f32[1,10,1,256]{3,2,1,0:T(1,128)S(1)}, f32[1,10,1,256]{3,2,1,0:T(1,128)S(1)}, u32[]{:S(2)}, u32[]{:S(2)}) collective-permute-start(f32[1,10,1,256]{3,2,1,0:T(1,128)S(1)} %get-tuple-element.58), channel_id=1, source_target_pairs={{0,1},{1,2},{2,3},{4,5},{5,6},{6,7},{8,9},{9,10},{10,11},{12,13},{... | collective-permute-start | bytes 30728 | tf_op jit(solution)/shard_map/ppermute | solution.py:28
  282.9 19.7 %collective-permute-start.43 = (f32[1,10,1,256]{3,2,1,0:T(1,128)S(1)}, f32[1,10,1,256]{3,2,1,0:T(1,128)S(1)}, u32[]{:S(2)}, u32[]{:S(2)}) collective-permute-start(f32[1,10,1,256]{3,2,1,0:T(1,128)S(1)} %get-tuple-element.59), channel_id=1, source_target_pairs={{1,0},{2,1},{3,2},{5,4},{6,5},{7,6},{9,8},{10,9},{11,10},{13,12},{... | collective-permute-start | bytes 30728 | tf_op jit(solution)/shard_map/ppermute | solution.py:29
  284.2 52.7 %collective-permute-start.60 = (f32[1,1,8,128]{3,2,1,0:T(8,128)S(1)}, f32[1,1,8,128]{3,2,1,0:T(8,128)S(1)}, u32[]{:S(2)}, u32[]{:S(2)}) collective-permute-start(f32[1,1,8,128]{3,2,1,0:T(8,128)S(1)} %broadcast.122), channel_id=1, source_target_pairs={{0,4},{4,8},{8,12},{12,16},{16,20},{20,24},{24,28},{1,5},{5,9},{9,... | collective-permute-start | bytes 12296 | tf_op jit(solution)/shard_map/ppermute | solution.py:28
  286.4 51.8 %collective-permute-start.61 = (f32[1,1,8,128]{3,2,1,0:T(8,128)S(1)}, f32[1,1,8,128]{3,2,1,0:T(8,128)S(1)}, u32[]{:S(2)}, u32[]{:S(2)}) collective-permute-start(f32[1,1,8,128]{3,2,1,0:T(8,128)S(1)} %broadcast.122), channel_id=1, source_target_pairs={{4,0},{8,4},{12,8},{16,12},{20,16},{24,20},{28,24},{5,1},{9,5},{13... | collective-permute-start | bytes 12296 | tf_op jit(solution)/shard_map/ppermute | solution.py:29
  311.5 7.8 %collective-permute-start.46 = (f32[1,10,1,256]{3,2,1,0:T(1,128)S(1)}, f32[1,10,1,256]{3,2,1,0:T(1,128)S(1)}, u32[]{:S(2)}, u32[]{:S(2)}) collective-permute-start(f32[1,10,1,256]{3,2,1,0:T(1,128)S(1)} %get-tuple-element.56), channel_id=1, source_target_pairs={{0,1},{1,2},{2,3},{4,5},{5,6},{6,7},{8,9},{9,10},{10,11},{12,13},{... | collective-permute-start | bytes 30728 | tf_op jit(solution)/shard_map/ppermute | solution.py:28
  315.8 5.7 %collective-permute-start.47 = (f32[1,10,1,256]{3,2,1,0:T(1,128)S(1)}, f32[1,10,1,256]{3,2,1,0:T(1,128)S(1)}, u32[]{:S(2)}, u32[]{:S(2)}) collective-permute-start(f32[1,10,1,256]{3,2,1,0:T(1,128)S(1)} %get-tuple-element.57), channel_id=1, source_target_pairs={{1,0},{2,1},{3,2},{5,4},{6,5},{7,6},{9,8},{10,9},{11,10},{13,12},{... | collective-permute-start | bytes 30728 | tf_op jit(solution)/shard_map/ppermute | solution.py:29
  317.1 8.2 %collective-permute-start.56 = (f32[1,1,8,128]{3,2,1,0:T(8,128)S(1)}, f32[1,1,8,128]{3,2,1,0:T(8,128)S(1)}, u32[]{:S(2)}, u32[]{:S(2)}) collective-permute-start(f32[1,1,8,128]{3,2,1,0:T(8,128)S(1)} %get-tuple-element.102), channel_id=1, source_target_pairs={{0,4},{4,8},{8,12},{12,16},{16,20},{20,24},{24,28},{1,5},{5,9},{9,... | collective-permute-start | bytes 12296 | tf_op jit(solution)/shard_map/ppermute | solution.py:28
  319.3 7.9 %collective-permute-start.57 = (f32[1,1,8,128]{3,2,1,0:T(8,128)S(1)}, f32[1,1,8,128]{3,2,1,0:T(8,128)S(1)}, u32[]{:S(2)}, u32[]{:S(2)}) collective-permute-start(f32[1,1,8,128]{3,2,1,0:T(8,128)S(1)} %get-tuple-element.103), channel_id=1, source_target_pairs={{4,0},{8,4},{12,8},{16,12},{20,16},{24,20},{28,24},{5,1},{9,5},{13... | collective-permute-start | bytes 12296 | tf_op jit(solution)/shard_map/ppermute | solution.py:29
  321.8 9.7 %collective-permute-start.48 = (f32[1,1,16,256]{3,2,1,0:T(8,128)S(1)}, f32[1,1,16,256]{3,2,1,0:T(8,128)S(1)}, u32[]{:S(2)}, u32[]{:S(2)}) collective-permute-start(f32[1,1,16,256]{3,2,1,0:T(8,128)S(1)} %get-tuple-element.68), channel_id=1, source_target_pairs={{0,4},{4,8},{8,12},{12,16},{16,20},{20,24},{24,28},{1,5},{5,9},{9,... | collective-permute-start | bytes 49160 | tf_op jit(solution)/shard_map/ppermute | solution.py:28
  325.3 7.5 %collective-permute-start.49 = (f32[1,1,16,256]{3,2,1,0:T(8,128)S(1)}, f32[1,1,16,256]{3,2,1,0:T(8,128)S(1)}, u32[]{:S(2)}, u32[]{:S(2)}) collective-permute-start(f32[1,1,16,256]{3,2,1,0:T(8,128)S(1)} %get-tuple-element.69), channel_id=1, source_target_pairs={{4,0},{8,4},{12,8},{16,12},{20,16},{24,20},{28,24},{5,1},{9,5},{13... | collective-permute-start | bytes 49160 | tf_op jit(solution)/shard_map/ppermute | solution.py:29
  327.2 22.3 %collective-permute-start.58 = (f32[1,6,1,128]{3,2,1,0:T(1,128)S(1)}, f32[1,6,1,128]{3,2,1,0:T(1,128)S(1)}, u32[]{:S(2)}, u32[]{:S(2)}) collective-permute-start(f32[1,6,1,128]{3,2,1,0:T(1,128)S(1)} %get-tuple-element.90), channel_id=1, source_target_pairs={{0,1},{1,2},{2,3},{4,5},{5,6},{6,7},{8,9},{9,10},{10,11},{12,13},{... | collective-permute-start | bytes 9224 | tf_op jit(solution)/shard_map/ppermute | solution.py:28
  331.5 20.0 %collective-permute-start.59 = (f32[1,6,1,128]{3,2,1,0:T(1,128)S(1)}, f32[1,6,1,128]{3,2,1,0:T(1,128)S(1)}, u32[]{:S(2)}, u32[]{:S(2)}) collective-permute-start(f32[1,6,1,128]{3,2,1,0:T(1,128)S(1)} %get-tuple-element.91), channel_id=1, source_target_pairs={{1,0},{2,1},{3,2},{5,4},{6,5},{7,6},{9,8},{10,9},{11,10},{13,12},{... | collective-permute-start | bytes 9224 | tf_op jit(solution)/shard_map/ppermute | solution.py:29
  332.8 10.3 %collective-permute-start.50 = (f32[1,10,1,256]{3,2,1,0:T(1,128)S(1)}, f32[1,10,1,256]{3,2,1,0:T(1,128)S(1)}, u32[]{:S(2)}, u32[]{:S(2)}) collective-permute-start(f32[1,10,1,256]{3,2,1,0:T(1,128)S(1)} %get-tuple-element.54), channel_id=1, source_target_pairs={{0,1},{1,2},{2,3},{4,5},{5,6},{6,7},{8,9},{9,10},{10,11},{12,13},{... | collective-permute-start | bytes 30728 | tf_op jit(solution)/shard_map/ppermute | solution.py:28
  336.9 7.5 %collective-permute-start.51 = (f32[1,10,1,256]{3,2,1,0:T(1,128)S(1)}, f32[1,10,1,256]{3,2,1,0:T(1,128)S(1)}, u32[]{:S(2)}, u32[]{:S(2)}) collective-permute-start(f32[1,10,1,256]{3,2,1,0:T(1,128)S(1)} %get-tuple-element.55), channel_id=1, source_target_pairs={{1,0},{2,1},{3,2},{5,4},{6,5},{7,6},{9,8},{10,9},{11,10},{13,12},{... | collective-permute-start | bytes 30728 | tf_op jit(solution)/shard_map/ppermute | solution.py:29
  338.3 22.9 %collective-permute-start.62 = (f32[1,6,1,128]{3,2,1,0:T(1,128)S(1)}, f32[1,6,1,128]{3,2,1,0:T(1,128)S(1)}, u32[]{:S(2)}, u32[]{:S(2)}) collective-permute-start(f32[1,6,1,128]{3,2,1,0:T(1,128)S(1)} %get-tuple-element.92), channel_id=1, source_target_pairs={{0,1},{1,2},{2,3},{4,5},{5,6},{6,7},{8,9},{9,10},{10,11},{12,13},{... | collective-permute-start | bytes 9224 | tf_op jit(solution)/shard_map/ppermute | solution.py:28
  343.2 18.0 %collective-permute-start.63 = (f32[1,6,1,128]{3,2,1,0:T(1,128)S(1)}, f32[1,6,1,128]{3,2,1,0:T(1,128)S(1)}, u32[]{:S(2)}, u32[]{:S(2)}) collective-permute-start(f32[1,6,1,128]{3,2,1,0:T(1,128)S(1)} %get-tuple-element.93), channel_id=1, source_target_pairs={{1,0},{2,1},{3,2},{5,4},{6,5},{7,6},{9,8},{10,9},{11,10},{13,12},{... | collective-permute-start | bytes 9224 | tf_op jit(solution)/shard_map/ppermute | solution.py:29
  344.8 6.8 %collective-permute-start.52 = (f32[1,1,16,256]{3,2,1,0:T(8,128)S(1)}, f32[1,1,16,256]{3,2,1,0:T(8,128)S(1)}, u32[]{:S(2)}, u32[]{:S(2)}) collective-permute-start(f32[1,1,16,256]{3,2,1,0:T(8,128)S(1)} %get-tuple-element.66), channel_id=1, source_target_pairs={{0,4},{4,8},{8,12},{12,16},{16,20},{20,24},{24,28},{1,5},{5,9},{9,... | collective-permute-start | bytes 49160 | tf_op jit(solution)/shard_map/ppermute | solution.py:28
  354.6 6.5 %collective-permute-start.54 = (f32[1,10,1,256]{3,2,1,0:T(1,128)S(1)}, f32[1,10,1,256]{3,2,1,0:T(1,128)S(1)}, u32[]{:S(2)}, u32[]{:S(2)}) collective-permute-start(f32[1,10,1,256]{3,2,1,0:T(1,128)S(1)} %get-tuple-element.52), channel_id=1, source_target_pairs={{0,1},{1,2},{2,3},{4,5},{5,6},{6,7},{8,9},{9,10},{10,11},{12,13},{... | collective-permute-start | bytes 30728 | tf_op jit(solution)/shard_map/ppermute | solution.py:28
  376.0 5.8 %collective-permute-start.66 = (f32[1,6,1,128]{3,2,1,0:T(1,128)S(1)}, f32[1,6,1,128]{3,2,1,0:T(1,128)S(1)}, u32[]{:S(2)}, u32[]{:S(2)}) collective-permute-start(f32[1,6,1,128]{3,2,1,0:T(1,128)S(1)} %get-tuple-element.88), channel_id=1, source_target_pairs={{0,1},{1,2},{2,3},{4,5},{5,6},{6,7},{8,9},{9,10},{10,11},{12,13},{... | collective-permute-start | bytes 9224 | tf_op jit(solution)/shard_map/ppermute | solution.py:28
  (40 other events, 260.3 us)
where the time goes:
time: 434 us; the launch traced here: 432 us
  starting transfers between devices  213 us (49%)
  local copies, waits for them, and re-layouts  96.7 us (22%)
  waiting for transfers between devices  70.1 us (16%)
  other arithmetic  49.5 us (11%)
    ppermute x40, starting transfers between devices, extended(): before = lax.ppermute(last, axis, up)  147 us
    ppermute x40, waiting for transfers between devices, extended(): after = lax.ppermute(initial, axis, down)  70 us
    reshape x1, local copies, waits for them, and re-layouts, block_mean(): values.reshape((grid_shape[0] // 2, 2, grid_shape[1] // 2, 2, grid_shape[...  69.1 us
    ppermute x40, starting transfers between devices, extended(): after = lax.ppermute(initial, axis, down)  65.5 us
    reduce_sum x2, other arithmetic, block_mean(): return jnp.sum(blocks, axis=(1, 3, 5)) * 0.125  24.8 us
    select_n x12, other arithmetic, body(): solution = jnp.where(colour, (source + term) / diagonal, solution)  15 us
    mul x1, local copies, waits for them, and re-layouts, block_mean(): return jnp.sum(blocks, axis=(1, 3, 5)) * 0.125  9.79 us
  transfers between devices with their start and end apart: 80, of which 21 were waited for; matrix products, arithmetic and copies ran while one was open for 27% of the time, Pallas kernels for 0%

commit v1 on v0

v1 whole, which is shorter than its diff:
```python
import jax
import jax.numpy as jnp
from jax import lax
from jax.experimental import pallas as pl
from jax.experimental.pallas import tpu as pltpu
from jax.sharding import PartitionSpec as P

F32 = jnp.float32
HP = 3
HIGHEST = lax.Precision.HIGHEST


def tiled(tile, rows, lanes):
    wide = jnp.concatenate([tile] * (lanes // 128), axis=1)
    return jnp.concatenate([wide] * (rows // 8), axis=0)


def even_mask(rows, lanes):
    row = lax.broadcasted_iota(jnp.int32, (8, 128), 0)
    lane = lax.broadcasted_iota(jnp.int32, (8, 128), 1)
    return tiled((row + lane) & 1, rows, lanes) == 0


def pick(mask, a, b):
    return jnp.where(mask, a, b)


def row_index(lanes):
    return lax.broadcasted_iota(jnp.int32, (8, lanes), 0)


def lane_edge(value, at_start):
    lanes = value.shape[1]
    lane = lax.broadcasted_iota(jnp.int32, (value.shape[0], 128), 1)
    if at_start:
        edge = pick(lane == 0, 0.0, value[:, :128])
        return edge if lanes == 128 else jnp.concatenate([edge, value[:, 128:]], axis=1)
    edge = pick(lane == 127, 0.0, value[:, lanes - 128 :])
    return edge if lanes == 128 else jnp.concatenate([value[:, : lanes - 128], edge], axis=1)


def neighbours(ref, colour, p, pairs, even):
    other = 1 - colour
    x = ref[other, p]
    below = ref[other, jnp.maximum(p - 1, 0)]
    above = ref[other, jnp.minimum(p + 1, pairs - 1)]
    far = pick(even, below, above) if colour == 0 else pick(even, above, below)
    rows, lanes = x.shape
    return (
        x,
        far,
        pltpu.roll(x, 1, 0),
        pltpu.roll(x, rows - 1, 0),
        pltpu.roll(x, 1, 1),
        pltpu.roll(x, lanes - 1, 1),
    )


def span(own, layers):
    extra = (layers + 1) // 2
    return HP - extra, HP + own + extra


def relax_level(K, S, U, W, D, R, own, depth, residual_layers):
    _, pairs, rows, lanes = K.shape
    even = even_mask(rows, lanes)

    def setup(colour, layers):
        first, last = span(own, layers)

        def step(p, carry):
            near = list(neighbours(K, colour, p, pairs, even))
            near[4] = lane_edge(near[4], True)
            near[5] = lane_edge(near[5], False)
            centre = K[colour, p]
            total = near[0]
            for value in near[1:]:
                total = total + value
            diag = 3.0 * centre + 0.5 * total
            inverse = pick(centre > 0.0, 1.0 / diag, 0.0)
            half = 0.5 * inverse
            for i, value in enumerate(near):
                weight = (centre + value) * half
                if i == 4:
                    weight = lane_edge(weight, True)
                if i == 5:
                    weight = lane_edge(weight, False)
                W[colour * 6 + i, p] = weight
            D[colour, p] = diag
            start = S[colour, p] * inverse
            S[colour, p] = start
            if colour == 0:
                U[0, p] = start
            return carry

        lax.fori_loop(first, last, step, 0)
        zero = jnp.zeros((rows, lanes), F32)
        for p in list(range(first)) + list(range(last, pairs)):
            U[colour, p] = zero

    def relaxed(colour, p):
        near = neighbours(U, colour, p, pairs, even)
        total = S[colour, p]
        for i, value in enumerate(near):
            total = total + W[colour * 6 + i, p] * value
        return total

    def half_sweep(colour, layers):
        first, last = span(own, layers)

        def step(p, carry):
            U[colour, p] = relaxed(colour, p)
            return carry

        lax.fori_loop(first, last, step, 0)

    setup(0, depth)
    setup(1, depth - 1)
    half_sweep(1, depth - 1)
    half_sweep(0, depth - 2)
    half_sweep(1, depth - 3)
    first, last = span(own, residual_layers)

    def left(p, carry):
        for colour in (0, 1):
            rest = D[colour, p] * (relaxed(colour, p) - U[colour, p])
            R[colour, p - first + R_PAD[residual_layers]] = rest[8 : rows - 8]
        return carry

    lax.fori_loop(first, last, left, 0)


R_PAD = {0: 2, 1: 0}


def store_field(U, out, own, even):
    rows = U.shape[2]
    for p in range(own):
        red = U[0, HP + p, 8 : rows - 8]
        black = U[1, HP + p, 8 : rows - 8]
        out[2 * p] = pick(even, red, black)
        out[2 * p + 1] = pick(even, black, red)


def restrict_planes(R, at, even):
    red, black = R[0, at], R[1, at]
    odd_below = pick(even, R[1, at - 1], R[0, at - 1])
    even_above = pick(even, R[0, at + 1], R[1, at + 1])
    return (3.0 * (red + black) + (odd_below + even_above)) * 0.125


def row_restriction(rows):
    half = rows // 2
    j = lax.broadcasted_iota(jnp.int32, (half + 8, rows), 0)
    m = lax.broadcasted_iota(jnp.int32, (half + 8, rows), 1)
    inner = (m == 2 * j) | (m == 2 * j + 1)
    outer = (m == 2 * j - 1) | (m == 2 * j + 2)
    main = pick(inner, 0.375, pick(outer, 0.125, 0.0))
    ends = pick(((j == half) & (m == 0)) | ((j == half + 1) & (m == rows - 1)), 0.125, 0.0)
    return pick(j < half, main, ends).astype(F32)


def row_sum(rows):
    j = 2 * lax.broadcasted_iota(jnp.int32, (rows // 2, rows), 0)
    m = lax.broadcasted_iota(jnp.int32, (rows // 2, rows), 1)
    return pick((m == j) | (m == j + 1), 1.0, 0.0).astype(F32)


def product(a, b):
    return jnp.dot(a, b, precision=HIGHEST, preferred_element_type=F32)


def lane_restriction(lanes):
    m = lax.broadcasted_iota(jnp.int32, (lanes, lanes // 2), 0)
    i = 2 * lax.broadcasted_iota(jnp.int32, (lanes, lanes // 2), 1)
    inner = (m == i) | (m == i + 1)
    outer = (m == i - 1) | (m == i + 2)
    return pick(inner, 1.5, pick(outer, 0.5, 0.0)).astype(F32)


def lane_mean(lanes):
    m = lax.broadcasted_iota(jnp.int32, (lanes, lanes // 2), 0)
    i = 2 * lax.broadcasted_iota(jnp.int32, (lanes, lanes // 2), 1)
    return pick((m == i) | (m == i + 1), 0.125, 0.0).astype(F32)


def coarsen(K, R, Z, Zk, even_own, own, s_pairs, r_pad, k_pairs):
    rows, lanes = R.shape[2:]
    half = rows // 2
    block = half + 8
    for q, pair in enumerate(s_pairs):
        Z[block * q : block * (q + 1)] = product(
            row_restriction(rows), restrict_planes(R, pair + r_pad, even_own))
    for q, pair in enumerate(k_pairs):
        total = K[0, HP + pair, 8 : 8 + rows] + K[1, HP + pair, 8 : 8 + rows]
        Zk[half * q : half * (q + 1)] = product(row_sum(rows), total)
    source = product(Z[...], lane_restriction(lanes))
    mean = product(Zk[...], lane_mean(lanes))
    return source, mean, half, len(s_pairs)


def row_messages(source, mean, half, count, s_at, k_at, planes, to_low, to_high):
    lanes = source.shape[1]
    block = half + 8
    for q in range(planes):
        low, high = [], []
        if q - s_at in range(count):
            at = block * (q - s_at)
            low += [source[at + half : at + half + 1], source[at : at + 4]]
            high += [source[at + half + 1 : at + half + 2], source[at + half - 4 : at + half]]
            pad = [jnp.zeros((3, lanes), F32)]
        else:
            pad = [jnp.zeros((8, lanes), F32)]
        low, high = low + pad, high + pad
        if q - k_at in range(mean.shape[0] // half):
            at = half * (q - k_at)
            low += [mean[at : at + 5]]
            high += [mean[at + half - 5 : at + half]]
            pad = [jnp.zeros((3, lanes), F32)]
        else:
            pad = [jnp.zeros((8, lanes), F32)]
        to_low[q] = jnp.concatenate(low + pad, axis=0)
        to_high[q] = jnp.concatenate(high + pad, axis=0)


def pack_rows_kernel(s_low, s_high, k_low, k_high, to_low, to_high):
    lanes = s_low.shape[2]
    even = even_mask(8, lanes)

    def step(p, carry):
        def pair(ref):
            a, b = ref[2 * p], ref[2 * p + 1]
            return pick(even, a, b), pick(even, b, a)

        sr, sb = pair(s_low)
        kr, kb = pair(k_low)
        to_low[0, p] = jnp.concatenate([kr[0:4], sr[0:4]], axis=0)
        to_low[1, p] = jnp.concatenate([kb[0:5], sb[0:3]], axis=0)
        sr, sb = pair(s_high)
        kr, kb = pair(k_high)
        to_high[0, p] = jnp.concatenate([kr[4:8], sr[4:8]], axis=0)
        to_high[1, p] = jnp.concatenate([kb[3:8], sb[5:8]], axis=0)
        return carry

    lax.fori_loop(0, s_low.shape[0] // 2, step, 0)


def pack_planes_kernel(s, k, from_low, from_high, to_down, to_up):
    planes, rows, lanes = s.shape
    even = even_mask(8, lanes)

    def edges(p, of_k):
        lr, lb = from_low[0, p], from_low[1, p]
        hr, hb = from_high[0, p], from_high[1, p]
        if of_k:
            red = jnp.concatenate([lr[0:4], hr[0:4]], axis=0)
            black = jnp.concatenate([lb[1:5], hb[0:4]], axis=0)
        else:
            red = jnp.concatenate([lr[4:8], hr[4:8]], axis=0)
            black = jnp.concatenate([lb[4:8], hb[5:8], hb[7:8]], axis=0)
        return pick(even, red, black), pick(even, black, red)

    def put(out, at, ref, plane, of_k):
        out[at, 0:rows] = ref[plane]
        out[at, rows : rows + 8] = edges(plane // 2, of_k)[plane % 2]

    for j in range(4):
        put(to_down, j, s, j, False)
        put(to_up, j, s, planes - 4 + j, False)
    for j in range(5):
        put(to_down, 4 + j, k, j, True)
        put(to_up, 4 + j, k, planes - 5 + j, True)


def fine_kernel(s, k, from_low, from_high, from_down, from_up,
                field, source_out, mean_out, to_low, to_high,
                K, S, U, W, D, R, Z, Zk):
    planes, rows, lanes = s.shape
    own = planes // 2
    wide = rows + 16
    even = even_mask(8, lanes)
    even_own = even_mask(rows, lanes)
    row = row_index(lanes)
    zero8 = jnp.zeros((8, lanes), F32)
    zero = jnp.zeros((wide, lanes), F32)

    def fill(p, carry):
        at = HP + p
        lr, lb = from_low[0, p], from_low[1, p]
        hr, hb = from_high[0, p], from_high[1, p]
        K[0, at, 0:8] = pick(row >= 4, pltpu.roll(lr, 4, 0), 0.0)
        K[1, at, 0:8] = pick(row >= 3, pltpu.roll(lb, 3, 0), 0.0)
        S[0, at, 0:8] = pick(row >= 4, lr, 0.0)
        S[1, at, 0:8] = pick(row >= 5, lb, 0.0)
        K[0, at, 8 + rows : wide] = pick(row < 4, hr, 0.0)
        K[1, at, 8 + rows : wide] = pick(row < 5, hb, 0.0)
        S[0, at, 8 + rows : wide] = pick(row < 4, pltpu.roll(hr, 4, 0), 0.0)
        S[1, at, 8 + rows : wide] = pick(row < 3, pltpu.roll(hb, 3, 0), 0.0)
        for ref, to in ((s, S), (k, K)):
            a, b = ref[2 * p], ref[2 * p + 1]
            to[0, at, 8 : 8 + rows] = pick(even_own, a, b)
            to[1, at, 8 : 8 + rows] = pick(even_own, b, a)
        return carry

    lax.fori_loop(0, own, fill, 0)

    def halo(to, at, ref, first, second):
        def part(rows_of):
            a = zero8 if first is None else rows_of(first)
            b = zero8 if second is None else rows_of(second)
            return a, b

        def put(start, a, b, mask):
            to[0, at, start : start + a.shape[0]] = pick(mask, a, b)
            to[1, at, start : start + a.shape[0]] = pick(mask, b, a)

        a, b = part(lambda j: pick(row >= 4, pltpu.roll(ref[j, rows : rows + 8], 4, 0), 0.0))
        put(0, a, b, even)
        a, b = part(lambda j: pick(row < 4, pltpu.roll(ref[j, rows : rows + 8], 4, 0), 0.0))
        put(8 + rows, a, b, even)
        big = jnp.zeros((rows, lanes), F32)
        a = big if first is None else ref[first, 0:rows]
        b = big if second is None else ref[second, 0:rows]
        put(8, a, b, even_own)

    halo(S, 1, from_down, 0, 1)
    halo(S, 2, from_down, 2, 3)
    halo(K, 0, from_down, None, 4)
    halo(K, 1, from_down, 5, 6)
    halo(K, 2, from_down, 7, 8)
    halo(S, HP + own, from_up, 0, 1)
    halo(S, HP + own + 1, from_up, 2, 3)
    halo(K, HP + own, from_up, 4, 5)
    halo(K, HP + own + 1, from_up, 6, 7)
    halo(K, HP + own + 2, from_up, 8, None)
    relax_level(K, S, U, W, D, R, own, 4, 0)
    store_field(U, field, own, even_own)
    zero = jnp.zeros((rows, lanes), F32)
    for colour in (0, 1):
        for at in (0, 1, own + 2, own + 3):
            R[colour, at] = zero
    source, mean, half, count = coarsen(
        K, R, Z, Zk, even_own, own, range(-1, own + 1), 2, range(own))
    for q in range(count):
        at = (half + 8) * q
        source_out[q] = source[at : at + half]
    for q in range(own):
        mean_out[q] = mean[half * q : half * (q + 1)]
    row_messages(source, mean, half, count, 0, 1, own + 2, to_low, to_high)


def widen(own_rows, mine_low, mine_high, got_low, got_high):
    rows, lanes = own_rows.shape
    row = row_index(lanes)
    low = pltpu.roll(got_low[0:8], 3, 0)
    low = pick(row >= 4, low, 0.0) + pick(row == 7, pltpu.roll(mine_low[0:8], 7, 0), 0.0)
    high = pick(row < 4, pltpu.roll(got_high[0:8], 7, 0), 0.0)
    high = high + pick(row == 0, mine_high[0:8], 0.0)
    first = pick(row == 0, got_low[0:8], 0.0)
    last = pick(row == 7, pltpu.roll(got_high[0:8], 7, 0), 0.0)
    if rows == 8:
        return jnp.concatenate([low, own_rows + first + last, high], axis=0)
    return jnp.concatenate(
        [low, own_rows[0:8] + first, own_rows[8 : rows - 8], own_rows[rows - 8 :] + last, high]
        if rows > 16 else
        [low, own_rows[0:8] + first, own_rows[8:16] + last, high], axis=0)


def widen_mean(own_rows, got_low, got_high):
    rows, lanes = own_rows.shape
    row = row_index(lanes)
    low = pick(row >= 3, pltpu.roll(got_low[8:16], 3, 0), 0.0)
    high = pick(row < 5, got_high[8:16], 0.0)
    return jnp.concatenate([low, own_rows, high], axis=0)


def middle_planes_kernel(source, mean, to_low, to_high, from_low, from_high,
                         S, K, to_down, to_up):
    planes = mean.shape[0]
    for q in range(planes + 2):
        value = widen(source[q], to_low[q], to_high[q], from_low[q], from_high[q])
        S[q] = value
        if q < 6:
            to_down[q] = value
        if q >= planes - 4:
            to_up[q - planes + 4] = value
    for q in range(planes):
        value = widen_mean(mean[q], from_low[q + 1], from_high[q + 1])
        K[q] = value
        if q < 6:
            to_down[6 + q] = value
        if q >= planes - 6:
            to_up[12 + q - planes] = value


def middle_kernel(s, k, from_down, from_up,
                  field, source_out, mean_out, to_low, to_high,
                  K, S, U, W, D, R, Z, Zk):
    planes, wide, lanes = k.shape
    own = planes // 2
    rows = wide - 16
    even = even_mask(wide, lanes)
    even_own = even_mask(rows, lanes)
    zero = jnp.zeros((wide, lanes), F32)

    def source_plane(i):
        if i < -5 or i > planes + 4:
            return zero
        if i < -1:
            return from_down[i + 5]
        if i == -1:
            return from_down[4] + s[0]
        if i == 0:
            return s[1] + from_down[5]
        if i < planes - 1:
            return s[i + 1]
        if i == planes - 1:
            return s[planes] + from_up[0]
        if i == planes:
            return from_up[1] + s[planes + 1]
        return from_up[i - planes + 1]

    def mean_plane(i):
        if i < 0:
            return from_down[12 + i]
        if i < planes:
            return k[i]
        return from_up[6 + i - planes]

    for p in range(-HP, own + HP):
        for to, plane in ((S, source_plane), (K, mean_plane)):
            a, b = plane(2 * p), plane(2 * p + 1)
            to[0, HP + p] = pick(even, a, b)
            to[1, HP + p] = pick(even, b, a)
    relax_level(K, S, U, W, D, R, own, 5, 1)
    store_field(U, field, own, even_own)
    source, mean, half, count = coarsen(
        K, R, Z, Zk, even_own, own, range(own), 1, range(-1, own + 1))
    for q in range(count):
        at = (half + 8) * q
        source_out[q] = source[at : at + half]
    for q in range(own + 2):
        mean_out[q] = mean[half * q : half * (q + 1)]
    row_messages(source, mean, half, count, 1, 0, own + 2, to_low, to_high)


def coarse_planes_kernel(source, mean, to_low, to_high, from_low, from_high,
                         S, K, to_down, to_up):
    planes = source.shape[0]
    for q in range(planes):
        value = widen(source[q], to_low[q + 1], to_high[q + 1], from_low[q + 1], from_high[q + 1])
        S[q] = value
        if q < 4:
            to_down[q] = value
        if q >= planes - 4:
            to_up[q - planes + 4] = value
    for q in range(planes + 2):
        value = widen_mean(mean[q], from_low[q], from_high[q])
        if 1 <= q <= planes:
            K[q - 1] = value
        if 1 <= q <= 5:
            to_down[3 + q] = value
        if planes - 4 <= q <= planes:
            to_up[8 + q - planes] = value


def coarse_kernel(s, k, from_down, from_up, field, rest, K, S, U, W, D, R):
    planes, wide, lanes = k.shape
    own = planes // 2
    rows = wide - 16
    even = even_mask(wide, lanes)
    even_own = even_mask(rows, lanes)
    zero = jnp.zeros((wide, lanes), F32)

    def source_plane(i):
        if i < -4 or i > planes + 3:
            return zero
        if i < 0:
            return from_down[4 + i]
        return s[i] if i < planes else from_up[i - planes]

    def mean_plane(i):
        if i < -5 or i > planes + 4:
            return zero
        if i < 0:
            return from_down[9 + i]
        return k[i] if i < planes else from_up[4 + i - planes]

    for p in range(-HP, own + HP):
        for to, plane in ((S, source_plane), (K, mean_plane)):
            a, b = plane(2 * p), plane(2 * p + 1)
            to[0, HP + p] = pick(even, a, b)
            to[1, HP + p] = pick(even, b, a)
    relax_level(K, S, U, W, D, R, own, 4, 0)
    store_field(U, field, own, even_own)
    for p in range(own):
        red, black = R[0, p + 2], R[1, p + 2]
        rest[2 * p] = pick(even_own, red, black)
        rest[2 * p + 1] = pick(even_own, black, red)


def call(kernel, outs, scratch, *args, in_specs=None, name=None):
    extra = {} if in_specs is None else {"in_specs": in_specs, "grid": (1,)}
    if in_specs is not None:
        extra["out_specs"] = [pl.BlockSpec(o, lambda i, n=len(o): (0,) * n) for o in outs]
    return pl.pallas_call(
        kernel,
        out_shape=[jax.ShapeDtypeStruct(o, F32) for o in outs],
        scratch_shapes=[pltpu.VMEM(shape, F32) for shape in scratch],
        name=name,
        **extra,
    )(*args)


def level_scratch(own, wide, lanes, r_pairs):
    pairs = own + 2 * HP
    return [
        (2, pairs, wide, lanes),
        (2, pairs, wide, lanes),
        (2, pairs, wide, lanes),
        (12, pairs, wide, lanes),
        (2, pairs, wide, lanes),
        (2, r_pairs, wide - 16, lanes),
    ]


def exchange(to_low, to_high, axis):
    size = lax.axis_size(axis)
    up = [(i, i + 1) for i in range(size - 1)]
    down = [(i + 1, i) for i in range(size - 1)]
    return lax.ppermute(to_high, axis, up), lax.ppermute(to_low, axis, down)


def body(right_side, coefficient):
    s, k = right_side, coefficient
    planes, rows, lanes = s.shape
    own = planes // 2
    wide = rows + 16

    low = pl.BlockSpec((planes, 8, lanes), lambda i: (0, 0, 0))
    high = pl.BlockSpec((planes, 8, lanes), lambda i: (0, rows // 8 - 1, 0))
    message = (2, own, 8, lanes)
    to_low, to_high = call(pack_rows_kernel, [message] * 2, [], s, s, k, k,
                           in_specs=[low, high, low, high], name="pack_rows")
    from_low, from_high = exchange(to_low, to_high, "inner")
    message = (9, rows + 8, lanes)
    to_down, to_up = call(pack_planes_kernel, [message] * 2, [], s, k, from_low, from_high,
                          name="pack_planes")
    from_down, from_up = exchange(to_down, to_up, "outer")

    count, half = own + 2, rows // 2
    message = (own + 2, 16, lanes // 2)
    field0, source, mean, to_low, to_high = call(
        fine_kernel,
        [s.shape, (count, half, lanes // 2), (own, half, lanes // 2), message, message],
        level_scratch(own, wide, lanes, own + 4)
        + [((half + 8) * count, lanes), (half * own, lanes)],
        s, k, from_low, from_high, from_down, from_up, name="fine_level")

    planes, rows, lanes = own, half, lanes // 2
    own, wide = planes // 2, rows + 16
    from_low, from_high = exchange(to_low, to_high, "inner")
    message = (12, wide, lanes)
    s1, k1, to_down, to_up = call(
        middle_planes_kernel, [(planes + 2, wide, lanes), (planes, wide, lanes), message, message], [],
        source, mean, to_low, to_high, from_low, from_high, name="middle_planes")
    from_down, from_up = exchange(to_down, to_up, "outer")
    half = rows // 2
    message = (own + 2, 16, lanes // 2)
    field1, source, mean, to_low, to_high = call(
        middle_kernel,
        [(planes, rows, lanes), (own, half, lanes // 2), (own + 2, half, lanes // 2), message, message],
        level_scratch(own, wide, lanes, own + 2)
        + [((half + 8) * own, lanes), (half * (own + 2), lanes)],
        s1, k1, from_down, from_up, name="middle_level")

    planes, rows, lanes = own, half, lanes // 2
    own, wide = planes // 2, rows + 16
    from_low, from_high = exchange(to_low, to_high, "inner")
    message = (9, wide, lanes)
    s2, k2, to_down, to_up = call(
        coarse_planes_kernel, [(planes, wide, lanes), (planes, wide, lanes), message, message], [],
        source, mean, to_low, to_high, from_low, from_high, name="coarse_planes")
    from_down, from_up = exchange(to_down, to_up, "outer")
    field2, rest = call(
        coarse_kernel, [(planes, rows, lanes)] * 2, level_scratch(own, wide, lanes, own + 4),
        s2, k2, from_down, from_up, name="coarse_level")
    return field0, field1, field2, rest


def solution(mesh):
    spec = P("outer", "inner", None)
    return jax.shard_map(body, mesh=mesh, in_specs=(spec, spec), out_specs=(spec,) * 4, check_vma=False)
```

time: 434 us -> 116 us (0.27)
  the two profiles are of different devices: /device:TPU:1 before, /device:TPU:13 now
where the time goes in v1:
time: 116 us; the launch traced here: 115 us
  waiting for transfers between devices  39.7 us (34%)
  Pallas kernels  35.7 us (31%)
  starting transfers between devices  34.9 us (30%)
  local copies, waits for them, and re-layouts  4.3 us (4%)
    ppermute x12, waiting for transfers between devices, exchange(): return (lax.ppermute(to_high, axis, up), lax.ppermute(to_low, axis, down))  39.7 us
    pallas_call x7, Pallas kernels, call(): pl.pallas_call(kernel, out_shape=[jax.ShapeDtypeStruct(o, F32) for o in o...  35.7 us
    ppermute x12, starting transfers between devices, exchange(): return (lax.ppermute(to_high, axis, up), lax.ppermute(to_low, axis, down))  34.9 us
    unnamed x24, local copies, waits for them, and re-layouts  4.3 us
  transfers between devices with their start and end apart: 12, of which 11 were waited for; matrix products, arithmetic and copies ran while one was open for 0% of the time, Pallas kernels for 0%

profile of v1, /device:TPU:13, one launch (start us, length us, event | category | flops | bytes accessed | tf_op | source)
XLA Modules:
  0.0 115.4 jit_solution(6454765483856914355)
XLA Ops:
  0.6 2.1 %pack_rows.1 = (f32[2,8,8,512]{3,2,1,0:T(8,128)}, f32[2,8,8,512]{3,2,1,0:T(8,128)}) custom-call(f32[16,32,512]{2,1,0:T(8,128)} %s.3, f32[16,32,512]{2,1,0:T(8,128)} %s.3, f32[16,32,512]{2,1,0:T(8,128)} %k.3, f32[16,32,512]{2,1,0:T(8,128)} %k.3), custom_call_target="tpu_custom_call" | custom-call | tf_op jit(solution)/shard_map/pack_rows/pallas_call | solution.py:506
  2.7 3.1 %collective-permute-start = (f32[2,8,8,512]{3,2,1,0:T(8,128)}, f32[2,8,8,512]{3,2,1,0:T(8,128)S(1)}, u32[]{:S(2)}, u32[]{:S(2)}) collective-permute-start(f32[2,8,8,512]{3,2,1,0:T(8,128)} %get-tuple-element.28), channel_id=1, source_target_pairs={{0,1},{1,2},{2,3},{4,5},{5,6},{6,7},{8,9},{9,10},{10,11},{12,13},{... | collective-permute-start | bytes 786440 | tf_op jit(solution)/shard_map/ppermute | solution.py:531
  5.8 3.1 %collective-permute-start.1 = (f32[2,8,8,512]{3,2,1,0:T(8,128)}, f32[2,8,8,512]{3,2,1,0:T(8,128)S(1)}, u32[]{:S(2)}, u32[]{:S(2)}) collective-permute-start(f32[2,8,8,512]{3,2,1,0:T(8,128)} %get-tuple-element.29), channel_id=1, source_target_pairs={{1,0},{2,1},{3,2},{5,4},{6,5},{7,6},{9,8},{10,9},{11,10},{13,12},{... | collective-permute-start | bytes 786440 | tf_op jit(solution)/shard_map/ppermute | solution.py:531
  8.9 4.0 %collective-permute-done.from_low = f32[2,8,8,512]{3,2,1,0:T(8,128)S(1)} collective-permute-done((f32[2,8,8,512]{3,2,1,0:T(8,128)}, f32[2,8,8,512]{3,2,1,0:T(8,128)S(1)}, u32[]{:S(2)}, u32[]{:S(2)}) %collective-permute-start) | collective-permute-done | bytes 262176 | tf_op jit(solution)/shard_map/ppermute | solution.py:531
  12.9 0.0 copy-start
  12.9 3.8 %collective-permute-done.1.from_high = f32[2,8,8,512]{3,2,1,0:T(8,128)S(1)} collective-permute-done((f32[2,8,8,512]{3,2,1,0:T(8,128)}, f32[2,8,8,512]{3,2,1,0:T(8,128)S(1)}, u32[]{:S(2)}, u32[]{:S(2)}) %collective-permute-start.1) | collective-permute-done | bytes 262176 | tf_op jit(solution)/shard_map/ppermute | solution.py:531
  16.7 0.0 copy-done
  16.7 0.0 copy-start.1
  16.7 0.7 copy-done.1
  17.4 2.9 %pack_planes.1 = (f32[9,40,512]{2,1,0:T(8,128)}, f32[9,40,512]{2,1,0:T(8,128)}) custom-call(f32[16,32,512]{2,1,0:T(8,128)} %s.3, f32[16,32,512]{2,1,0:T(8,128)} %k.3, f32[2,8,8,512]{3,2,1,0:T(8,128)} %copy-done, f32[2,8,8,512]{3,2,1,0:T(8,128)} %copy-done.1), custom_call_target="tpu_custom_call" | custom-call | tf_op jit(solution)/shard_map/pack_planes/pallas_call | solution.py:506
  20.3 4.6 %collective-permute-start.2 = (f32[9,40,512]{2,1,0:T(8,128)}, f32[9,40,512]{2,1,0:T(8,128)S(1)}, u32[]{:S(2)}, u32[]{:S(2)}) collective-permute-start(f32[9,40,512]{2,1,0:T(8,128)} %get-tuple-element.30), channel_id=1, source_target_pairs={{0,4},{4,8},{8,12},{12,16},{16,20},{20,24},{24,28},{1,5},{5,9},{9,... | collective-permute-start | bytes 2211848 | tf_op jit(solution)/shard_map/ppermute | solution.py:531
  24.9 1.9 %collective-permute-start.3 = (f32[9,40,512]{2,1,0:T(8,128)}, f32[9,40,512]{2,1,0:T(8,128)S(1)}, u32[]{:S(2)}, u32[]{:S(2)}) collective-permute-start(f32[9,40,512]{2,1,0:T(8,128)} %get-tuple-element.31), channel_id=1, source_target_pairs={{4,0},{8,4},{12,8},{16,12},{20,16},{24,20},{28,24},{5,1},{9,5},{13... | collective-permute-start | bytes 2211848 | tf_op jit(solution)/shard_map/ppermute | solution.py:531
  26.9 6.8 %collective-permute-done.2.from_down = f32[9,40,512]{2,1,0:T(8,128)S(1)} collective-permute-done((f32[9,40,512]{2,1,0:T(8,128)}, f32[9,40,512]{2,1,0:T(8,128)S(1)}, u32[]{:S(2)}, u32[]{:S(2)}) %collective-permute-start.2) | collective-permute-done | bytes 737312 | tf_op jit(solution)/shard_map/ppermute | solution.py:531
  33.6 0.0 copy-start.2
  33.6 4.3 %collective-permute-done.3.from_up = f32[9,40,512]{2,1,0:T(8,128)S(1)} collective-permute-done((f32[9,40,512]{2,1,0:T(8,128)}, f32[9,40,512]{2,1,0:T(8,128)S(1)}, u32[]{:S(2)}, u32[]{:S(2)}) %collective-permute-start.3) | collective-permute-done | bytes 737312 | tf_op jit(solution)/shard_map/ppermute | solution.py:531
  37.9 0.0 copy-done.2
  37.9 0.0 copy-start.3
  37.9 0.9 copy-done.3
  38.8 15.8 %fine_level.1 = (f32[16,32,512]{2,1,0:T(8,128)}, f32[10,16,256]{2,1,0:T(8,128)}, f32[8,16,256]{2,1,0:T(8,128)}, f32[10,16,256]{2,1,0:T(8,128)}, f32[10,16,256]{2,1,0:T(8,128)}) custom-call(f32[16,32,512]{2,1,0:T(8,128)} %s.3, f32[16,32,512]{2,1,0:T(8,128)} %k.3, f32[2,8,8,512]{3,2,1,0:T(8,128)} %copy-done, f32[2,8,8,512]{3,2,1,0:T(8,128)} %copy-done.1, ...), custom_call_target="tpu_custom_call" | custom-call | tf_op jit(solution)/shard_map/fine_level/pallas_call | solution.py:506
  54.6 4.9 %collective-permute-start.5 = (f32[10,16,256]{2,1,0:T(8,128)}, f32[10,16,256]{2,1,0:T(8,128)S(1)}, u32[]{:S(2)}, u32[]{:S(2)}) collective-permute-start(f32[10,16,256]{2,1,0:T(8,128)} %get-tuple-element.35.to_low), channel_id=1, source_target_pairs={{1,0},{2,1},{3,2},{5,4},{6,5},{7,6},{9,8},{10,9},{11,10},{13,12},{... | collective-permute-start | bytes 491528 | tf_op jit(solution)/shard_map/ppermute | solution.py:531
  59.5 1.9 %collective-permute-start.4 = (f32[10,16,256]{2,1,0:T(8,128)}, f32[10,16,256]{2,1,0:T(8,128)S(1)}, u32[]{:S(2)}, u32[]{:S(2)}) collective-permute-start(f32[10,16,256]{2,1,0:T(8,128)} %get-tuple-element.36.to_high), channel_id=1, source_target_pairs={{0,1},{1,2},{2,3},{4,5},{5,6},{6,7},{8,9},{9,10},{10,11},{12,13},{... | collective-permute-start | bytes 491528 | tf_op jit(solution)/shard_map/ppermute | solution.py:531
  61.4 2.4 %collective-permute-done.5.from_high = f32[10,16,256]{2,1,0:T(8,128)S(1)} collective-permute-done((f32[10,16,256]{2,1,0:T(8,128)}, f32[10,16,256]{2,1,0:T(8,128)S(1)}, u32[]{:S(2)}, u32[]{:S(2)}) %collective-permute-start.5) | collective-permute-done | bytes 163872 | tf_op jit(solution)/shard_map/ppermute | solution.py:531
  63.8 4.1 %collective-permute-done.4.from_low = f32[10,16,256]{2,1,0:T(8,128)S(1)} collective-permute-done((f32[10,16,256]{2,1,0:T(8,128)}, f32[10,16,256]{2,1,0:T(8,128)S(1)}, u32[]{:S(2)}, u32[]{:S(2)}) %collective-permute-start.4) | collective-permute-done | bytes 163872 | tf_op jit(solution)/shard_map/ppermute | solution.py:531
  67.9 0.0 copy-done.6
  67.9 0.7 copy-done.7
  68.6 2.4 %middle_planes.1 = (f32[10,32,256]{2,1,0:T(8,128)}, f32[8,32,256]{2,1,0:T(8,128)}, f32[12,32,256]{2,1,0:T(8,128)}, f32[12,32,256]{2,1,0:T(8,128)}) custom-call(f32[10,16,256]{2,1,0:T(8,128)} %get-tuple-element.33.source, f32[8,16,256]{2,1,0:T(8,128)} %get-tuple-element.34.mean, f32[10,16,256]{2,1,0:T(8,128)} %get-tuple-element.35.to_low, ...), custom_call_target="tpu_custom_call" | custom-call | tf_op jit(solution)/shard_map/middle_planes/pallas_call | solution.py:506
  71.0 3.3 %collective-permute-start.6 = (f32[12,32,256]{2,1,0:T(8,128)}, f32[12,32,256]{2,1,0:T(8,128)S(1)}, u32[]{:S(2)}, u32[]{:S(2)}) collective-permute-start(f32[12,32,256]{2,1,0:T(8,128)} %get-tuple-element.39), channel_id=1, source_target_pairs={{0,4},{4,8},{8,12},{12,16},{16,20},{20,24},{24,28},{1,5},{5,9},{9,... | collective-permute-start | bytes 1179656 | tf_op jit(solution)/shard_map/ppermute | solution.py:531
  74.3 1.9 %collective-permute-start.7 = (f32[12,32,256]{2,1,0:T(8,128)}, f32[12,32,256]{2,1,0:T(8,128)S(1)}, u32[]{:S(2)}, u32[]{:S(2)}) collective-permute-start(f32[12,32,256]{2,1,0:T(8,128)} %get-tuple-element.40), channel_id=1, source_target_pairs={{4,0},{8,4},{12,8},{16,12},{20,16},{24,20},{28,24},{5,1},{9,5},{13... | collective-permute-start | bytes 1179656 | tf_op jit(solution)/shard_map/ppermute | solution.py:531
  76.2 3.1 %collective-permute-done.6.from_down = f32[12,32,256]{2,1,0:T(8,128)S(1)} collective-permute-done((f32[12,32,256]{2,1,0:T(8,128)}, f32[12,32,256]{2,1,0:T(8,128)S(1)}, u32[]{:S(2)}, u32[]{:S(2)}) %collective-permute-start.6) | collective-permute-done | bytes 393248 | tf_op jit(solution)/shard_map/ppermute | solution.py:531
  79.3 4.3 %collective-permute-done.7.from_up = f32[12,32,256]{2,1,0:T(8,128)S(1)} collective-permute-done((f32[12,32,256]{2,1,0:T(8,128)}, f32[12,32,256]{2,1,0:T(8,128)S(1)}, u32[]{:S(2)}, u32[]{:S(2)}) %collective-permute-start.7) | collective-permute-done | bytes 393248 | tf_op jit(solution)/shard_map/ppermute | solution.py:531
  83.6 0.0 copy-done.4
  83.6 0.8 copy-done.5
  84.4 7.0 %middle_level.1 = (f32[8,16,256]{2,1,0:T(8,128)}, f32[4,8,128]{2,1,0:T(8,128)}, f32[6,8,128]{2,1,0:T(8,128)}, f32[6,16,128]{2,1,0:T(8,128)}, f32[6,16,128]{2,1,0:T(8,128)}) custom-call(f32[10,32,256]{2,1,0:T(8,128)} %get-tuple-element.37.s, f32[8,32,256]{2,1,0:T(8,128)} %get-tuple-element.38.k, f32[12,32,256]{2,1,0:T(8,128)} %copy-done.4, ...), custom_call_target="tpu_custom_call" | custom-call | tf_op jit(solution)/shard_map/middle_level/pallas_call | solution.py:506
  91.3 1.9 %collective-permute-start.9 = (f32[6,16,128]{2,1,0:T(8,128)}, f32[6,16,128]{2,1,0:T(8,128)S(1)}, u32[]{:S(2)}, u32[]{:S(2)}) collective-permute-start(f32[6,16,128]{2,1,0:T(8,128)} %get-tuple-element.44.to_low), channel_id=1, source_target_pairs={{1,0},{2,1},{3,2},{5,4},{6,5},{7,6},{9,8},{10,9},{11,10},{13,12},{... | collective-permute-start | bytes 147464 | tf_op jit(solution)/shard_map/ppermute | solution.py:531
  93.3 3.4 %collective-permute-start.8 = (f32[6,16,128]{2,1,0:T(8,128)}, f32[6,16,128]{2,1,0:T(8,128)S(1)}, u32[]{:S(2)}, u32[]{:S(2)}) collective-permute-start(f32[6,16,128]{2,1,0:T(8,128)} %get-tuple-element.45.to_high), channel_id=1, source_target_pairs={{0,1},{1,2},{2,3},{4,5},{5,6},{6,7},{8,9},{9,10},{10,11},{12,13},{... | collective-permute-start | bytes 147464 | tf_op jit(solution)/shard_map/ppermute | solution.py:531
  96.6 0.0 collective-permute-done.9.from_high
  96.6 0.0 copy-start.10
  96.6 2.6 %collective-permute-done.8.from_low = f32[6,16,128]{2,1,0:T(8,128)S(1)} collective-permute-done((f32[6,16,128]{2,1,0:T(8,128)}, f32[6,16,128]{2,1,0:T(8,128)S(1)}, u32[]{:S(2)}, u32[]{:S(2)}) %collective-permute-start.8) | collective-permute-done | bytes 49184 | tf_op jit(solution)/shard_map/ppermute | solution.py:531
  99.2 0.0 copy-done.10
  99.2 0.6 copy-done.11
  99.8 1.6 %coarse_planes.1 = (f32[4,24,128]{2,1,0:T(8,128)}, f32[4,24,128]{2,1,0:T(8,128)}, f32[9,24,128]{2,1,0:T(8,128)}, f32[9,24,128]{2,1,0:T(8,128)}) custom-call(f32[4,8,128]{2,1,0:T(8,128)} %get-tuple-element.42.source, f32[6,8,128]{2,1,0:T(8,128)} %get-tuple-element.43.mean, f32[6,16,128]{2,1,0:T(8,128)} %get-tuple-element.44.to_low, ...), custom_call_target="tpu_custom_call" | custom-call | tf_op jit(solution)/shard_map/coarse_planes/pallas_call | solution.py:506
  101.5 3.0 %collective-permute-start.10 = (f32[9,24,128]{2,1,0:T(8,128)}, f32[9,24,128]{2,1,0:T(8,128)S(1)}, u32[]{:S(2)}, u32[]{:S(2)}) collective-permute-start(f32[9,24,128]{2,1,0:T(8,128)} %get-tuple-element.48), channel_id=1, source_target_pairs={{0,4},{4,8},{8,12},{12,16},{16,20},{20,24},{24,28},{1,5},{5,9},{9,... | collective-permute-start | bytes 331784 | tf_op jit(solution)/shard_map/ppermute | solution.py:531
  104.5 1.9 %collective-permute-start.11 = (f32[9,24,128]{2,1,0:T(8,128)}, f32[9,24,128]{2,1,0:T(8,128)S(1)}, u32[]{:S(2)}, u32[]{:S(2)}) collective-permute-start(f32[9,24,128]{2,1,0:T(8,128)} %get-tuple-element.49), channel_id=1, source_target_pairs={{4,0},{8,4},{12,8},{16,12},{20,16},{24,20},{28,24},{5,1},{9,5},{13... | collective-permute-start | bytes 331784 | tf_op jit(solution)/shard_map/ppermute | solution.py:531
  106.4 0.1 collective-permute-done.10.from_down
  106.6 4.2 %collective-permute-done.11.from_up = f32[9,24,128]{2,1,0:T(8,128)S(1)} collective-permute-done((f32[9,24,128]{2,1,0:T(8,128)}, f32[9,24,128]{2,1,0:T(8,128)S(1)}, u32[]{:S(2)}, u32[]{:S(2)}) %collective-permute-start.11) | collective-permute-done | bytes 110624 | tf_op jit(solution)/shard_map/ppermute | solution.py:531
  110.8 0.0 copy-done.8
  110.8 0.6 copy-done.9
  111.4 3.9 %coarse_level.1 = (f32[4,8,128]{2,1,0:T(8,128)}, f32[4,8,128]{2,1,0:T(8,128)}) custom-call(f32[4,24,128]{2,1,0:T(8,128)} %get-tuple-element.46.s, f32[4,24,128]{2,1,0:T(8,128)} %get-tuple-element.47.k, f32[9,24,128]{2,1,0:T(8,128)} %copy-done.8, f32[9,24,128]{2,1,0:T(8,128)} %copy-done.9), custom_call_target="tpu_custom_call" | custom-call | tf_op jit(solution)/shard_map/coarse_level/pallas_call | solution.py:506
  (7 shorter events, 0.0 us)
Async XLA Ops:
  2.7 10.2 %collective-permute-start = (f32[2,8,8,512]{3,2,1,0:T(8,128)}, f32[2,8,8,512]{3,2,1,0:T(8,128)S(1)}, u32[]{:S(2)}, u32[]{:S(2)}) collective-permute-start(f32[2,8,8,512]{3,2,1,0:T(8,128)} %get-tuple-element.28), channel_id=1, source_target_pairs={{0,1},{1,2},{2,3},{4,5},{5,6},{6,7},{8,9},{9,10},{10,11},{12,13},{... | collective-permute-start | bytes 786440 | tf_op jit(solution)/shard_map/ppermute | solution.py:531
  5.8 10.9 %collective-permute-start.1 = (f32[2,8,8,512]{3,2,1,0:T(8,128)}, f32[2,8,8,512]{3,2,1,0:T(8,128)S(1)}, u32[]{:S(2)}, u32[]{:S(2)}) collective-permute-start(f32[2,8,8,512]{3,2,1,0:T(8,128)} %get-tuple-element.29), channel_id=1, source_target_pairs={{1,0},{2,1},{3,2},{5,4},{6,5},{7,6},{9,8},{10,9},{11,10},{13,12},{... | collective-permute-start | bytes 786440 | tf_op jit(solution)/shard_map/ppermute | solution.py:531
  12.9 3.8 %copy-start = (f32[2,8,8,512]{3,2,1,0:T(8,128)}, f32[2,8,8,512]{3,2,1,0:T(8,128)S(1)}, u32[]{:S(2)}) copy-start(f32[2,8,8,512]{3,2,1,0:T(8,128)S(1)} %collective-permute-done.from_low) | copy-start | bytes 786436
  16.7 0.7 copy-start.1
  20.3 13.3 %collective-permute-start.2 = (f32[9,40,512]{2,1,0:T(8,128)}, f32[9,40,512]{2,1,0:T(8,128)S(1)}, u32[]{:S(2)}, u32[]{:S(2)}) collective-permute-start(f32[9,40,512]{2,1,0:T(8,128)} %get-tuple-element.30), channel_id=1, source_target_pairs={{0,4},{4,8},{8,12},{12,16},{16,20},{20,24},{24,28},{1,5},{5,9},{9,... | collective-permute-start | bytes 2211848 | tf_op jit(solution)/shard_map/ppermute | solution.py:531
  24.9 13.0 %collective-permute-start.3 = (f32[9,40,512]{2,1,0:T(8,128)}, f32[9,40,512]{2,1,0:T(8,128)S(1)}, u32[]{:S(2)}, u32[]{:S(2)}) collective-permute-start(f32[9,40,512]{2,1,0:T(8,128)} %get-tuple-element.31), channel_id=1, source_target_pairs={{4,0},{8,4},{12,8},{16,12},{20,16},{24,20},{28,24},{5,1},{9,5},{13... | collective-permute-start | bytes 2211848 | tf_op jit(solution)/shard_map/ppermute | solution.py:531
  33.6 4.3 %copy-start.2 = (f32[9,40,512]{2,1,0:T(8,128)}, f32[9,40,512]{2,1,0:T(8,128)S(1)}, u32[]{:S(2)}) copy-start(f32[9,40,512]{2,1,0:T(8,128)S(1)} %collective-permute-done.2.from_down) | copy-start | bytes 2211844
  37.9 0.9 copy-start.3
  54.6 9.2 %collective-permute-start.5 = (f32[10,16,256]{2,1,0:T(8,128)}, f32[10,16,256]{2,1,0:T(8,128)S(1)}, u32[]{:S(2)}, u32[]{:S(2)}) collective-permute-start(f32[10,16,256]{2,1,0:T(8,128)} %get-tuple-element.35.to_low), channel_id=1, source_target_pairs={{1,0},{2,1},{3,2},{5,4},{6,5},{7,6},{9,8},{10,9},{11,10},{13,12},{... | collective-permute-start | bytes 491528 | tf_op jit(solution)/shard_map/ppermute | solution.py:531
  59.5 8.4 %collective-permute-start.4 = (f32[10,16,256]{2,1,0:T(8,128)}, f32[10,16,256]{2,1,0:T(8,128)S(1)}, u32[]{:S(2)}, u32[]{:S(2)}) collective-permute-start(f32[10,16,256]{2,1,0:T(8,128)} %get-tuple-element.36.to_high), channel_id=1, source_target_pairs={{0,1},{1,2},{2,3},{4,5},{5,6},{6,7},{8,9},{9,10},{10,11},{12,13},{... | collective-permute-start | bytes 491528 | tf_op jit(solution)/shard_map/ppermute | solution.py:531
  63.8 4.1 %copy-start.6 = (f32[10,16,256]{2,1,0:T(8,128)}, f32[10,16,256]{2,1,0:T(8,128)S(1)}, u32[]{:S(2)}) copy-start(f32[10,16,256]{2,1,0:T(8,128)S(1)} %collective-permute-done.5.from_high) | copy-start | bytes 491524
  67.9 0.7 copy-start.7
  71.0 8.3 %collective-permute-start.6 = (f32[12,32,256]{2,1,0:T(8,128)}, f32[12,32,256]{2,1,0:T(8,128)S(1)}, u32[]{:S(2)}, u32[]{:S(2)}) collective-permute-start(f32[12,32,256]{2,1,0:T(8,128)} %get-tuple-element.39), channel_id=1, source_target_pairs={{0,4},{4,8},{8,12},{12,16},{16,20},{20,24},{24,28},{1,5},{5,9},{9,... | collective-permute-start | bytes 1179656 | tf_op jit(solution)/shard_map/ppermute | solution.py:531
  74.3 9.3 %collective-permute-start.7 = (f32[12,32,256]{2,1,0:T(8,128)}, f32[12,32,256]{2,1,0:T(8,128)S(1)}, u32[]{:S(2)}, u32[]{:S(2)}) collective-permute-start(f32[12,32,256]{2,1,0:T(8,128)} %get-tuple-element.40), channel_id=1, source_target_pairs={{4,0},{8,4},{12,8},{16,12},{20,16},{24,20},{28,24},{5,1},{9,5},{13... | collective-permute-start | bytes 1179656 | tf_op jit(solution)/shard_map/ppermute | solution.py:531
  79.3 4.3 %copy-start.4 = (f32[12,32,256]{2,1,0:T(8,128)}, f32[12,32,256]{2,1,0:T(8,128)S(1)}, u32[]{:S(2)}) copy-start(f32[12,32,256]{2,1,0:T(8,128)S(1)} %collective-permute-done.6.from_down) | copy-start | bytes 1179652
  83.6 0.8 copy-start.5
  91.3 5.3 %collective-permute-start.9 = (f32[6,16,128]{2,1,0:T(8,128)}, f32[6,16,128]{2,1,0:T(8,128)S(1)}, u32[]{:S(2)}, u32[]{:S(2)}) collective-permute-start(f32[6,16,128]{2,1,0:T(8,128)} %get-tuple-element.44.to_low), channel_id=1, source_target_pairs={{1,0},{2,1},{3,2},{5,4},{6,5},{7,6},{9,8},{10,9},{11,10},{13,12},{... | collective-permute-start | bytes 147464 | tf_op jit(solution)/shard_map/ppermute | solution.py:531
  93.3 5.9 %collective-permute-start.8 = (f32[6,16,128]{2,1,0:T(8,128)}, f32[6,16,128]{2,1,0:T(8,128)S(1)}, u32[]{:S(2)}, u32[]{:S(2)}) collective-permute-start(f32[6,16,128]{2,1,0:T(8,128)} %get-tuple-element.45.to_high), channel_id=1, source_target_pairs={{0,1},{1,2},{2,3},{4,5},{5,6},{6,7},{8,9},{9,10},{10,11},{12,13},{... | collective-permute-start | bytes 147464 | tf_op jit(solution)/shard_map/ppermute | solution.py:531
  96.6 2.6 %copy-start.10 = (f32[6,16,128]{2,1,0:T(8,128)}, f32[6,16,128]{2,1,0:T(8,128)S(1)}, u32[]{:S(2)}) copy-start(f32[6,16,128]{2,1,0:T(8,128)S(1)} %collective-permute-done.9.from_high) | copy-start | bytes 147460
  99.2 0.6 copy-start.11
  101.5 5.1 %collective-permute-start.10 = (f32[9,24,128]{2,1,0:T(8,128)}, f32[9,24,128]{2,1,0:T(8,128)S(1)}, u32[]{:S(2)}, u32[]{:S(2)}) collective-permute-start(f32[9,24,128]{2,1,0:T(8,128)} %get-tuple-element.48), channel_id=1, source_target_pairs={{0,4},{4,8},{8,12},{12,16},{16,20},{20,24},{24,28},{1,5},{5,9},{9,... | collective-permute-start | bytes 331784 | tf_op jit(solution)/shard_map/ppermute | solution.py:531
  104.5 6.3 %collective-permute-start.11 = (f32[9,24,128]{2,1,0:T(8,128)}, f32[9,24,128]{2,1,0:T(8,128)S(1)}, u32[]{:S(2)}, u32[]{:S(2)}) collective-permute-start(f32[9,24,128]{2,1,0:T(8,128)} %get-tuple-element.49), channel_id=1, source_target_pairs={{4,0},{8,4},{12,8},{16,12},{20,16},{24,20},{28,24},{5,1},{9,5},{13... | collective-permute-start | bytes 331784 | tf_op jit(solution)/shard_map/ppermute | solution.py:531
  106.6 4.2 %copy-start.8 = (f32[9,24,128]{2,1,0:T(8,128)}, f32[9,24,128]{2,1,0:T(8,128)S(1)}, u32[]{:S(2)}) copy-start(f32[9,24,128]{2,1,0:T(8,128)S(1)} %collective-permute-done.10.from_down) | copy-start | bytes 331780
  110.8 0.6 copy-start.9

commit v2 on v1

--- a/solution.py
+++ b/solution.py
@@ -42,8 +42,11 @@
 def neighbours(ref, colour, p, pairs, even):
     other = 1 - colour
     x = ref[other, p]
-    below = ref[other, jnp.maximum(p - 1, 0)]
-    above = ref[other, jnp.minimum(p + 1, pairs - 1)]
+    if isinstance(p, int):
+        below, above = ref[other, max(p - 1, 0)], ref[other, min(p + 1, pairs - 1)]
+    else:
+        below = ref[other, jnp.maximum(p - 1, 0)]
+        above = ref[other, jnp.minimum(p + 1, pairs - 1)]
     far = pick(even, below, above) if colour == 0 else pick(even, above, below)
     rows, lanes = x.shape
     return (
@@ -61,7 +64,15 @@
     return HP - extra, HP + own + extra
 
 
-def relax_level(K, S, U, W, D, R, own, depth, residual_layers):
+def over(first, last, step, unrolled):
+    if unrolled:
+        for p in range(first, last):
+            step(p, 0)
+    else:
+        lax.fori_loop(first, last, step, 0)
+
+
+def relax_level(K, S, U, W, D, R, own, depth, residual_layers, inset, unrolled):
     _, pairs, rows, lanes = K.shape
     even = even_mask(rows, lanes)
 
@@ -93,7 +104,7 @@
                 U[0, p] = start
             return carry
 
-        lax.fori_loop(first, last, step, 0)
+        over(first, last, step, unrolled)
         zero = jnp.zeros((rows, lanes), F32)
         for p in list(range(first)) + list(range(last, pairs)):
             U[colour, p] = zero
@@ -112,7 +123,7 @@
             U[colour, p] = relaxed(colour, p)
             return carry
 
-        lax.fori_loop(first, last, step, 0)
+        over(first, last, step, unrolled)
 
     setup(0, depth)
     setup(1, depth - 1)
@@ -124,20 +135,21 @@
     def left(p, carry):
         for colour in (0, 1):
             rest = D[colour, p] * (relaxed(colour, p) - U[colour, p])
-            R[colour, p - first + R_PAD[residual_layers]] = rest[8 : rows - 8]
+            R[colour, p - first + R_PAD[residual_layers]] = rest[inset : rows - inset]
         return carry
 
-    lax.fori_loop(first, last, left, 0)
+    over(first, last, left, unrolled)
 
 
 R_PAD = {0: 2, 1: 0}
 
 
 def store_field(U, out, own, even):
-    rows = U.shape[2]
+    rows = out.shape[1]
+    first = (U.shape[2] - rows) // 2
     for p in range(own):
-        red = U[0, HP + p, 8 : rows - 8]
-        black = U[1, HP + p, 8 : rows - 8]
+        red = U[0, HP + p, first : first + rows]
+        black = U[1, HP + p, first : first + rows]
         out[2 * p] = pick(even, red, black)
         out[2 * p + 1] = pick(even, black, red)
 
@@ -149,15 +161,18 @@
     return (3.0 * (red + black) + (odd_below + even_above)) * 0.125
 
 
-def row_restriction(rows):
+def row_restriction(rows, ends):
     half = rows // 2
-    j = lax.broadcasted_iota(jnp.int32, (half + 8, rows), 0)
-    m = lax.broadcasted_iota(jnp.int32, (half + 8, rows), 1)
+    shape = (half + 8 if ends else half, rows)
+    j = lax.broadcasted_iota(jnp.int32, shape, 0)
+    m = lax.broadcasted_iota(jnp.int32, shape, 1)
     inner = (m == 2 * j) | (m == 2 * j + 1)
     outer = (m == 2 * j - 1) | (m == 2 * j + 2)
-    main = pick(inner, 0.375, pick(outer, 0.125, 0.0))
-    ends = pick(((j == half) & (m == 0)) | ((j == half + 1) & (m == rows - 1)), 0.125, 0.0)
-    return pick(j < half, main, ends).astype(F32)
+    main = pick(inner, 0.375, pick(outer, 0.125, 0.0)).astype(F32)
+    if not ends:
+        return main
+    edge = pick(((j == half) & (m == 0)) | ((j == half + 1) & (m == rows - 1)), 0.125, 0.0)
+    return pick(j < half, main, edge).astype(F32)
 
 
 def row_sum(rows):
@@ -182,45 +197,6 @@
     m = lax.broadcasted_iota(jnp.int32, (lanes, lanes // 2), 0)
     i = 2 * lax.broadcasted_iota(jnp.int32, (lanes, lanes // 2), 1)
     return pick((m == i) | (m == i + 1), 0.125, 0.0).astype(F32)
-
-
-def coarsen(K, R, Z, Zk, even_own, own, s_pairs, r_pad, k_pairs):
-    rows, lanes = R.shape[2:]
-    half = rows // 2
-    block = half + 8
-    for q, pair in enumerate(s_pairs):
-        Z[block * q : block * (q + 1)] = product(
-            row_restriction(rows), restrict_planes(R, pair + r_pad, even_own))
-    for q, pair in enumerate(k_pairs):
-        total = K[0, HP + pair, 8 : 8 + rows] + K[1, HP + pair, 8 : 8 + rows]
-        Zk[half * q : half * (q + 1)] = product(row_sum(rows), total)
-    source = product(Z[...], lane_restriction(lanes))
-    mean = product(Zk[...], lane_mean(lanes))
-    return source, mean, half, len(s_pairs)
-
-
-def row_messages(source, mean, half, count, s_at, k_at, planes, to_low, to_high):
-    lanes = source.shape[1]
-    block = half + 8
-    for q in range(planes):
-        low, high = [], []
-        if q - s_at in range(count):
-            at = block * (q - s_at)
-            low += [source[at + half : at + half + 1], source[at : at + 4]]
-            high += [source[at + half + 1 : at + half + 2], source[at + half - 4 : at + half]]
-            pad = [jnp.zeros((3, lanes), F32)]
-        else:
-            pad = [jnp.zeros((8, lanes), F32)]
-        low, high = low + pad, high + pad
-        if q - k_at in range(mean.shape[0] // half):
-            at = half * (q - k_at)
-            low += [mean[at : at + 5]]
-            high += [mean[at + half - 5 : at + half]]
-            pad = [jnp.zeros((3, lanes), F32)]
-        else:
-            pad = [jnp.zeros((8, lanes), F32)]
-        to_low[q] = jnp.concatenate(low + pad, axis=0)
-        to_high[q] = jnp.concatenate(high + pad, axis=0)
 
 
 def pack_rows_kernel(s_low, s_high, k_low, k_high, to_low, to_high):
@@ -272,9 +248,19 @@
         put(to_up, 4 + j, k, planes - 5 + j, True)
 
 
+def mean_kernel(k, out, Z):
+    planes, rows, lanes = k.shape
+    half = rows // 2
+    for q in range(planes // 2):
+        Z[half * q : half * (q + 1)] = product(row_sum(rows), k[2 * q] + k[2 * q + 1])
+    mean = product(Z[...], lane_mean(lanes))
+    for q in range(planes // 2):
+        out[q] = mean[half * q : half * (q + 1)]
+
+
 def fine_kernel(s, k, from_low, from_high, from_down, from_up,
-                field, source_out, mean_out, to_low, to_high,
-                K, S, U, W, D, R, Z, Zk):
+                field, source_out, to_low, to_high,
+                K, S, U, W, D, R, Z):
     planes, rows, lanes = s.shape
     own = planes // 2
     wide = rows + 16
@@ -333,74 +319,59 @@
     halo(K, HP + own, from_up, 4, 5)
     halo(K, HP + own + 1, from_up, 6, 7)
     halo(K, HP + own + 2, from_up, 8, None)
-    relax_level(K, S, U, W, D, R, own, 4, 0)
+    relax_level(K, S, U, W, D, R, own, 4, 0, 8, False)
     store_field(U, field, own, even_own)
     zero = jnp.zeros((rows, lanes), F32)
     for colour in (0, 1):
         for at in (0, 1, own + 2, own + 3):
             R[colour, at] = zero
-    source, mean, half, count = coarsen(
-        K, R, Z, Zk, even_own, own, range(-1, own + 1), 2, range(own))
-    for q in range(count):
-        at = (half + 8) * q
-        source_out[q] = source[at : at + half]
-    for q in range(own):
-        mean_out[q] = mean[half * q : half * (q + 1)]
-    row_messages(source, mean, half, count, 0, 1, own + 2, to_low, to_high)
-
-
-def widen(own_rows, mine_low, mine_high, got_low, got_high):
-    rows, lanes = own_rows.shape
-    row = row_index(lanes)
-    low = pltpu.roll(got_low[0:8], 3, 0)
-    low = pick(row >= 4, low, 0.0) + pick(row == 7, pltpu.roll(mine_low[0:8], 7, 0), 0.0)
-    high = pick(row < 4, pltpu.roll(got_high[0:8], 7, 0), 0.0)
-    high = high + pick(row == 0, mine_high[0:8], 0.0)
-    first = pick(row == 0, got_low[0:8], 0.0)
-    last = pick(row == 7, pltpu.roll(got_high[0:8], 7, 0), 0.0)
-    if rows == 8:
-        return jnp.concatenate([low, own_rows + first + last, high], axis=0)
-    return jnp.concatenate(
-        [low, own_rows[0:8] + first, own_rows[8 : rows - 8], own_rows[rows - 8 :] + last, high]
-        if rows > 16 else
-        [low, own_rows[0:8] + first, own_rows[8:16] + last, high], axis=0)
-
-
-def widen_mean(own_rows, got_low, got_high):
-    rows, lanes = own_rows.shape
-    row = row_index(lanes)
-    low = pick(row >= 3, pltpu.roll(got_low[8:16], 3, 0), 0.0)
-    high = pick(row < 5, got_high[8:16], 0.0)
-    return jnp.concatenate([low, own_rows, high], axis=0)
-
-
-def middle_planes_kernel(source, mean, to_low, to_high, from_low, from_high,
-                         S, K, to_down, to_up):
-    planes = mean.shape[0]
-    for q in range(planes + 2):
-        value = widen(source[q], to_low[q], to_high[q], from_low[q], from_high[q])
-        S[q] = value
-        if q < 6:
-            to_down[q] = value
-        if q >= planes - 4:
-            to_up[q - planes + 4] = value
+    half = rows // 2
+    block = half + 8
+    for q in range(own + 2):
+        Z[block * q : block * (q + 1)] = product(
+            row_restriction(rows, True), restrict_planes(R, q + 1, even_own))
+    source = product(Z[...], lane_restriction(lanes))
+    row = lax.broadcasted_iota(jnp.int32, (half, lanes // 2), 0)
+    for q in range(own + 2):
+        at = block * q
+        rows_of = source[at : at + half]
+        source_out[q] = rows_of
+        to_low[q] = pick(row == half - 1, source[at + half : at + half + 1], rows_of)
+        to_high[q] = pick(row == 0, source[at + half + 1 : at + half + 2], rows_of)
+
+
+def mean_planes_kernel(own_rows, from_low, from_high, K, to_down, to_up):
+    planes, rows, _ = own_rows.shape
     for q in range(planes):
-        value = widen_mean(mean[q], from_low[q + 1], from_high[q + 1])
-        K[q] = value
-        if q < 6:
-            to_down[6 + q] = value
-        if q >= planes - 6:
-            to_up[12 + q - planes] = value
-
-
-def middle_kernel(s, k, from_down, from_up,
-                  field, source_out, mean_out, to_low, to_high,
+        for out, at in ((K, q), (to_down, q), (to_up, q - planes + 6)):
+            if 0 <= at < out.shape[0]:
+                out[at, 0:rows] = from_low[q]
+                out[at, rows : 2 * rows] = own_rows[q]
+                out[at, 2 * rows : 3 * rows] = from_high[q]
+
+
+def source_planes_kernel(own_rows, to_low, to_high, from_low, from_high, S, to_down, to_up):
+    planes, rows, lanes = own_rows.shape
+    row = lax.broadcasted_iota(jnp.int32, (rows, lanes), 0)
+    first, last = row == 0, row == rows - 1
+    for q in range(planes):
+        got_low, got_high = from_low[q], from_high[q]
+        low = pick(first, 0.0, got_low) + pick(last, to_low[q], 0.0)
+        mine = own_rows[q] + pick(first, got_low, 0.0) + pick(last, got_high, 0.0)
+        high = pick(last, 0.0, got_high) + pick(first, to_high[q], 0.0)
+        for out, at in ((S, q), (to_down, q), (to_up, q - planes + 6)):
+            if 0 <= at < out.shape[0]:
+                out[at, 0:rows] = low
+                out[at, rows : 2 * rows] = mine
+                out[at, 2 * rows : 3 * rows] = high
+
+
+def middle_kernel(s, k, from_down, from_up, k_down, k_up,
+                  field, s_next, k_next, to_down, to_up,
                   K, S, U, W, D, R, Z, Zk):
     planes, wide, lanes = k.shape
     own = planes // 2
-    rows = wide - 16
     even = even_mask(wide, lanes)
-    even_own = even_mask(rows, lanes)
     zero = jnp.zeros((wide, lanes), F32)
 
     def source_plane(i):
@@ -422,52 +393,49 @@
 
     def mean_plane(i):
         if i < 0:
-            return from_down[12 + i]
+            return k_down[6 + i]
         if i < planes:
             return k[i]
-        return from_up[6 + i - planes]
+        return k_up[i - planes]
 
     for p in range(-HP, own + HP):
         for to, plane in ((S, source_plane), (K, mean_plane)):
             a, b = plane(2 * p), plane(2 * p + 1)
             to[0, HP + p] = pick(even, a, b)
             to[1, HP + p] = pick(even, b, a)
-    relax_level(K, S, U, W, D, R, own, 5, 1)
-    store_field(U, field, own, even_own)
-    source, mean, half, count = coarsen(
-        K, R, Z, Zk, even_own, own, range(own), 1, range(-1, own + 1))
-    for q in range(count):
-        at = (half + 8) * q
-        source_out[q] = source[at : at + half]
+    relax_level(K, S, U, W, D, R, own, 5, 1, 0, True)
+    rows = field.shape[1]
+    store_field(U, field, own, even_mask(rows, lanes))
+    half = wide // 2
+    for q in range(own):
+        Z[half * q : half * (q + 1)] = product(
+            row_restriction(wide, False), restrict_planes(R, q + 1, even))
     for q in range(own + 2):
-        mean_out[q] = mean[half * q : half * (q + 1)]
-    row_messages(source, mean, half, count, 1, 0, own + 2, to_low, to_high)
-
-
-def coarse_planes_kernel(source, mean, to_low, to_high, from_low, from_high,
-                         S, K, to_down, to_up):
-    planes = source.shape[0]
-    for q in range(planes):
-        value = widen(source[q], to_low[q + 1], to_high[q + 1], from_low[q + 1], from_high[q + 1])
-        S[q] = value
+        total = K[0, HP - 1 + q] + K[1, HP - 1 + q]
+        Zk[half * q : half * (q + 1)] = product(row_sum(wide), total)
+    source = product(Z[...], lane_restriction(lanes))
+    mean = product(Zk[...], lane_mean(lanes))
+    for q in range(own):
+        value = source[half * q : half * (q + 1)]
+        s_next[q] = value
         if q < 4:
             to_down[q] = value
-        if q >= planes - 4:
-            to_up[q - planes + 4] = value
-    for q in range(planes + 2):
-        value = widen_mean(mean[q], from_low[q], from_high[q])
-        if 1 <= q <= planes:
-            K[q - 1] = value
+        if q >= own - 4:
+            to_up[q - own + 4] = value
+    for q in range(own + 2):
+        value = mean[half * q : half * (q + 1)]
+        if 1 <= q <= own:
+            k_next[q - 1] = value
         if 1 <= q <= 5:
             to_down[3 + q] = value
-        if planes - 4 <= q <= planes:
-            to_up[8 + q - planes] = value
+        if own - 4 <= q <= own:
+            to_up[8 + q - own] = value
 
 
 def coarse_kernel(s, k, from_down, from_up, field, rest, K, S, U, W, D, R):
     planes, wide, lanes = k.shape
     own = planes // 2
-    rows = wide - 16
+    rows = field.shape[1]
     even = even_mask(wide, lanes)
     even_own = even_mask(rows, lanes)
     zero = jnp.zeros((wide, lanes), F32)
@@ -491,7 +459,7 @@
             a, b = plane(2 * p), plane(2 * p + 1)
             to[0, HP + p] = pick(even, a, b)
             to[1, HP + p] = pick(even, b, a)
-    relax_level(K, S, U, W, D, R, own, 4, 0)
+    relax_level(K, S, U, W, D, R, own, 4, 0, (wide - rows) // 2, True)
     store_field(U, field, own, even_own)
     for p in range(own):
         red, black = R[0, p + 2], R[1, p + 2]
@@ -512,16 +480,10 @@
     )(*args)
 
 
-def level_scratch(own, wide, lanes, r_pairs):
+def level_scratch(own, wide, lanes, r_pairs, r_rows):
     pairs = own + 2 * HP
-    return [
-        (2, pairs, wide, lanes),
-        (2, pairs, wide, lanes),
-        (2, pairs, wide, lanes),
-        (12, pairs, wide, lanes),
-        (2, pairs, wide, lanes),
-        (2, r_pairs, wide - 16, lanes),
-    ]
+    block = (2, pairs, wide, lanes)
+    return [block, block, block, (12, pairs, wide, lanes), block, (2, r_pairs, r_rows, lanes)]
 
 
 def exchange(to_low, to_high, axis):
@@ -543,47 +505,47 @@
     to_low, to_high = call(pack_rows_kernel, [message] * 2, [], s, s, k, k,
                            in_specs=[low, high, low, high], name="pack_rows")
     from_low, from_high = exchange(to_low, to_high, "inner")
+    half, next_lanes = rows // 2, lanes // 2
+    (mean,) = call(mean_kernel, [(own, half, next_lanes)], [(half * own, lanes)], k, name="mean")
     message = (9, rows + 8, lanes)
     to_down, to_up = call(pack_planes_kernel, [message] * 2, [], s, k, from_low, from_high,
                           name="pack_planes")
+    mean, to_down, to_up = lax.optimization_barrier((mean, to_down, to_up))
     from_down, from_up = exchange(to_down, to_up, "outer")
-
-    count, half = own + 2, rows // 2
-    message = (own + 2, 16, lanes // 2)
-    field0, source, mean, to_low, to_high = call(
-        fine_kernel,
-        [s.shape, (count, half, lanes // 2), (own, half, lanes // 2), message, message],
-        level_scratch(own, wide, lanes, own + 4)
-        + [((half + 8) * count, lanes), (half * own, lanes)],
+    mean_low, mean_high = exchange(mean, mean, "inner")
+
+    count = own + 2
+    message = (count, half, next_lanes)
+    field0, source, to_low, to_high = call(
+        fine_kernel, [s.shape, message, message, message],
+        level_scratch(own, wide, lanes, own + 4, rows) + [((half + 8) * count, lanes)],
         s, k, from_low, from_high, from_down, from_up, name="fine_level")
 
-    planes, rows, lanes = own, half, lanes // 2
-    own, wide = planes // 2, rows + 16
+    planes, rows, lanes = own, half, next_lanes
+    own, wide = planes // 2, 3 * rows
+    mean_low, mean_high, to_low, to_high = lax.optimization_barrier((mean_low, mean_high, to_low, to_high))
     from_low, from_high = exchange(to_low, to_high, "inner")
-    message = (12, wide, lanes)
-    s1, k1, to_down, to_up = call(
-        middle_planes_kernel, [(planes + 2, wide, lanes), (planes, wide, lanes), message, message], [],
-        source, mean, to_low, to_high, from_low, from_high, name="middle_planes")
+    message = (6, wide, lanes)
+    k1, to_down, to_up = call(
+        mean_planes_kernel, [(planes, wide, lanes), message, message], [],
+        mean, mean_low, mean_high, name="mean_planes")
+    k_down, k_up = exchange(to_down, to_up, "outer")
+    s1, to_down, to_up = call(
+        source_planes_kernel, [(planes + 2, wide, lanes), message, message], [],
+        source, to_low, to_high, from_low, from_high, name="source_planes")
     from_down, from_up = exchange(to_down, to_up, "outer")
-    half = rows // 2
-    message = (own + 2, 16, lanes // 2)
-    field1, source, mean, to_low, to_high = call(
-        middle_kernel,
-        [(planes, rows, lanes), (own, half, lanes // 2), (own + 2, half, lanes // 2), message, message],
-        level_scratch(own, wide, lanes, own + 2)
-        + [((half + 8) * own, lanes), (half * (own + 2), lanes)],
-        s1, k1, from_down, from_up, name="middle_level")
-
-    planes, rows, lanes = own, half, lanes // 2
-    own, wide = planes // 2, rows + 16
-    from_low, from_high = exchange(to_low, to_high, "inner")
-    message = (9, wide, lanes)
-    s2, k2, to_down, to_up = call(
-        coarse_planes_kernel, [(planes, wide, lanes), (planes, wide, lanes), message, message], [],
-        source, mean, to_low, to_high, from_low, from_high, name="coarse_planes")
+    half, next_lanes = wide // 2, lanes // 2
+    block, message = (own, half, next_lanes), (9, half, next_lanes)
+    field1, s2, k2, to_down, to_up = call(
+        middle_kernel, [(planes, rows, lanes), block, block, message, message],
+        level_scratch(own, wide, lanes, own + 2, wide) + [(half * own, lanes), (half * (own + 2), lanes)],
+        s1, k1, from_down, from_up, k_down, k_up, name="middle_level")
+
+    planes, rows, wide, lanes = own, rows // 2, half, next_lanes
+    own = planes // 2
     from_down, from_up = exchange(to_down, to_up, "outer")
     field2, rest = call(
-        coarse_kernel, [(planes, rows, lanes)] * 2, level_scratch(own, wide, lanes, own + 4),
+        coarse_kernel, [(planes, rows, lanes)] * 2, level_scratch(own, wide, lanes, own + 4, rows),
         s2, k2, from_down, from_up, name="coarse_level")
     return field0, field1, field2, rest
 

time: 116 us -> 99.9 us (0.86)
  the two profiles are of different devices: /device:TPU:13 before, /device:TPU:1 now
where the time goes in v2:
time: 99.9 us; the launch traced here: 98.9 us
  Pallas kernels  34.5 us (35%)
  starting transfers between devices  34.5 us (35%)
  waiting for transfers between devices  25.4 us (25%)
  local copies, waits for them, and re-layouts  3.71 us (4%)
    ppermute x14, starting transfers between devices, exchange(): return (lax.ppermute(to_high, axis, up), lax.ppermute(to_low, axis, down))  34.5 us
    pallas_call x8, Pallas kernels, call(): pl.pallas_call(kernel, out_shape=[jax.ShapeDtypeStruct(o, F32) for o in o...  34.5 us
    ppermute x14, waiting for transfers between devices, exchange(): return (lax.ppermute(to_high, axis, up), lax.ppermute(to_low, axis, down))  25.4 us
    unnamed x30, local copies, waits for them, and re-layouts  3.71 us
  transfers between devices with their start and end apart: 14, of which 7 were waited for; matrix products, arithmetic and copies ran while one was open for 0% of the time, Pallas kernels for 23%

profile of v2, /device:TPU:1, one launch (start us, length us, event | category | flops | bytes accessed | tf_op | source)
XLA Modules:
  0.0 98.9 jit_solution(14658508651530240621)
XLA Ops:
  0.6 2.1 %pack_rows.1 = (f32[2,8,8,512]{3,2,1,0:T(8,128)}, f32[2,8,8,512]{3,2,1,0:T(8,128)}) custom-call(f32[16,32,512]{2,1,0:T(8,128)} %s.3, f32[16,32,512]{2,1,0:T(8,128)} %s.3, f32[16,32,512]{2,1,0:T(8,128)} %k.5, f32[16,32,512]{2,1,0:T(8,128)} %k.5), custom_call_target="tpu_custom_call" | custom-call | tf_op jit(solution)/shard_map/pack_rows/pallas_call | solution.py:474
  2.7 3.9 %collective-permute-start = (f32[2,8,8,512]{3,2,1,0:T(8,128)}, f32[2,8,8,512]{3,2,1,0:T(8,128)S(1)}, u32[]{:S(2)}, u32[]{:S(2)}) collective-permute-start(f32[2,8,8,512]{3,2,1,0:T(8,128)} %get-tuple-element.32), channel_id=1, source_target_pairs={{0,1},{1,2},{2,3},{4,5},{5,6},{6,7},{8,9},{9,10},{10,11},{12,13},{... | collective-permute-start | bytes 786440 | tf_op jit(solution)/shard_map/ppermute | solution.py:493
  6.7 1.3 %collective-permute-start.1 = (f32[2,8,8,512]{3,2,1,0:T(8,128)}, f32[2,8,8,512]{3,2,1,0:T(8,128)S(1)}, u32[]{:S(2)}, u32[]{:S(2)}) collective-permute-start(f32[2,8,8,512]{3,2,1,0:T(8,128)} %get-tuple-element.33), channel_id=1, source_target_pairs={{1,0},{2,1},{3,2},{5,4},{6,5},{7,6},{9,8},{10,9},{11,10},{13,12},{... | collective-permute-start | bytes 786440 | tf_op jit(solution)/shard_map/ppermute | solution.py:493
  8.0 2.8 %mean.1.own_rows = f32[8,16,256]{2,1,0:T(8,128)} custom-call(f32[16,32,512]{2,1,0:T(8,128)} %k.5), custom_call_target="tpu_custom_call" | custom-call | tf_op jit(solution)/shard_map/mean/pallas_call | solution.py:474
  10.8 1.1 %collective-permute-done.from_low = f32[2,8,8,512]{3,2,1,0:T(8,128)S(1)} collective-permute-done((f32[2,8,8,512]{3,2,1,0:T(8,128)}, f32[2,8,8,512]{3,2,1,0:T(8,128)S(1)}, u32[]{:S(2)}, u32[]{:S(2)}) %collective-permute-start) | collective-permute-done | bytes 262176 | tf_op jit(solution)/shard_map/ppermute | solution.py:493
  11.9 7.5 %collective-permute-done.1.from_high = f32[2,8,8,512]{3,2,1,0:T(8,128)S(1)} collective-permute-done((f32[2,8,8,512]{3,2,1,0:T(8,128)}, f32[2,8,8,512]{3,2,1,0:T(8,128)S(1)}, u32[]{:S(2)}, u32[]{:S(2)}) %collective-permute-start.1) | collective-permute-done | bytes 262176 | tf_op jit(solution)/shard_map/ppermute | solution.py:493
  19.4 0.0 copy-done
  19.4 0.7 copy-done.1
  20.1 2.9 %pack_planes.1 = (f32[9,40,512]{2,1,0:T(8,128)}, f32[9,40,512]{2,1,0:T(8,128)}) custom-call(f32[16,32,512]{2,1,0:T(8,128)} %s.3, f32[16,32,512]{2,1,0:T(8,128)} %k.5, f32[2,8,8,512]{3,2,1,0:T(8,128)} %copy-done, f32[2,8,8,512]{3,2,1,0:T(8,128)} %copy-done.1), custom_call_target="tpu_custom_call" | custom-call | tf_op jit(solution)/shard_map/pack_planes/pallas_call | solution.py:474
  23.0 4.6 %collective-permute-start.2 = (f32[9,40,512]{2,1,0:T(8,128)}, f32[9,40,512]{2,1,0:T(8,128)S(1)}, u32[]{:S(2)}, u32[]{:S(2)}) collective-permute-start(f32[9,40,512]{2,1,0:T(8,128)} %get-tuple-element.36), channel_id=1, source_target_pairs={{0,4},{4,8},{8,12},{12,16},{16,20},{20,24},{24,28},{1,5},{5,9},{9,... | collective-permute-start | bytes 2211848 | tf_op jit(solution)/shard_map/ppermute | solution.py:493
  27.6 1.9 %collective-permute-start.3 = (f32[9,40,512]{2,1,0:T(8,128)}, f32[9,40,512]{2,1,0:T(8,128)S(1)}, u32[]{:S(2)}, u32[]{:S(2)}) collective-permute-start(f32[9,40,512]{2,1,0:T(8,128)} %get-tuple-element.37), channel_id=1, source_target_pairs={{4,0},{8,4},{12,8},{16,12},{20,16},{24,20},{28,24},{5,1},{9,5},{13... | collective-permute-start | bytes 2211848 | tf_op jit(solution)/shard_map/ppermute | solution.py:493
  29.5 0.0 copy-done.4
  29.5 3.1 %collective-permute-start.4 = (f32[8,16,256]{2,1,0:T(8,128)S(1)}, f32[8,16,256]{2,1,0:T(8,128)S(1)}, u32[]{:S(2)}, u32[]{:S(2)}) collective-permute-start(f32[8,16,256]{2,1,0:T(8,128)S(1)} %copy-done.4), channel_id=1, source_target_pairs={{0,1},{1,2},{2,3},{4,5},{5,6},{6,7},{8,9},{9,10},{10,11},{12,13},{... | collective-permute-start | bytes 393224 | tf_op jit(solution)/shard_map/ppermute | solution.py:493
  32.6 1.3 %collective-permute-start.5 = (f32[8,16,256]{2,1,0:T(8,128)S(1)}, f32[8,16,256]{2,1,0:T(8,128)S(1)}, u32[]{:S(2)}, u32[]{:S(2)}) collective-permute-start(f32[8,16,256]{2,1,0:T(8,128)S(1)} %copy-done.4), channel_id=1, source_target_pairs={{1,0},{2,1},{3,2},{5,4},{6,5},{7,6},{9,8},{10,9},{11,10},{13,12},{... | collective-permute-start | bytes 393224 | tf_op jit(solution)/shard_map/ppermute | solution.py:493
  33.9 2.3 %collective-permute-done.2.from_down = f32[9,40,512]{2,1,0:T(8,128)S(1)} collective-permute-done((f32[9,40,512]{2,1,0:T(8,128)}, f32[9,40,512]{2,1,0:T(8,128)S(1)}, u32[]{:S(2)}, u32[]{:S(2)}) %collective-permute-start.2) | collective-permute-done | bytes 737312 | tf_op jit(solution)/shard_map/ppermute | solution.py:493
  36.3 4.3 %collective-permute-done.3.from_up = f32[9,40,512]{2,1,0:T(8,128)S(1)} collective-permute-done((f32[9,40,512]{2,1,0:T(8,128)}, f32[9,40,512]{2,1,0:T(8,128)S(1)}, u32[]{:S(2)}, u32[]{:S(2)}) %collective-permute-start.3) | collective-permute-done | bytes 737312 | tf_op jit(solution)/shard_map/ppermute | solution.py:493
  40.6 0.0 copy-done.2
  40.6 0.9 copy-done.3
  41.5 15.2 %fine_level.1 = (f32[16,32,512]{2,1,0:T(8,128)}, f32[10,16,256]{2,1,0:T(8,128)}, f32[10,16,256]{2,1,0:T(8,128)}, f32[10,16,256]{2,1,0:T(8,128)}) custom-call(f32[16,32,512]{2,1,0:T(8,128)} %s.3, f32[16,32,512]{2,1,0:T(8,128)} %k.5, f32[2,8,8,512]{3,2,1,0:T(8,128)} %copy-done, f32[2,8,8,512]{3,2,1,0:T(8,128)} %copy-done.1, f32[9,40,512]{2,1,0:T(8,128)} %copy-done.2, ...), custom_call_target="tpu_custom_call" | custom-call | tf_op jit(solution)/shard_map/fine_level/pallas_call | solution.py:474
  56.7 0.0 collective-permute-done.4.from_low
  56.7 0.0 collective-permute-done.5.from_high
  56.8 3.1 %collective-permute-start.6 = (f32[10,16,256]{2,1,0:T(8,128)}, f32[10,16,256]{2,1,0:T(8,128)S(1)}, u32[]{:S(2)}, u32[]{:S(2)}) collective-permute-start(f32[10,16,256]{2,1,0:T(8,128)} %get-tuple-element.44.to_high), channel_id=1, source_target_pairs={{0,1},{1,2},{2,3},{4,5},{5,6},{6,7},{8,9},{9,10},{10,11},{12,13},{... | collective-permute-start | bytes 491528 | tf_op jit(solution)/shard_map/ppermute | solution.py:493
  59.9 1.3 %collective-permute-start.7 = (f32[10,16,256]{2,1,0:T(8,128)}, f32[10,16,256]{2,1,0:T(8,128)S(1)}, u32[]{:S(2)}, u32[]{:S(2)}) collective-permute-start(f32[10,16,256]{2,1,0:T(8,128)} %get-tuple-element.43.to_low), channel_id=1, source_target_pairs={{1,0},{2,1},{3,2},{5,4},{6,5},{7,6},{9,8},{10,9},{11,10},{13,12},{... | collective-permute-start | bytes 491528 | tf_op jit(solution)/shard_map/ppermute | solution.py:493
  61.2 0.0 copy-done.11
  61.2 0.0 copy-done.12
  61.2 2.1 %mean_planes.1 = (f32[8,48,256]{2,1,0:T(8,128)}, f32[6,48,256]{2,1,0:T(8,128)}, f32[6,48,256]{2,1,0:T(8,128)}) custom-call(f32[8,16,256]{2,1,0:T(8,128)} %mean.1.own_rows, f32[8,16,256]{2,1,0:T(8,128)} %copy-done.11, f32[8,16,256]{2,1,0:T(8,128)} %copy-done.12), custom_call_target="tpu_custom_call" | custom-call | tf_op jit(solution)/shard_map/mean_planes/pallas_call | solution.py:474
  63.3 2.1 %collective-permute-start.10 = (f32[6,48,256]{2,1,0:T(8,128)}, f32[6,48,256]{2,1,0:T(8,128)S(1)}, u32[]{:S(2)}, u32[]{:S(2)}) collective-permute-start(f32[6,48,256]{2,1,0:T(8,128)} %get-tuple-element.51), channel_id=1, source_target_pairs={{0,4},{4,8},{8,12},{12,16},{16,20},{20,24},{24,28},{1,5},{5,9},{9,... | collective-permute-start | bytes 884744 | tf_op jit(solution)/shard_map/ppermute | solution.py:493
  65.4 2.2 %collective-permute-start.11 = (f32[6,48,256]{2,1,0:T(8,128)}, f32[6,48,256]{2,1,0:T(8,128)S(1)}, u32[]{:S(2)}, u32[]{:S(2)}) collective-permute-start(f32[6,48,256]{2,1,0:T(8,128)} %get-tuple-element.52), channel_id=1, source_target_pairs={{4,0},{8,4},{12,8},{16,12},{20,16},{24,20},{28,24},{5,1},{9,5},{13... | collective-permute-start | bytes 884744 | tf_op jit(solution)/shard_map/ppermute | solution.py:493
  67.6 0.0 collective-permute-done.6.from_low
  67.6 0.0 collective-permute-done.7.from_high
  67.6 0.0 copy-start.10
  67.7 0.6 copy-done.9
  68.3 0.1 copy-done.10
  68.3 2.3 %source_planes.1 = (f32[10,48,256]{2,1,0:T(8,128)}, f32[6,48,256]{2,1,0:T(8,128)}, f32[6,48,256]{2,1,0:T(8,128)}) custom-call(f32[10,16,256]{2,1,0:T(8,128)} %get-tuple-element.39.own_rows, f32[10,16,256]{2,1,0:T(8,128)} %get-tuple-element.43.to_low, f32[10,16,256]{2,1,0:T(8,128)} %get-tuple-element.44.to_high, f32[10,16,256]{2,1,0:T(8,128)} %copy-done.9, ...), custom_call_target="tpu_custom_call" | custom-call | tf_op jit(solution)/shard_map/source_planes/pallas_call | solution.py:474
  70.6 3.3 %collective-permute-start.8 = (f32[6,48,256]{2,1,0:T(8,128)}, f32[6,48,256]{2,1,0:T(8,128)S(1)}, u32[]{:S(2)}, u32[]{:S(2)}) collective-permute-start(f32[6,48,256]{2,1,0:T(8,128)} %get-tuple-element.49), channel_id=1, source_target_pairs={{0,4},{4,8},{8,12},{12,16},{16,20},{20,24},{24,28},{1,5},{5,9},{9,... | collective-permute-start | bytes 884744 | tf_op jit(solution)/shard_map/ppermute | solution.py:493
  74.0 1.9 %collective-permute-start.9 = (f32[6,48,256]{2,1,0:T(8,128)}, f32[6,48,256]{2,1,0:T(8,128)S(1)}, u32[]{:S(2)}, u32[]{:S(2)}) collective-permute-start(f32[6,48,256]{2,1,0:T(8,128)} %get-tuple-element.50), channel_id=1, source_target_pairs={{4,0},{8,4},{12,8},{16,12},{20,16},{24,20},{28,24},{5,1},{9,5},{13... | collective-permute-start | bytes 884744 | tf_op jit(solution)/shard_map/ppermute | solution.py:493
  75.9 0.0 collective-permute-done.10.k_down
  75.9 0.0 collective-permute-done.11.k_up
  75.9 2.0 %collective-permute-done.8.from_down = f32[6,48,256]{2,1,0:T(8,128)S(1)} collective-permute-done((f32[6,48,256]{2,1,0:T(8,128)}, f32[6,48,256]{2,1,0:T(8,128)S(1)}, u32[]{:S(2)}, u32[]{:S(2)}) %collective-permute-start.8) | collective-permute-done | bytes 294944 | tf_op jit(solution)/shard_map/ppermute | solution.py:493
  77.9 4.3 %collective-permute-done.9.from_up = f32[6,48,256]{2,1,0:T(8,128)S(1)} collective-permute-done((f32[6,48,256]{2,1,0:T(8,128)}, f32[6,48,256]{2,1,0:T(8,128)S(1)}, u32[]{:S(2)}, u32[]{:S(2)}) %collective-permute-start.9) | collective-permute-done | bytes 294944 | tf_op jit(solution)/shard_map/ppermute | solution.py:493
  82.2 0.7 copy-done.8
  82.9 5.1 %middle_level.1 = (f32[8,16,256]{2,1,0:T(8,128)}, f32[4,24,128]{2,1,0:T(8,128)}, f32[4,24,128]{2,1,0:T(8,128)}, f32[9,24,128]{2,1,0:T(8,128)}, f32[9,24,128]{2,1,0:T(8,128)}) custom-call(f32[10,48,256]{2,1,0:T(8,128)} %get-tuple-element.45.s, f32[8,48,256]{2,1,0:T(8,128)} %get-tuple-element.48.k, f32[6,48,256]{2,1,0:T(8,128)} %copy-done.7, ...), custom_call_target="tpu_custom_call" | custom-call | tf_op jit(solution)/shard_map/middle_level/pallas_call | solution.py:474
  88.1 1.9 %collective-permute-start.12 = (f32[9,24,128]{2,1,0:T(8,128)}, f32[9,24,128]{2,1,0:T(8,128)S(1)}, u32[]{:S(2)}, u32[]{:S(2)}) collective-permute-start(f32[9,24,128]{2,1,0:T(8,128)} %get-tuple-element.56), channel_id=1, source_target_pairs={{0,4},{4,8},{8,12},{12,16},{16,20},{20,24},{24,28},{1,5},{5,9},{9,... | collective-permute-start | bytes 331784 | tf_op jit(solution)/shard_map/ppermute | solution.py:493
  90.0 2.4 %collective-permute-start.13 = (f32[9,24,128]{2,1,0:T(8,128)}, f32[9,24,128]{2,1,0:T(8,128)S(1)}, u32[]{:S(2)}, u32[]{:S(2)}) collective-permute-start(f32[9,24,128]{2,1,0:T(8,128)} %get-tuple-element.57), channel_id=1, source_target_pairs={{4,0},{8,4},{12,8},{16,12},{20,16},{24,20},{28,24},{5,1},{9,5},{13... | collective-permute-start | bytes 331784 | tf_op jit(solution)/shard_map/ppermute | solution.py:493
  92.4 0.0 collective-permute-done.12.from_down
  92.4 3.8 %collective-permute-done.13.from_up = f32[9,24,128]{2,1,0:T(8,128)S(1)} collective-permute-done((f32[9,24,128]{2,1,0:T(8,128)}, f32[9,24,128]{2,1,0:T(8,128)S(1)}, u32[]{:S(2)}, u32[]{:S(2)}) %collective-permute-start.13) | collective-permute-done | bytes 110624 | tf_op jit(solution)/shard_map/ppermute | solution.py:493
  96.3 0.6 copy-done.14
  96.9 2.0 %coarse_level.1 = (f32[4,8,128]{2,1,0:T(8,128)}, f32[4,8,128]{2,1,0:T(8,128)}) custom-call(f32[4,24,128]{2,1,0:T(8,128)} %get-tuple-element.54.s, f32[4,24,128]{2,1,0:T(8,128)} %get-tuple-element.55.k, f32[9,24,128]{2,1,0:T(8,128)} %copy-done.13, f32[9,24,128]{2,1,0:T(8,128)} %copy-done.14), custom_call_target="tpu_custom_call" | custom-call | tf_op jit(solution)/shard_map/coarse_level/pallas_call | solution.py:474
  (18 shorter events, 0.0 us)
Async XLA Ops:
  2.7 9.2 %collective-permute-start = (f32[2,8,8,512]{3,2,1,0:T(8,128)}, f32[2,8,8,512]{3,2,1,0:T(8,128)S(1)}, u32[]{:S(2)}, u32[]{:S(2)}) collective-permute-start(f32[2,8,8,512]{3,2,1,0:T(8,128)} %get-tuple-element.32), channel_id=1, source_target_pairs={{0,1},{1,2},{2,3},{4,5},{5,6},{6,7},{8,9},{9,10},{10,11},{12,13},{... | collective-permute-start | bytes 786440 | tf_op jit(solution)/shard_map/ppermute | solution.py:493
  6.7 12.7 %collective-permute-start.1 = (f32[2,8,8,512]{3,2,1,0:T(8,128)}, f32[2,8,8,512]{3,2,1,0:T(8,128)S(1)}, u32[]{:S(2)}, u32[]{:S(2)}) collective-permute-start(f32[2,8,8,512]{3,2,1,0:T(8,128)} %get-tuple-element.33), channel_id=1, source_target_pairs={{1,0},{2,1},{3,2},{5,4},{6,5},{7,6},{9,8},{10,9},{11,10},{13,12},{... | collective-permute-start | bytes 786440 | tf_op jit(solution)/shard_map/ppermute | solution.py:493
  10.8 18.7 %copy-start.4 = (f32[8,16,256]{2,1,0:T(8,128)S(1)}, f32[8,16,256]{2,1,0:T(8,128)}, u32[]{:S(2)}) copy-start(f32[8,16,256]{2,1,0:T(8,128)} %mean.1.own_rows) | copy-start | bytes 393220
  11.9 7.5 %copy-start = (f32[2,8,8,512]{3,2,1,0:T(8,128)}, f32[2,8,8,512]{3,2,1,0:T(8,128)S(1)}, u32[]{:S(2)}) copy-start(f32[2,8,8,512]{3,2,1,0:T(8,128)S(1)} %collective-permute-done.from_low) | copy-start | bytes 786436
  19.4 0.7 copy-start.1
  23.0 13.3 %collective-permute-start.2 = (f32[9,40,512]{2,1,0:T(8,128)}, f32[9,40,512]{2,1,0:T(8,128)S(1)}, u32[]{:S(2)}, u32[]{:S(2)}) collective-permute-start(f32[9,40,512]{2,1,0:T(8,128)} %get-tuple-element.36), channel_id=1, source_target_pairs={{0,4},{4,8},{8,12},{12,16},{16,20},{20,24},{24,28},{1,5},{5,9},{9,... | collective-permute-start | bytes 2211848 | tf_op jit(solution)/shard_map/ppermute | solution.py:493
  27.6 13.0 %collective-permute-start.3 = (f32[9,40,512]{2,1,0:T(8,128)}, f32[9,40,512]{2,1,0:T(8,128)S(1)}, u32[]{:S(2)}, u32[]{:S(2)}) collective-permute-start(f32[9,40,512]{2,1,0:T(8,128)} %get-tuple-element.37), channel_id=1, source_target_pairs={{4,0},{8,4},{12,8},{16,12},{20,16},{24,20},{28,24},{5,1},{9,5},{13... | collective-permute-start | bytes 2211848 | tf_op jit(solution)/shard_map/ppermute | solution.py:493
  29.5 27.2 %collective-permute-start.4 = (f32[8,16,256]{2,1,0:T(8,128)S(1)}, f32[8,16,256]{2,1,0:T(8,128)S(1)}, u32[]{:S(2)}, u32[]{:S(2)}) collective-permute-start(f32[8,16,256]{2,1,0:T(8,128)S(1)} %copy-done.4), channel_id=1, source_target_pairs={{0,1},{1,2},{2,3},{4,5},{5,6},{6,7},{8,9},{9,10},{10,11},{12,13},{... | collective-permute-start | bytes 393224 | tf_op jit(solution)/shard_map/ppermute | solution.py:493
  32.6 24.1 %collective-permute-start.5 = (f32[8,16,256]{2,1,0:T(8,128)S(1)}, f32[8,16,256]{2,1,0:T(8,128)S(1)}, u32[]{:S(2)}, u32[]{:S(2)}) collective-permute-start(f32[8,16,256]{2,1,0:T(8,128)S(1)} %copy-done.4), channel_id=1, source_target_pairs={{1,0},{2,1},{3,2},{5,4},{6,5},{7,6},{9,8},{10,9},{11,10},{13,12},{... | collective-permute-start | bytes 393224 | tf_op jit(solution)/shard_map/ppermute | solution.py:493
  36.3 4.3 %copy-start.2 = (f32[9,40,512]{2,1,0:T(8,128)}, f32[9,40,512]{2,1,0:T(8,128)S(1)}, u32[]{:S(2)}) copy-start(f32[9,40,512]{2,1,0:T(8,128)S(1)} %collective-permute-done.2.from_down) | copy-start | bytes 2211844
  40.6 0.9 copy-start.3
  56.7 4.5 %copy-start.11 = (f32[8,16,256]{2,1,0:T(8,128)}, f32[8,16,256]{2,1,0:T(8,128)S(1)}, u32[]{:S(2)}) copy-start(f32[8,16,256]{2,1,0:T(8,128)S(1)} %collective-permute-done.4.from_low) | copy-start | bytes 393220
  56.7 4.5 %copy-start.12 = (f32[8,16,256]{2,1,0:T(8,128)}, f32[8,16,256]{2,1,0:T(8,128)S(1)}, u32[]{:S(2)}) copy-start(f32[8,16,256]{2,1,0:T(8,128)S(1)} %collective-permute-done.5.from_high) | copy-start | bytes 393220
  56.8 10.9 %collective-permute-start.6 = (f32[10,16,256]{2,1,0:T(8,128)}, f32[10,16,256]{2,1,0:T(8,128)S(1)}, u32[]{:S(2)}, u32[]{:S(2)}) collective-permute-start(f32[10,16,256]{2,1,0:T(8,128)} %get-tuple-element.44.to_high), channel_id=1, source_target_pairs={{0,1},{1,2},{2,3},{4,5},{5,6},{6,7},{8,9},{9,10},{10,11},{12,13},{... | collective-permute-start | bytes 491528 | tf_op jit(solution)/shard_map/ppermute | solution.py:493
  59.9 7.8 %collective-permute-start.7 = (f32[10,16,256]{2,1,0:T(8,128)}, f32[10,16,256]{2,1,0:T(8,128)S(1)}, u32[]{:S(2)}, u32[]{:S(2)}) collective-permute-start(f32[10,16,256]{2,1,0:T(8,128)} %get-tuple-element.43.to_low), channel_id=1, source_target_pairs={{1,0},{2,1},{3,2},{5,4},{6,5},{7,6},{9,8},{10,9},{11,10},{13,12},{... | collective-permute-start | bytes 491528 | tf_op jit(solution)/shard_map/ppermute | solution.py:493
  63.3 12.6 %collective-permute-start.10 = (f32[6,48,256]{2,1,0:T(8,128)}, f32[6,48,256]{2,1,0:T(8,128)S(1)}, u32[]{:S(2)}, u32[]{:S(2)}) collective-permute-start(f32[6,48,256]{2,1,0:T(8,128)} %get-tuple-element.51), channel_id=1, source_target_pairs={{0,4},{4,8},{8,12},{12,16},{16,20},{20,24},{24,28},{1,5},{5,9},{9,... | collective-permute-start | bytes 884744 | tf_op jit(solution)/shard_map/ppermute | solution.py:493
  65.4 10.5 %collective-permute-start.11 = (f32[6,48,256]{2,1,0:T(8,128)}, f32[6,48,256]{2,1,0:T(8,128)S(1)}, u32[]{:S(2)}, u32[]{:S(2)}) collective-permute-start(f32[6,48,256]{2,1,0:T(8,128)} %get-tuple-element.52), channel_id=1, source_target_pairs={{4,0},{8,4},{12,8},{16,12},{20,16},{24,20},{28,24},{5,1},{9,5},{13... | collective-permute-start | bytes 884744 | tf_op jit(solution)/shard_map/ppermute | solution.py:493
  67.6 0.7 copy-start.9
  67.6 0.7 copy-start.10
  70.6 7.3 %collective-permute-start.8 = (f32[6,48,256]{2,1,0:T(8,128)}, f32[6,48,256]{2,1,0:T(8,128)S(1)}, u32[]{:S(2)}, u32[]{:S(2)}) collective-permute-start(f32[6,48,256]{2,1,0:T(8,128)} %get-tuple-element.49), channel_id=1, source_target_pairs={{0,4},{4,8},{8,12},{12,16},{16,20},{20,24},{24,28},{1,5},{5,9},{9,... | collective-permute-start | bytes 884744 | tf_op jit(solution)/shard_map/ppermute | solution.py:493
  74.0 8.3 %collective-permute-start.9 = (f32[6,48,256]{2,1,0:T(8,128)}, f32[6,48,256]{2,1,0:T(8,128)S(1)}, u32[]{:S(2)}, u32[]{:S(2)}) collective-permute-start(f32[6,48,256]{2,1,0:T(8,128)} %get-tuple-element.50), channel_id=1, source_target_pairs={{4,0},{8,4},{12,8},{16,12},{20,16},{24,20},{28,24},{5,1},{9,5},{13... | collective-permute-start | bytes 884744 | tf_op jit(solution)/shard_map/ppermute | solution.py:493
  75.9 6.3 %copy-start.5 = (f32[6,48,256]{2,1,0:T(8,128)}, f32[6,48,256]{2,1,0:T(8,128)S(1)}, u32[]{:S(2)}) copy-start(f32[6,48,256]{2,1,0:T(8,128)S(1)} %collective-permute-done.10.k_down) | copy-start | bytes 884740
  75.9 6.3 %copy-start.6 = (f32[6,48,256]{2,1,0:T(8,128)}, f32[6,48,256]{2,1,0:T(8,128)S(1)}, u32[]{:S(2)}) copy-start(f32[6,48,256]{2,1,0:T(8,128)S(1)} %collective-permute-done.11.k_up) | copy-start | bytes 884740
  77.9 4.3 %copy-start.7 = (f32[6,48,256]{2,1,0:T(8,128)}, f32[6,48,256]{2,1,0:T(8,128)S(1)}, u32[]{:S(2)}) copy-start(f32[6,48,256]{2,1,0:T(8,128)S(1)} %collective-permute-done.8.from_down) | copy-start | bytes 884740
  82.2 0.7 copy-start.8
  88.1 4.3 %collective-permute-start.12 = (f32[9,24,128]{2,1,0:T(8,128)}, f32[9,24,128]{2,1,0:T(8,128)S(1)}, u32[]{:S(2)}, u32[]{:S(2)}) collective-permute-start(f32[9,24,128]{2,1,0:T(8,128)} %get-tuple-element.56), channel_id=1, source_target_pairs={{0,4},{4,8},{8,12},{12,16},{16,20},{20,24},{24,28},{1,5},{5,9},{9,... | collective-permute-start | bytes 331784 | tf_op jit(solution)/shard_map/ppermute | solution.py:493
  90.0 6.3 %collective-permute-start.13 = (f32[9,24,128]{2,1,0:T(8,128)}, f32[9,24,128]{2,1,0:T(8,128)S(1)}, u32[]{:S(2)}, u32[]{:S(2)}) collective-permute-start(f32[9,24,128]{2,1,0:T(8,128)} %get-tuple-element.57), channel_id=1, source_target_pairs={{4,0},{8,4},{12,8},{16,12},{20,16},{24,20},{28,24},{5,1},{9,5},{13... | collective-permute-start | bytes 331784 | tf_op jit(solution)/shard_map/ppermute | solution.py:493
  92.4 3.9 %copy-start.13 = (f32[9,24,128]{2,1,0:T(8,128)}, f32[9,24,128]{2,1,0:T(8,128)S(1)}, u32[]{:S(2)}) copy-start(f32[9,24,128]{2,1,0:T(8,128)S(1)} %collective-permute-done.12.from_down) | copy-start | bytes 331780
  96.2 0.6 copy-start.14

commit v3 on v2

--- a/solution.py
+++ b/solution.py
@@ -467,14 +467,29 @@
         rest[2 * p + 1] = pick(even_own, black, red)
 
 
-def call(kernel, outs, scratch, *args, in_specs=None, name=None):
-    extra = {} if in_specs is None else {"in_specs": in_specs, "grid": (1,)}
-    if in_specs is not None:
-        extra["out_specs"] = [pl.BlockSpec(o, lambda i, n=len(o): (0,) * n) for o in outs]
+def limit(scratch):
+    words = 0
+    for shape in scratch:
+        size = 1
+        for n in shape:
+            size *= n
+        words += size
+    return 4 * words + (12 << 20)
+
+
+def call(kernel, outs, scratch, *args, in_specs=None, name=None, results=()):
+    extra = {}
+    if in_specs is None:
+        args = [pltpu.with_memory_space_constraint(a, pltpu.VMEM) for a in args]
+    else:
+        extra = {"in_specs": in_specs, "grid": (1,)}
+        extra["out_specs"] = [pl.BlockSpec(memory_space=pltpu.VMEM) for _ in outs]
     return pl.pallas_call(
         kernel,
-        out_shape=[jax.ShapeDtypeStruct(o, F32) for o in outs],
+        out_shape=[jax.ShapeDtypeStruct(o, F32) if i in results else pltpu.VMEM(o, F32)
+                   for i, o in enumerate(outs)],
         scratch_shapes=[pltpu.VMEM(shape, F32) for shape in scratch],
+        compiler_params=pltpu.CompilerParams(vmem_limit_bytes=limit(scratch)),
         name=name,
         **extra,
     )(*args)

time: 99.9 us -> 84.2 us (0.84)
  Pallas kernels: 34.5 us -> 16.7 us
  local copies, waits for them, and re-layouts: 3.71 us -> 5.29 us
  starting transfers between devices: 34.5 us -> 35.7 us
    pallas_call x8, Pallas kernels: 34.5 us -> 16.7 us  [call(): pl.pallas_call(kernel, out_shape=[jax.ShapeDtypeStruct(o, F32) if i in re...]
    unnamed x30 -> x12, local copies, waits for them, and re-layouts: 3.71 us -> 5.29 us
    ppermute x14, starting transfers between devices: 34.5 us -> 35.7 us  [exchange(): return (lax.ppermute(to_high, axis, up), lax.ppermute(to_low, axis, down))]
  transfers between devices with their start and end apart: 14 -> 14, of which waited for: 7 -> 8; matrix products, arithmetic and copies ran while one was open for 0% -> 2% of each run, Pallas kernels for 23% -> 16%
where the time goes in v3:
time: 84.2 us; the launch traced here: 83.7 us
  starting transfers between devices  35.7 us (42%)
  waiting for transfers between devices  25.1 us (30%)
  Pallas kernels  16.7 us (20%)
  local copies, waits for them, and re-layouts  5.29 us (6%)
  between operations  0.86 us (1%)
    ppermute x14, starting transfers between devices, exchange(): return (lax.ppermute(to_high, axis, up), lax.ppermute(to_low, axis, down))  35.7 us
    ppermute x14, waiting for transfers between devices, exchange(): return (lax.ppermute(to_high, axis, up), lax.ppermute(to_low, axis, down))  25.1 us
    pallas_call x8, Pallas kernels, call(): pl.pallas_call(kernel, out_shape=[jax.ShapeDtypeStruct(o, F32) if i in re...  16.7 us
    unnamed x12, local copies, waits for them, and re-layouts  5.29 us
  transfers between devices with their start and end apart: 14, of which 8 were waited for; matrix products, arithmetic and copies ran while one was open for 2% of the time, Pallas kernels for 16%

profile of v3, /device:TPU:1, one launch (start us, length us, event | category | flops | bytes accessed | tf_op | source)
XLA Modules:
  0.0 83.7 jit_solution(16414853794493893390)
XLA Ops:
  0.6 0.0 copy-start
  0.6 1.2 %copy-done = f32[16,32,512]{2,1,0:T(8,128)S(1)} copy-done((f32[16,32,512]{2,1,0:T(8,128)S(1)}, f32[16,32,512]{2,1,0:T(8,128)}, u32[]{:S(2)}) %copy-start) | copy-done | bytes 1048600
  1.9 0.0 copy-start.2
  1.9 1.2 %copy-done.2 = f32[16,32,512]{2,1,0:T(8,128)S(1)} copy-done((f32[16,32,512]{2,1,0:T(8,128)S(1)}, f32[16,32,512]{2,1,0:T(8,128)}, u32[]{:S(2)}) %copy-start.2) | copy-done | bytes 1048600
  3.1 0.0 copy-start.1
  3.1 0.2 pack_rows.1
  3.3 0.0 copy-start.3
  3.3 4.1 %collective-permute-start = (f32[2,8,8,512]{3,2,1,0:T(8,128)S(1)}, f32[2,8,8,512]{3,2,1,0:T(8,128)S(1)}, u32[]{:S(2)}, u32[]{:S(2)}) collective-permute-start(f32[2,8,8,512]{3,2,1,0:T(8,128)S(1)} %get-tuple-element.32), channel_id=1, source_target_pairs={{0,1},{1,2},{2,3},{4,5},{5,6},{6,7},{8,9},{9,10},{10,11},{12,13},{... | collective-permute-start | bytes 786440 | tf_op jit(solution)/shard_map/ppermute | solution.py:508
  7.4 1.3 %collective-permute-start.1 = (f32[2,8,8,512]{3,2,1,0:T(8,128)S(1)}, f32[2,8,8,512]{3,2,1,0:T(8,128)S(1)}, u32[]{:S(2)}, u32[]{:S(2)}) collective-permute-start(f32[2,8,8,512]{3,2,1,0:T(8,128)S(1)} %get-tuple-element.33), channel_id=1, source_target_pairs={{1,0},{2,1},{3,2},{5,4},{6,5},{7,6},{9,8},{10,9},{11,10},{13,12},{... | collective-permute-start | bytes 786440 | tf_op jit(solution)/shard_map/ppermute | solution.py:508
  8.7 0.0 copy-done.1
  8.7 1.0 %mean.1.own_rows = f32[8,16,256]{2,1,0:T(8,128)S(1)} custom-call(f32[16,32,512]{2,1,0:T(8,128)S(1)} %copy-done.1), custom_call_target="tpu_custom_call" | custom-call | tf_op jit(solution)/shard_map/mean/pallas_call | solution.py:487
  9.6 2.7 %collective-permute-done.from_low = f32[2,8,8,512]{3,2,1,0:T(8,128)S(1)} collective-permute-done((f32[2,8,8,512]{3,2,1,0:T(8,128)S(1)}, f32[2,8,8,512]{3,2,1,0:T(8,128)S(1)}, u32[]{:S(2)}, u32[]{:S(2)}) %collective-permute-start) | collective-permute-done | bytes 262176 | tf_op jit(solution)/shard_map/ppermute | solution.py:508
  12.3 7.6 %collective-permute-done.1.from_high = f32[2,8,8,512]{3,2,1,0:T(8,128)S(1)} collective-permute-done((f32[2,8,8,512]{3,2,1,0:T(8,128)S(1)}, f32[2,8,8,512]{3,2,1,0:T(8,128)S(1)}, u32[]{:S(2)}, u32[]{:S(2)}) %collective-permute-start.1) | collective-permute-done | bytes 262176 | tf_op jit(solution)/shard_map/ppermute | solution.py:508
  19.9 0.0 copy-done.3
  19.9 0.1 pack_planes.1
  20.0 4.6 %collective-permute-start.2 = (f32[9,40,512]{2,1,0:T(8,128)S(1)}, f32[9,40,512]{2,1,0:T(8,128)S(1)}, u32[]{:S(2)}, u32[]{:S(2)}) collective-permute-start(f32[9,40,512]{2,1,0:T(8,128)S(1)} %get-tuple-element.36), channel_id=1, source_target_pairs={{0,4},{4,8},{8,12},{12,16},{16,20},{20,24},{24,28},{1,5},{5,9},{9,... | collective-permute-start | bytes 2211848 | tf_op jit(solution)/shard_map/ppermute | solution.py:508
  24.6 1.9 %collective-permute-start.3 = (f32[9,40,512]{2,1,0:T(8,128)S(1)}, f32[9,40,512]{2,1,0:T(8,128)S(1)}, u32[]{:S(2)}, u32[]{:S(2)}) collective-permute-start(f32[9,40,512]{2,1,0:T(8,128)S(1)} %get-tuple-element.37), channel_id=1, source_target_pairs={{4,0},{8,4},{12,8},{16,12},{20,16},{24,20},{28,24},{5,1},{9,5},{13... | collective-permute-start | bytes 2211848 | tf_op jit(solution)/shard_map/ppermute | solution.py:508
  26.6 3.1 %collective-permute-start.4 = (f32[8,16,256]{2,1,0:T(8,128)S(1)}, f32[8,16,256]{2,1,0:T(8,128)S(1)}, u32[]{:S(2)}, u32[]{:S(2)}) collective-permute-start(f32[8,16,256]{2,1,0:T(8,128)S(1)} %mean.1.own_rows), channel_id=1, source_target_pairs={{0,1},{1,2},{2,3},{4,5},{5,6},{6,7},{8,9},{9,10},{10,11},{12,13},{... | collective-permute-start | bytes 393224 | tf_op jit(solution)/shard_map/ppermute | solution.py:508
  29.7 1.3 %collective-permute-start.5 = (f32[8,16,256]{2,1,0:T(8,128)S(1)}, f32[8,16,256]{2,1,0:T(8,128)S(1)}, u32[]{:S(2)}, u32[]{:S(2)}) collective-permute-start(f32[8,16,256]{2,1,0:T(8,128)S(1)} %mean.1.own_rows), channel_id=1, source_target_pairs={{1,0},{2,1},{3,2},{5,4},{6,5},{7,6},{9,8},{10,9},{11,10},{13,12},{... | collective-permute-start | bytes 393224 | tf_op jit(solution)/shard_map/ppermute | solution.py:508
  31.0 2.0 %collective-permute-done.2.from_down = f32[9,40,512]{2,1,0:T(8,128)S(1)} collective-permute-done((f32[9,40,512]{2,1,0:T(8,128)S(1)}, f32[9,40,512]{2,1,0:T(8,128)S(1)}, u32[]{:S(2)}, u32[]{:S(2)}) %collective-permute-start.2) | collective-permute-done | bytes 737312 | tf_op jit(solution)/shard_map/ppermute | solution.py:508
  33.0 4.4 %collective-permute-done.3.from_up = f32[9,40,512]{2,1,0:T(8,128)S(1)} collective-permute-done((f32[9,40,512]{2,1,0:T(8,128)S(1)}, f32[9,40,512]{2,1,0:T(8,128)S(1)}, u32[]{:S(2)}, u32[]{:S(2)}) %collective-permute-start.3) | collective-permute-done | bytes 737312 | tf_op jit(solution)/shard_map/ppermute | solution.py:508
  37.4 12.0 %fine_level.1 = (f32[16,32,512]{2,1,0:T(8,128)S(1)}, f32[10,16,256]{2,1,0:T(8,128)S(1)}, f32[10,16,256]{2,1,0:T(8,128)S(1)}, f32[10,16,256]{2,1,0:T(8,128)S(1)}) custom-call(f32[16,32,512]{2,1,0:T(8,128)S(1)} %copy-done.3, f32[16,32,512]{2,1,0:T(8,128)S(1)} %copy-done.1, f32[2,8,8,512]{3,2,1,0:T(8,128)S(1)} %collective-permute-done.from_low, ...), custom_call_target="tpu_custom_call" | custom-call | tf_op jit(solution)/shard_map/fine_level/pallas_call | solution.py:487
  49.5 0.0 collective-permute-done.4.from_low
  49.5 0.0 collective-permute-done.5.from_high
  49.5 3.1 %collective-permute-start.6 = (f32[10,16,256]{2,1,0:T(8,128)S(1)}, f32[10,16,256]{2,1,0:T(8,128)S(1)}, u32[]{:S(2)}, u32[]{:S(2)}) collective-permute-start(f32[10,16,256]{2,1,0:T(8,128)S(1)} %get-tuple-element.44.to_high), channel_id=1, source_target_pairs={{0,1},{1,2},{2,3},{4,5},{5,6},{6,7},{8,9},{9,10},{10,11},{12,13},{... | collective-permute-start | bytes 491528 | tf_op jit(solution)/shard_map/ppermute | solution.py:508
  52.6 1.3 %collective-permute-start.7 = (f32[10,16,256]{2,1,0:T(8,128)S(1)}, f32[10,16,256]{2,1,0:T(8,128)S(1)}, u32[]{:S(2)}, u32[]{:S(2)}) collective-permute-start(f32[10,16,256]{2,1,0:T(8,128)S(1)} %get-tuple-element.43.to_low), channel_id=1, source_target_pairs={{1,0},{2,1},{3,2},{5,4},{6,5},{7,6},{9,8},{10,9},{11,10},{13,12},{... | collective-permute-start | bytes 491528 | tf_op jit(solution)/shard_map/ppermute | solution.py:508
  53.9 0.1 mean_planes.1
  54.0 2.0 %collective-permute-start.10 = (f32[6,48,256]{2,1,0:T(8,128)S(1)}, f32[6,48,256]{2,1,0:T(8,128)S(1)}, u32[]{:S(2)}, u32[]{:S(2)}) collective-permute-start(f32[6,48,256]{2,1,0:T(8,128)S(1)} %get-tuple-element.51), channel_id=1, source_target_pairs={{0,4},{4,8},{8,12},{12,16},{16,20},{20,24},{24,28},{1,5},{5,9},{9,... | collective-permute-start | bytes 884744 | tf_op jit(solution)/shard_map/ppermute | solution.py:508
  56.0 2.3 %collective-permute-start.11 = (f32[6,48,256]{2,1,0:T(8,128)S(1)}, f32[6,48,256]{2,1,0:T(8,128)S(1)}, u32[]{:S(2)}, u32[]{:S(2)}) collective-permute-start(f32[6,48,256]{2,1,0:T(8,128)S(1)} %get-tuple-element.52), channel_id=1, source_target_pairs={{4,0},{8,4},{12,8},{16,12},{20,16},{24,20},{28,24},{5,1},{9,5},{13... | collective-permute-start | bytes 884744 | tf_op jit(solution)/shard_map/ppermute | solution.py:508
  58.3 0.0 collective-permute-done.6.from_low
  58.3 0.3 collective-permute-done.7.from_high
  58.7 0.1 source_planes.1
  58.7 4.3 %collective-permute-start.8 = (f32[6,48,256]{2,1,0:T(8,128)S(1)}, f32[6,48,256]{2,1,0:T(8,128)S(1)}, u32[]{:S(2)}, u32[]{:S(2)}) collective-permute-start(f32[6,48,256]{2,1,0:T(8,128)S(1)} %get-tuple-element.49), channel_id=1, source_target_pairs={{0,4},{4,8},{8,12},{12,16},{16,20},{20,24},{24,28},{1,5},{5,9},{9,... | collective-permute-start | bytes 884744 | tf_op jit(solution)/shard_map/ppermute | solution.py:508
  63.1 1.9 %collective-permute-start.9 = (f32[6,48,256]{2,1,0:T(8,128)S(1)}, f32[6,48,256]{2,1,0:T(8,128)S(1)}, u32[]{:S(2)}, u32[]{:S(2)}) collective-permute-start(f32[6,48,256]{2,1,0:T(8,128)S(1)} %get-tuple-element.50), channel_id=1, source_target_pairs={{4,0},{8,4},{12,8},{16,12},{20,16},{24,20},{28,24},{5,1},{9,5},{13... | collective-permute-start | bytes 884744 | tf_op jit(solution)/shard_map/ppermute | solution.py:508
  65.0 0.0 collective-permute-done.10.k_down
  65.0 0.0 collective-permute-done.11.k_up
  65.0 1.7 %collective-permute-done.8.from_down = f32[6,48,256]{2,1,0:T(8,128)S(1)} collective-permute-done((f32[6,48,256]{2,1,0:T(8,128)S(1)}, f32[6,48,256]{2,1,0:T(8,128)S(1)}, u32[]{:S(2)}, u32[]{:S(2)}) %collective-permute-start.8) | collective-permute-done | bytes 294944 | tf_op jit(solution)/shard_map/ppermute | solution.py:508
  66.7 4.4 %collective-permute-done.9.from_up = f32[6,48,256]{2,1,0:T(8,128)S(1)} collective-permute-done((f32[6,48,256]{2,1,0:T(8,128)S(1)}, f32[6,48,256]{2,1,0:T(8,128)S(1)}, u32[]{:S(2)}, u32[]{:S(2)}) %collective-permute-start.9) | collective-permute-done | bytes 294944 | tf_op jit(solution)/shard_map/ppermute | solution.py:508
  71.1 2.9 %middle_level.1 = (f32[8,16,256]{2,1,0:T(8,128)S(1)}, f32[4,24,128]{2,1,0:T(8,128)S(1)}, f32[4,24,128]{2,1,0:T(8,128)S(1)}, f32[9,24,128]{2,1,0:T(8,128)S(1)}, f32[9,24,128]{2,1,0:T(8,128)S(1)}) custom-call(f32[10,48,256]{2,1,0:T(8,128)S(1)} %get-tuple-element.45.s, f32[8,48,256]{2,1,0:T(8,128)S(1)} %get-tuple-element.48.k, ...), custom_call_target="tpu_custom_call" | custom-call | tf_op jit(solution)/shard_map/middle_level/pallas_call | solution.py:487
  74.0 1.9 %collective-permute-start.12 = (f32[9,24,128]{2,1,0:T(8,128)S(1)}, f32[9,24,128]{2,1,0:T(8,128)S(1)}, u32[]{:S(2)}, u32[]{:S(2)}) collective-permute-start(f32[9,24,128]{2,1,0:T(8,128)S(1)} %get-tuple-element.56), channel_id=1, source_target_pairs={{0,4},{4,8},{8,12},{12,16},{16,20},{20,24},{24,28},{1,5},{5,9},{9,... | collective-permute-start | bytes 331784 | tf_op jit(solution)/shard_map/ppermute | solution.py:508
  76.0 2.4 %collective-permute-start.13 = (f32[9,24,128]{2,1,0:T(8,128)S(1)}, f32[9,24,128]{2,1,0:T(8,128)S(1)}, u32[]{:S(2)}, u32[]{:S(2)}) collective-permute-start(f32[9,24,128]{2,1,0:T(8,128)S(1)} %get-tuple-element.57), channel_id=1, source_target_pairs={{4,0},{8,4},{12,8},{16,12},{20,16},{24,20},{28,24},{5,1},{9,5},{13... | collective-permute-start | bytes 331784 | tf_op jit(solution)/shard_map/ppermute | solution.py:508
  78.4 1.0 %copy.6 = f32[16,32,512]{2,1,0:T(8,128)} copy(f32[16,32,512]{2,1,0:T(8,128)S(1)} %get-tuple-element.60) | data formatting | bytes 2097152
  79.4 0.7 copy.7
  80.0 0.0 collective-permute-done.12.from_down
  80.0 2.0 %collective-permute-done.13.from_up = f32[9,24,128]{2,1,0:T(8,128)S(1)} collective-permute-done((f32[9,24,128]{2,1,0:T(8,128)S(1)}, f32[9,24,128]{2,1,0:T(8,128)S(1)}, u32[]{:S(2)}, u32[]{:S(2)}) %collective-permute-start.13) | collective-permute-done | bytes 110624 | tf_op jit(solution)/shard_map/ppermute | solution.py:508
  82.0 0.4 coarse_level.1
  82.4 0.6 copy.8
  83.1 0.6 copy.9
Async XLA Ops:
  0.6 1.2 %copy-start = (f32[16,32,512]{2,1,0:T(8,128)S(1)}, f32[16,32,512]{2,1,0:T(8,128)}, u32[]{:S(2)}) copy-start(f32[16,32,512]{2,1,0:T(8,128)} %k.5) | copy-start | bytes 3145732
  1.9 1.2 %copy-start.2 = (f32[16,32,512]{2,1,0:T(8,128)S(1)}, f32[16,32,512]{2,1,0:T(8,128)}, u32[]{:S(2)}) copy-start(f32[16,32,512]{2,1,0:T(8,128)} %s.3) | copy-start | bytes 3145732
  3.1 5.6 %copy-start.1 = (f32[16,32,512]{2,1,0:T(8,128)S(1)}, f32[16,32,512]{2,1,0:T(8,128)}, u32[]{:S(2)}) copy-start(f32[16,32,512]{2,1,0:T(8,128)} %k.5) | copy-start | bytes 3145732
  3.3 16.6 %copy-start.3 = (f32[16,32,512]{2,1,0:T(8,128)S(1)}, f32[16,32,512]{2,1,0:T(8,128)}, u32[]{:S(2)}) copy-start(f32[16,32,512]{2,1,0:T(8,128)} %s.3) | copy-start | bytes 3145732
  3.3 9.0 %collective-permute-start = (f32[2,8,8,512]{3,2,1,0:T(8,128)S(1)}, f32[2,8,8,512]{3,2,1,0:T(8,128)S(1)}, u32[]{:S(2)}, u32[]{:S(2)}) collective-permute-start(f32[2,8,8,512]{3,2,1,0:T(8,128)S(1)} %get-tuple-element.32), channel_id=1, source_target_pairs={{0,1},{1,2},{2,3},{4,5},{5,6},{6,7},{8,9},{9,10},{10,11},{12,13},{... | collective-permute-start | bytes 786440 | tf_op jit(solution)/shard_map/ppermute | solution.py:508
  7.4 12.5 %collective-permute-start.1 = (f32[2,8,8,512]{3,2,1,0:T(8,128)S(1)}, f32[2,8,8,512]{3,2,1,0:T(8,128)S(1)}, u32[]{:S(2)}, u32[]{:S(2)}) collective-permute-start(f32[2,8,8,512]{3,2,1,0:T(8,128)S(1)} %get-tuple-element.33), channel_id=1, source_target_pairs={{1,0},{2,1},{3,2},{5,4},{6,5},{7,6},{9,8},{10,9},{11,10},{13,12},{... | collective-permute-start | bytes 786440 | tf_op jit(solution)/shard_map/ppermute | solution.py:508
  20.0 13.0 %collective-permute-start.2 = (f32[9,40,512]{2,1,0:T(8,128)S(1)}, f32[9,40,512]{2,1,0:T(8,128)S(1)}, u32[]{:S(2)}, u32[]{:S(2)}) collective-permute-start(f32[9,40,512]{2,1,0:T(8,128)S(1)} %get-tuple-element.36), channel_id=1, source_target_pairs={{0,4},{4,8},{8,12},{12,16},{16,20},{20,24},{24,28},{1,5},{5,9},{9,... | collective-permute-start | bytes 2211848 | tf_op jit(solution)/shard_map/ppermute | solution.py:508
  24.6 12.8 %collective-permute-start.3 = (f32[9,40,512]{2,1,0:T(8,128)S(1)}, f32[9,40,512]{2,1,0:T(8,128)S(1)}, u32[]{:S(2)}, u32[]{:S(2)}) collective-permute-start(f32[9,40,512]{2,1,0:T(8,128)S(1)} %get-tuple-element.37), channel_id=1, source_target_pairs={{4,0},{8,4},{12,8},{16,12},{20,16},{24,20},{28,24},{5,1},{9,5},{13... | collective-permute-start | bytes 2211848 | tf_op jit(solution)/shard_map/ppermute | solution.py:508
  26.6 22.9 %collective-permute-start.4 = (f32[8,16,256]{2,1,0:T(8,128)S(1)}, f32[8,16,256]{2,1,0:T(8,128)S(1)}, u32[]{:S(2)}, u32[]{:S(2)}) collective-permute-start(f32[8,16,256]{2,1,0:T(8,128)S(1)} %mean.1.own_rows), channel_id=1, source_target_pairs={{0,1},{1,2},{2,3},{4,5},{5,6},{6,7},{8,9},{9,10},{10,11},{12,13},{... | collective-permute-start | bytes 393224 | tf_op jit(solution)/shard_map/ppermute | solution.py:508
  29.7 19.8 %collective-permute-start.5 = (f32[8,16,256]{2,1,0:T(8,128)S(1)}, f32[8,16,256]{2,1,0:T(8,128)S(1)}, u32[]{:S(2)}, u32[]{:S(2)}) collective-permute-start(f32[8,16,256]{2,1,0:T(8,128)S(1)} %mean.1.own_rows), channel_id=1, source_target_pairs={{1,0},{2,1},{3,2},{5,4},{6,5},{7,6},{9,8},{10,9},{11,10},{13,12},{... | collective-permute-start | bytes 393224 | tf_op jit(solution)/shard_map/ppermute | solution.py:508
  49.5 8.9 %collective-permute-start.6 = (f32[10,16,256]{2,1,0:T(8,128)S(1)}, f32[10,16,256]{2,1,0:T(8,128)S(1)}, u32[]{:S(2)}, u32[]{:S(2)}) collective-permute-start(f32[10,16,256]{2,1,0:T(8,128)S(1)} %get-tuple-element.44.to_high), channel_id=1, source_target_pairs={{0,1},{1,2},{2,3},{4,5},{5,6},{6,7},{8,9},{9,10},{10,11},{12,13},{... | collective-permute-start | bytes 491528 | tf_op jit(solution)/shard_map/ppermute | solution.py:508
  52.6 6.1 %collective-permute-start.7 = (f32[10,16,256]{2,1,0:T(8,128)S(1)}, f32[10,16,256]{2,1,0:T(8,128)S(1)}, u32[]{:S(2)}, u32[]{:S(2)}) collective-permute-start(f32[10,16,256]{2,1,0:T(8,128)S(1)} %get-tuple-element.43.to_low), channel_id=1, source_target_pairs={{1,0},{2,1},{3,2},{5,4},{6,5},{7,6},{9,8},{10,9},{11,10},{13,12},{... | collective-permute-start | bytes 491528 | tf_op jit(solution)/shard_map/ppermute | solution.py:508
  54.0 11.0 %collective-permute-start.10 = (f32[6,48,256]{2,1,0:T(8,128)S(1)}, f32[6,48,256]{2,1,0:T(8,128)S(1)}, u32[]{:S(2)}, u32[]{:S(2)}) collective-permute-start(f32[6,48,256]{2,1,0:T(8,128)S(1)} %get-tuple-element.51), channel_id=1, source_target_pairs={{0,4},{4,8},{8,12},{12,16},{16,20},{20,24},{24,28},{1,5},{5,9},{9,... | collective-permute-start | bytes 884744 | tf_op jit(solution)/shard_map/ppermute | solution.py:508
  56.0 9.0 %collective-permute-start.11 = (f32[6,48,256]{2,1,0:T(8,128)S(1)}, f32[6,48,256]{2,1,0:T(8,128)S(1)}, u32[]{:S(2)}, u32[]{:S(2)}) collective-permute-start(f32[6,48,256]{2,1,0:T(8,128)S(1)} %get-tuple-element.52), channel_id=1, source_target_pairs={{4,0},{8,4},{12,8},{16,12},{20,16},{24,20},{28,24},{5,1},{9,5},{13... | collective-permute-start | bytes 884744 | tf_op jit(solution)/shard_map/ppermute | solution.py:508
  58.7 8.0 %collective-permute-start.8 = (f32[6,48,256]{2,1,0:T(8,128)S(1)}, f32[6,48,256]{2,1,0:T(8,128)S(1)}, u32[]{:S(2)}, u32[]{:S(2)}) collective-permute-start(f32[6,48,256]{2,1,0:T(8,128)S(1)} %get-tuple-element.49), channel_id=1, source_target_pairs={{0,4},{4,8},{8,12},{12,16},{16,20},{20,24},{24,28},{1,5},{5,9},{9,... | collective-permute-start | bytes 884744 | tf_op jit(solution)/shard_map/ppermute | solution.py:508
  63.1 8.0 %collective-permute-start.9 = (f32[6,48,256]{2,1,0:T(8,128)S(1)}, f32[6,48,256]{2,1,0:T(8,128)S(1)}, u32[]{:S(2)}, u32[]{:S(2)}) collective-permute-start(f32[6,48,256]{2,1,0:T(8,128)S(1)} %get-tuple-element.50), channel_id=1, source_target_pairs={{4,0},{8,4},{12,8},{16,12},{20,16},{24,20},{28,24},{5,1},{9,5},{13... | collective-permute-start | bytes 884744 | tf_op jit(solution)/shard_map/ppermute | solution.py:508
  74.0 6.0 %collective-permute-start.12 = (f32[9,24,128]{2,1,0:T(8,128)S(1)}, f32[9,24,128]{2,1,0:T(8,128)S(1)}, u32[]{:S(2)}, u32[]{:S(2)}) collective-permute-start(f32[9,24,128]{2,1,0:T(8,128)S(1)} %get-tuple-element.56), channel_id=1, source_target_pairs={{0,4},{4,8},{8,12},{12,16},{16,20},{20,24},{24,28},{1,5},{5,9},{9,... | collective-permute-start | bytes 331784 | tf_op jit(solution)/shard_map/ppermute | solution.py:508
  76.0 6.1 %collective-permute-start.13 = (f32[9,24,128]{2,1,0:T(8,128)S(1)}, f32[9,24,128]{2,1,0:T(8,128)S(1)}, u32[]{:S(2)}, u32[]{:S(2)}) collective-permute-start(f32[9,24,128]{2,1,0:T(8,128)S(1)} %get-tuple-element.57), channel_id=1, source_target_pairs={{4,0},{8,4},{12,8},{16,12},{20,16},{24,20},{28,24},{5,1},{9,5},{13... | collective-permute-start | bytes 331784 | tf_op jit(solution)/shard_map/ppermute | solution.py:508

commit v4 on v3

--- a/solution.py
+++ b/solution.py
@@ -319,7 +319,7 @@
     halo(K, HP + own, from_up, 4, 5)
     halo(K, HP + own + 1, from_up, 6, 7)
     halo(K, HP + own + 2, from_up, 8, None)
-    relax_level(K, S, U, W, D, R, own, 4, 0, 8, False)
+    relax_level(K, S, U, W, D, R, own, 4, 0, 8, True)
     store_field(U, field, own, even_own)
     zero = jnp.zeros((rows, lanes), F32)
     for colour in (0, 1):

time: 84.2 us -> 79.8 us (0.948)
  Pallas kernels: 16.7 us -> 12.3 us
    pallas_call x8, Pallas kernels: 16.7 us -> 12.3 us  [call(): pl.pallas_call(kernel, out_shape=[jax.ShapeDtypeStruct(o, F32) if i in re...]
  transfers between devices with their start and end apart: 14 -> 14, of which waited for: 8 -> 8; matrix products, arithmetic and copies ran while one was open for 2% -> 2% of each run, Pallas kernels for 16% -> 11%
where the time goes in v4:
time: 79.8 us; the launch traced here: 79.3 us
  starting transfers between devices  35.8 us (45%)
  waiting for transfers between devices  24.9 us (31%)
  Pallas kernels  12.3 us (15%)
  local copies, waits for them, and re-layouts  5.29 us (7%)
  between operations  0.86 us (1%)
    ppermute x14, starting transfers between devices, exchange(): return (lax.ppermute(to_high, axis, up), lax.ppermute(to_low, axis, down))  35.8 us
    ppermute x14, waiting for transfers between devices, exchange(): return (lax.ppermute(to_high, axis, up), lax.ppermute(to_low, axis, down))  24.9 us
    pallas_call x8, Pallas kernels, call(): pl.pallas_call(kernel, out_shape=[jax.ShapeDtypeStruct(o, F32) if i in re...  12.3 us
    unnamed x12, local copies, waits for them, and re-layouts  5.29 us
  transfers between devices with their start and end apart: 14, of which 8 were waited for; matrix products, arithmetic and copies ran while one was open for 2% of the time, Pallas kernels for 11%

profile of v4, /device:TPU:1, one launch (start us, length us, event | category | flops | bytes accessed | tf_op | source)
XLA Modules:
  0.0 79.3 jit_solution(420930934480633873)
XLA Ops:
  0.6 0.0 copy-start
  0.6 1.2 %copy-done = f32[16,32,512]{2,1,0:T(8,128)S(1)} copy-done((f32[16,32,512]{2,1,0:T(8,128)S(1)}, f32[16,32,512]{2,1,0:T(8,128)}, u32[]{:S(2)}) %copy-start) | copy-done | bytes 1048600
  1.9 0.0 copy-start.2
  1.9 1.2 %copy-done.2 = f32[16,32,512]{2,1,0:T(8,128)S(1)} copy-done((f32[16,32,512]{2,1,0:T(8,128)S(1)}, f32[16,32,512]{2,1,0:T(8,128)}, u32[]{:S(2)}) %copy-start.2) | copy-done | bytes 1048600
  3.1 0.0 copy-start.1
  3.1 0.2 pack_rows.1
  3.3 0.0 copy-start.3
  3.3 4.1 %collective-permute-start = (f32[2,8,8,512]{3,2,1,0:T(8,128)S(1)}, f32[2,8,8,512]{3,2,1,0:T(8,128)S(1)}, u32[]{:S(2)}, u32[]{:S(2)}) collective-permute-start(f32[2,8,8,512]{3,2,1,0:T(8,128)S(1)} %get-tuple-element.32), channel_id=1, source_target_pairs={{0,1},{1,2},{2,3},{4,5},{5,6},{6,7},{8,9},{9,10},{10,11},{12,13},{... | collective-permute-start | bytes 786440 | tf_op jit(solution)/shard_map/ppermute | solution.py:508
  7.4 1.3 %collective-permute-start.1 = (f32[2,8,8,512]{3,2,1,0:T(8,128)S(1)}, f32[2,8,8,512]{3,2,1,0:T(8,128)S(1)}, u32[]{:S(2)}, u32[]{:S(2)}) collective-permute-start(f32[2,8,8,512]{3,2,1,0:T(8,128)S(1)} %get-tuple-element.33), channel_id=1, source_target_pairs={{1,0},{2,1},{3,2},{5,4},{6,5},{7,6},{9,8},{10,9},{11,10},{13,12},{... | collective-permute-start | bytes 786440 | tf_op jit(solution)/shard_map/ppermute | solution.py:508
  8.7 0.0 copy-done.1
  8.7 1.0 %mean.1.own_rows = f32[8,16,256]{2,1,0:T(8,128)S(1)} custom-call(f32[16,32,512]{2,1,0:T(8,128)S(1)} %copy-done.1), custom_call_target="tpu_custom_call" | custom-call | tf_op jit(solution)/shard_map/mean/pallas_call | solution.py:487
  9.6 2.7 %collective-permute-done.from_low = f32[2,8,8,512]{3,2,1,0:T(8,128)S(1)} collective-permute-done((f32[2,8,8,512]{3,2,1,0:T(8,128)S(1)}, f32[2,8,8,512]{3,2,1,0:T(8,128)S(1)}, u32[]{:S(2)}, u32[]{:S(2)}) %collective-permute-start) | collective-permute-done | bytes 262176 | tf_op jit(solution)/shard_map/ppermute | solution.py:508
  12.3 7.6 %collective-permute-done.1.from_high = f32[2,8,8,512]{3,2,1,0:T(8,128)S(1)} collective-permute-done((f32[2,8,8,512]{3,2,1,0:T(8,128)S(1)}, f32[2,8,8,512]{3,2,1,0:T(8,128)S(1)}, u32[]{:S(2)}, u32[]{:S(2)}) %collective-permute-start.1) | collective-permute-done | bytes 262176 | tf_op jit(solution)/shard_map/ppermute | solution.py:508
  19.9 0.0 copy-done.3
  19.9 0.1 pack_planes.1
  20.0 4.6 %collective-permute-start.2 = (f32[9,40,512]{2,1,0:T(8,128)S(1)}, f32[9,40,512]{2,1,0:T(8,128)S(1)}, u32[]{:S(2)}, u32[]{:S(2)}) collective-permute-start(f32[9,40,512]{2,1,0:T(8,128)S(1)} %get-tuple-element.36), channel_id=1, source_target_pairs={{0,4},{4,8},{8,12},{12,16},{16,20},{20,24},{24,28},{1,5},{5,9},{9,... | collective-permute-start | bytes 2211848 | tf_op jit(solution)/shard_map/ppermute | solution.py:508
  24.6 1.9 %collective-permute-start.3 = (f32[9,40,512]{2,1,0:T(8,128)S(1)}, f32[9,40,512]{2,1,0:T(8,128)S(1)}, u32[]{:S(2)}, u32[]{:S(2)}) collective-permute-start(f32[9,40,512]{2,1,0:T(8,128)S(1)} %get-tuple-element.37), channel_id=1, source_target_pairs={{4,0},{8,4},{12,8},{16,12},{20,16},{24,20},{28,24},{5,1},{9,5},{13... | collective-permute-start | bytes 2211848 | tf_op jit(solution)/shard_map/ppermute | solution.py:508
  26.6 3.1 %collective-permute-start.4 = (f32[8,16,256]{2,1,0:T(8,128)S(1)}, f32[8,16,256]{2,1,0:T(8,128)S(1)}, u32[]{:S(2)}, u32[]{:S(2)}) collective-permute-start(f32[8,16,256]{2,1,0:T(8,128)S(1)} %mean.1.own_rows), channel_id=1, source_target_pairs={{0,1},{1,2},{2,3},{4,5},{5,6},{6,7},{8,9},{9,10},{10,11},{12,13},{... | collective-permute-start | bytes 393224 | tf_op jit(solution)/shard_map/ppermute | solution.py:508
  29.7 1.3 %collective-permute-start.5 = (f32[8,16,256]{2,1,0:T(8,128)S(1)}, f32[8,16,256]{2,1,0:T(8,128)S(1)}, u32[]{:S(2)}, u32[]{:S(2)}) collective-permute-start(f32[8,16,256]{2,1,0:T(8,128)S(1)} %mean.1.own_rows), channel_id=1, source_target_pairs={{1,0},{2,1},{3,2},{5,4},{6,5},{7,6},{9,8},{10,9},{11,10},{13,12},{... | collective-permute-start | bytes 393224 | tf_op jit(solution)/shard_map/ppermute | solution.py:508
  31.0 2.0 %collective-permute-done.2.from_down = f32[9,40,512]{2,1,0:T(8,128)S(1)} collective-permute-done((f32[9,40,512]{2,1,0:T(8,128)S(1)}, f32[9,40,512]{2,1,0:T(8,128)S(1)}, u32[]{:S(2)}, u32[]{:S(2)}) %collective-permute-start.2) | collective-permute-done | bytes 737312 | tf_op jit(solution)/shard_map/ppermute | solution.py:508
  33.0 4.4 %collective-permute-done.3.from_up = f32[9,40,512]{2,1,0:T(8,128)S(1)} collective-permute-done((f32[9,40,512]{2,1,0:T(8,128)S(1)}, f32[9,40,512]{2,1,0:T(8,128)S(1)}, u32[]{:S(2)}, u32[]{:S(2)}) %collective-permute-start.3) | collective-permute-done | bytes 737312 | tf_op jit(solution)/shard_map/ppermute | solution.py:508
  37.4 7.6 %fine_level.1 = (f32[16,32,512]{2,1,0:T(8,128)S(1)}, f32[10,16,256]{2,1,0:T(8,128)S(1)}, f32[10,16,256]{2,1,0:T(8,128)S(1)}, f32[10,16,256]{2,1,0:T(8,128)S(1)}) custom-call(f32[16,32,512]{2,1,0:T(8,128)S(1)} %copy-done.3, f32[16,32,512]{2,1,0:T(8,128)S(1)} %copy-done.1, f32[2,8,8,512]{3,2,1,0:T(8,128)S(1)} %collective-permute-done.from_low, ...), custom_call_target="tpu_custom_call" | custom-call | tf_op jit(solution)/shard_map/fine_level/pallas_call | solution.py:487
  45.1 0.0 collective-permute-done.4.from_low
  45.1 0.0 collective-permute-done.5.from_high
  45.1 3.1 %collective-permute-start.6 = (f32[10,16,256]{2,1,0:T(8,128)S(1)}, f32[10,16,256]{2,1,0:T(8,128)S(1)}, u32[]{:S(2)}, u32[]{:S(2)}) collective-permute-start(f32[10,16,256]{2,1,0:T(8,128)S(1)} %get-tuple-element.44.to_high), channel_id=1, source_target_pairs={{0,1},{1,2},{2,3},{4,5},{5,6},{6,7},{8,9},{9,10},{10,11},{12,13},{... | collective-permute-start | bytes 491528 | tf_op jit(solution)/shard_map/ppermute | solution.py:508
  48.2 1.3 %collective-permute-start.7 = (f32[10,16,256]{2,1,0:T(8,128)S(1)}, f32[10,16,256]{2,1,0:T(8,128)S(1)}, u32[]{:S(2)}, u32[]{:S(2)}) collective-permute-start(f32[10,16,256]{2,1,0:T(8,128)S(1)} %get-tuple-element.43.to_low), channel_id=1, source_target_pairs={{1,0},{2,1},{3,2},{5,4},{6,5},{7,6},{9,8},{10,9},{11,10},{13,12},{... | collective-permute-start | bytes 491528 | tf_op jit(solution)/shard_map/ppermute | solution.py:508
  49.5 0.1 mean_planes.1
  49.6 2.0 %collective-permute-start.10 = (f32[6,48,256]{2,1,0:T(8,128)S(1)}, f32[6,48,256]{2,1,0:T(8,128)S(1)}, u32[]{:S(2)}, u32[]{:S(2)}) collective-permute-start(f32[6,48,256]{2,1,0:T(8,128)S(1)} %get-tuple-element.51), channel_id=1, source_target_pairs={{0,4},{4,8},{8,12},{12,16},{16,20},{20,24},{24,28},{1,5},{5,9},{9,... | collective-permute-start | bytes 884744 | tf_op jit(solution)/shard_map/ppermute | solution.py:508
  51.6 2.3 %collective-permute-start.11 = (f32[6,48,256]{2,1,0:T(8,128)S(1)}, f32[6,48,256]{2,1,0:T(8,128)S(1)}, u32[]{:S(2)}, u32[]{:S(2)}) collective-permute-start(f32[6,48,256]{2,1,0:T(8,128)S(1)} %get-tuple-element.52), channel_id=1, source_target_pairs={{4,0},{8,4},{12,8},{16,12},{20,16},{24,20},{28,24},{5,1},{9,5},{13... | collective-permute-start | bytes 884744 | tf_op jit(solution)/shard_map/ppermute | solution.py:508
  53.9 0.0 collective-permute-done.6.from_low
  53.9 0.3 collective-permute-done.7.from_high
  54.3 0.1 source_planes.1
  54.3 4.3 %collective-permute-start.8 = (f32[6,48,256]{2,1,0:T(8,128)S(1)}, f32[6,48,256]{2,1,0:T(8,128)S(1)}, u32[]{:S(2)}, u32[]{:S(2)}) collective-permute-start(f32[6,48,256]{2,1,0:T(8,128)S(1)} %get-tuple-element.49), channel_id=1, source_target_pairs={{0,4},{4,8},{8,12},{12,16},{16,20},{20,24},{24,28},{1,5},{5,9},{9,... | collective-permute-start | bytes 884744 | tf_op jit(solution)/shard_map/ppermute | solution.py:508
  58.7 2.1 %collective-permute-start.9 = (f32[6,48,256]{2,1,0:T(8,128)S(1)}, f32[6,48,256]{2,1,0:T(8,128)S(1)}, u32[]{:S(2)}, u32[]{:S(2)}) collective-permute-start(f32[6,48,256]{2,1,0:T(8,128)S(1)} %get-tuple-element.50), channel_id=1, source_target_pairs={{4,0},{8,4},{12,8},{16,12},{20,16},{24,20},{28,24},{5,1},{9,5},{13... | collective-permute-start | bytes 884744 | tf_op jit(solution)/shard_map/ppermute | solution.py:508
  60.8 0.0 collective-permute-done.10.k_down
  60.8 0.0 collective-permute-done.11.k_up
  60.8 1.5 %collective-permute-done.8.from_down = f32[6,48,256]{2,1,0:T(8,128)S(1)} collective-permute-done((f32[6,48,256]{2,1,0:T(8,128)S(1)}, f32[6,48,256]{2,1,0:T(8,128)S(1)}, u32[]{:S(2)}, u32[]{:S(2)}) %collective-permute-start.8) | collective-permute-done | bytes 294944 | tf_op jit(solution)/shard_map/ppermute | solution.py:508
  62.3 4.4 %collective-permute-done.9.from_up = f32[6,48,256]{2,1,0:T(8,128)S(1)} collective-permute-done((f32[6,48,256]{2,1,0:T(8,128)S(1)}, f32[6,48,256]{2,1,0:T(8,128)S(1)}, u32[]{:S(2)}, u32[]{:S(2)}) %collective-permute-start.9) | collective-permute-done | bytes 294944 | tf_op jit(solution)/shard_map/ppermute | solution.py:508
  66.7 2.9 %middle_level.1 = (f32[8,16,256]{2,1,0:T(8,128)S(1)}, f32[4,24,128]{2,1,0:T(8,128)S(1)}, f32[4,24,128]{2,1,0:T(8,128)S(1)}, f32[9,24,128]{2,1,0:T(8,128)S(1)}, f32[9,24,128]{2,1,0:T(8,128)S(1)}) custom-call(f32[10,48,256]{2,1,0:T(8,128)S(1)} %get-tuple-element.45.s, f32[8,48,256]{2,1,0:T(8,128)S(1)} %get-tuple-element.48.k, ...), custom_call_target="tpu_custom_call" | custom-call | tf_op jit(solution)/shard_map/middle_level/pallas_call | solution.py:487
  69.7 1.9 %collective-permute-start.12 = (f32[9,24,128]{2,1,0:T(8,128)S(1)}, f32[9,24,128]{2,1,0:T(8,128)S(1)}, u32[]{:S(2)}, u32[]{:S(2)}) collective-permute-start(f32[9,24,128]{2,1,0:T(8,128)S(1)} %get-tuple-element.56), channel_id=1, source_target_pairs={{0,4},{4,8},{8,12},{12,16},{16,20},{20,24},{24,28},{1,5},{5,9},{9,... | collective-permute-start | bytes 331784 | tf_op jit(solution)/shard_map/ppermute | solution.py:508
  71.6 2.4 %collective-permute-start.13 = (f32[9,24,128]{2,1,0:T(8,128)S(1)}, f32[9,24,128]{2,1,0:T(8,128)S(1)}, u32[]{:S(2)}, u32[]{:S(2)}) collective-permute-start(f32[9,24,128]{2,1,0:T(8,128)S(1)} %get-tuple-element.57), channel_id=1, source_target_pairs={{4,0},{8,4},{12,8},{16,12},{20,16},{24,20},{28,24},{5,1},{9,5},{13... | collective-permute-start | bytes 331784 | tf_op jit(solution)/shard_map/ppermute | solution.py:508
  74.0 1.0 %copy.6 = f32[16,32,512]{2,1,0:T(8,128)} copy(f32[16,32,512]{2,1,0:T(8,128)S(1)} %get-tuple-element.60) | data formatting | bytes 2097152
  75.0 0.7 copy.7
  75.6 0.0 collective-permute-done.12.from_down
  75.6 2.0 %collective-permute-done.13.from_up = f32[9,24,128]{2,1,0:T(8,128)S(1)} collective-permute-done((f32[9,24,128]{2,1,0:T(8,128)S(1)}, f32[9,24,128]{2,1,0:T(8,128)S(1)}, u32[]{:S(2)}, u32[]{:S(2)}) %collective-permute-start.13) | collective-permute-done | bytes 110624 | tf_op jit(solution)/shard_map/ppermute | solution.py:508
  77.7 0.4 coarse_level.1
  78.1 0.6 copy.8
  78.7 0.6 copy.9
Async XLA Ops:
  0.6 1.2 %copy-start = (f32[16,32,512]{2,1,0:T(8,128)S(1)}, f32[16,32,512]{2,1,0:T(8,128)}, u32[]{:S(2)}) copy-start(f32[16,32,512]{2,1,0:T(8,128)} %k.5) | copy-start | bytes 3145732
  1.9 1.2 %copy-start.2 = (f32[16,32,512]{2,1,0:T(8,128)S(1)}, f32[16,32,512]{2,1,0:T(8,128)}, u32[]{:S(2)}) copy-start(f32[16,32,512]{2,1,0:T(8,128)} %s.3) | copy-start | bytes 3145732
  3.1 5.6 %copy-start.1 = (f32[16,32,512]{2,1,0:T(8,128)S(1)}, f32[16,32,512]{2,1,0:T(8,128)}, u32[]{:S(2)}) copy-start(f32[16,32,512]{2,1,0:T(8,128)} %k.5) | copy-start | bytes 3145732
  3.3 16.6 %copy-start.3 = (f32[16,32,512]{2,1,0:T(8,128)S(1)}, f32[16,32,512]{2,1,0:T(8,128)}, u32[]{:S(2)}) copy-start(f32[16,32,512]{2,1,0:T(8,128)} %s.3) | copy-start | bytes 3145732
  3.3 9.0 %collective-permute-start = (f32[2,8,8,512]{3,2,1,0:T(8,128)S(1)}, f32[2,8,8,512]{3,2,1,0:T(8,128)S(1)}, u32[]{:S(2)}, u32[]{:S(2)}) collective-permute-start(f32[2,8,8,512]{3,2,1,0:T(8,128)S(1)} %get-tuple-element.32), channel_id=1, source_target_pairs={{0,1},{1,2},{2,3},{4,5},{5,6},{6,7},{8,9},{9,10},{10,11},{12,13},{... | collective-permute-start | bytes 786440 | tf_op jit(solution)/shard_map/ppermute | solution.py:508
  7.4 12.5 %collective-permute-start.1 = (f32[2,8,8,512]{3,2,1,0:T(8,128)S(1)}, f32[2,8,8,512]{3,2,1,0:T(8,128)S(1)}, u32[]{:S(2)}, u32[]{:S(2)}) collective-permute-start(f32[2,8,8,512]{3,2,1,0:T(8,128)S(1)} %get-tuple-element.33), channel_id=1, source_target_pairs={{1,0},{2,1},{3,2},{5,4},{6,5},{7,6},{9,8},{10,9},{11,10},{13,12},{... | collective-permute-start | bytes 786440 | tf_op jit(solution)/shard_map/ppermute | solution.py:508
  20.0 13.0 %collective-permute-start.2 = (f32[9,40,512]{2,1,0:T(8,128)S(1)}, f32[9,40,512]{2,1,0:T(8,128)S(1)}, u32[]{:S(2)}, u32[]{:S(2)}) collective-permute-start(f32[9,40,512]{2,1,0:T(8,128)S(1)} %get-tuple-element.36), channel_id=1, source_target_pairs={{0,4},{4,8},{8,12},{12,16},{16,20},{20,24},{24,28},{1,5},{5,9},{9,... | collective-permute-start | bytes 2211848 | tf_op jit(solution)/shard_map/ppermute | solution.py:508
  24.6 12.8 %collective-permute-start.3 = (f32[9,40,512]{2,1,0:T(8,128)S(1)}, f32[9,40,512]{2,1,0:T(8,128)S(1)}, u32[]{:S(2)}, u32[]{:S(2)}) collective-permute-start(f32[9,40,512]{2,1,0:T(8,128)S(1)} %get-tuple-element.37), channel_id=1, source_target_pairs={{4,0},{8,4},{12,8},{16,12},{20,16},{24,20},{28,24},{5,1},{9,5},{13... | collective-permute-start | bytes 2211848 | tf_op jit(solution)/shard_map/ppermute | solution.py:508
  26.6 18.5 %collective-permute-start.4 = (f32[8,16,256]{2,1,0:T(8,128)S(1)}, f32[8,16,256]{2,1,0:T(8,128)S(1)}, u32[]{:S(2)}, u32[]{:S(2)}) collective-permute-start(f32[8,16,256]{2,1,0:T(8,128)S(1)} %mean.1.own_rows), channel_id=1, source_target_pairs={{0,1},{1,2},{2,3},{4,5},{5,6},{6,7},{8,9},{9,10},{10,11},{12,13},{... | collective-permute-start | bytes 393224 | tf_op jit(solution)/shard_map/ppermute | solution.py:508
  29.7 15.4 %collective-permute-start.5 = (f32[8,16,256]{2,1,0:T(8,128)S(1)}, f32[8,16,256]{2,1,0:T(8,128)S(1)}, u32[]{:S(2)}, u32[]{:S(2)}) collective-permute-start(f32[8,16,256]{2,1,0:T(8,128)S(1)} %mean.1.own_rows), channel_id=1, source_target_pairs={{1,0},{2,1},{3,2},{5,4},{6,5},{7,6},{9,8},{10,9},{11,10},{13,12},{... | collective-permute-start | bytes 393224 | tf_op jit(solution)/shard_map/ppermute | solution.py:508
  45.1 8.9 %collective-permute-start.6 = (f32[10,16,256]{2,1,0:T(8,128)S(1)}, f32[10,16,256]{2,1,0:T(8,128)S(1)}, u32[]{:S(2)}, u32[]{:S(2)}) collective-permute-start(f32[10,16,256]{2,1,0:T(8,128)S(1)} %get-tuple-element.44.to_high), channel_id=1, source_target_pairs={{0,1},{1,2},{2,3},{4,5},{5,6},{6,7},{8,9},{9,10},{10,11},{12,13},{... | collective-permute-start | bytes 491528 | tf_op jit(solution)/shard_map/ppermute | solution.py:508
  48.2 6.1 %collective-permute-start.7 = (f32[10,16,256]{2,1,0:T(8,128)S(1)}, f32[10,16,256]{2,1,0:T(8,128)S(1)}, u32[]{:S(2)}, u32[]{:S(2)}) collective-permute-start(f32[10,16,256]{2,1,0:T(8,128)S(1)} %get-tuple-element.43.to_low), channel_id=1, source_target_pairs={{1,0},{2,1},{3,2},{5,4},{6,5},{7,6},{9,8},{10,9},{11,10},{13,12},{... | collective-permute-start | bytes 491528 | tf_op jit(solution)/shard_map/ppermute | solution.py:508
  49.6 11.2 %collective-permute-start.10 = (f32[6,48,256]{2,1,0:T(8,128)S(1)}, f32[6,48,256]{2,1,0:T(8,128)S(1)}, u32[]{:S(2)}, u32[]{:S(2)}) collective-permute-start(f32[6,48,256]{2,1,0:T(8,128)S(1)} %get-tuple-element.51), channel_id=1, source_target_pairs={{0,4},{4,8},{8,12},{12,16},{16,20},{20,24},{24,28},{1,5},{5,9},{9,... | collective-permute-start | bytes 884744 | tf_op jit(solution)/shard_map/ppermute | solution.py:508
  51.6 9.2 %collective-permute-start.11 = (f32[6,48,256]{2,1,0:T(8,128)S(1)}, f32[6,48,256]{2,1,0:T(8,128)S(1)}, u32[]{:S(2)}, u32[]{:S(2)}) collective-permute-start(f32[6,48,256]{2,1,0:T(8,128)S(1)} %get-tuple-element.52), channel_id=1, source_target_pairs={{4,0},{8,4},{12,8},{16,12},{20,16},{24,20},{28,24},{5,1},{9,5},{13... | collective-permute-start | bytes 884744 | tf_op jit(solution)/shard_map/ppermute | solution.py:508
  54.3 8.0 %collective-permute-start.8 = (f32[6,48,256]{2,1,0:T(8,128)S(1)}, f32[6,48,256]{2,1,0:T(8,128)S(1)}, u32[]{:S(2)}, u32[]{:S(2)}) collective-permute-start(f32[6,48,256]{2,1,0:T(8,128)S(1)} %get-tuple-element.49), channel_id=1, source_target_pairs={{0,4},{4,8},{8,12},{12,16},{16,20},{20,24},{24,28},{1,5},{5,9},{9,... | collective-permute-start | bytes 884744 | tf_op jit(solution)/shard_map/ppermute | solution.py:508
  58.7 8.0 %collective-permute-start.9 = (f32[6,48,256]{2,1,0:T(8,128)S(1)}, f32[6,48,256]{2,1,0:T(8,128)S(1)}, u32[]{:S(2)}, u32[]{:S(2)}) collective-permute-start(f32[6,48,256]{2,1,0:T(8,128)S(1)} %get-tuple-element.50), channel_id=1, source_target_pairs={{4,0},{8,4},{12,8},{16,12},{20,16},{24,20},{28,24},{5,1},{9,5},{13... | collective-permute-start | bytes 884744 | tf_op jit(solution)/shard_map/ppermute | solution.py:508
  69.7 6.0 %collective-permute-start.12 = (f32[9,24,128]{2,1,0:T(8,128)S(1)}, f32[9,24,128]{2,1,0:T(8,128)S(1)}, u32[]{:S(2)}, u32[]{:S(2)}) collective-permute-start(f32[9,24,128]{2,1,0:T(8,128)S(1)} %get-tuple-element.56), channel_id=1, source_target_pairs={{0,4},{4,8},{8,12},{12,16},{16,20},{20,24},{24,28},{1,5},{5,9},{9,... | collective-permute-start | bytes 331784 | tf_op jit(solution)/shard_map/ppermute | solution.py:508
  71.6 6.1 %collective-permute-start.13 = (f32[9,24,128]{2,1,0:T(8,128)S(1)}, f32[9,24,128]{2,1,0:T(8,128)S(1)}, u32[]{:S(2)}, u32[]{:S(2)}) collective-permute-start(f32[9,24,128]{2,1,0:T(8,128)S(1)} %get-tuple-element.57), channel_id=1, source_target_pairs={{4,0},{8,4},{12,8},{16,12},{20,16},{24,20},{28,24},{5,1},{9,5},{13... | collective-permute-start | bytes 331784 | tf_op jit(solution)/shard_map/ppermute | solution.py:508

commit v5 on v4

--- a/solution.py
+++ b/solution.py
@@ -23,6 +23,38 @@
 
 def pick(mask, a, b):
     return jnp.where(mask, a, b)
+
+
+def odd_on(axis):
+    return lax.axis_index(axis) % 2 == 1
+
+
+def choose(odd, a, b):
+    return lax.select(jnp.full(a.shape, odd), a, b)
+
+
+class Got:
+    def __init__(self, a, b, odd, upper):
+        self.first, self.second = (a, b) if upper else (b, a)
+        self.odd = odd
+        self.shape = a.shape
+
+    def __getitem__(self, at):
+        return choose(self.odd, self.first[at], self.second[at])
+
+
+def got_pair(a, b, axis):
+    odd = odd_on(axis)
+    return Got(a, b, odd, False), Got(a, b, odd, True)
+
+
+class Send:
+    def __init__(self, a, b, axis):
+        self.a, self.b, self.odd = a, b, odd_on(axis)
+
+    def put(self, at, low, high):
+        self.a[at] = choose(self.odd, high, low)
+        self.b[at] = choose(self.odd, low, high)
 
 
 def row_index(lanes):
@@ -199,31 +231,30 @@
     return pick((m == i) | (m == i + 1), 0.125, 0.0).astype(F32)
 
 
-def pack_rows_kernel(s_low, s_high, k_low, k_high, to_low, to_high):
+def pack_rows_kernel(s_low, s_high, k_low, k_high, to_a, to_b):
     lanes = s_low.shape[2]
     even = even_mask(8, lanes)
+    send = Send(to_a, to_b, "inner")
+    cat = lambda *parts: jnp.concatenate(parts, axis=0)
 
     def step(p, carry):
         def pair(ref):
             a, b = ref[2 * p], ref[2 * p + 1]
             return pick(even, a, b), pick(even, b, a)
 
-        sr, sb = pair(s_low)
-        kr, kb = pair(k_low)
-        to_low[0, p] = jnp.concatenate([kr[0:4], sr[0:4]], axis=0)
-        to_low[1, p] = jnp.concatenate([kb[0:5], sb[0:3]], axis=0)
-        sr, sb = pair(s_high)
-        kr, kb = pair(k_high)
-        to_high[0, p] = jnp.concatenate([kr[4:8], sr[4:8]], axis=0)
-        to_high[1, p] = jnp.concatenate([kb[3:8], sb[5:8]], axis=0)
+        ls, lk, hs, hk = pair(s_low), pair(k_low), pair(s_high), pair(k_high)
+        send.put((0, p), cat(lk[0][0:4], ls[0][0:4]), cat(hk[0][4:8], hs[0][4:8]))
+        send.put((1, p), cat(lk[1][0:5], ls[1][0:3]), cat(hk[1][3:8], hs[1][5:8]))
         return carry
 
-    lax.fori_loop(0, s_low.shape[0] // 2, step, 0)
-
-
-def pack_planes_kernel(s, k, from_low, from_high, to_down, to_up):
+    lax.fori_loop(0, s_low.shape[0] // 2, step, 0, unroll=True)
+
+
+def pack_planes_kernel(s, k, from_a, from_b, to_a, to_b):
     planes, rows, lanes = s.shape
     even = even_mask(8, lanes)
+    from_low, from_high = got_pair(from_a, from_b, "inner")
+    send = Send(to_a, to_b, "outer")
 
     def edges(p, of_k):
         lr, lb = from_low[0, p], from_low[1, p]
@@ -236,16 +267,15 @@
             black = jnp.concatenate([lb[4:8], hb[5:8], hb[7:8]], axis=0)
         return pick(even, red, black), pick(even, black, red)
 
-    def put(out, at, ref, plane, of_k):
-        out[at, 0:rows] = ref[plane]
-        out[at, rows : rows + 8] = edges(plane // 2, of_k)[plane % 2]
+    def put(at, ref, down, up, of_k):
+        send.put((at, slice(0, rows)), ref[down], ref[up])
+        send.put((at, slice(rows, rows + 8)),
+                 edges(down // 2, of_k)[down % 2], edges(up // 2, of_k)[up % 2])
 
     for j in range(4):
-        put(to_down, j, s, j, False)
-        put(to_up, j, s, planes - 4 + j, False)
+        put(j, s, j, planes - 4 + j, False)
     for j in range(5):
-        put(to_down, 4 + j, k, j, True)
-        put(to_up, 4 + j, k, planes - 5 + j, True)
+        put(4 + j, k, j, planes - 5 + j, True)
 
 
 def mean_kernel(k, out, Z):
@@ -258,9 +288,12 @@
         out[q] = mean[half * q : half * (q + 1)]
 
 
-def fine_kernel(s, k, from_low, from_high, from_down, from_up,
-                field, source_out, to_low, to_high,
+def fine_kernel(s, k, row_a, row_b, plane_a, plane_b,
+                field, source_out, to_a, to_b,
                 K, S, U, W, D, R, Z):
+    from_low, from_high = got_pair(row_a, row_b, "inner")
+    from_down, from_up = got_pair(plane_a, plane_b, "outer")
+    send = Send(to_a, to_b, "inner")
     planes, rows, lanes = s.shape
     own = planes // 2
     wide = rows + 16
@@ -336,39 +369,49 @@
         at = block * q
         rows_of = source[at : at + half]
         source_out[q] = rows_of
-        to_low[q] = pick(row == half - 1, source[at + half : at + half + 1], rows_of)
-        to_high[q] = pick(row == 0, source[at + half + 1 : at + half + 2], rows_of)
-
-
-def mean_planes_kernel(own_rows, from_low, from_high, K, to_down, to_up):
-    planes, rows, _ = own_rows.shape
+        send.put(q, pick(row == half - 1, source[at + half : at + half + 1], rows_of),
+                 pick(row == 0, source[at + half + 1 : at + half + 2], rows_of))
+
+
+def widen_planes(K, send, planes, of):
     for q in range(planes):
-        for out, at in ((K, q), (to_down, q), (to_up, q - planes + 6)):
-            if 0 <= at < out.shape[0]:
-                out[at, 0:rows] = from_low[q]
-                out[at, rows : 2 * rows] = own_rows[q]
-                out[at, 2 * rows : 3 * rows] = from_high[q]
-
-
-def source_planes_kernel(own_rows, to_low, to_high, from_low, from_high, S, to_down, to_up):
+        K[q] = of(q)
+    for j in range(6):
+        send.put(j, K[j], K[planes - 6 + j])
+
+
+def mean_planes_kernel(own_rows, from_a, from_b, K, to_a, to_b):
+    from_low, from_high = got_pair(from_a, from_b, "inner")
+
+    def of(q):
+        return jnp.concatenate([from_low[q], own_rows[q], from_high[q]], axis=0)
+
+    widen_planes(K, Send(to_a, to_b, "outer"), own_rows.shape[0], of)
+
+
+def source_planes_kernel(own_rows, sent_a, sent_b, from_a, from_b, S, to_a, to_b):
     planes, rows, lanes = own_rows.shape
     row = lax.broadcasted_iota(jnp.int32, (rows, lanes), 0)
     first, last = row == 0, row == rows - 1
-    for q in range(planes):
+    to_low, to_high = got_pair(sent_a, sent_b, "inner")
+    from_low, from_high = got_pair(from_a, from_b, "inner")
+
+    def of(q):
         got_low, got_high = from_low[q], from_high[q]
         low = pick(first, 0.0, got_low) + pick(last, to_low[q], 0.0)
         mine = own_rows[q] + pick(first, got_low, 0.0) + pick(last, got_high, 0.0)
         high = pick(last, 0.0, got_high) + pick(first, to_high[q], 0.0)
-        for out, at in ((S, q), (to_down, q), (to_up, q - planes + 6)):
-            if 0 <= at < out.shape[0]:
-                out[at, 0:rows] = low
-                out[at, rows : 2 * rows] = mine
-                out[at, 2 * rows : 3 * rows] = high
-
-
-def middle_kernel(s, k, from_down, from_up, k_down, k_up,
-                  field, s_next, k_next, to_down, to_up,
+        return jnp.concatenate([low, mine, high], axis=0)
+
+    widen_planes(S, Send(to_a, to_b, "outer"), planes, of)
+
+
+def middle_kernel(s, k, source_a, source_b, mean_a, mean_b,
+                  field, s_next, k_next, to_a, to_b,
                   K, S, U, W, D, R, Z, Zk):
+    from_down, from_up = got_pair(source_a, source_b, "outer")
+    k_down, k_up = got_pair(mean_a, mean_b, "outer")
+    send = Send(to_a, to_b, "outer")
     planes, wide, lanes = k.shape
     own = planes // 2
     even = even_mask(wide, lanes)
@@ -416,23 +459,17 @@
     source = product(Z[...], lane_restriction(lanes))
     mean = product(Zk[...], lane_mean(lanes))
     for q in range(own):
-        value = source[half * q : half * (q + 1)]
-        s_next[q] = value
-        if q < 4:
-            to_down[q] = value
-        if q >= own - 4:
-            to_up[q - own + 4] = value
-    for q in range(own + 2):
-        value = mean[half * q : half * (q + 1)]
-        if 1 <= q <= own:
-            k_next[q - 1] = value
-        if 1 <= q <= 5:
-            to_down[3 + q] = value
-        if own - 4 <= q <= own:
-            to_up[8 + q - own] = value
-
-
-def coarse_kernel(s, k, from_down, from_up, field, rest, K, S, U, W, D, R):
+        s_next[q] = source[half * q : half * (q + 1)]
+        k_next[q] = mean[half * (q + 1) : half * (q + 2)]
+    for j in range(4):
+        send.put(j, s_next[j], s_next[own - 4 + j])
+    for j in range(5):
+        send.put(4 + j, mean[half * (1 + j) : half * (2 + j)],
+                 mean[half * (own - 4 + j) : half * (own - 3 + j)])
+
+
+def coarse_kernel(s, k, from_a, from_b, field, rest, K, S, U, W, D, R):
+    from_down, from_up = got_pair(from_a, from_b, "outer")
     planes, wide, lanes = k.shape
     own = planes // 2
     rows = field.shape[1]
@@ -477,17 +514,19 @@
     return 4 * words + (12 << 20)
 
 
-def call(kernel, outs, scratch, *args, in_specs=None, name=None, results=()):
+def call(kernel, outs, scratch, *args, in_specs=None, name=None, results=False):
     extra = {}
     if in_specs is None:
         args = [pltpu.with_memory_space_constraint(a, pltpu.VMEM) for a in args]
     else:
+        args = [pltpu.with_memory_space_constraint(a, pltpu.HBM) for a in args]
         extra = {"in_specs": in_specs, "grid": (1,)}
         extra["out_specs"] = [pl.BlockSpec(memory_space=pltpu.VMEM) for _ in outs]
+    if results:
+        extra = {"out_specs": [pl.BlockSpec(memory_space=pltpu.VMEM) for _ in outs]}
     return pl.pallas_call(
         kernel,
-        out_shape=[jax.ShapeDtypeStruct(o, F32) if i in results else pltpu.VMEM(o, F32)
-                   for i, o in enumerate(outs)],
+        out_shape=[jax.ShapeDtypeStruct(o, F32) if results else pltpu.VMEM(o, F32) for o in outs],
         scratch_shapes=[pltpu.VMEM(shape, F32) for shape in scratch],
         compiler_params=pltpu.CompilerParams(vmem_limit_bytes=limit(scratch)),
         name=name,
@@ -501,11 +540,14 @@
     return [block, block, block, (12, pairs, wide, lanes), block, (2, r_pairs, r_rows, lanes)]
 
 
-def exchange(to_low, to_high, axis):
+def exchange(a, b, axis):
     size = lax.axis_size(axis)
-    up = [(i, i + 1) for i in range(size - 1)]
-    down = [(i + 1, i) for i in range(size - 1)]
-    return lax.ppermute(to_high, axis, up), lax.ppermute(to_low, axis, down)
+
+    def swapped(x, first):
+        pairs = [(i, i + 1) for i in range(first, size - 1, 2)]
+        return lax.ppermute(x, axis, pairs + [(j, i) for i, j in pairs])
+
+    return swapped(a, 1), swapped(b, 0)
 
 
 def body(right_side, coefficient):
@@ -517,51 +559,49 @@
     low = pl.BlockSpec((planes, 8, lanes), lambda i: (0, 0, 0))
     high = pl.BlockSpec((planes, 8, lanes), lambda i: (0, rows // 8 - 1, 0))
     message = (2, own, 8, lanes)
-    to_low, to_high = call(pack_rows_kernel, [message] * 2, [], s, s, k, k,
-                           in_specs=[low, high, low, high], name="pack_rows")
-    from_low, from_high = exchange(to_low, to_high, "inner")
+    sent = call(pack_rows_kernel, [message] * 2, [], s, s, k, k,
+                in_specs=[low, high, low, high], name="pack_rows")
+    row_halo = exchange(*sent, "inner")
     half, next_lanes = rows // 2, lanes // 2
     (mean,) = call(mean_kernel, [(own, half, next_lanes)], [(half * own, lanes)], k, name="mean")
     message = (9, rows + 8, lanes)
-    to_down, to_up = call(pack_planes_kernel, [message] * 2, [], s, k, from_low, from_high,
-                          name="pack_planes")
-    mean, to_down, to_up = lax.optimization_barrier((mean, to_down, to_up))
-    from_down, from_up = exchange(to_down, to_up, "outer")
-    mean_low, mean_high = exchange(mean, mean, "inner")
+    to_a, to_b = call(pack_planes_kernel, [message] * 2, [], s, k, *row_halo, name="pack_planes")
+    mean, to_a, to_b = lax.optimization_barrier((mean, to_a, to_b))
+    plane_halo = exchange(to_a, to_b, "outer")
+    mean_halo = exchange(mean, mean, "inner")
 
     count = own + 2
     message = (count, half, next_lanes)
-    field0, source, to_low, to_high = call(
+    field0, source, to_a, to_b = call(
         fine_kernel, [s.shape, message, message, message],
         level_scratch(own, wide, lanes, own + 4, rows) + [((half + 8) * count, lanes)],
-        s, k, from_low, from_high, from_down, from_up, name="fine_level")
+        s, k, *row_halo, *plane_halo, name="fine_level")
 
     planes, rows, lanes = own, half, next_lanes
     own, wide = planes // 2, 3 * rows
-    mean_low, mean_high, to_low, to_high = lax.optimization_barrier((mean_low, mean_high, to_low, to_high))
-    from_low, from_high = exchange(to_low, to_high, "inner")
+    *mean_halo, to_a, to_b = lax.optimization_barrier((*mean_halo, to_a, to_b))
+    row_halo = exchange(to_a, to_b, "inner")
     message = (6, wide, lanes)
-    k1, to_down, to_up = call(
+    k1, *sent = call(
         mean_planes_kernel, [(planes, wide, lanes), message, message], [],
-        mean, mean_low, mean_high, name="mean_planes")
-    k_down, k_up = exchange(to_down, to_up, "outer")
-    s1, to_down, to_up = call(
+        mean, *mean_halo, name="mean_planes")
+    mean_halo = exchange(*sent, "outer")
+    s1, *sent = call(
         source_planes_kernel, [(planes + 2, wide, lanes), message, message], [],
-        source, to_low, to_high, from_low, from_high, name="source_planes")
-    from_down, from_up = exchange(to_down, to_up, "outer")
+        source, to_a, to_b, *row_halo, name="source_planes")
+    source_halo = exchange(*sent, "outer")
     half, next_lanes = wide // 2, lanes // 2
     block, message = (own, half, next_lanes), (9, half, next_lanes)
-    field1, s2, k2, to_down, to_up = call(
+    field1, s2, k2, *sent = call(
         middle_kernel, [(planes, rows, lanes), block, block, message, message],
         level_scratch(own, wide, lanes, own + 2, wide) + [(half * own, lanes), (half * (own + 2), lanes)],
-        s1, k1, from_down, from_up, k_down, k_up, name="middle_level")
+        s1, k1, *source_halo, *mean_halo, name="middle_level")
 
     planes, rows, wide, lanes = own, rows // 2, half, next_lanes
     own = planes // 2
-    from_down, from_up = exchange(to_down, to_up, "outer")
     field2, rest = call(
         coarse_kernel, [(planes, rows, lanes)] * 2, level_scratch(own, wide, lanes, own + 4, rows),
-        s2, k2, from_down, from_up, name="coarse_level")
+        s2, k2, *exchange(*sent, "outer"), name="coarse_level", results=True)
     return field0, field1, field2, rest
 
 

time: 79.8 us -> 69.5 us (0.87)
  starting transfers between devices: 35.8 us -> 30.2 us
  local copies, waits for them, and re-layouts: 5.29 us -> 1.64 us
  waiting for transfers between devices: 24.9 us -> 22.1 us
  Pallas kernels: 12.3 us -> 14.4 us
    ppermute x14, starting transfers between devices: 35.8 us -> 30.2 us  [swapped(): return lax.ppermute(x, axis, pairs + [(j, i) for i, j in pairs])]
    unnamed x12 -> x6, local copies, waits for them, and re-layouts: 5.29 us -> 1.64 us
    ppermute x14, waiting for transfers between devices: 24.9 us -> 22.1 us  [swapped(): return lax.ppermute(x, axis, pairs + [(j, i) for i, j in pairs])]
    pallas_call x8, Pallas kernels: 12.3 us -> 14.4 us  [call(): pl.pallas_call(kernel, out_shape=[jax.ShapeDtypeStruct(o, F32) if results...]
  transfers between devices with their start and end apart: 14 -> 14, of which waited for: 8 -> 5; matrix products, arithmetic and copies ran while one was open for 2% -> 2% of each run, Pallas kernels for 11% -> 13%
where the time goes in v5:
time: 69.5 us; the launch traced here: 69.2 us
  starting transfers between devices  30.2 us (43%)
  waiting for transfers between devices  22.1 us (32%)
  Pallas kernels  14.4 us (21%)
  local copies, waits for them, and re-layouts  1.64 us (2%)
  between operations  0.83 us (1%)
    ppermute x14, starting transfers between devices, swapped(): return lax.ppermute(x, axis, pairs + [(j, i) for i, j in pairs])  30.2 us
    ppermute x14, waiting for transfers between devices, swapped(): return lax.ppermute(x, axis, pairs + [(j, i) for i, j in pairs])  22.1 us
    pallas_call x8, Pallas kernels, call(): pl.pallas_call(kernel, out_shape=[jax.ShapeDtypeStruct(o, F32) if results...  14.4 us
    unnamed x6, local copies, waits for them, and re-layouts  1.64 us
  transfers between devices with their start and end apart: 14, of which 5 were waited for; matrix products, arithmetic and copies ran while one was open for 2% of the time, Pallas kernels for 13%

profile of v5, /device:TPU:1, one launch (start us, length us, event | category | flops | bytes accessed | tf_op | source)
XLA Modules:
  0.0 69.2 jit_solution(9119253967407065154)
XLA Ops:
  0.6 0.0 copy-start
  0.6 1.4 %pack_rows.1 = (f32[2,8,8,512]{3,2,1,0:T(8,128)S(1)}, f32[2,8,8,512]{3,2,1,0:T(8,128)S(1)}) custom-call(f32[16,32,512]{2,1,0:T(8,128)} %s.3, f32[16,32,512]{2,1,0:T(8,128)} %s.3, f32[16,32,512]{2,1,0:T(8,128)} %k.5, f32[16,32,512]{2,1,0:T(8,128)} %k.5), custom_call_target="tpu_custom_call" | custom-call | tf_op jit(solution)/shard_map/pack_rows/pallas_call | solution.py:527
  2.0 0.0 copy-start.1
  2.0 0.8 %collective-permute-start = (f32[2,8,8,512]{3,2,1,0:T(8,128)S(1)}, f32[2,8,8,512]{3,2,1,0:T(8,128)S(1)}, u32[]{:S(2)}, u32[]{:S(2)}) collective-permute-start(f32[2,8,8,512]{3,2,1,0:T(8,128)S(1)} %get-tuple-element.32), channel_id=1, source_target_pairs={{1,2},{2,1},{5,6},{6,5},{9,10},{10,9},{13,14},{14,13},{17,18},{18,... | collective-permute-start | bytes 786440 | tf_op jit(solution)/shard_map/ppermute | solution.py:548
  2.8 4.5 %collective-permute-start.1 = (f32[2,8,8,512]{3,2,1,0:T(8,128)S(1)}, f32[2,8,8,512]{3,2,1,0:T(8,128)S(1)}, u32[]{:S(2)}, u32[]{:S(2)}) collective-permute-start(f32[2,8,8,512]{3,2,1,0:T(8,128)S(1)} %get-tuple-element.33), channel_id=1, source_target_pairs={{0,1},{2,3},{1,0},{3,2},{4,5},{6,7},{5,4},{7,6},{8,9},{10,11},{9,8... | collective-permute-start | bytes 786440 | tf_op jit(solution)/shard_map/ppermute | solution.py:548
  7.4 0.0 copy-done
  7.4 1.0 %mean.1.own_rows = f32[8,16,256]{2,1,0:T(8,128)S(1)} custom-call(f32[16,32,512]{2,1,0:T(8,128)S(1)} %copy-done), custom_call_target="tpu_custom_call" | custom-call | tf_op jit(solution)/shard_map/mean/pallas_call | solution.py:527
  8.3 0.0 collective-permute-done.from_a.row_a
  8.4 10.3 %collective-permute-done.1.from_b.row_b = f32[2,8,8,512]{3,2,1,0:T(8,128)S(1)} collective-permute-done((f32[2,8,8,512]{3,2,1,0:T(8,128)S(1)}, f32[2,8,8,512]{3,2,1,0:T(8,128)S(1)}, u32[]{:S(2)}, u32[]{:S(2)}) %collective-permute-start.1) | collective-permute-done | bytes 262176 | tf_op jit(solution)/shard_map/ppermute | solution.py:548
  18.6 0.0 copy-done.1
  18.6 0.1 pack_planes.1
  18.8 4.6 %collective-permute-start.2 = (f32[9,40,512]{2,1,0:T(8,128)S(1)}, f32[9,40,512]{2,1,0:T(8,128)S(1)}, u32[]{:S(2)}, u32[]{:S(2)}) collective-permute-start(f32[9,40,512]{2,1,0:T(8,128)S(1)} %get-tuple-element.36), channel_id=1, source_target_pairs={{4,8},{12,16},{20,24},{8,4},{16,12},{24,20},{5,9},{13,17},{21,25},... | collective-permute-start | bytes 2211848 | tf_op jit(solution)/shard_map/ppermute | solution.py:548
  23.4 0.1 collective-permute-start.3
  23.5 0.7 collective-permute-start.4
  24.2 1.7 %collective-permute-start.5 = (f32[8,16,256]{2,1,0:T(8,128)S(1)}, f32[8,16,256]{2,1,0:T(8,128)S(1)}, u32[]{:S(2)}, u32[]{:S(2)}) collective-permute-start(f32[8,16,256]{2,1,0:T(8,128)S(1)} %mean.1.own_rows), channel_id=1, source_target_pairs={{0,1},{2,3},{1,0},{3,2},{4,5},{6,7},{5,4},{7,6},{8,9},{10,11},{9,8... | collective-permute-start | bytes 393224 | tf_op jit(solution)/shard_map/ppermute | solution.py:548
  25.9 6.8 %collective-permute-done.2.plane_a = f32[9,40,512]{2,1,0:T(8,128)S(1)} collective-permute-done((f32[9,40,512]{2,1,0:T(8,128)S(1)}, f32[9,40,512]{2,1,0:T(8,128)S(1)}, u32[]{:S(2)}, u32[]{:S(2)}) %collective-permute-start.2) | collective-permute-done | bytes 737312 | tf_op jit(solution)/shard_map/ppermute | solution.py:548
  32.7 0.0 collective-permute-done.3.plane_b
  32.7 7.7 %fine_level.1 = (f32[16,32,512]{2,1,0:T(8,128)S(1)}, f32[10,16,256]{2,1,0:T(8,128)S(1)}, f32[10,16,256]{2,1,0:T(8,128)S(1)}, f32[10,16,256]{2,1,0:T(8,128)S(1)}) custom-call(f32[16,32,512]{2,1,0:T(8,128)S(1)} %copy-done.1, f32[16,32,512]{2,1,0:T(8,128)S(1)} %copy-done, f32[2,8,8,512]{3,2,1,0:T(8,128)S(1)} %collective-permute-done.from_a.row_a, ...), custom_call_target="tpu_custom_call" | custom-call | tf_op jit(solution)/shard_map/fine_level/pallas_call | solution.py:527
  40.4 0.0 collective-permute-done.4.from_a
  40.4 0.0 collective-permute-done.5.from_b
  40.4 0.7 collective-permute-start.6
  41.1 1.8 %collective-permute-start.7 = (f32[10,16,256]{2,1,0:T(8,128)S(1)}, f32[10,16,256]{2,1,0:T(8,128)S(1)}, u32[]{:S(2)}, u32[]{:S(2)}) collective-permute-start(f32[10,16,256]{2,1,0:T(8,128)S(1)} %get-tuple-element.44.sent_b), channel_id=1, source_target_pairs={{0,1},{2,3},{1,0},{3,2},{4,5},{6,7},{5,4},{7,6},{8,9},{10,11},{9,8... | collective-permute-start | bytes 491528 | tf_op jit(solution)/shard_map/ppermute | solution.py:548
  42.9 0.1 mean_planes.1
  43.0 4.0 %collective-permute-start.10 = (f32[6,48,256]{2,1,0:T(8,128)S(1)}, f32[6,48,256]{2,1,0:T(8,128)S(1)}, u32[]{:S(2)}, u32[]{:S(2)}) collective-permute-start(f32[6,48,256]{2,1,0:T(8,128)S(1)} %get-tuple-element.51), channel_id=1, source_target_pairs={{4,8},{12,16},{20,24},{8,4},{16,12},{24,20},{5,9},{13,17},{21,25},... | collective-permute-start | bytes 884744 | tf_op jit(solution)/shard_map/ppermute | solution.py:548
  47.0 0.1 collective-permute-start.11
  47.1 0.0 collective-permute-done.6.from_a
  47.1 0.2 collective-permute-done.7.from_b
  47.3 0.1 source_planes.1
  47.4 7.5 %collective-permute-start.8 = (f32[6,48,256]{2,1,0:T(8,128)S(1)}, f32[6,48,256]{2,1,0:T(8,128)S(1)}, u32[]{:S(2)}, u32[]{:S(2)}) collective-permute-start(f32[6,48,256]{2,1,0:T(8,128)S(1)} %get-tuple-element.49), channel_id=1, source_target_pairs={{4,8},{12,16},{20,24},{8,4},{16,12},{24,20},{5,9},{13,17},{21,25},... | collective-permute-start | bytes 884744 | tf_op jit(solution)/shard_map/ppermute | solution.py:548
  54.9 0.1 collective-permute-start.9
  54.9 0.0 collective-permute-done.10.mean_a
  55.0 0.0 collective-permute-done.11.mean_b
  55.0 4.1 %collective-permute-done.8.source_a = f32[6,48,256]{2,1,0:T(8,128)S(1)} collective-permute-done((f32[6,48,256]{2,1,0:T(8,128)S(1)}, f32[6,48,256]{2,1,0:T(8,128)S(1)}, u32[]{:S(2)}, u32[]{:S(2)}) %collective-permute-start.8) | collective-permute-done | bytes 294944 | tf_op jit(solution)/shard_map/ppermute | solution.py:548
  59.1 0.0 collective-permute-done.9.source_b
  59.1 3.0 %middle_level.1 = (f32[8,16,256]{2,1,0:T(8,128)S(1)}, f32[4,24,128]{2,1,0:T(8,128)S(1)}, f32[4,24,128]{2,1,0:T(8,128)S(1)}, f32[9,24,128]{2,1,0:T(8,128)S(1)}, f32[9,24,128]{2,1,0:T(8,128)S(1)}) custom-call(f32[10,48,256]{2,1,0:T(8,128)S(1)} %get-tuple-element.45.s, f32[8,48,256]{2,1,0:T(8,128)S(1)} %get-tuple-element.48.k, ...), custom_call_target="tpu_custom_call" | custom-call | tf_op jit(solution)/shard_map/middle_level/pallas_call | solution.py:527
  62.1 3.6 %collective-permute-start.12 = (f32[9,24,128]{2,1,0:T(8,128)S(1)}, f32[9,24,128]{2,1,0:T(8,128)S(1)}, u32[]{:S(2)}, u32[]{:S(2)}) collective-permute-start(f32[9,24,128]{2,1,0:T(8,128)S(1)} %get-tuple-element.56), channel_id=1, source_target_pairs={{4,8},{12,16},{20,24},{8,4},{16,12},{24,20},{5,9},{13,17},{21,25},... | collective-permute-start | bytes 331784 | tf_op jit(solution)/shard_map/ppermute | solution.py:548
  65.7 0.1 collective-permute-start.13
  65.8 1.0 %copy.6 = f32[16,32,512]{2,1,0:T(8,128)} copy(f32[16,32,512]{2,1,0:T(8,128)S(1)} %get-tuple-element.60) | data formatting | bytes 2097152
  66.8 0.7 copy.7
  67.4 0.7 %collective-permute-done.12.from_a = f32[9,24,128]{2,1,0:T(8,128)S(1)} collective-permute-done((f32[9,24,128]{2,1,0:T(8,128)S(1)}, f32[9,24,128]{2,1,0:T(8,128)S(1)}, u32[]{:S(2)}, u32[]{:S(2)}) %collective-permute-start.12) | collective-permute-done | bytes 110624 | tf_op jit(solution)/shard_map/ppermute | solution.py:548
  68.1 0.0 collective-permute-done.13.from_b
  68.1 1.0 %coarse_level.1 = (f32[4,8,128]{2,1,0:T(8,128)}, f32[4,8,128]{2,1,0:T(8,128)}) custom-call(f32[4,24,128]{2,1,0:T(8,128)S(1)} %get-tuple-element.54.s, f32[4,24,128]{2,1,0:T(8,128)S(1)} %get-tuple-element.55.k, f32[9,24,128]{2,1,0:T(8,128)S(1)} %collective-permute-done.12.from_a, f32[9,24,128]{2,1,0:T(8,128)S(1)} %collective-permute-done.13.from_b), custom_call_target="tpu_custom_call" | custom-call | tf_op jit(solution)/shard_map/coarse_level/pallas_call | solution.py:527
Async XLA Ops:
  0.6 6.8 %copy-start = (f32[16,32,512]{2,1,0:T(8,128)S(1)}, f32[16,32,512]{2,1,0:T(8,128)}, u32[]{:S(2)}) copy-start(f32[16,32,512]{2,1,0:T(8,128)} %k.5) | copy-start | bytes 3145732
  2.0 16.6 %copy-start.1 = (f32[16,32,512]{2,1,0:T(8,128)S(1)}, f32[16,32,512]{2,1,0:T(8,128)}, u32[]{:S(2)}) copy-start(f32[16,32,512]{2,1,0:T(8,128)} %s.3) | copy-start | bytes 3145732
  2.0 6.3 %collective-permute-start = (f32[2,8,8,512]{3,2,1,0:T(8,128)S(1)}, f32[2,8,8,512]{3,2,1,0:T(8,128)S(1)}, u32[]{:S(2)}, u32[]{:S(2)}) collective-permute-start(f32[2,8,8,512]{3,2,1,0:T(8,128)S(1)} %get-tuple-element.32), channel_id=1, source_target_pairs={{1,2},{2,1},{5,6},{6,5},{9,10},{10,9},{13,14},{14,13},{17,18},{18,... | collective-permute-start | bytes 786440 | tf_op jit(solution)/shard_map/ppermute | solution.py:548
  2.8 15.8 %collective-permute-start.1 = (f32[2,8,8,512]{3,2,1,0:T(8,128)S(1)}, f32[2,8,8,512]{3,2,1,0:T(8,128)S(1)}, u32[]{:S(2)}, u32[]{:S(2)}) collective-permute-start(f32[2,8,8,512]{3,2,1,0:T(8,128)S(1)} %get-tuple-element.33), channel_id=1, source_target_pairs={{0,1},{2,3},{1,0},{3,2},{4,5},{6,7},{5,4},{7,6},{8,9},{10,11},{9,8... | collective-permute-start | bytes 786440 | tf_op jit(solution)/shard_map/ppermute | solution.py:548
  18.8 13.9 %collective-permute-start.2 = (f32[9,40,512]{2,1,0:T(8,128)S(1)}, f32[9,40,512]{2,1,0:T(8,128)S(1)}, u32[]{:S(2)}, u32[]{:S(2)}) collective-permute-start(f32[9,40,512]{2,1,0:T(8,128)S(1)} %get-tuple-element.36), channel_id=1, source_target_pairs={{4,8},{12,16},{20,24},{8,4},{16,12},{24,20},{5,9},{13,17},{21,25},... | collective-permute-start | bytes 2211848 | tf_op jit(solution)/shard_map/ppermute | solution.py:548
  23.4 9.3 %collective-permute-start.3 = (f32[9,40,512]{2,1,0:T(8,128)S(1)}, f32[9,40,512]{2,1,0:T(8,128)S(1)}, u32[]{:S(2)}, u32[]{:S(2)}) collective-permute-start(f32[9,40,512]{2,1,0:T(8,128)S(1)} %get-tuple-element.37), channel_id=1, source_target_pairs={{0,4},{8,12},{16,20},{24,28},{4,0},{12,8},{20,16},{28,24},{1,5},{9... | collective-permute-start | bytes 2211848 | tf_op jit(solution)/shard_map/ppermute | solution.py:548
  23.5 16.9 %collective-permute-start.4 = (f32[8,16,256]{2,1,0:T(8,128)S(1)}, f32[8,16,256]{2,1,0:T(8,128)S(1)}, u32[]{:S(2)}, u32[]{:S(2)}) collective-permute-start(f32[8,16,256]{2,1,0:T(8,128)S(1)} %mean.1.own_rows), channel_id=1, source_target_pairs={{1,2},{2,1},{5,6},{6,5},{9,10},{10,9},{13,14},{14,13},{17,18},{18,... | collective-permute-start | bytes 393224 | tf_op jit(solution)/shard_map/ppermute | solution.py:548
  24.2 16.3 %collective-permute-start.5 = (f32[8,16,256]{2,1,0:T(8,128)S(1)}, f32[8,16,256]{2,1,0:T(8,128)S(1)}, u32[]{:S(2)}, u32[]{:S(2)}) collective-permute-start(f32[8,16,256]{2,1,0:T(8,128)S(1)} %mean.1.own_rows), channel_id=1, source_target_pairs={{0,1},{2,3},{1,0},{3,2},{4,5},{6,7},{5,4},{7,6},{8,9},{10,11},{9,8... | collective-permute-start | bytes 393224 | tf_op jit(solution)/shard_map/ppermute | solution.py:548
  40.4 6.7 %collective-permute-start.6 = (f32[10,16,256]{2,1,0:T(8,128)S(1)}, f32[10,16,256]{2,1,0:T(8,128)S(1)}, u32[]{:S(2)}, u32[]{:S(2)}) collective-permute-start(f32[10,16,256]{2,1,0:T(8,128)S(1)} %get-tuple-element.43.sent_a), channel_id=1, source_target_pairs={{1,2},{2,1},{5,6},{6,5},{9,10},{10,9},{13,14},{14,13},{17,18},{18,... | collective-permute-start | bytes 491528 | tf_op jit(solution)/shard_map/ppermute | solution.py:548
  41.1 6.2 %collective-permute-start.7 = (f32[10,16,256]{2,1,0:T(8,128)S(1)}, f32[10,16,256]{2,1,0:T(8,128)S(1)}, u32[]{:S(2)}, u32[]{:S(2)}) collective-permute-start(f32[10,16,256]{2,1,0:T(8,128)S(1)} %get-tuple-element.44.sent_b), channel_id=1, source_target_pairs={{0,1},{2,3},{1,0},{3,2},{4,5},{6,7},{5,4},{7,6},{8,9},{10,11},{9,8... | collective-permute-start | bytes 491528 | tf_op jit(solution)/shard_map/ppermute | solution.py:548
  43.0 12.0 %collective-permute-start.10 = (f32[6,48,256]{2,1,0:T(8,128)S(1)}, f32[6,48,256]{2,1,0:T(8,128)S(1)}, u32[]{:S(2)}, u32[]{:S(2)}) collective-permute-start(f32[6,48,256]{2,1,0:T(8,128)S(1)} %get-tuple-element.51), channel_id=1, source_target_pairs={{4,8},{12,16},{20,24},{8,4},{16,12},{24,20},{5,9},{13,17},{21,25},... | collective-permute-start | bytes 884744 | tf_op jit(solution)/shard_map/ppermute | solution.py:548
  47.0 7.9 %collective-permute-start.11 = (f32[6,48,256]{2,1,0:T(8,128)S(1)}, f32[6,48,256]{2,1,0:T(8,128)S(1)}, u32[]{:S(2)}, u32[]{:S(2)}) collective-permute-start(f32[6,48,256]{2,1,0:T(8,128)S(1)} %get-tuple-element.52), channel_id=1, source_target_pairs={{0,4},{8,12},{16,20},{24,28},{4,0},{12,8},{20,16},{28,24},{1,5},{9... | collective-permute-start | bytes 884744 | tf_op jit(solution)/shard_map/ppermute | solution.py:548
  47.4 11.7 %collective-permute-start.8 = (f32[6,48,256]{2,1,0:T(8,128)S(1)}, f32[6,48,256]{2,1,0:T(8,128)S(1)}, u32[]{:S(2)}, u32[]{:S(2)}) collective-permute-start(f32[6,48,256]{2,1,0:T(8,128)S(1)} %get-tuple-element.49), channel_id=1, source_target_pairs={{4,8},{12,16},{20,24},{8,4},{16,12},{24,20},{5,9},{13,17},{21,25},... | collective-permute-start | bytes 884744 | tf_op jit(solution)/shard_map/ppermute | solution.py:548
  54.9 4.2 %collective-permute-start.9 = (f32[6,48,256]{2,1,0:T(8,128)S(1)}, f32[6,48,256]{2,1,0:T(8,128)S(1)}, u32[]{:S(2)}, u32[]{:S(2)}) collective-permute-start(f32[6,48,256]{2,1,0:T(8,128)S(1)} %get-tuple-element.50), channel_id=1, source_target_pairs={{0,4},{8,12},{16,20},{24,28},{4,0},{12,8},{20,16},{28,24},{1,5},{9... | collective-permute-start | bytes 884744 | tf_op jit(solution)/shard_map/ppermute | solution.py:548
  62.1 6.1 %collective-permute-start.12 = (f32[9,24,128]{2,1,0:T(8,128)S(1)}, f32[9,24,128]{2,1,0:T(8,128)S(1)}, u32[]{:S(2)}, u32[]{:S(2)}) collective-permute-start(f32[9,24,128]{2,1,0:T(8,128)S(1)} %get-tuple-element.56), channel_id=1, source_target_pairs={{4,8},{12,16},{20,24},{8,4},{16,12},{24,20},{5,9},{13,17},{21,25},... | collective-permute-start | bytes 331784 | tf_op jit(solution)/shard_map/ppermute | solution.py:548
  65.7 2.4 %collective-permute-start.13 = (f32[9,24,128]{2,1,0:T(8,128)S(1)}, f32[9,24,128]{2,1,0:T(8,128)S(1)}, u32[]{:S(2)}, u32[]{:S(2)}) collective-permute-start(f32[9,24,128]{2,1,0:T(8,128)S(1)} %get-tuple-element.57), channel_id=1, source_target_pairs={{0,4},{8,12},{16,20},{24,28},{4,0},{12,8},{20,16},{28,24},{1,5},{9... | collective-permute-start | bytes 331784 | tf_op jit(solution)/shard_map/ppermute | solution.py:548

commit v6 on v5

--- a/solution.py
+++ b/solution.py
@@ -93,29 +93,44 @@
 
 def span(own, layers):
     extra = (layers + 1) // 2
-    return HP - extra, HP + own + extra
-
-
-def over(first, last, step, unrolled):
-    if unrolled:
-        for p in range(first, last):
-            step(p, 0)
-    else:
-        lax.fori_loop(first, last, step, 0)
-
-
-def relax_level(K, S, U, W, D, R, own, depth, residual_layers, inset, unrolled):
-    _, pairs, rows, lanes = K.shape
-    even = even_mask(rows, lanes)
-
-    def setup(colour, layers):
-        first, last = span(own, layers)
-
-        def step(p, carry):
-            near = list(neighbours(K, colour, p, pairs, even))
+    return range(HP - extra, HP + own + extra)
+
+
+class Store:
+    def __init__(self, ref, start=0, early=None, held=()):
+        self.ref, self.start = ref, start
+        self.early = {key: early for key in held}
+
+    def place(self, at):
+        first, p, *rest = at
+        early = self.early.get((first, p))
+        if early is not None:
+            return early.ref, (first, p - early.start, *rest)
+        return self.ref, (first, p - self.start, *rest)
+
+    def __getitem__(self, at):
+        ref, at = self.place(at)
+        return ref[at]
+
+    def __setitem__(self, at, value):
+        self.early.pop((at[0], at[1]), None)
+        ref, at = self.place(at)
+        ref[at] = value
+
+
+class Level:
+    def __init__(self, K, S, U, W, D, own, shape):
+        self.K, self.S, self.U, self.W, self.D, self.own = K, S, U, W, D, own
+        self.pairs = own + 2 * HP
+        self.rows, self.lanes = shape
+        self.even = even_mask(self.rows, self.lanes)
+
+    def setup(self, colour, pairs, inverse_out=None):
+        for p in pairs:
+            near = list(neighbours(self.K, colour, p, self.pairs, self.even))
             near[4] = lane_edge(near[4], True)
             near[5] = lane_edge(near[5], False)
-            centre = K[colour, p]
+            centre = self.K[colour, p]
             total = near[0]
             for value in near[1:]:
                 total = total + value
@@ -128,57 +143,66 @@
                     weight = lane_edge(weight, True)
                 if i == 5:
                     weight = lane_edge(weight, False)
-                W[colour * 6 + i, p] = weight
-            D[colour, p] = diag
-            start = S[colour, p] * inverse
-            S[colour, p] = start
-            if colour == 0:
-                U[0, p] = start
-            return carry
-
-        over(first, last, step, unrolled)
-        zero = jnp.zeros((rows, lanes), F32)
-        for p in list(range(first)) + list(range(last, pairs)):
-            U[colour, p] = zero
-
-    def relaxed(colour, p):
-        near = neighbours(U, colour, p, pairs, even)
-        total = S[colour, p]
+                self.W[colour * 6 + i, p] = weight
+            self.D[colour, p] = diag
+            if inverse_out is not None:
+                inverse_out[colour, p] = inverse
+            else:
+                self.begin(colour, p, inverse)
+
+    def begin(self, colour, p, inverse):
+        start = self.S[colour, p] * inverse
+        self.S[colour, p] = start
+        if colour == 0:
+            self.U[0, p] = start
+
+    def clear(self, colour, pairs):
+        zero = jnp.zeros((self.rows, self.lanes), F32)
+        for p in range(self.pairs):
+            if p not in pairs:
+                self.U[colour, p] = zero
+
+    def relaxed(self, colour, p):
+        near = neighbours(self.U, colour, p, self.pairs, self.even)
+        total = self.S[colour, p]
         for i, value in enumerate(near):
-            total = total + W[colour * 6 + i, p] * value
+            total = total + self.W[colour * 6 + i, p] * value
         return total
 
-    def half_sweep(colour, layers):
-        first, last = span(own, layers)
-
-        def step(p, carry):
-            U[colour, p] = relaxed(colour, p)
-            return carry
-
-        over(first, last, step, unrolled)
-
-    setup(0, depth)
-    setup(1, depth - 1)
-    half_sweep(1, depth - 1)
-    half_sweep(0, depth - 2)
-    half_sweep(1, depth - 3)
-    first, last = span(own, residual_layers)
-
-    def left(p, carry):
+    def sweep(self, colour, pairs):
+        for p in pairs:
+            self.U[colour, p] = self.relaxed(colour, p)
+
+    def residual(self, R, pairs, pad, inset):
+        for i, p in enumerate(pairs):
+            for colour in (0, 1):
+                rest = self.D[colour, p] * (self.relaxed(colour, p) - self.U[colour, p])
+                R[colour, i + pad] = rest[inset : self.rows - inset]
+
+    def all_setup(self, depth, inverse_out=None):
         for colour in (0, 1):
-            rest = D[colour, p] * (relaxed(colour, p) - U[colour, p])
-            R[colour, p - first + R_PAD[residual_layers]] = rest[inset : rows - inset]
-        return carry
-
-    over(first, last, left, unrolled)
-
-
-R_PAD = {0: 2, 1: 0}
-
-
-def store_field(U, out, own, even):
+            self.setup(colour, span(self.own, depth - colour), inverse_out)
+
+    def all_clear(self, depth):
+        for colour in (0, 1):
+            self.clear(colour, span(self.own, depth - colour))
+
+    def all_sweeps(self, depth):
+        for i, colour in enumerate((1, 0, 1)):
+            self.sweep(colour, span(self.own, depth - 1 - i))
+
+
+def without(pairs, inner):
+    return [p for p in pairs if p not in inner]
+
+
+def inner_span(own, margin):
+    return range(HP + margin, HP + own - margin)
+
+
+def store_field(U, out, own, even, wide):
     rows = out.shape[1]
-    first = (U.shape[2] - rows) // 2
+    first = (wide - rows) // 2
     for p in range(own):
         red = U[0, HP + p, first : first + rows]
         black = U[1, HP + p, first : first + rows]
@@ -288,22 +312,16 @@
         out[q] = mean[half * q : half * (q + 1)]
 
 
-def fine_kernel(s, k, row_a, row_b, plane_a, plane_b,
-                field, source_out, to_a, to_b,
-                K, S, U, W, D, R, Z):
-    from_low, from_high = got_pair(row_a, row_b, "inner")
-    from_down, from_up = got_pair(plane_a, plane_b, "outer")
-    send = Send(to_a, to_b, "inner")
+def fine_prepare_kernel(s, k, row_a, row_b, *arrays):
     planes, rows, lanes = s.shape
     own = planes // 2
     wide = rows + 16
-    even = even_mask(8, lanes)
+    from_low, from_high = got_pair(row_a, row_b, "inner")
     even_own = even_mask(rows, lanes)
     row = row_index(lanes)
-    zero8 = jnp.zeros((8, lanes), F32)
-    zero = jnp.zeros((wide, lanes), F32)
-
-    def fill(p, carry):
+    K, S, U, W, D = [Store(ref, HP) for ref in arrays]
+
+    def fill(p):
         at = HP + p
         lr, lb = from_low[0, p], from_low[1, p]
         hr, hb = from_high[0, p], from_high[1, p]
@@ -319,9 +337,38 @@
             a, b = ref[2 * p], ref[2 * p + 1]
             to[0, at, 8 : 8 + rows] = pick(even_own, a, b)
             to[1, at, 8 : 8 + rows] = pick(even_own, b, a)
-        return carry
-
-    lax.fori_loop(0, own, fill, 0)
+
+    for p in range(own):
+        fill(p)
+    level = Level(K, S, U, W, D, own, (wide, lanes))
+    level.setup(0, inner_span(own, 1))
+    level.setup(1, inner_span(own, 1))
+    level.sweep(1, inner_span(own, 2))
+    level.sweep(0, inner_span(own, 3))
+
+
+def fine_kernel(plane_a, plane_b, K0, S0, U0, W0, D0,
+                field, source_out, to_a, to_b, K1, S1, U1, W1, D1, R, Z):
+    from_down, from_up = got_pair(plane_a, plane_b, "outer")
+    send = Send(to_a, to_b, "inner")
+    planes, rows, lanes = field.shape
+    own = planes // 2
+    wide = rows + 16
+    even = even_mask(8, lanes)
+    even_own = even_mask(rows, lanes)
+    row = row_index(lanes)
+    zero8 = jnp.zeros((8, lanes), F32)
+
+    def store(ref, early, firsts, pairs):
+        return Store(ref, 0, Store(early, HP), [(i, p) for i in firsts for p in pairs])
+
+    inside = inner_span(own, 1)
+    K = store(K1, K0, (0, 1), inner_span(own, 0))
+    S = store(S1, S0, (0, 1), inner_span(own, 0))
+    W = store(W1, W0, range(12), inside)
+    D = store(D1, D0, (0, 1), inside)
+    U = store(U1, U0, (0,), inside)
+    U.early.update({(1, p): Store(U0, HP) for p in inner_span(own, 2)})
 
     def halo(to, at, ref, first, second):
         def part(rows_of):
@@ -352,8 +399,15 @@
     halo(K, HP + own, from_up, 4, 5)
     halo(K, HP + own + 1, from_up, 6, 7)
     halo(K, HP + own + 2, from_up, 8, None)
-    relax_level(K, S, U, W, D, R, own, 4, 0, 8, True)
-    store_field(U, field, own, even_own)
+    level = Level(K, S, U, W, D, own, (wide, lanes))
+    for colour in (0, 1):
+        level.setup(colour, without(span(own, 4 - colour), inner_span(own, 1)))
+    level.all_clear(4)
+    level.sweep(1, without(span(own, 3), inner_span(own, 2)))
+    level.sweep(0, without(span(own, 2), inner_span(own, 3)))
+    level.sweep(1, span(own, 1))
+    level.residual(R, span(own, 0), 2, 8)
+    store_field(U, field, own, even_own, wide)
     zero = jnp.zeros((rows, lanes), F32)
     for colour in (0, 1):
         for at in (0, 1, own + 2, own + 3):
@@ -389,6 +443,24 @@
     widen_planes(K, Send(to_a, to_b, "outer"), own_rows.shape[0], of)
 
 
+def middle_setup_kernel(k, from_a, from_b, K, W, D, I):
+    from_down, from_up = got_pair(from_a, from_b, "outer")
+    _, pairs, wide, lanes = K.shape
+    planes = k.shape[0]
+    even = even_mask(wide, lanes)
+
+    def plane(i):
+        if i < 0:
+            return from_down[6 + i]
+        return k[i] if i < planes else from_up[i - planes]
+
+    for p in range(pairs):
+        a, b = plane(2 * (p - HP)), plane(2 * (p - HP) + 1)
+        K[0, p] = pick(even, a, b)
+        K[1, p] = pick(even, b, a)
+    Level(K, None, None, W, D, pairs - 2 * HP, (wide, lanes)).all_setup(5, I)
+
+
 def source_planes_kernel(own_rows, sent_a, sent_b, from_a, from_b, S, to_a, to_b):
     planes, rows, lanes = own_rows.shape
     row = lax.broadcasted_iota(jnp.int32, (rows, lanes), 0)
@@ -406,13 +478,13 @@
     widen_planes(S, Send(to_a, to_b, "outer"), planes, of)
 
 
-def middle_kernel(s, k, source_a, source_b, mean_a, mean_b,
+def middle_kernel(s, source_a, source_b, K, W, D, I,
                   field, s_next, k_next, to_a, to_b,
-                  K, S, U, W, D, R, Z, Zk):
+                  S, U, R, Z, Zk):
     from_down, from_up = got_pair(source_a, source_b, "outer")
-    k_down, k_up = got_pair(mean_a, mean_b, "outer")
     send = Send(to_a, to_b, "outer")
-    planes, wide, lanes = k.shape
+    planes = field.shape[0]
+    _, pairs, wide, lanes = K.shape
     own = planes // 2
     even = even_mask(wide, lanes)
     zero = jnp.zeros((wide, lanes), F32)
@@ -434,21 +506,19 @@
             return from_up[1] + s[planes + 1]
         return from_up[i - planes + 1]
 
-    def mean_plane(i):
-        if i < 0:
-            return k_down[6 + i]
-        if i < planes:
-            return k[i]
-        return k_up[i - planes]
-
+    level = Level(K, S, U, W, D, own, (wide, lanes))
     for p in range(-HP, own + HP):
-        for to, plane in ((S, source_plane), (K, mean_plane)):
-            a, b = plane(2 * p), plane(2 * p + 1)
-            to[0, HP + p] = pick(even, a, b)
-            to[1, HP + p] = pick(even, b, a)
-    relax_level(K, S, U, W, D, R, own, 5, 1, 0, True)
+        a, b = source_plane(2 * p), source_plane(2 * p + 1)
+        S[0, HP + p] = pick(even, a, b)
+        S[1, HP + p] = pick(even, b, a)
+    for colour in (0, 1):
+        for p in span(own, 5 - colour):
+            level.begin(colour, p, I[colour, p])
+    level.all_clear(5)
+    level.all_sweeps(5)
+    level.residual(R, span(own, 1), 0, 0)
     rows = field.shape[1]
-    store_field(U, field, own, even_mask(rows, lanes))
+    store_field(U, field, own, even_mask(rows, lanes), wide)
     half = wide // 2
     for q in range(own):
         Z[half * q : half * (q + 1)] = product(
@@ -496,8 +566,12 @@
             a, b = plane(2 * p), plane(2 * p + 1)
             to[0, HP + p] = pick(even, a, b)
             to[1, HP + p] = pick(even, b, a)
-    relax_level(K, S, U, W, D, R, own, 4, 0, (wide - rows) // 2, True)
-    store_field(U, field, own, even_own)
+    level = Level(K, S, U, W, D, own, (wide, lanes))
+    level.all_setup(4)
+    level.all_clear(4)
+    level.all_sweeps(4)
+    level.residual(R, span(own, 0), 2, (wide - rows) // 2)
+    store_field(U, field, own, even_own, wide)
     for p in range(own):
         red, black = R[0, p + 2], R[1, p + 2]
         rest[2 * p] = pick(even_own, red, black)
@@ -534,10 +608,9 @@
     )(*args)
 
 
-def level_scratch(own, wide, lanes, r_pairs, r_rows):
-    pairs = own + 2 * HP
-    block = (2, pairs, wide, lanes)
-    return [block, block, block, (12, pairs, wide, lanes), block, (2, r_pairs, r_rows, lanes)]
+def level_arrays(own, wide, lanes):
+    block = (2, own + 2 * HP, wide, lanes)
+    return [block, block, block, (12, *block[1:]), block]
 
 
 def exchange(a, b, axis):
@@ -568,14 +641,18 @@
     to_a, to_b = call(pack_planes_kernel, [message] * 2, [], s, k, *row_halo, name="pack_planes")
     mean, to_a, to_b = lax.optimization_barrier((mean, to_a, to_b))
     plane_halo = exchange(to_a, to_b, "outer")
+    arrays = level_arrays(own, wide, lanes)
+    early = [(a[0], own, wide, lanes) for a in arrays]
+    prepared = call(fine_prepare_kernel, early, [], s, k, *row_halo, name="fine_prepare")
+    mean, *prepared = lax.optimization_barrier((mean, *prepared))
     mean_halo = exchange(mean, mean, "inner")
 
     count = own + 2
     message = (count, half, next_lanes)
     field0, source, to_a, to_b = call(
         fine_kernel, [s.shape, message, message, message],
-        level_scratch(own, wide, lanes, own + 4, rows) + [((half + 8) * count, lanes)],
-        s, k, *row_halo, *plane_halo, name="fine_level")
+        [*arrays, (2, own + 4, rows, lanes), ((half + 8) * count, lanes)],
+        *plane_halo, *prepared, name="fine_level")
 
     planes, rows, lanes = own, half, next_lanes
     own, wide = planes // 2, 3 * rows
@@ -586,6 +663,9 @@
         mean_planes_kernel, [(planes, wide, lanes), message, message], [],
         mean, *mean_halo, name="mean_planes")
     mean_halo = exchange(*sent, "outer")
+    K, S, U, W, D = level_arrays(own, wide, lanes)
+    constants = call(middle_setup_kernel, [K, W, D, K], [], k1, *mean_halo, name="middle_setup")
+    message = (6, wide, lanes)
     s1, *sent = call(
         source_planes_kernel, [(planes + 2, wide, lanes), message, message], [],
         source, to_a, to_b, *row_halo, name="source_planes")
@@ -594,13 +674,14 @@
     block, message = (own, half, next_lanes), (9, half, next_lanes)
     field1, s2, k2, *sent = call(
         middle_kernel, [(planes, rows, lanes), block, block, message, message],
-        level_scratch(own, wide, lanes, own + 2, wide) + [(half * own, lanes), (half * (own + 2), lanes)],
-        s1, k1, *source_halo, *mean_halo, name="middle_level")
+        [S, U, (2, own + 2, wide, lanes), (half * own, lanes), (half * (own + 2), lanes)],
+        s1, *source_halo, *constants, name="middle_level")
 
     planes, rows, wide, lanes = own, rows // 2, half, next_lanes
     own = planes // 2
     field2, rest = call(
-        coarse_kernel, [(planes, rows, lanes)] * 2, level_scratch(own, wide, lanes, own + 4, rows),
+        coarse_kernel, [(planes, rows, lanes)] * 2,
+        [*level_arrays(own, wide, lanes), (2, own + 4, rows, lanes)],
         s2, k2, *exchange(*sent, "outer"), name="coarse_level", results=True)
     return field0, field1, field2, rest
 

time: 69.5 us -> 66.5 us (0.957)
  starting transfers between devices: 30.2 us -> 25.6 us
  Pallas kernels: 14.4 us -> 15.3 us
  waiting for transfers between devices: 22.1 us -> 22.9 us
    ppermute x14, starting transfers between devices: 30.2 us -> 25.6 us  [swapped(): return lax.ppermute(x, axis, pairs + [(j, i) for i, j in pairs])]
    pallas_call x8 -> x10, Pallas kernels: 14.4 us -> 15.3 us  [call(): pl.pallas_call(kernel, out_shape=[jax.ShapeDtypeStruct(o, F32) if results...]
    ppermute x14, waiting for transfers between devices: 22.1 us -> 22.9 us  [swapped(): return lax.ppermute(x, axis, pairs + [(j, i) for i, j in pairs])]
  transfers between devices with their start and end apart: 14 -> 14, of which waited for: 5 -> 5; matrix products, arithmetic and copies ran while one was open for 2% -> 2% of each run, Pallas kernels for 13% -> 16%
where the time goes in v6:
time: 66.5 us; the launch traced here: 66.2 us
  starting transfers between devices  25.6 us (38%)
  waiting for transfers between devices  22.9 us (34%)
  Pallas kernels  15.3 us (23%)
  local copies, waits for them, and re-layouts  1.64 us (2%)
  between operations  0.85 us (1%)
    ppermute x14, starting transfers between devices, swapped(): return lax.ppermute(x, axis, pairs + [(j, i) for i, j in pairs])  25.6 us
    ppermute x14, waiting for transfers between devices, swapped(): return lax.ppermute(x, axis, pairs + [(j, i) for i, j in pairs])  22.9 us
    pallas_call x10, Pallas kernels, call(): pl.pallas_call(kernel, out_shape=[jax.ShapeDtypeStruct(o, F32) if results...  15.3 us
    unnamed x6, local copies, waits for them, and re-layouts  1.64 us
  transfers between devices with their start and end apart: 14, of which 5 were waited for; matrix products, arithmetic and copies ran while one was open for 2% of the time, Pallas kernels for 16%

profile of v6, /device:TPU:1, one launch (start us, length us, event | category | flops | bytes accessed | tf_op | source)
XLA Modules:
  0.0 66.2 jit_solution(5960643732973513106)
XLA Ops:
  0.6 0.0 copy-start
  0.6 1.4 %pack_rows.1 = (f32[2,8,8,512]{3,2,1,0:T(8,128)S(1)}, f32[2,8,8,512]{3,2,1,0:T(8,128)S(1)}) custom-call(f32[16,32,512]{2,1,0:T(8,128)} %s.3, f32[16,32,512]{2,1,0:T(8,128)} %s.3, f32[16,32,512]{2,1,0:T(8,128)} %k.5, f32[16,32,512]{2,1,0:T(8,128)} %k.5), custom_call_target="tpu_custom_call" | custom-call | tf_op jit(solution)/shard_map/pack_rows/pallas_call | solution.py:601
  2.0 0.0 copy-start.1
  2.0 0.8 %collective-permute-start = (f32[2,8,8,512]{3,2,1,0:T(8,128)S(1)}, f32[2,8,8,512]{3,2,1,0:T(8,128)S(1)}, u32[]{:S(2)}, u32[]{:S(2)}) collective-permute-start(f32[2,8,8,512]{3,2,1,0:T(8,128)S(1)} %get-tuple-element.47), channel_id=1, source_target_pairs={{1,2},{2,1},{5,6},{6,5},{9,10},{10,9},{13,14},{14,13},{17,18},{18,... | collective-permute-start | bytes 786440 | tf_op jit(solution)/shard_map/ppermute | solution.py:621
  2.8 4.5 %collective-permute-start.1 = (f32[2,8,8,512]{3,2,1,0:T(8,128)S(1)}, f32[2,8,8,512]{3,2,1,0:T(8,128)S(1)}, u32[]{:S(2)}, u32[]{:S(2)}) collective-permute-start(f32[2,8,8,512]{3,2,1,0:T(8,128)S(1)} %get-tuple-element.48), channel_id=1, source_target_pairs={{0,1},{2,3},{1,0},{3,2},{4,5},{6,7},{5,4},{7,6},{8,9},{10,11},{9,8... | collective-permute-start | bytes 786440 | tf_op jit(solution)/shard_map/ppermute | solution.py:621
  7.4 0.0 copy-done
  7.4 1.0 %mean.1.own_rows = f32[8,16,256]{2,1,0:T(8,128)S(1)} custom-call(f32[16,32,512]{2,1,0:T(8,128)S(1)} %copy-done), custom_call_target="tpu_custom_call" | custom-call | tf_op jit(solution)/shard_map/mean/pallas_call | solution.py:601
  8.3 0.0 collective-permute-done.from_a.row_a
  8.4 10.3 %collective-permute-done.1.from_b.row_b = f32[2,8,8,512]{3,2,1,0:T(8,128)S(1)} collective-permute-done((f32[2,8,8,512]{3,2,1,0:T(8,128)S(1)}, f32[2,8,8,512]{3,2,1,0:T(8,128)S(1)}, u32[]{:S(2)}, u32[]{:S(2)}) %collective-permute-start.1) | collective-permute-done | bytes 262176 | tf_op jit(solution)/shard_map/ppermute | solution.py:621
  18.6 0.0 copy-done.1
  18.6 0.1 pack_planes.1
  18.8 4.6 %collective-permute-start.2 = (f32[9,40,512]{2,1,0:T(8,128)S(1)}, f32[9,40,512]{2,1,0:T(8,128)S(1)}, u32[]{:S(2)}, u32[]{:S(2)}) collective-permute-start(f32[9,40,512]{2,1,0:T(8,128)S(1)} %get-tuple-element.51), channel_id=1, source_target_pairs={{4,8},{12,16},{20,24},{8,4},{16,12},{24,20},{5,9},{13,17},{21,25},... | collective-permute-start | bytes 2211848 | tf_op jit(solution)/shard_map/ppermute | solution.py:621
  23.4 0.1 collective-permute-start.3
  23.5 2.6 %fine_prepare.1 = (f32[2,8,48,512]{3,2,1,0:T(8,128)S(1)}, f32[2,8,48,512]{3,2,1,0:T(8,128)S(1)}, f32[2,8,48,512]{3,2,1,0:T(8,128)S(1)}, f32[12,8,48,512]{3,2,1,0:T(8,128)S(1)}, f32[2,8,48,512]{3,2,1,0:T(8,128)S(1)}) custom-call(f32[16,32,512]{2,1,0:T(8,128)S(1)} %copy-done.1, f32[16,32,512]{2,1,0:T(8,128)S(1)} %copy-done, ...), custom_call_target="tpu_custom_call" | custom-call | tf_op jit(solution)/shard_map/fine_prepare/pallas_call | solution.py:601
  26.1 0.1 collective-permute-start.5
  26.2 0.7 %collective-permute-start.4 = (f32[8,16,256]{2,1,0:T(8,128)S(1)}, f32[8,16,256]{2,1,0:T(8,128)S(1)}, u32[]{:S(2)}, u32[]{:S(2)}) collective-permute-start(f32[8,16,256]{2,1,0:T(8,128)S(1)} %mean.1.own_rows), channel_id=1, source_target_pairs={{1,2},{2,1},{5,6},{6,5},{9,10},{10,9},{13,14},{14,13},{17,18},{18,... | collective-permute-start | bytes 393224 | tf_op jit(solution)/shard_map/ppermute | solution.py:621
  26.9 5.7 %collective-permute-done.2.plane_a = f32[9,40,512]{2,1,0:T(8,128)S(1)} collective-permute-done((f32[9,40,512]{2,1,0:T(8,128)S(1)}, f32[9,40,512]{2,1,0:T(8,128)S(1)}, u32[]{:S(2)}, u32[]{:S(2)}) %collective-permute-start.2) | collective-permute-done | bytes 737312 | tf_op jit(solution)/shard_map/ppermute | solution.py:621
  32.5 0.0 collective-permute-done.3.plane_b
  32.5 5.6 %fine_level.1 = (f32[16,32,512]{2,1,0:T(8,128)S(1)}, f32[10,16,256]{2,1,0:T(8,128)S(1)}, f32[10,16,256]{2,1,0:T(8,128)S(1)}, f32[10,16,256]{2,1,0:T(8,128)S(1)}) custom-call(f32[9,40,512]{2,1,0:T(8,128)S(1)} %collective-permute-done.2.plane_a, f32[9,40,512]{2,1,0:T(8,128)S(1)} %collective-permute-done.3.plane_b, f32[2,8,48,512]{3,2,1,0:T(8,128)S(1)} %get-tuple-element.59.K0, ...), custom_call_target="tpu_custom_call" | custom-call | tf_op jit(solution)/shard_map/fine_level/pallas_call | solution.py:601
  38.1 0.0 collective-permute-done.5.from_b
  38.1 0.0 collective-permute-done.4.from_a
  38.2 0.7 %collective-permute-start.6 = (f32[10,16,256]{2,1,0:T(8,128)S(1)}, f32[10,16,256]{2,1,0:T(8,128)S(1)}, u32[]{:S(2)}, u32[]{:S(2)}) collective-permute-start(f32[10,16,256]{2,1,0:T(8,128)S(1)} %get-tuple-element.69.sent_a), channel_id=1, source_target_pairs={{1,2},{2,1},{5,6},{6,5},{9,10},{10,9},{13,14},{14,13},{17,18},{18,... | collective-permute-start | bytes 491528 | tf_op jit(solution)/shard_map/ppermute | solution.py:621
  38.8 1.7 %collective-permute-start.7 = (f32[10,16,256]{2,1,0:T(8,128)S(1)}, f32[10,16,256]{2,1,0:T(8,128)S(1)}, u32[]{:S(2)}, u32[]{:S(2)}) collective-permute-start(f32[10,16,256]{2,1,0:T(8,128)S(1)} %get-tuple-element.70.sent_b), channel_id=1, source_target_pairs={{0,1},{2,3},{1,0},{3,2},{4,5},{6,7},{5,4},{7,6},{8,9},{10,11},{9,8... | collective-permute-start | bytes 491528 | tf_op jit(solution)/shard_map/ppermute | solution.py:621
  40.6 0.1 mean_planes.1
  40.6 4.2 %collective-permute-start.10 = (f32[6,48,256]{2,1,0:T(8,128)S(1)}, f32[6,48,256]{2,1,0:T(8,128)S(1)}, u32[]{:S(2)}, u32[]{:S(2)}) collective-permute-start(f32[6,48,256]{2,1,0:T(8,128)S(1)} %get-tuple-element.77), channel_id=1, source_target_pairs={{4,8},{12,16},{20,24},{8,4},{16,12},{24,20},{5,9},{13,17},{21,25},... | collective-permute-start | bytes 884744 | tf_op jit(solution)/shard_map/ppermute | solution.py:621
  44.8 0.1 collective-permute-start.11
  44.9 0.0 collective-permute-done.6.from_a
  44.9 3.3 %collective-permute-done.7.from_b = f32[10,16,256]{2,1,0:T(8,128)S(1)} collective-permute-done((f32[10,16,256]{2,1,0:T(8,128)S(1)}, f32[10,16,256]{2,1,0:T(8,128)S(1)}, u32[]{:S(2)}, u32[]{:S(2)}) %collective-permute-start.7) | collective-permute-done | bytes 163872 | tf_op jit(solution)/shard_map/ppermute | solution.py:621
  48.2 0.1 source_planes.1
  48.3 4.3 %collective-permute-start.8 = (f32[6,48,256]{2,1,0:T(8,128)S(1)}, f32[6,48,256]{2,1,0:T(8,128)S(1)}, u32[]{:S(2)}, u32[]{:S(2)}) collective-permute-start(f32[6,48,256]{2,1,0:T(8,128)S(1)} %get-tuple-element.72), channel_id=1, source_target_pairs={{4,8},{12,16},{20,24},{8,4},{16,12},{24,20},{5,9},{13,17},{21,25},... | collective-permute-start | bytes 884744 | tf_op jit(solution)/shard_map/ppermute | solution.py:621
  52.7 0.1 collective-permute-start.9
  52.7 0.0 collective-permute-done.10.from_a
  52.8 0.0 collective-permute-done.11.from_b
  52.8 1.2 %middle_setup.1 = (f32[2,10,48,256]{3,2,1,0:T(8,128)S(1)}, f32[12,10,48,256]{3,2,1,0:T(8,128)S(1)}, f32[2,10,48,256]{3,2,1,0:T(8,128)S(1)}, f32[2,10,48,256]{3,2,1,0:T(8,128)S(1)}) custom-call(f32[8,48,256]{2,1,0:T(8,128)S(1)} %get-tuple-element.76.k, f32[6,48,256]{2,1,0:T(8,128)S(1)} %collective-permute-done.10.from_a, ...), custom_call_target="tpu_custom_call" | custom-call | tf_op jit(solution)/shard_map/middle_setup/pallas_call | solution.py:601
  53.9 2.9 %collective-permute-done.8.source_a = f32[6,48,256]{2,1,0:T(8,128)S(1)} collective-permute-done((f32[6,48,256]{2,1,0:T(8,128)S(1)}, f32[6,48,256]{2,1,0:T(8,128)S(1)}, u32[]{:S(2)}, u32[]{:S(2)}) %collective-permute-start.8) | collective-permute-done | bytes 294944 | tf_op jit(solution)/shard_map/ppermute | solution.py:621
  56.9 0.0 collective-permute-done.9.source_b
  56.9 2.3 %middle_level.1 = (f32[8,16,256]{2,1,0:T(8,128)S(1)}, f32[4,24,128]{2,1,0:T(8,128)S(1)}, f32[4,24,128]{2,1,0:T(8,128)S(1)}, f32[9,24,128]{2,1,0:T(8,128)S(1)}, f32[9,24,128]{2,1,0:T(8,128)S(1)}) custom-call(f32[10,48,256]{2,1,0:T(8,128)S(1)} %get-tuple-element.71.s, f32[6,48,256]{2,1,0:T(8,128)S(1)} %collective-permute-done.8.source_a, ...), custom_call_target="tpu_custom_call" | custom-call | tf_op jit(solution)/shard_map/middle_level/pallas_call | solution.py:601
  59.1 3.6 %collective-permute-start.12 = (f32[9,24,128]{2,1,0:T(8,128)S(1)}, f32[9,24,128]{2,1,0:T(8,128)S(1)}, u32[]{:S(2)}, u32[]{:S(2)}) collective-permute-start(f32[9,24,128]{2,1,0:T(8,128)S(1)} %get-tuple-element.86), channel_id=1, source_target_pairs={{4,8},{12,16},{20,24},{8,4},{16,12},{24,20},{5,9},{13,17},{21,25},... | collective-permute-start | bytes 331784 | tf_op jit(solution)/shard_map/ppermute | solution.py:621
  62.8 0.1 collective-permute-start.13
  62.9 1.0 %copy.6 = f32[16,32,512]{2,1,0:T(8,128)} copy(f32[16,32,512]{2,1,0:T(8,128)S(1)} %get-tuple-element.90) | data formatting | bytes 2097152
  63.8 0.7 copy.7
  64.5 0.7 %collective-permute-done.12.from_a = f32[9,24,128]{2,1,0:T(8,128)S(1)} collective-permute-done((f32[9,24,128]{2,1,0:T(8,128)S(1)}, f32[9,24,128]{2,1,0:T(8,128)S(1)}, u32[]{:S(2)}, u32[]{:S(2)}) %collective-permute-start.12) | collective-permute-done | bytes 110624 | tf_op jit(solution)/shard_map/ppermute | solution.py:621
  65.2 0.0 collective-permute-done.13.from_b
  65.2 1.0 %coarse_level.1 = (f32[4,8,128]{2,1,0:T(8,128)}, f32[4,8,128]{2,1,0:T(8,128)}) custom-call(f32[4,24,128]{2,1,0:T(8,128)S(1)} %get-tuple-element.84.s, f32[4,24,128]{2,1,0:T(8,128)S(1)} %get-tuple-element.85.k, f32[9,24,128]{2,1,0:T(8,128)S(1)} %collective-permute-done.12.from_a, f32[9,24,128]{2,1,0:T(8,128)S(1)} %collective-permute-done.13.from_b), custom_call_target="tpu_custom_call" | custom-call | tf_op jit(solution)/shard_map/coarse_level/pallas_call | solution.py:601
Async XLA Ops:
  0.6 6.8 %copy-start = (f32[16,32,512]{2,1,0:T(8,128)S(1)}, f32[16,32,512]{2,1,0:T(8,128)}, u32[]{:S(2)}) copy-start(f32[16,32,512]{2,1,0:T(8,128)} %k.5) | copy-start | bytes 3145732
  2.0 16.6 %copy-start.1 = (f32[16,32,512]{2,1,0:T(8,128)S(1)}, f32[16,32,512]{2,1,0:T(8,128)}, u32[]{:S(2)}) copy-start(f32[16,32,512]{2,1,0:T(8,128)} %s.3) | copy-start | bytes 3145732
  2.0 6.3 %collective-permute-start = (f32[2,8,8,512]{3,2,1,0:T(8,128)S(1)}, f32[2,8,8,512]{3,2,1,0:T(8,128)S(1)}, u32[]{:S(2)}, u32[]{:S(2)}) collective-permute-start(f32[2,8,8,512]{3,2,1,0:T(8,128)S(1)} %get-tuple-element.47), channel_id=1, source_target_pairs={{1,2},{2,1},{5,6},{6,5},{9,10},{10,9},{13,14},{14,13},{17,18},{18,... | collective-permute-start | bytes 786440 | tf_op jit(solution)/shard_map/ppermute | solution.py:621
  2.8 15.8 %collective-permute-start.1 = (f32[2,8,8,512]{3,2,1,0:T(8,128)S(1)}, f32[2,8,8,512]{3,2,1,0:T(8,128)S(1)}, u32[]{:S(2)}, u32[]{:S(2)}) collective-permute-start(f32[2,8,8,512]{3,2,1,0:T(8,128)S(1)} %get-tuple-element.48), channel_id=1, source_target_pairs={{0,1},{2,3},{1,0},{3,2},{4,5},{6,7},{5,4},{7,6},{8,9},{10,11},{9,8... | collective-permute-start | bytes 786440 | tf_op jit(solution)/shard_map/ppermute | solution.py:621
  18.8 13.8 %collective-permute-start.2 = (f32[9,40,512]{2,1,0:T(8,128)S(1)}, f32[9,40,512]{2,1,0:T(8,128)S(1)}, u32[]{:S(2)}, u32[]{:S(2)}) collective-permute-start(f32[9,40,512]{2,1,0:T(8,128)S(1)} %get-tuple-element.51), channel_id=1, source_target_pairs={{4,8},{12,16},{20,24},{8,4},{16,12},{24,20},{5,9},{13,17},{21,25},... | collective-permute-start | bytes 2211848 | tf_op jit(solution)/shard_map/ppermute | solution.py:621
  23.4 9.1 %collective-permute-start.3 = (f32[9,40,512]{2,1,0:T(8,128)S(1)}, f32[9,40,512]{2,1,0:T(8,128)S(1)}, u32[]{:S(2)}, u32[]{:S(2)}) collective-permute-start(f32[9,40,512]{2,1,0:T(8,128)S(1)} %get-tuple-element.52), channel_id=1, source_target_pairs={{0,4},{8,12},{16,20},{24,28},{4,0},{12,8},{20,16},{28,24},{1,5},{9... | collective-permute-start | bytes 2211848 | tf_op jit(solution)/shard_map/ppermute | solution.py:621
  26.1 12.0 %collective-permute-start.5 = (f32[8,16,256]{2,1,0:T(8,128)S(1)}, f32[8,16,256]{2,1,0:T(8,128)S(1)}, u32[]{:S(2)}, u32[]{:S(2)}) collective-permute-start(f32[8,16,256]{2,1,0:T(8,128)S(1)} %mean.1.own_rows), channel_id=1, source_target_pairs={{0,1},{2,3},{1,0},{3,2},{4,5},{6,7},{5,4},{7,6},{8,9},{10,11},{9,8... | collective-permute-start | bytes 393224 | tf_op jit(solution)/shard_map/ppermute | solution.py:621
  26.2 12.0 %collective-permute-start.4 = (f32[8,16,256]{2,1,0:T(8,128)S(1)}, f32[8,16,256]{2,1,0:T(8,128)S(1)}, u32[]{:S(2)}, u32[]{:S(2)}) collective-permute-start(f32[8,16,256]{2,1,0:T(8,128)S(1)} %mean.1.own_rows), channel_id=1, source_target_pairs={{1,2},{2,1},{5,6},{6,5},{9,10},{10,9},{13,14},{14,13},{17,18},{18,... | collective-permute-start | bytes 393224 | tf_op jit(solution)/shard_map/ppermute | solution.py:621
  38.2 6.8 %collective-permute-start.6 = (f32[10,16,256]{2,1,0:T(8,128)S(1)}, f32[10,16,256]{2,1,0:T(8,128)S(1)}, u32[]{:S(2)}, u32[]{:S(2)}) collective-permute-start(f32[10,16,256]{2,1,0:T(8,128)S(1)} %get-tuple-element.69.sent_a), channel_id=1, source_target_pairs={{1,2},{2,1},{5,6},{6,5},{9,10},{10,9},{13,14},{14,13},{17,18},{18,... | collective-permute-start | bytes 491528 | tf_op jit(solution)/shard_map/ppermute | solution.py:621
  38.8 9.4 %collective-permute-start.7 = (f32[10,16,256]{2,1,0:T(8,128)S(1)}, f32[10,16,256]{2,1,0:T(8,128)S(1)}, u32[]{:S(2)}, u32[]{:S(2)}) collective-permute-start(f32[10,16,256]{2,1,0:T(8,128)S(1)} %get-tuple-element.70.sent_b), channel_id=1, source_target_pairs={{0,1},{2,3},{1,0},{3,2},{4,5},{6,7},{5,4},{7,6},{8,9},{10,11},{9,8... | collective-permute-start | bytes 491528 | tf_op jit(solution)/shard_map/ppermute | solution.py:621
  40.6 12.1 %collective-permute-start.10 = (f32[6,48,256]{2,1,0:T(8,128)S(1)}, f32[6,48,256]{2,1,0:T(8,128)S(1)}, u32[]{:S(2)}, u32[]{:S(2)}) collective-permute-start(f32[6,48,256]{2,1,0:T(8,128)S(1)} %get-tuple-element.77), channel_id=1, source_target_pairs={{4,8},{12,16},{20,24},{8,4},{16,12},{24,20},{5,9},{13,17},{21,25},... | collective-permute-start | bytes 884744 | tf_op jit(solution)/shard_map/ppermute | solution.py:621
  44.8 7.9 %collective-permute-start.11 = (f32[6,48,256]{2,1,0:T(8,128)S(1)}, f32[6,48,256]{2,1,0:T(8,128)S(1)}, u32[]{:S(2)}, u32[]{:S(2)}) collective-permute-start(f32[6,48,256]{2,1,0:T(8,128)S(1)} %get-tuple-element.78), channel_id=1, source_target_pairs={{0,4},{8,12},{16,20},{24,28},{4,0},{12,8},{20,16},{28,24},{1,5},{9... | collective-permute-start | bytes 884744 | tf_op jit(solution)/shard_map/ppermute | solution.py:621
  48.3 8.5 %collective-permute-start.8 = (f32[6,48,256]{2,1,0:T(8,128)S(1)}, f32[6,48,256]{2,1,0:T(8,128)S(1)}, u32[]{:S(2)}, u32[]{:S(2)}) collective-permute-start(f32[6,48,256]{2,1,0:T(8,128)S(1)} %get-tuple-element.72), channel_id=1, source_target_pairs={{4,8},{12,16},{20,24},{8,4},{16,12},{24,20},{5,9},{13,17},{21,25},... | collective-permute-start | bytes 884744 | tf_op jit(solution)/shard_map/ppermute | solution.py:621
  52.7 4.2 %collective-permute-start.9 = (f32[6,48,256]{2,1,0:T(8,128)S(1)}, f32[6,48,256]{2,1,0:T(8,128)S(1)}, u32[]{:S(2)}, u32[]{:S(2)}) collective-permute-start(f32[6,48,256]{2,1,0:T(8,128)S(1)} %get-tuple-element.73), channel_id=1, source_target_pairs={{0,4},{8,12},{16,20},{24,28},{4,0},{12,8},{20,16},{28,24},{1,5},{9... | collective-permute-start | bytes 884744 | tf_op jit(solution)/shard_map/ppermute | solution.py:621
  59.1 6.1 %collective-permute-start.12 = (f32[9,24,128]{2,1,0:T(8,128)S(1)}, f32[9,24,128]{2,1,0:T(8,128)S(1)}, u32[]{:S(2)}, u32[]{:S(2)}) collective-permute-start(f32[9,24,128]{2,1,0:T(8,128)S(1)} %get-tuple-element.86), channel_id=1, source_target_pairs={{4,8},{12,16},{20,24},{8,4},{16,12},{24,20},{5,9},{13,17},{21,25},... | collective-permute-start | bytes 331784 | tf_op jit(solution)/shard_map/ppermute | solution.py:621
  62.8 2.4 %collective-permute-start.13 = (f32[9,24,128]{2,1,0:T(8,128)S(1)}, f32[9,24,128]{2,1,0:T(8,128)S(1)}, u32[]{:S(2)}, u32[]{:S(2)}) collective-permute-start(f32[9,24,128]{2,1,0:T(8,128)S(1)} %get-tuple-element.87), channel_id=1, source_target_pairs={{0,4},{8,12},{16,20},{24,28},{4,0},{12,8},{20,16},{28,24},{1,5},{9... | collective-permute-start | bytes 331784 | tf_op jit(solution)/shard_map/ppermute | solution.py:621

commit v7 on v6

--- a/solution.py
+++ b/solution.py
@@ -255,51 +255,73 @@
     return pick((m == i) | (m == i + 1), 0.125, 0.0).astype(F32)
 
 
-def pack_rows_kernel(s_low, s_high, k_low, k_high, to_a, to_b):
-    lanes = s_low.shape[2]
+def pack_rows_kernel(s_low, s_high, k_low, k_high, end_a, end_b, inner_a, inner_b):
+    planes, _, lanes = s_low.shape
+    own = planes // 2
     even = even_mask(8, lanes)
-    send = Send(to_a, to_b, "inner")
+    ends, inner = Send(end_a, end_b, "inner"), Send(inner_a, inner_b, "inner")
     cat = lambda *parts: jnp.concatenate(parts, axis=0)
 
-    def step(p, carry):
+    for p in range(own):
         def pair(ref):
             a, b = ref[2 * p], ref[2 * p + 1]
             return pick(even, a, b), pick(even, b, a)
 
         ls, lk, hs, hk = pair(s_low), pair(k_low), pair(s_high), pair(k_high)
-        send.put((0, p), cat(lk[0][0:4], ls[0][0:4]), cat(hk[0][4:8], hs[0][4:8]))
-        send.put((1, p), cat(lk[1][0:5], ls[1][0:3]), cat(hk[1][3:8], hs[1][5:8]))
-        return carry
-
-    lax.fori_loop(0, s_low.shape[0] // 2, step, 0, unroll=True)
+        send, at = (inner, p - 2) if 2 <= p < own - 2 else (ends, p if p < 2 else p - own + 4)
+        send.put((0, at), cat(lk[0][0:4], ls[0][0:4]), cat(hk[0][4:8], hs[0][4:8]))
+        send.put((1, at), cat(lk[1][0:5], ls[1][0:3]), cat(hk[1][3:8], hs[1][5:8]))
+
+
+def rows_from(got, p, own):
+    ends, inner = got
+    if 2 <= p < own - 2:
+        return inner[0, p - 2], inner[1, p - 2]
+    at = p if p < 2 else p - own + 4
+    return ends[0, at], ends[1, at]
+
+
+def between(row, first, last):
+    return (row >= first) & (row <= last)
 
 
 def pack_planes_kernel(s, k, from_a, from_b, to_a, to_b):
     planes, rows, lanes = s.shape
+    own = planes // 2
     even = even_mask(8, lanes)
-    from_low, from_high = got_pair(from_a, from_b, "inner")
+    even_own = even_mask(rows, lanes)
+    row = row_index(lanes)
+    low, high = got_pair(from_a, from_b, "inner")
     send = Send(to_a, to_b, "outer")
 
-    def edges(p, of_k):
-        lr, lb = from_low[0, p], from_low[1, p]
-        hr, hb = from_high[0, p], from_high[1, p]
+    def edges(plane, of_k):
+        lr, lb = rows_from((low, None), plane // 2, own)
+        hr, hb = rows_from((high, None), plane // 2, own)
         if of_k:
             red = jnp.concatenate([lr[0:4], hr[0:4]], axis=0)
             black = jnp.concatenate([lb[1:5], hb[0:4]], axis=0)
         else:
             red = jnp.concatenate([lr[4:8], hr[4:8]], axis=0)
             black = jnp.concatenate([lb[4:8], hb[5:8], hb[7:8]], axis=0)
-        return pick(even, red, black), pick(even, black, red)
-
-    def put(at, ref, down, up, of_k):
-        send.put((at, slice(0, rows)), ref[down], ref[up])
-        send.put((at, slice(rows, rows + 8)),
-                 edges(down // 2, of_k)[down % 2], edges(up // 2, of_k)[up % 2])
-
+        return (pick(even, red, black), pick(even, black, red))[plane % 2]
+
+    def corners(plane):
+        tiles = []
+        for d in (1, 2, 3):
+            source = edges(plane(d), False)
+            mean = pltpu.roll(edges(plane(5 - d), True), 4, 0)
+            tiles.append(pick(between(row, d, 7 - d), source, mean))
+        return tiles + [edges(plane(1), True)]
+
+    for j in range(3):
+        send.put(j, s[j], s[planes - 3 + j])
     for j in range(4):
-        put(j, s, j, planes - 4 + j, False)
-    for j in range(5):
-        put(4 + j, k, j, planes - 5 + j, True)
+        send.put(3 + j, k[j], k[planes - 4 + j])
+    send.put(7, pick(even_own, pltpu.roll(k[4], 1, 1), s[3]),
+             pick(even_own, s[planes - 4], pltpu.roll(k[planes - 5], 1, 1)))
+    down, up = corners(lambda d: d - 1), corners(lambda d: planes - d)
+    for i in range(4):
+        send.put((8, slice(8 * i, 8 * i + 8)), down[i], up[i])
 
 
 def mean_kernel(k, out, Z):
@@ -312,19 +334,19 @@
         out[q] = mean[half * q : half * (q + 1)]
 
 
-def fine_prepare_kernel(s, k, row_a, row_b, *arrays):
+def fine_prepare_kernel(s, k, end_a, end_b, inner_a, inner_b, *arrays):
     planes, rows, lanes = s.shape
     own = planes // 2
     wide = rows + 16
-    from_low, from_high = got_pair(row_a, row_b, "inner")
+    from_low, from_high = zip(got_pair(end_a, end_b, "inner"), got_pair(inner_a, inner_b, "inner"))
     even_own = even_mask(rows, lanes)
     row = row_index(lanes)
     K, S, U, W, D = [Store(ref, HP) for ref in arrays]
 
     def fill(p):
         at = HP + p
-        lr, lb = from_low[0, p], from_low[1, p]
-        hr, hb = from_high[0, p], from_high[1, p]
+        lr, lb = rows_from(from_low, p, own)
+        hr, hb = rows_from(from_high, p, own)
         K[0, at, 0:8] = pick(row >= 4, pltpu.roll(lr, 4, 0), 0.0)
         K[1, at, 0:8] = pick(row >= 3, pltpu.roll(lb, 3, 0), 0.0)
         S[0, at, 0:8] = pick(row >= 4, lr, 0.0)
@@ -354,11 +376,9 @@
     planes, rows, lanes = field.shape
     own = planes // 2
     wide = rows + 16
-    even = even_mask(8, lanes)
+    even = even_mask(wide, lanes)
     even_own = even_mask(rows, lanes)
     row = row_index(lanes)
-    zero8 = jnp.zeros((8, lanes), F32)
-
     def store(ref, early, firsts, pairs):
         return Store(ref, 0, Store(early, HP), [(i, p) for i in firsts for p in pairs])
 
@@ -370,35 +390,47 @@
     U = store(U1, U0, (0,), inside)
     U.early.update({(1, p): Store(U0, HP) for p in inner_span(own, 2)})
 
-    def halo(to, at, ref, first, second):
-        def part(rows_of):
-            a = zero8 if first is None else rows_of(first)
-            b = zero8 if second is None else rows_of(second)
-            return a, b
-
-        def put(start, a, b, mask):
-            to[0, at, start : start + a.shape[0]] = pick(mask, a, b)
-            to[1, at, start : start + a.shape[0]] = pick(mask, b, a)
-
-        a, b = part(lambda j: pick(row >= 4, pltpu.roll(ref[j, rows : rows + 8], 4, 0), 0.0))
-        put(0, a, b, even)
-        a, b = part(lambda j: pick(row < 4, pltpu.roll(ref[j, rows : rows + 8], 4, 0), 0.0))
-        put(8 + rows, a, b, even)
-        big = jnp.zeros((rows, lanes), F32)
-        a = big if first is None else ref[first, 0:rows]
-        b = big if second is None else ref[second, 0:rows]
-        put(8, a, b, even_own)
-
-    halo(S, 1, from_down, 0, 1)
-    halo(S, 2, from_down, 2, 3)
-    halo(K, 0, from_down, None, 4)
-    halo(K, 1, from_down, 5, 6)
-    halo(K, 2, from_down, 7, 8)
-    halo(S, HP + own, from_up, 0, 1)
-    halo(S, HP + own + 1, from_up, 2, 3)
-    halo(K, HP + own, from_up, 4, 5)
-    halo(K, HP + own + 1, from_up, 6, 7)
-    halo(K, HP + own + 2, from_up, 8, None)
+    def framed(low_edge, middle, high_edge):
+        return jnp.concatenate(
+            [pick(row >= 4, low_edge, 0.0), middle, pick(row < 4, high_edge, 0.0)], axis=0)
+
+    def source_at(got, d, up):
+        if d == 4:
+            mixed = got[7]
+            middle = pick(even_own, 0.0, mixed) if up else pick(even_own, mixed, 0.0)
+            edge = jnp.zeros((8, lanes), F32)
+        else:
+            middle = got[d - 1 if up else 3 - d]
+            edge = pick(between(row, d, 7 - d), got[8, 8 * d - 8 : 8 * d], 0.0)
+            edge = pltpu.roll(edge, 4, 0)
+        return framed(edge, middle, edge)
+
+    def mean_at(got, d, up):
+        edge = jnp.zeros((8, lanes), F32)
+        if d == 6:
+            return jnp.zeros((wide, lanes), F32)
+        if d == 5:
+            mixed = pltpu.roll(got[7], lanes - 1, 1)
+            middle = pick(even_own, 0.0, mixed) if up else pick(even_own, mixed, 0.0)
+        else:
+            middle = got[2 + d if up else 7 - d]
+            if d == 1:
+                edge = pltpu.roll(got[8, 24:32], 4, 0)
+            else:
+                edge = pick(between(row, 5 - d, 2 + d), 0.0, got[8, 8 * (4 - d) : 8 * (5 - d)])
+        return framed(edge, middle, edge)
+
+    for j in range(HP):
+        for to, plane in ((K, mean_at), (S, source_at)):
+            if to is S and j == 2:
+                continue
+            near, far = 2 * j + 1, 2 * j + 2
+            a, b = plane(from_up, near, True), plane(from_up, far, True)
+            to[0, HP + own + j] = pick(even, a, b)
+            to[1, HP + own + j] = pick(even, b, a)
+            a, b = plane(from_down, far, False), plane(from_down, near, False)
+            to[0, HP - 1 - j] = pick(even, a, b)
+            to[1, HP - 1 - j] = pick(even, b, a)
     level = Level(K, S, U, W, D, own, (wide, lanes))
     for colour in (0, 1):
         level.setup(colour, without(span(own, 4 - colour), inner_span(own, 1)))
@@ -588,7 +620,7 @@
     return 4 * words + (12 << 20)
 
 
-def call(kernel, outs, scratch, *args, in_specs=None, name=None, results=False):
+def call(kernel, outs, scratch, *args, in_specs=None, name=None, results=False, cost=None):
     extra = {}
     if in_specs is None:
         args = [pltpu.with_memory_space_constraint(a, pltpu.VMEM) for a in args]
@@ -604,6 +636,7 @@
         scratch_shapes=[pltpu.VMEM(shape, F32) for shape in scratch],
         compiler_params=pltpu.CompilerParams(vmem_limit_bytes=limit(scratch)),
         name=name,
+        cost_estimate=cost,
         **extra,
     )(*args)
 
@@ -631,20 +664,22 @@
 
     low = pl.BlockSpec((planes, 8, lanes), lambda i: (0, 0, 0))
     high = pl.BlockSpec((planes, 8, lanes), lambda i: (0, rows // 8 - 1, 0))
-    message = (2, own, 8, lanes)
-    sent = call(pack_rows_kernel, [message] * 2, [], s, s, k, k,
-                in_specs=[low, high, low, high], name="pack_rows")
-    row_halo = exchange(*sent, "inner")
+    ends, inner = (2, 4, 8, lanes), (2, own - 4, 8, lanes)
+    end_a, end_b, inner_a, inner_b = call(
+        pack_rows_kernel, [ends, ends, inner, inner], [], s, s, k, k,
+        in_specs=[low, high, low, high], name="pack_rows")
+    end_halo = exchange(end_a, end_b, "inner")
+    inner_halo = exchange(inner_a, inner_b, "inner")
     half, next_lanes = rows // 2, lanes // 2
     (mean,) = call(mean_kernel, [(own, half, next_lanes)], [(half * own, lanes)], k, name="mean")
-    message = (9, rows + 8, lanes)
-    to_a, to_b = call(pack_planes_kernel, [message] * 2, [], s, k, *row_halo, name="pack_planes")
+    message = (9, rows, lanes)
+    to_a, to_b = call(pack_planes_kernel, [message] * 2, [], s, k, *end_halo, name="pack_planes")
     mean, to_a, to_b = lax.optimization_barrier((mean, to_a, to_b))
     plane_halo = exchange(to_a, to_b, "outer")
     arrays = level_arrays(own, wide, lanes)
     early = [(a[0], own, wide, lanes) for a in arrays]
-    prepared = call(fine_prepare_kernel, early, [], s, k, *row_halo, name="fine_prepare")
-    mean, *prepared = lax.optimization_barrier((mean, *prepared))
+    prepared = call(fine_prepare_kernel, early, [], s, k, *end_halo, *inner_halo,
+                    name="fine_prepare", cost=pl.CostEstimate(0, 100 << 20, 0))
     mean_halo = exchange(mean, mean, "inner")
 
     count = own + 2

time: 66.5 us -> 62.9 us (0.946)
  waiting for transfers between devices: 22.9 us -> 10 us
  starting transfers between devices: 25.6 us -> 34.7 us
    ppermute x14 -> x16, waiting for transfers between devices: 22.9 us -> 10 us  [swapped(): return lax.ppermute(x, axis, pairs + [(j, i) for i, j in pairs])]
    ppermute x14 -> x16, starting transfers between devices: 25.6 us -> 34.7 us  [swapped(): return lax.ppermute(x, axis, pairs + [(j, i) for i, j in pairs])]
  transfers between devices with their start and end apart: 14 -> 16, of which waited for: 5 -> 4; matrix products, arithmetic and copies ran while one was open for 2% -> 3% of each run, Pallas kernels for 16% -> 17%
where the time goes in v7:
time: 62.9 us; the launch traced here: 62.6 us
  starting transfers between devices  34.7 us (55%)
  Pallas kernels  15.3 us (24%)
  waiting for transfers between devices  10 us (16%)
  local copies, waits for them, and re-layouts  1.64 us (3%)
  between operations  0.89 us (1%)
    ppermute x16, starting transfers between devices, swapped(): return lax.ppermute(x, axis, pairs + [(j, i) for i, j in pairs])  34.7 us
    pallas_call x10, Pallas kernels, call(): pl.pallas_call(kernel, out_shape=[jax.ShapeDtypeStruct(o, F32) if results...  15.3 us
    ppermute x16, waiting for transfers between devices, swapped(): return lax.ppermute(x, axis, pairs + [(j, i) for i, j in pairs])  10 us
    unnamed x6, local copies, waits for them, and re-layouts  1.64 us
  transfers between devices with their start and end apart: 16, of which 4 were waited for; matrix products, arithmetic and copies ran while one was open for 3% of the time, Pallas kernels for 17%

profile of v7, /device:TPU:1, one launch (start us, length us, event | category | flops | bytes accessed | tf_op | source)
XLA Modules:
  0.0 62.6 jit_solution(11596637573774829927)
XLA Ops:
  0.6 0.0 copy-start
  0.6 1.4 %pack_rows.1 = (f32[2,4,8,512]{3,2,1,0:T(8,128)S(1)}, f32[2,4,8,512]{3,2,1,0:T(8,128)S(1)}, f32[2,4,8,512]{3,2,1,0:T(8,128)S(1)}, f32[2,4,8,512]{3,2,1,0:T(8,128)S(1)}) custom-call(f32[16,32,512]{2,1,0:T(8,128)} %s.3, f32[16,32,512]{2,1,0:T(8,128)} %s.3, f32[16,32,512]{2,1,0:T(8,128)} %k.5, f32[16,32,512]{2,1,0:T(8,128)} %k.5), custom_call_target="tpu_custom_call" | custom-call | tf_op jit(solution)/shard_map/pack_rows/pallas_call | solution.py:633
  2.0 0.0 copy-start.1
  2.0 0.8 %collective-permute-start = (f32[2,4,8,512]{3,2,1,0:T(8,128)S(1)}, f32[2,4,8,512]{3,2,1,0:T(8,128)S(1)}, u32[]{:S(2)}, u32[]{:S(2)}) collective-permute-start(f32[2,4,8,512]{3,2,1,0:T(8,128)S(1)} %get-tuple-element.43), channel_id=1, source_target_pairs={{1,2},{2,1},{5,6},{6,5},{9,10},{10,9},{13,14},{14,13},{17,18},{18,... | collective-permute-start | bytes 393224 | tf_op jit(solution)/shard_map/ppermute | solution.py:654
  2.8 4.5 %collective-permute-start.1 = (f32[2,4,8,512]{3,2,1,0:T(8,128)S(1)}, f32[2,4,8,512]{3,2,1,0:T(8,128)S(1)}, u32[]{:S(2)}, u32[]{:S(2)}) collective-permute-start(f32[2,4,8,512]{3,2,1,0:T(8,128)S(1)} %get-tuple-element.44), channel_id=1, source_target_pairs={{0,1},{2,3},{1,0},{3,2},{4,5},{6,7},{5,4},{7,6},{8,9},{10,11},{9,8... | collective-permute-start | bytes 393224 | tf_op jit(solution)/shard_map/ppermute | solution.py:654
  7.4 0.0 copy-done
  7.4 1.0 %mean.1.own_rows = f32[8,16,256]{2,1,0:T(8,128)S(1)} custom-call(f32[16,32,512]{2,1,0:T(8,128)S(1)} %copy-done), custom_call_target="tpu_custom_call" | custom-call | tf_op jit(solution)/shard_map/mean/pallas_call | solution.py:633
  8.3 0.0 collective-permute-done.from_a.end_a
  8.4 4.7 %collective-permute-done.1.from_b.end_b = f32[2,4,8,512]{3,2,1,0:T(8,128)S(1)} collective-permute-done((f32[2,4,8,512]{3,2,1,0:T(8,128)S(1)}, f32[2,4,8,512]{3,2,1,0:T(8,128)S(1)}, u32[]{:S(2)}, u32[]{:S(2)}) %collective-permute-start.1) | collective-permute-done | bytes 131104 | tf_op jit(solution)/shard_map/ppermute | solution.py:654
  13.0 0.0 copy-done.1
  13.0 0.1 pack_planes.1
  13.2 4.6 %collective-permute-start.2 = (f32[9,32,512]{2,1,0:T(8,128)S(1)}, f32[9,32,512]{2,1,0:T(8,128)S(1)}, u32[]{:S(2)}, u32[]{:S(2)}) collective-permute-start(f32[9,32,512]{2,1,0:T(8,128)S(1)} %get-tuple-element.47), channel_id=1, source_target_pairs={{4,8},{12,16},{20,24},{8,4},{16,12},{24,20},{5,9},{13,17},{21,25},... | collective-permute-start | bytes 1769480 | tf_op jit(solution)/shard_map/ppermute | solution.py:654
  17.8 0.1 collective-permute-start.3
  17.9 0.7 %collective-permute-start.4 = (f32[2,4,8,512]{3,2,1,0:T(8,128)S(1)}, f32[2,4,8,512]{3,2,1,0:T(8,128)S(1)}, u32[]{:S(2)}, u32[]{:S(2)}) collective-permute-start(f32[2,4,8,512]{3,2,1,0:T(8,128)S(1)} %get-tuple-element.49), channel_id=1, source_target_pairs={{1,2},{2,1},{5,6},{6,5},{9,10},{10,9},{13,14},{14,13},{17,18},{18,... | collective-permute-start | bytes 393224 | tf_op jit(solution)/shard_map/ppermute | solution.py:654
  18.6 2.0 %collective-permute-start.5 = (f32[2,4,8,512]{3,2,1,0:T(8,128)S(1)}, f32[2,4,8,512]{3,2,1,0:T(8,128)S(1)}, u32[]{:S(2)}, u32[]{:S(2)}) collective-permute-start(f32[2,4,8,512]{3,2,1,0:T(8,128)S(1)} %get-tuple-element.50), channel_id=1, source_target_pairs={{0,1},{2,3},{1,0},{3,2},{4,5},{6,7},{5,4},{7,6},{8,9},{10,11},{9,8... | collective-permute-start | bytes 393224 | tf_op jit(solution)/shard_map/ppermute | solution.py:654
  20.6 0.7 %collective-permute-start.6 = (f32[8,16,256]{2,1,0:T(8,128)S(1)}, f32[8,16,256]{2,1,0:T(8,128)S(1)}, u32[]{:S(2)}, u32[]{:S(2)}) collective-permute-start(f32[8,16,256]{2,1,0:T(8,128)S(1)} %mean.1.own_rows), channel_id=1, source_target_pairs={{1,2},{2,1},{5,6},{6,5},{9,10},{10,9},{13,14},{14,13},{17,18},{18,... | collective-permute-start | bytes 393224 | tf_op jit(solution)/shard_map/ppermute | solution.py:654
  21.2 0.0 collective-permute-done.4.inner_a
  21.2 3.5 %collective-permute-start.7 = (f32[8,16,256]{2,1,0:T(8,128)S(1)}, f32[8,16,256]{2,1,0:T(8,128)S(1)}, u32[]{:S(2)}, u32[]{:S(2)}) collective-permute-start(f32[8,16,256]{2,1,0:T(8,128)S(1)} %mean.1.own_rows), channel_id=1, source_target_pairs={{0,1},{2,3},{1,0},{3,2},{4,5},{6,7},{5,4},{7,6},{8,9},{10,11},{9,8... | collective-permute-start | bytes 393224 | tf_op jit(solution)/shard_map/ppermute | solution.py:654
  24.7 1.7 %collective-permute-done.5.inner_b = f32[2,4,8,512]{3,2,1,0:T(8,128)S(1)} collective-permute-done((f32[2,4,8,512]{3,2,1,0:T(8,128)S(1)}, f32[2,4,8,512]{3,2,1,0:T(8,128)S(1)}, u32[]{:S(2)}, u32[]{:S(2)}) %collective-permute-start.5) | collective-permute-done | bytes 131104 | tf_op jit(solution)/shard_map/ppermute | solution.py:654
  26.4 2.6 %fine_prepare.1 = (f32[2,8,48,512]{3,2,1,0:T(8,128)S(1)}, f32[2,8,48,512]{3,2,1,0:T(8,128)S(1)}, f32[2,8,48,512]{3,2,1,0:T(8,128)S(1)}, f32[12,8,48,512]{3,2,1,0:T(8,128)S(1)}, f32[2,8,48,512]{3,2,1,0:T(8,128)S(1)}) custom-call(f32[16,32,512]{2,1,0:T(8,128)S(1)} %copy-done.1, f32[16,32,512]{2,1,0:T(8,128)S(1)} %copy-done, ...), custom_call_target="tpu_custom_call" | custom-call | tf_op jit(solution)/shard_map/fine_prepare/pallas_call | solution.py:633
  29.0 0.0 collective-permute-done.2.plane_a
  29.0 0.0 collective-permute-done.3.plane_b
  29.0 5.6 %fine_level.1 = (f32[16,32,512]{2,1,0:T(8,128)S(1)}, f32[10,16,256]{2,1,0:T(8,128)S(1)}, f32[10,16,256]{2,1,0:T(8,128)S(1)}, f32[10,16,256]{2,1,0:T(8,128)S(1)}) custom-call(f32[9,32,512]{2,1,0:T(8,128)S(1)} %collective-permute-done.2.plane_a, f32[9,32,512]{2,1,0:T(8,128)S(1)} %collective-permute-done.3.plane_b, f32[2,8,48,512]{3,2,1,0:T(8,128)S(1)} %get-tuple-element.51.K0, ...), custom_call_target="tpu_custom_call" | custom-call | tf_op jit(solution)/shard_map/fine_level/pallas_call | solution.py:633
  34.6 0.0 collective-permute-done.6.from_a
  34.6 0.0 collective-permute-done.7.from_b
  34.6 0.7 %collective-permute-start.8 = (f32[10,16,256]{2,1,0:T(8,128)S(1)}, f32[10,16,256]{2,1,0:T(8,128)S(1)}, u32[]{:S(2)}, u32[]{:S(2)}) collective-permute-start(f32[10,16,256]{2,1,0:T(8,128)S(1)} %get-tuple-element.61.sent_a), channel_id=1, source_target_pairs={{1,2},{2,1},{5,6},{6,5},{9,10},{10,9},{13,14},{14,13},{17,18},{18,... | collective-permute-start | bytes 491528 | tf_op jit(solution)/shard_map/ppermute | solution.py:654
  35.3 1.7 %collective-permute-start.9 = (f32[10,16,256]{2,1,0:T(8,128)S(1)}, f32[10,16,256]{2,1,0:T(8,128)S(1)}, u32[]{:S(2)}, u32[]{:S(2)}) collective-permute-start(f32[10,16,256]{2,1,0:T(8,128)S(1)} %get-tuple-element.62.sent_b), channel_id=1, source_target_pairs={{0,1},{2,3},{1,0},{3,2},{4,5},{6,7},{5,4},{7,6},{8,9},{10,11},{9,8... | collective-permute-start | bytes 491528 | tf_op jit(solution)/shard_map/ppermute | solution.py:654
  37.0 0.1 mean_planes.1
  37.1 5.9 %collective-permute-start.12 = (f32[6,48,256]{2,1,0:T(8,128)S(1)}, f32[6,48,256]{2,1,0:T(8,128)S(1)}, u32[]{:S(2)}, u32[]{:S(2)}) collective-permute-start(f32[6,48,256]{2,1,0:T(8,128)S(1)} %get-tuple-element.69), channel_id=1, source_target_pairs={{4,8},{12,16},{20,24},{8,4},{16,12},{24,20},{5,9},{13,17},{21,25},... | collective-permute-start | bytes 884744 | tf_op jit(solution)/shard_map/ppermute | solution.py:654
  43.1 0.1 collective-permute-start.13
  43.1 0.0 collective-permute-done.8.from_a
  43.1 0.0 collective-permute-done.9.from_b
  43.2 0.1 source_planes.1
  43.3 5.7 %collective-permute-start.10 = (f32[6,48,256]{2,1,0:T(8,128)S(1)}, f32[6,48,256]{2,1,0:T(8,128)S(1)}, u32[]{:S(2)}, u32[]{:S(2)}) collective-permute-start(f32[6,48,256]{2,1,0:T(8,128)S(1)} %get-tuple-element.64), channel_id=1, source_target_pairs={{4,8},{12,16},{20,24},{8,4},{16,12},{24,20},{5,9},{13,17},{21,25},... | collective-permute-start | bytes 884744 | tf_op jit(solution)/shard_map/ppermute | solution.py:654
  49.0 0.1 collective-permute-start.11
  49.1 0.0 collective-permute-done.12.from_a
  49.1 0.0 collective-permute-done.13.from_b
  49.1 1.2 %middle_setup.1 = (f32[2,10,48,256]{3,2,1,0:T(8,128)S(1)}, f32[12,10,48,256]{3,2,1,0:T(8,128)S(1)}, f32[2,10,48,256]{3,2,1,0:T(8,128)S(1)}, f32[2,10,48,256]{3,2,1,0:T(8,128)S(1)}) custom-call(f32[8,48,256]{2,1,0:T(8,128)S(1)} %get-tuple-element.68.k, f32[6,48,256]{2,1,0:T(8,128)S(1)} %collective-permute-done.12.from_a, ...), custom_call_target="tpu_custom_call" | custom-call | tf_op jit(solution)/shard_map/middle_setup/pallas_call | solution.py:633
  50.2 2.9 %collective-permute-done.10.source_a = f32[6,48,256]{2,1,0:T(8,128)S(1)} collective-permute-done((f32[6,48,256]{2,1,0:T(8,128)S(1)}, f32[6,48,256]{2,1,0:T(8,128)S(1)}, u32[]{:S(2)}, u32[]{:S(2)}) %collective-permute-start.10) | collective-permute-done | bytes 294944 | tf_op jit(solution)/shard_map/ppermute | solution.py:654
  53.2 0.0 collective-permute-done.11.source_b
  53.2 2.3 %middle_level.1 = (f32[8,16,256]{2,1,0:T(8,128)S(1)}, f32[4,24,128]{2,1,0:T(8,128)S(1)}, f32[4,24,128]{2,1,0:T(8,128)S(1)}, f32[9,24,128]{2,1,0:T(8,128)S(1)}, f32[9,24,128]{2,1,0:T(8,128)S(1)}) custom-call(f32[10,48,256]{2,1,0:T(8,128)S(1)} %get-tuple-element.63.s, f32[6,48,256]{2,1,0:T(8,128)S(1)} %collective-permute-done.10.source_a, ...), custom_call_target="tpu_custom_call" | custom-call | tf_op jit(solution)/shard_map/middle_level/pallas_call | solution.py:633
  55.5 3.6 %collective-permute-start.14 = (f32[9,24,128]{2,1,0:T(8,128)S(1)}, f32[9,24,128]{2,1,0:T(8,128)S(1)}, u32[]{:S(2)}, u32[]{:S(2)}) collective-permute-start(f32[9,24,128]{2,1,0:T(8,128)S(1)} %get-tuple-element.78), channel_id=1, source_target_pairs={{4,8},{12,16},{20,24},{8,4},{16,12},{24,20},{5,9},{13,17},{21,25},... | collective-permute-start | bytes 331784 | tf_op jit(solution)/shard_map/ppermute | solution.py:654
  59.1 0.1 collective-permute-start.15
  59.2 1.0 %copy.6 = f32[16,32,512]{2,1,0:T(8,128)} copy(f32[16,32,512]{2,1,0:T(8,128)S(1)} %get-tuple-element.82) | data formatting | bytes 2097152
  60.2 0.7 %copy.7 = f32[8,16,256]{2,1,0:T(8,128)} copy(f32[8,16,256]{2,1,0:T(8,128)S(1)} %get-tuple-element.83) | data formatting | bytes 262144
  60.8 0.7 %collective-permute-done.14.from_a = f32[9,24,128]{2,1,0:T(8,128)S(1)} collective-permute-done((f32[9,24,128]{2,1,0:T(8,128)S(1)}, f32[9,24,128]{2,1,0:T(8,128)S(1)}, u32[]{:S(2)}, u32[]{:S(2)}) %collective-permute-start.14) | collective-permute-done | bytes 110624 | tf_op jit(solution)/shard_map/ppermute | solution.py:654
  61.5 0.0 collective-permute-done.15.from_b
  61.5 1.0 %coarse_level.1 = (f32[4,8,128]{2,1,0:T(8,128)}, f32[4,8,128]{2,1,0:T(8,128)}) custom-call(f32[4,24,128]{2,1,0:T(8,128)S(1)} %get-tuple-element.76.s, f32[4,24,128]{2,1,0:T(8,128)S(1)} %get-tuple-element.77.k, f32[9,24,128]{2,1,0:T(8,128)S(1)} %collective-permute-done.14.from_a, f32[9,24,128]{2,1,0:T(8,128)S(1)} %collective-permute-done.15.from_b), custom_call_target="tpu_custom_call" | custom-call | tf_op jit(solution)/shard_map/coarse_level/pallas_call | solution.py:633
Async XLA Ops:
  0.6 6.8 %copy-start = (f32[16,32,512]{2,1,0:T(8,128)S(1)}, f32[16,32,512]{2,1,0:T(8,128)}, u32[]{:S(2)}) copy-start(f32[16,32,512]{2,1,0:T(8,128)} %k.5) | copy-start | bytes 3145732
  2.0 11.0 %copy-start.1 = (f32[16,32,512]{2,1,0:T(8,128)S(1)}, f32[16,32,512]{2,1,0:T(8,128)}, u32[]{:S(2)}) copy-start(f32[16,32,512]{2,1,0:T(8,128)} %s.3) | copy-start | bytes 3145732
  2.0 6.3 %collective-permute-start = (f32[2,4,8,512]{3,2,1,0:T(8,128)S(1)}, f32[2,4,8,512]{3,2,1,0:T(8,128)S(1)}, u32[]{:S(2)}, u32[]{:S(2)}) collective-permute-start(f32[2,4,8,512]{3,2,1,0:T(8,128)S(1)} %get-tuple-element.43), channel_id=1, source_target_pairs={{1,2},{2,1},{5,6},{6,5},{9,10},{10,9},{13,14},{14,13},{17,18},{18,... | collective-permute-start | bytes 393224 | tf_op jit(solution)/shard_map/ppermute | solution.py:654
  2.8 10.2 %collective-permute-start.1 = (f32[2,4,8,512]{3,2,1,0:T(8,128)S(1)}, f32[2,4,8,512]{3,2,1,0:T(8,128)S(1)}, u32[]{:S(2)}, u32[]{:S(2)}) collective-permute-start(f32[2,4,8,512]{3,2,1,0:T(8,128)S(1)} %get-tuple-element.44), channel_id=1, source_target_pairs={{0,1},{2,3},{1,0},{3,2},{4,5},{6,7},{5,4},{7,6},{8,9},{10,11},{9,8... | collective-permute-start | bytes 393224 | tf_op jit(solution)/shard_map/ppermute | solution.py:654
  13.2 15.8 %collective-permute-start.2 = (f32[9,32,512]{2,1,0:T(8,128)S(1)}, f32[9,32,512]{2,1,0:T(8,128)S(1)}, u32[]{:S(2)}, u32[]{:S(2)}) collective-permute-start(f32[9,32,512]{2,1,0:T(8,128)S(1)} %get-tuple-element.47), channel_id=1, source_target_pairs={{4,8},{12,16},{20,24},{8,4},{16,12},{24,20},{5,9},{13,17},{21,25},... | collective-permute-start | bytes 1769480 | tf_op jit(solution)/shard_map/ppermute | solution.py:654
  17.8 11.2 %collective-permute-start.3 = (f32[9,32,512]{2,1,0:T(8,128)S(1)}, f32[9,32,512]{2,1,0:T(8,128)S(1)}, u32[]{:S(2)}, u32[]{:S(2)}) collective-permute-start(f32[9,32,512]{2,1,0:T(8,128)S(1)} %get-tuple-element.48), channel_id=1, source_target_pairs={{0,4},{8,12},{16,20},{24,28},{4,0},{12,8},{20,16},{28,24},{1,5},{9... | collective-permute-start | bytes 1769480 | tf_op jit(solution)/shard_map/ppermute | solution.py:654
  17.9 3.3 %collective-permute-start.4 = (f32[2,4,8,512]{3,2,1,0:T(8,128)S(1)}, f32[2,4,8,512]{3,2,1,0:T(8,128)S(1)}, u32[]{:S(2)}, u32[]{:S(2)}) collective-permute-start(f32[2,4,8,512]{3,2,1,0:T(8,128)S(1)} %get-tuple-element.49), channel_id=1, source_target_pairs={{1,2},{2,1},{5,6},{6,5},{9,10},{10,9},{13,14},{14,13},{17,18},{18,... | collective-permute-start | bytes 393224 | tf_op jit(solution)/shard_map/ppermute | solution.py:654
  18.6 7.8 %collective-permute-start.5 = (f32[2,4,8,512]{3,2,1,0:T(8,128)S(1)}, f32[2,4,8,512]{3,2,1,0:T(8,128)S(1)}, u32[]{:S(2)}, u32[]{:S(2)}) collective-permute-start(f32[2,4,8,512]{3,2,1,0:T(8,128)S(1)} %get-tuple-element.50), channel_id=1, source_target_pairs={{0,1},{2,3},{1,0},{3,2},{4,5},{6,7},{5,4},{7,6},{8,9},{10,11},{9,8... | collective-permute-start | bytes 393224 | tf_op jit(solution)/shard_map/ppermute | solution.py:654
  20.6 14.1 %collective-permute-start.6 = (f32[8,16,256]{2,1,0:T(8,128)S(1)}, f32[8,16,256]{2,1,0:T(8,128)S(1)}, u32[]{:S(2)}, u32[]{:S(2)}) collective-permute-start(f32[8,16,256]{2,1,0:T(8,128)S(1)} %mean.1.own_rows), channel_id=1, source_target_pairs={{1,2},{2,1},{5,6},{6,5},{9,10},{10,9},{13,14},{14,13},{17,18},{18,... | collective-permute-start | bytes 393224 | tf_op jit(solution)/shard_map/ppermute | solution.py:654
  21.2 13.4 %collective-permute-start.7 = (f32[8,16,256]{2,1,0:T(8,128)S(1)}, f32[8,16,256]{2,1,0:T(8,128)S(1)}, u32[]{:S(2)}, u32[]{:S(2)}) collective-permute-start(f32[8,16,256]{2,1,0:T(8,128)S(1)} %mean.1.own_rows), channel_id=1, source_target_pairs={{0,1},{2,3},{1,0},{3,2},{4,5},{6,7},{5,4},{7,6},{8,9},{10,11},{9,8... | collective-permute-start | bytes 393224 | tf_op jit(solution)/shard_map/ppermute | solution.py:654
  34.6 8.5 %collective-permute-start.8 = (f32[10,16,256]{2,1,0:T(8,128)S(1)}, f32[10,16,256]{2,1,0:T(8,128)S(1)}, u32[]{:S(2)}, u32[]{:S(2)}) collective-permute-start(f32[10,16,256]{2,1,0:T(8,128)S(1)} %get-tuple-element.61.sent_a), channel_id=1, source_target_pairs={{1,2},{2,1},{5,6},{6,5},{9,10},{10,9},{13,14},{14,13},{17,18},{18,... | collective-permute-start | bytes 491528 | tf_op jit(solution)/shard_map/ppermute | solution.py:654
  35.3 7.8 %collective-permute-start.9 = (f32[10,16,256]{2,1,0:T(8,128)S(1)}, f32[10,16,256]{2,1,0:T(8,128)S(1)}, u32[]{:S(2)}, u32[]{:S(2)}) collective-permute-start(f32[10,16,256]{2,1,0:T(8,128)S(1)} %get-tuple-element.62.sent_b), channel_id=1, source_target_pairs={{0,1},{2,3},{1,0},{3,2},{4,5},{6,7},{5,4},{7,6},{8,9},{10,11},{9,8... | collective-permute-start | bytes 491528 | tf_op jit(solution)/shard_map/ppermute | solution.py:654
  37.1 11.9 %collective-permute-start.12 = (f32[6,48,256]{2,1,0:T(8,128)S(1)}, f32[6,48,256]{2,1,0:T(8,128)S(1)}, u32[]{:S(2)}, u32[]{:S(2)}) collective-permute-start(f32[6,48,256]{2,1,0:T(8,128)S(1)} %get-tuple-element.69), channel_id=1, source_target_pairs={{4,8},{12,16},{20,24},{8,4},{16,12},{24,20},{5,9},{13,17},{21,25},... | collective-permute-start | bytes 884744 | tf_op jit(solution)/shard_map/ppermute | solution.py:654
  43.1 6.0 %collective-permute-start.13 = (f32[6,48,256]{2,1,0:T(8,128)S(1)}, f32[6,48,256]{2,1,0:T(8,128)S(1)}, u32[]{:S(2)}, u32[]{:S(2)}) collective-permute-start(f32[6,48,256]{2,1,0:T(8,128)S(1)} %get-tuple-element.70), channel_id=1, source_target_pairs={{0,4},{8,12},{16,20},{24,28},{4,0},{12,8},{20,16},{28,24},{1,5},{9... | collective-permute-start | bytes 884744 | tf_op jit(solution)/shard_map/ppermute | solution.py:654
  43.3 9.9 %collective-permute-start.10 = (f32[6,48,256]{2,1,0:T(8,128)S(1)}, f32[6,48,256]{2,1,0:T(8,128)S(1)}, u32[]{:S(2)}, u32[]{:S(2)}) collective-permute-start(f32[6,48,256]{2,1,0:T(8,128)S(1)} %get-tuple-element.64), channel_id=1, source_target_pairs={{4,8},{12,16},{20,24},{8,4},{16,12},{24,20},{5,9},{13,17},{21,25},... | collective-permute-start | bytes 884744 | tf_op jit(solution)/shard_map/ppermute | solution.py:654
  49.0 4.2 %collective-permute-start.11 = (f32[6,48,256]{2,1,0:T(8,128)S(1)}, f32[6,48,256]{2,1,0:T(8,128)S(1)}, u32[]{:S(2)}, u32[]{:S(2)}) collective-permute-start(f32[6,48,256]{2,1,0:T(8,128)S(1)} %get-tuple-element.65), channel_id=1, source_target_pairs={{0,4},{8,12},{16,20},{24,28},{4,0},{12,8},{20,16},{28,24},{1,5},{9... | collective-permute-start | bytes 884744 | tf_op jit(solution)/shard_map/ppermute | solution.py:654
  55.5 6.1 %collective-permute-start.14 = (f32[9,24,128]{2,1,0:T(8,128)S(1)}, f32[9,24,128]{2,1,0:T(8,128)S(1)}, u32[]{:S(2)}, u32[]{:S(2)}) collective-permute-start(f32[9,24,128]{2,1,0:T(8,128)S(1)} %get-tuple-element.78), channel_id=1, source_target_pairs={{4,8},{12,16},{20,24},{8,4},{16,12},{24,20},{5,9},{13,17},{21,25},... | collective-permute-start | bytes 331784 | tf_op jit(solution)/shard_map/ppermute | solution.py:654
  59.1 2.4 %collective-permute-start.15 = (f32[9,24,128]{2,1,0:T(8,128)S(1)}, f32[9,24,128]{2,1,0:T(8,128)S(1)}, u32[]{:S(2)}, u32[]{:S(2)}) collective-permute-start(f32[9,24,128]{2,1,0:T(8,128)S(1)} %get-tuple-element.79), channel_id=1, source_target_pairs={{0,4},{8,12},{16,20},{24,28},{4,0},{12,8},{20,16},{28,24},{1,5},{9... | collective-permute-start | bytes 331784 | tf_op jit(solution)/shard_map/ppermute | solution.py:654

commit v8 on v7

--- a/solution.py
+++ b/solution.py
@@ -7,7 +7,6 @@
 
 F32 = jnp.float32
 HP = 3
-HIGHEST = lax.Precision.HIGHEST
 
 
 def tiled(tile, rows, lanes):
@@ -226,19 +225,32 @@
     outer = (m == 2 * j - 1) | (m == 2 * j + 2)
     main = pick(inner, 0.375, pick(outer, 0.125, 0.0)).astype(F32)
     if not ends:
-        return main
+        return main.astype(jnp.bfloat16)
     edge = pick(((j == half) & (m == 0)) | ((j == half + 1) & (m == rows - 1)), 0.125, 0.0)
-    return pick(j < half, main, edge).astype(F32)
+    return pick(j < half, main, edge).astype(F32).astype(jnp.bfloat16)
 
 
 def row_sum(rows):
     j = 2 * lax.broadcasted_iota(jnp.int32, (rows // 2, rows), 0)
     m = lax.broadcasted_iota(jnp.int32, (rows // 2, rows), 1)
-    return pick((m == j) | (m == j + 1), 1.0, 0.0).astype(F32)
+    return pick((m == j) | (m == j + 1), 1.0, 0.0).astype(F32).astype(jnp.bfloat16)
+
+
+def split(x):
+    parts = []
+    for _ in range(3):
+        part = x.astype(jnp.bfloat16)
+        parts.append(part)
+        x = x - part.astype(F32)
+    return parts
 
 
 def product(a, b):
-    return jnp.dot(a, b, precision=HIGHEST, preferred_element_type=F32)
+    if a.dtype == jnp.bfloat16:
+        parts = [jnp.dot(a, part, preferred_element_type=F32) for part in split(b)]
+    else:
+        parts = [jnp.dot(part, b, preferred_element_type=F32) for part in split(a)]
+    return (parts[2] + parts[1]) + parts[0]
 
 
 def lane_restriction(lanes):
@@ -246,13 +258,13 @@
     i = 2 * lax.broadcasted_iota(jnp.int32, (lanes, lanes // 2), 1)
     inner = (m == i) | (m == i + 1)
     outer = (m == i - 1) | (m == i + 2)
-    return pick(inner, 1.5, pick(outer, 0.5, 0.0)).astype(F32)
+    return pick(inner, 1.5, pick(outer, 0.5, 0.0)).astype(F32).astype(jnp.bfloat16)
 
 
 def lane_mean(lanes):
     m = lax.broadcasted_iota(jnp.int32, (lanes, lanes // 2), 0)
     i = 2 * lax.broadcasted_iota(jnp.int32, (lanes, lanes // 2), 1)
-    return pick((m == i) | (m == i + 1), 0.125, 0.0).astype(F32)
+    return pick((m == i) | (m == i + 1), 0.125, 0.0).astype(F32).astype(jnp.bfloat16)
 
 
 def pack_rows_kernel(s_low, s_high, k_low, k_high, end_a, end_b, inner_a, inner_b):
@@ -620,7 +632,7 @@
     return 4 * words + (12 << 20)
 
 
-def call(kernel, outs, scratch, *args, in_specs=None, name=None, results=False, cost=None):
+def call(kernel, outs, scratch, *args, in_specs=None, name=None, results=False):
     extra = {}
     if in_specs is None:
         args = [pltpu.with_memory_space_constraint(a, pltpu.VMEM) for a in args]
@@ -636,7 +648,6 @@
         scratch_shapes=[pltpu.VMEM(shape, F32) for shape in scratch],
         compiler_params=pltpu.CompilerParams(vmem_limit_bytes=limit(scratch)),
         name=name,
-        cost_estimate=cost,
         **extra,
     )(*args)
 
@@ -679,7 +690,7 @@
     arrays = level_arrays(own, wide, lanes)
     early = [(a[0], own, wide, lanes) for a in arrays]
     prepared = call(fine_prepare_kernel, early, [], s, k, *end_halo, *inner_halo,
-                    name="fine_prepare", cost=pl.CostEstimate(0, 100 << 20, 0))
+                    name="fine_prepare")
     mean_halo = exchange(mean, mean, "inner")
 
     count = own + 2

time: 62.9 us -> 62.5 us (level)
  Pallas kernels: 15.3 us -> 14.5 us
    pallas_call x10, Pallas kernels: 15.3 us -> 14.5 us  [call(): pl.pallas_call(kernel, out_shape=[jax.ShapeDtypeStruct(o, F32) if results...]
  transfers between devices with their start and end apart: 16 -> 16, of which waited for: 4 -> 4; matrix products, arithmetic and copies ran while one was open for 3% -> 3% of each run, Pallas kernels for 17% -> 16%
where the time goes in v8:
time: 62.5 us; the launch traced here: 62.2 us
  starting transfers between devices  34.7 us (56%)
  Pallas kernels  14.5 us (23%)
  waiting for transfers between devices  10.4 us (17%)
  local copies, waits for them, and re-layouts  1.64 us (3%)
  between operations  0.89 us (1%)
    ppermute x16, starting transfers between devices, swapped(): return lax.ppermute(x, axis, pairs + [(j, i) for i, j in pairs])  34.7 us
    pallas_call x10, Pallas kernels, call(): pl.pallas_call(kernel, out_shape=[jax.ShapeDtypeStruct(o, F32) if results...  14.5 us
    ppermute x16, waiting for transfers between devices, swapped(): return lax.ppermute(x, axis, pairs + [(j, i) for i, j in pairs])  10.4 us
    unnamed x6, local copies, waits for them, and re-layouts  1.64 us
  transfers between devices with their start and end apart: 16, of which 4 were waited for; matrix products, arithmetic and copies ran while one was open for 3% of the time, Pallas kernels for 16%

profile of v8, /device:TPU:1, one launch (start us, length us, event | category | flops | bytes accessed | tf_op | source)
XLA Modules:
  0.0 62.2 jit_solution(12453290218466680934)
XLA Ops:
  0.6 0.0 copy-start
  0.6 1.4 %pack_rows.1 = (f32[2,4,8,512]{3,2,1,0:T(8,128)S(1)}, f32[2,4,8,512]{3,2,1,0:T(8,128)S(1)}, f32[2,4,8,512]{3,2,1,0:T(8,128)S(1)}, f32[2,4,8,512]{3,2,1,0:T(8,128)S(1)}) custom-call(f32[16,32,512]{2,1,0:T(8,128)} %s.3, f32[16,32,512]{2,1,0:T(8,128)} %s.3, f32[16,32,512]{2,1,0:T(8,128)} %k.5, f32[16,32,512]{2,1,0:T(8,128)} %k.5), custom_call_target="tpu_custom_call" | custom-call | tf_op jit(solution)/shard_map/pack_rows/pallas_call | solution.py:645
  2.0 0.0 copy-start.1
  2.0 0.8 %collective-permute-start = (f32[2,4,8,512]{3,2,1,0:T(8,128)S(1)}, f32[2,4,8,512]{3,2,1,0:T(8,128)S(1)}, u32[]{:S(2)}, u32[]{:S(2)}) collective-permute-start(f32[2,4,8,512]{3,2,1,0:T(8,128)S(1)} %get-tuple-element.43), channel_id=1, source_target_pairs={{1,2},{2,1},{5,6},{6,5},{9,10},{10,9},{13,14},{14,13},{17,18},{18,... | collective-permute-start | bytes 393224 | tf_op jit(solution)/shard_map/ppermute | solution.py:665
  2.8 4.5 %collective-permute-start.1 = (f32[2,4,8,512]{3,2,1,0:T(8,128)S(1)}, f32[2,4,8,512]{3,2,1,0:T(8,128)S(1)}, u32[]{:S(2)}, u32[]{:S(2)}) collective-permute-start(f32[2,4,8,512]{3,2,1,0:T(8,128)S(1)} %get-tuple-element.44), channel_id=1, source_target_pairs={{0,1},{2,3},{1,0},{3,2},{4,5},{6,7},{5,4},{7,6},{8,9},{10,11},{9,8... | collective-permute-start | bytes 393224 | tf_op jit(solution)/shard_map/ppermute | solution.py:665
  7.4 0.0 copy-done
  7.4 0.5 mean.1.own_rows
  7.9 0.0 collective-permute-done.from_a.end_a
  7.9 5.1 %collective-permute-done.1.from_b.end_b = f32[2,4,8,512]{3,2,1,0:T(8,128)S(1)} collective-permute-done((f32[2,4,8,512]{3,2,1,0:T(8,128)S(1)}, f32[2,4,8,512]{3,2,1,0:T(8,128)S(1)}, u32[]{:S(2)}, u32[]{:S(2)}) %collective-permute-start.1) | collective-permute-done | bytes 131104 | tf_op jit(solution)/shard_map/ppermute | solution.py:665
  13.0 0.0 copy-done.1
  13.0 0.1 pack_planes.1
  13.2 4.6 %collective-permute-start.2 = (f32[9,32,512]{2,1,0:T(8,128)S(1)}, f32[9,32,512]{2,1,0:T(8,128)S(1)}, u32[]{:S(2)}, u32[]{:S(2)}) collective-permute-start(f32[9,32,512]{2,1,0:T(8,128)S(1)} %get-tuple-element.47), channel_id=1, source_target_pairs={{4,8},{12,16},{20,24},{8,4},{16,12},{24,20},{5,9},{13,17},{21,25},... | collective-permute-start | bytes 1769480 | tf_op jit(solution)/shard_map/ppermute | solution.py:665
  17.8 0.1 collective-permute-start.3
  17.9 0.7 %collective-permute-start.4 = (f32[2,4,8,512]{3,2,1,0:T(8,128)S(1)}, f32[2,4,8,512]{3,2,1,0:T(8,128)S(1)}, u32[]{:S(2)}, u32[]{:S(2)}) collective-permute-start(f32[2,4,8,512]{3,2,1,0:T(8,128)S(1)} %get-tuple-element.49), channel_id=1, source_target_pairs={{1,2},{2,1},{5,6},{6,5},{9,10},{10,9},{13,14},{14,13},{17,18},{18,... | collective-permute-start | bytes 393224 | tf_op jit(solution)/shard_map/ppermute | solution.py:665
  18.6 2.0 %collective-permute-start.5 = (f32[2,4,8,512]{3,2,1,0:T(8,128)S(1)}, f32[2,4,8,512]{3,2,1,0:T(8,128)S(1)}, u32[]{:S(2)}, u32[]{:S(2)}) collective-permute-start(f32[2,4,8,512]{3,2,1,0:T(8,128)S(1)} %get-tuple-element.50), channel_id=1, source_target_pairs={{0,1},{2,3},{1,0},{3,2},{4,5},{6,7},{5,4},{7,6},{8,9},{10,11},{9,8... | collective-permute-start | bytes 393224 | tf_op jit(solution)/shard_map/ppermute | solution.py:665
  20.6 0.7 %collective-permute-start.6 = (f32[8,16,256]{2,1,0:T(8,128)S(1)}, f32[8,16,256]{2,1,0:T(8,128)S(1)}, u32[]{:S(2)}, u32[]{:S(2)}) collective-permute-start(f32[8,16,256]{2,1,0:T(8,128)S(1)} %mean.1.own_rows), channel_id=1, source_target_pairs={{1,2},{2,1},{5,6},{6,5},{9,10},{10,9},{13,14},{14,13},{17,18},{18,... | collective-permute-start | bytes 393224 | tf_op jit(solution)/shard_map/ppermute | solution.py:665
  21.2 0.0 collective-permute-done.4.inner_a
  21.2 3.5 %collective-permute-start.7 = (f32[8,16,256]{2,1,0:T(8,128)S(1)}, f32[8,16,256]{2,1,0:T(8,128)S(1)}, u32[]{:S(2)}, u32[]{:S(2)}) collective-permute-start(f32[8,16,256]{2,1,0:T(8,128)S(1)} %mean.1.own_rows), channel_id=1, source_target_pairs={{0,1},{2,3},{1,0},{3,2},{4,5},{6,7},{5,4},{7,6},{8,9},{10,11},{9,8... | collective-permute-start | bytes 393224 | tf_op jit(solution)/shard_map/ppermute | solution.py:665
  24.7 1.7 %collective-permute-done.5.inner_b = f32[2,4,8,512]{3,2,1,0:T(8,128)S(1)} collective-permute-done((f32[2,4,8,512]{3,2,1,0:T(8,128)S(1)}, f32[2,4,8,512]{3,2,1,0:T(8,128)S(1)}, u32[]{:S(2)}, u32[]{:S(2)}) %collective-permute-start.5) | collective-permute-done | bytes 131104 | tf_op jit(solution)/shard_map/ppermute | solution.py:665
  26.4 2.6 %fine_prepare.1 = (f32[2,8,48,512]{3,2,1,0:T(8,128)S(1)}, f32[2,8,48,512]{3,2,1,0:T(8,128)S(1)}, f32[2,8,48,512]{3,2,1,0:T(8,128)S(1)}, f32[12,8,48,512]{3,2,1,0:T(8,128)S(1)}, f32[2,8,48,512]{3,2,1,0:T(8,128)S(1)}) custom-call(f32[16,32,512]{2,1,0:T(8,128)S(1)} %copy-done.1, f32[16,32,512]{2,1,0:T(8,128)S(1)} %copy-done, ...), custom_call_target="tpu_custom_call" | custom-call | tf_op jit(solution)/shard_map/fine_prepare/pallas_call | solution.py:645
  29.0 0.0 collective-permute-done.2.plane_a
  29.0 0.0 collective-permute-done.3.plane_b
  29.0 5.3 %fine_level.1 = (f32[16,32,512]{2,1,0:T(8,128)S(1)}, f32[10,16,256]{2,1,0:T(8,128)S(1)}, f32[10,16,256]{2,1,0:T(8,128)S(1)}, f32[10,16,256]{2,1,0:T(8,128)S(1)}) custom-call(f32[9,32,512]{2,1,0:T(8,128)S(1)} %collective-permute-done.2.plane_a, f32[9,32,512]{2,1,0:T(8,128)S(1)} %collective-permute-done.3.plane_b, f32[2,8,48,512]{3,2,1,0:T(8,128)S(1)} %get-tuple-element.51.K0, ...), custom_call_target="tpu_custom_call" | custom-call | tf_op jit(solution)/shard_map/fine_level/pallas_call | solution.py:645
  34.3 0.0 collective-permute-done.6.from_a
  34.3 0.0 collective-permute-done.7.from_b
  34.3 0.7 %collective-permute-start.8 = (f32[10,16,256]{2,1,0:T(8,128)S(1)}, f32[10,16,256]{2,1,0:T(8,128)S(1)}, u32[]{:S(2)}, u32[]{:S(2)}) collective-permute-start(f32[10,16,256]{2,1,0:T(8,128)S(1)} %get-tuple-element.61.sent_a), channel_id=1, source_target_pairs={{1,2},{2,1},{5,6},{6,5},{9,10},{10,9},{13,14},{14,13},{17,18},{18,... | collective-permute-start | bytes 491528 | tf_op jit(solution)/shard_map/ppermute | solution.py:665
  35.0 1.7 %collective-permute-start.9 = (f32[10,16,256]{2,1,0:T(8,128)S(1)}, f32[10,16,256]{2,1,0:T(8,128)S(1)}, u32[]{:S(2)}, u32[]{:S(2)}) collective-permute-start(f32[10,16,256]{2,1,0:T(8,128)S(1)} %get-tuple-element.62.sent_b), channel_id=1, source_target_pairs={{0,1},{2,3},{1,0},{3,2},{4,5},{6,7},{5,4},{7,6},{8,9},{10,11},{9,8... | collective-permute-start | bytes 491528 | tf_op jit(solution)/shard_map/ppermute | solution.py:665
  36.7 0.1 mean_planes.1
  36.8 5.9 %collective-permute-start.12 = (f32[6,48,256]{2,1,0:T(8,128)S(1)}, f32[6,48,256]{2,1,0:T(8,128)S(1)}, u32[]{:S(2)}, u32[]{:S(2)}) collective-permute-start(f32[6,48,256]{2,1,0:T(8,128)S(1)} %get-tuple-element.69), channel_id=1, source_target_pairs={{4,8},{12,16},{20,24},{8,4},{16,12},{24,20},{5,9},{13,17},{21,25},... | collective-permute-start | bytes 884744 | tf_op jit(solution)/shard_map/ppermute | solution.py:665
  42.8 0.1 collective-permute-start.13
  42.8 0.0 collective-permute-done.8.from_a
  42.8 0.0 collective-permute-done.9.from_b
  42.9 0.1 source_planes.1
  43.0 5.7 %collective-permute-start.10 = (f32[6,48,256]{2,1,0:T(8,128)S(1)}, f32[6,48,256]{2,1,0:T(8,128)S(1)}, u32[]{:S(2)}, u32[]{:S(2)}) collective-permute-start(f32[6,48,256]{2,1,0:T(8,128)S(1)} %get-tuple-element.64), channel_id=1, source_target_pairs={{4,8},{12,16},{20,24},{8,4},{16,12},{24,20},{5,9},{13,17},{21,25},... | collective-permute-start | bytes 884744 | tf_op jit(solution)/shard_map/ppermute | solution.py:665
  48.7 0.1 collective-permute-start.11
  48.8 0.0 collective-permute-done.12.from_a
  48.8 0.0 collective-permute-done.13.from_b
  48.8 1.2 %middle_setup.1 = (f32[2,10,48,256]{3,2,1,0:T(8,128)S(1)}, f32[12,10,48,256]{3,2,1,0:T(8,128)S(1)}, f32[2,10,48,256]{3,2,1,0:T(8,128)S(1)}, f32[2,10,48,256]{3,2,1,0:T(8,128)S(1)}) custom-call(f32[8,48,256]{2,1,0:T(8,128)S(1)} %get-tuple-element.68.k, f32[6,48,256]{2,1,0:T(8,128)S(1)} %collective-permute-done.12.from_a, ...), custom_call_target="tpu_custom_call" | custom-call | tf_op jit(solution)/shard_map/middle_setup/pallas_call | solution.py:645
  49.9 2.9 %collective-permute-done.10.source_a = f32[6,48,256]{2,1,0:T(8,128)S(1)} collective-permute-done((f32[6,48,256]{2,1,0:T(8,128)S(1)}, f32[6,48,256]{2,1,0:T(8,128)S(1)}, u32[]{:S(2)}, u32[]{:S(2)}) %collective-permute-start.10) | collective-permute-done | bytes 294944 | tf_op jit(solution)/shard_map/ppermute | solution.py:665
  52.9 0.0 collective-permute-done.11.source_b
  52.9 2.2 %middle_level.1 = (f32[8,16,256]{2,1,0:T(8,128)S(1)}, f32[4,24,128]{2,1,0:T(8,128)S(1)}, f32[4,24,128]{2,1,0:T(8,128)S(1)}, f32[9,24,128]{2,1,0:T(8,128)S(1)}, f32[9,24,128]{2,1,0:T(8,128)S(1)}) custom-call(f32[10,48,256]{2,1,0:T(8,128)S(1)} %get-tuple-element.63.s, f32[6,48,256]{2,1,0:T(8,128)S(1)} %collective-permute-done.10.source_a, ...), custom_call_target="tpu_custom_call" | custom-call | tf_op jit(solution)/shard_map/middle_level/pallas_call | solution.py:645
  55.1 3.6 %collective-permute-start.14 = (f32[9,24,128]{2,1,0:T(8,128)S(1)}, f32[9,24,128]{2,1,0:T(8,128)S(1)}, u32[]{:S(2)}, u32[]{:S(2)}) collective-permute-start(f32[9,24,128]{2,1,0:T(8,128)S(1)} %get-tuple-element.78), channel_id=1, source_target_pairs={{4,8},{12,16},{20,24},{8,4},{16,12},{24,20},{5,9},{13,17},{21,25},... | collective-permute-start | bytes 331784 | tf_op jit(solution)/shard_map/ppermute | solution.py:665
  58.7 0.1 collective-permute-start.15
  58.8 1.0 %copy.6 = f32[16,32,512]{2,1,0:T(8,128)} copy(f32[16,32,512]{2,1,0:T(8,128)S(1)} %get-tuple-element.82) | data formatting | bytes 2097152
  59.8 0.7 %copy.7 = f32[8,16,256]{2,1,0:T(8,128)} copy(f32[8,16,256]{2,1,0:T(8,128)S(1)} %get-tuple-element.83) | data formatting | bytes 262144
  60.4 0.7 %collective-permute-done.14.from_a = f32[9,24,128]{2,1,0:T(8,128)S(1)} collective-permute-done((f32[9,24,128]{2,1,0:T(8,128)S(1)}, f32[9,24,128]{2,1,0:T(8,128)S(1)}, u32[]{:S(2)}, u32[]{:S(2)}) %collective-permute-start.14) | collective-permute-done | bytes 110624 | tf_op jit(solution)/shard_map/ppermute | solution.py:665
  61.2 0.0 collective-permute-done.15.from_b
  61.2 1.0 %coarse_level.1 = (f32[4,8,128]{2,1,0:T(8,128)}, f32[4,8,128]{2,1,0:T(8,128)}) custom-call(f32[4,24,128]{2,1,0:T(8,128)S(1)} %get-tuple-element.76.s, f32[4,24,128]{2,1,0:T(8,128)S(1)} %get-tuple-element.77.k, f32[9,24,128]{2,1,0:T(8,128)S(1)} %collective-permute-done.14.from_a, f32[9,24,128]{2,1,0:T(8,128)S(1)} %collective-permute-done.15.from_b), custom_call_target="tpu_custom_call" | custom-call | tf_op jit(solution)/shard_map/coarse_level/pallas_call | solution.py:645
Async XLA Ops:
  0.6 6.8 %copy-start = (f32[16,32,512]{2,1,0:T(8,128)S(1)}, f32[16,32,512]{2,1,0:T(8,128)}, u32[]{:S(2)}) copy-start(f32[16,32,512]{2,1,0:T(8,128)} %k.5) | copy-start | bytes 3145732
  2.0 11.0 %copy-start.1 = (f32[16,32,512]{2,1,0:T(8,128)S(1)}, f32[16,32,512]{2,1,0:T(8,128)}, u32[]{:S(2)}) copy-start(f32[16,32,512]{2,1,0:T(8,128)} %s.3) | copy-start | bytes 3145732
  2.0 5.9 %collective-permute-start = (f32[2,4,8,512]{3,2,1,0:T(8,128)S(1)}, f32[2,4,8,512]{3,2,1,0:T(8,128)S(1)}, u32[]{:S(2)}, u32[]{:S(2)}) collective-permute-start(f32[2,4,8,512]{3,2,1,0:T(8,128)S(1)} %get-tuple-element.43), channel_id=1, source_target_pairs={{1,2},{2,1},{5,6},{6,5},{9,10},{10,9},{13,14},{14,13},{17,18},{18,... | collective-permute-start | bytes 393224 | tf_op jit(solution)/shard_map/ppermute | solution.py:665
  2.8 10.2 %collective-permute-start.1 = (f32[2,4,8,512]{3,2,1,0:T(8,128)S(1)}, f32[2,4,8,512]{3,2,1,0:T(8,128)S(1)}, u32[]{:S(2)}, u32[]{:S(2)}) collective-permute-start(f32[2,4,8,512]{3,2,1,0:T(8,128)S(1)} %get-tuple-element.44), channel_id=1, source_target_pairs={{0,1},{2,3},{1,0},{3,2},{4,5},{6,7},{5,4},{7,6},{8,9},{10,11},{9,8... | collective-permute-start | bytes 393224 | tf_op jit(solution)/shard_map/ppermute | solution.py:665
  13.2 15.8 %collective-permute-start.2 = (f32[9,32,512]{2,1,0:T(8,128)S(1)}, f32[9,32,512]{2,1,0:T(8,128)S(1)}, u32[]{:S(2)}, u32[]{:S(2)}) collective-permute-start(f32[9,32,512]{2,1,0:T(8,128)S(1)} %get-tuple-element.47), channel_id=1, source_target_pairs={{4,8},{12,16},{20,24},{8,4},{16,12},{24,20},{5,9},{13,17},{21,25},... | collective-permute-start | bytes 1769480 | tf_op jit(solution)/shard_map/ppermute | solution.py:665
  17.8 11.2 %collective-permute-start.3 = (f32[9,32,512]{2,1,0:T(8,128)S(1)}, f32[9,32,512]{2,1,0:T(8,128)S(1)}, u32[]{:S(2)}, u32[]{:S(2)}) collective-permute-start(f32[9,32,512]{2,1,0:T(8,128)S(1)} %get-tuple-element.48), channel_id=1, source_target_pairs={{0,4},{8,12},{16,20},{24,28},{4,0},{12,8},{20,16},{28,24},{1,5},{9... | collective-permute-start | bytes 1769480 | tf_op jit(solution)/shard_map/ppermute | solution.py:665
  17.9 3.3 %collective-permute-start.4 = (f32[2,4,8,512]{3,2,1,0:T(8,128)S(1)}, f32[2,4,8,512]{3,2,1,0:T(8,128)S(1)}, u32[]{:S(2)}, u32[]{:S(2)}) collective-permute-start(f32[2,4,8,512]{3,2,1,0:T(8,128)S(1)} %get-tuple-element.49), channel_id=1, source_target_pairs={{1,2},{2,1},{5,6},{6,5},{9,10},{10,9},{13,14},{14,13},{17,18},{18,... | collective-permute-start | bytes 393224 | tf_op jit(solution)/shard_map/ppermute | solution.py:665
  18.6 7.8 %collective-permute-start.5 = (f32[2,4,8,512]{3,2,1,0:T(8,128)S(1)}, f32[2,4,8,512]{3,2,1,0:T(8,128)S(1)}, u32[]{:S(2)}, u32[]{:S(2)}) collective-permute-start(f32[2,4,8,512]{3,2,1,0:T(8,128)S(1)} %get-tuple-element.50), channel_id=1, source_target_pairs={{0,1},{2,3},{1,0},{3,2},{4,5},{6,7},{5,4},{7,6},{8,9},{10,11},{9,8... | collective-permute-start | bytes 393224 | tf_op jit(solution)/shard_map/ppermute | solution.py:665
  20.6 13.8 %collective-permute-start.6 = (f32[8,16,256]{2,1,0:T(8,128)S(1)}, f32[8,16,256]{2,1,0:T(8,128)S(1)}, u32[]{:S(2)}, u32[]{:S(2)}) collective-permute-start(f32[8,16,256]{2,1,0:T(8,128)S(1)} %mean.1.own_rows), channel_id=1, source_target_pairs={{1,2},{2,1},{5,6},{6,5},{9,10},{10,9},{13,14},{14,13},{17,18},{18,... | collective-permute-start | bytes 393224 | tf_op jit(solution)/shard_map/ppermute | solution.py:665
  21.2 13.1 %collective-permute-start.7 = (f32[8,16,256]{2,1,0:T(8,128)S(1)}, f32[8,16,256]{2,1,0:T(8,128)S(1)}, u32[]{:S(2)}, u32[]{:S(2)}) collective-permute-start(f32[8,16,256]{2,1,0:T(8,128)S(1)} %mean.1.own_rows), channel_id=1, source_target_pairs={{0,1},{2,3},{1,0},{3,2},{4,5},{6,7},{5,4},{7,6},{8,9},{10,11},{9,8... | collective-permute-start | bytes 393224 | tf_op jit(solution)/shard_map/ppermute | solution.py:665
  34.3 8.5 %collective-permute-start.8 = (f32[10,16,256]{2,1,0:T(8,128)S(1)}, f32[10,16,256]{2,1,0:T(8,128)S(1)}, u32[]{:S(2)}, u32[]{:S(2)}) collective-permute-start(f32[10,16,256]{2,1,0:T(8,128)S(1)} %get-tuple-element.61.sent_a), channel_id=1, source_target_pairs={{1,2},{2,1},{5,6},{6,5},{9,10},{10,9},{13,14},{14,13},{17,18},{18,... | collective-permute-start | bytes 491528 | tf_op jit(solution)/shard_map/ppermute | solution.py:665
  35.0 7.8 %collective-permute-start.9 = (f32[10,16,256]{2,1,0:T(8,128)S(1)}, f32[10,16,256]{2,1,0:T(8,128)S(1)}, u32[]{:S(2)}, u32[]{:S(2)}) collective-permute-start(f32[10,16,256]{2,1,0:T(8,128)S(1)} %get-tuple-element.62.sent_b), channel_id=1, source_target_pairs={{0,1},{2,3},{1,0},{3,2},{4,5},{6,7},{5,4},{7,6},{8,9},{10,11},{9,8... | collective-permute-start | bytes 491528 | tf_op jit(solution)/shard_map/ppermute | solution.py:665
  36.8 12.0 %collective-permute-start.12 = (f32[6,48,256]{2,1,0:T(8,128)S(1)}, f32[6,48,256]{2,1,0:T(8,128)S(1)}, u32[]{:S(2)}, u32[]{:S(2)}) collective-permute-start(f32[6,48,256]{2,1,0:T(8,128)S(1)} %get-tuple-element.69), channel_id=1, source_target_pairs={{4,8},{12,16},{20,24},{8,4},{16,12},{24,20},{5,9},{13,17},{21,25},... | collective-permute-start | bytes 884744 | tf_op jit(solution)/shard_map/ppermute | solution.py:665
  42.8 6.0 %collective-permute-start.13 = (f32[6,48,256]{2,1,0:T(8,128)S(1)}, f32[6,48,256]{2,1,0:T(8,128)S(1)}, u32[]{:S(2)}, u32[]{:S(2)}) collective-permute-start(f32[6,48,256]{2,1,0:T(8,128)S(1)} %get-tuple-element.70), channel_id=1, source_target_pairs={{0,4},{8,12},{16,20},{24,28},{4,0},{12,8},{20,16},{28,24},{1,5},{9... | collective-permute-start | bytes 884744 | tf_op jit(solution)/shard_map/ppermute | solution.py:665
  43.0 9.9 %collective-permute-start.10 = (f32[6,48,256]{2,1,0:T(8,128)S(1)}, f32[6,48,256]{2,1,0:T(8,128)S(1)}, u32[]{:S(2)}, u32[]{:S(2)}) collective-permute-start(f32[6,48,256]{2,1,0:T(8,128)S(1)} %get-tuple-element.64), channel_id=1, source_target_pairs={{4,8},{12,16},{20,24},{8,4},{16,12},{24,20},{5,9},{13,17},{21,25},... | collective-permute-start | bytes 884744 | tf_op jit(solution)/shard_map/ppermute | solution.py:665
  48.7 4.2 %collective-permute-start.11 = (f32[6,48,256]{2,1,0:T(8,128)S(1)}, f32[6,48,256]{2,1,0:T(8,128)S(1)}, u32[]{:S(2)}, u32[]{:S(2)}) collective-permute-start(f32[6,48,256]{2,1,0:T(8,128)S(1)} %get-tuple-element.65), channel_id=1, source_target_pairs={{0,4},{8,12},{16,20},{24,28},{4,0},{12,8},{20,16},{28,24},{1,5},{9... | collective-permute-start | bytes 884744 | tf_op jit(solution)/shard_map/ppermute | solution.py:665
  55.1 6.1 %collective-permute-start.14 = (f32[9,24,128]{2,1,0:T(8,128)S(1)}, f32[9,24,128]{2,1,0:T(8,128)S(1)}, u32[]{:S(2)}, u32[]{:S(2)}) collective-permute-start(f32[9,24,128]{2,1,0:T(8,128)S(1)} %get-tuple-element.78), channel_id=1, source_target_pairs={{4,8},{12,16},{20,24},{8,4},{16,12},{24,20},{5,9},{13,17},{21,25},... | collective-permute-start | bytes 331784 | tf_op jit(solution)/shard_map/ppermute | solution.py:665
  58.7 2.4 %collective-permute-start.15 = (f32[9,24,128]{2,1,0:T(8,128)S(1)}, f32[9,24,128]{2,1,0:T(8,128)S(1)}, u32[]{:S(2)}, u32[]{:S(2)}) collective-permute-start(f32[9,24,128]{2,1,0:T(8,128)S(1)} %get-tuple-element.79), channel_id=1, source_target_pairs={{0,4},{8,12},{16,20},{24,28},{4,0},{12,8},{20,16},{28,24},{1,5},{9... | collective-permute-start | bytes 331784 | tf_op jit(solution)/shard_map/ppermute | solution.py:665

commit v9 on v8

--- a/solution.py
+++ b/solution.py
@@ -487,7 +487,7 @@
     widen_planes(K, Send(to_a, to_b, "outer"), own_rows.shape[0], of)
 
 
-def middle_setup_kernel(k, from_a, from_b, K, W, D, I):
+def middle_setup_kernel(k, from_a, from_b, K, W, D, I, k_next, Zk):
     from_down, from_up = got_pair(from_a, from_b, "outer")
     _, pairs, wide, lanes = K.shape
     planes = k.shape[0]
@@ -503,6 +503,12 @@
         K[0, p] = pick(even, a, b)
         K[1, p] = pick(even, b, a)
     Level(K, None, None, W, D, pairs - 2 * HP, (wide, lanes)).all_setup(5, I)
+    half = wide // 2
+    for q in range(pairs):
+        Zk[half * q : half * (q + 1)] = product(row_sum(wide), K[0, q] + K[1, q])
+    mean = product(Zk[...], lane_mean(lanes))
+    for q in range(pairs):
+        k_next[q] = mean[half * q : half * (q + 1)]
 
 
 def source_planes_kernel(own_rows, sent_a, sent_b, from_a, from_b, S, to_a, to_b):
@@ -522,9 +528,8 @@
     widen_planes(S, Send(to_a, to_b, "outer"), planes, of)
 
 
-def middle_kernel(s, source_a, source_b, K, W, D, I,
-                  field, s_next, k_next, to_a, to_b,
-                  S, U, R, Z, Zk):
+def middle_kernel(s, source_a, source_b, K, W, D, I, k_next,
+                  field, s_next, to_a, to_b, S, U, R, Z):
     from_down, from_up = got_pair(source_a, source_b, "outer")
     send = Send(to_a, to_b, "outer")
     planes = field.shape[0]
@@ -567,24 +572,18 @@
     for q in range(own):
         Z[half * q : half * (q + 1)] = product(
             row_restriction(wide, False), restrict_planes(R, q + 1, even))
-    for q in range(own + 2):
-        total = K[0, HP - 1 + q] + K[1, HP - 1 + q]
-        Zk[half * q : half * (q + 1)] = product(row_sum(wide), total)
     source = product(Z[...], lane_restriction(lanes))
-    mean = product(Zk[...], lane_mean(lanes))
     for q in range(own):
         s_next[q] = source[half * q : half * (q + 1)]
-        k_next[q] = mean[half * (q + 1) : half * (q + 2)]
     for j in range(4):
         send.put(j, s_next[j], s_next[own - 4 + j])
-    for j in range(5):
-        send.put(4 + j, mean[half * (1 + j) : half * (2 + j)],
-                 mean[half * (own - 4 + j) : half * (own - 3 + j)])
+    for j in range(2):
+        send.put(4 + j, k_next[HP + 3 + j], k_next[HP + own - 5 + j])
 
 
 def coarse_kernel(s, k, from_a, from_b, field, rest, K, S, U, W, D, R):
     from_down, from_up = got_pair(from_a, from_b, "outer")
-    planes, wide, lanes = k.shape
+    planes, wide, lanes = s.shape
     own = planes // 2
     rows = field.shape[1]
     even = even_mask(wide, lanes)
@@ -599,11 +598,11 @@
         return s[i] if i < planes else from_up[i - planes]
 
     def mean_plane(i):
-        if i < -5 or i > planes + 4:
-            return zero
-        if i < 0:
+        if -HP <= i < planes + HP:
+            return k[HP + i]
+        if i in (-5, -4):
             return from_down[9 + i]
-        return k[i] if i < planes else from_up[4 + i - planes]
+        return from_up[1 + i - planes] if i in (planes + 3, planes + 4) else zero
 
     for p in range(-HP, own + HP):
         for to, plane in ((S, source_plane), (K, mean_plane)):
@@ -710,18 +709,21 @@
         mean, *mean_halo, name="mean_planes")
     mean_halo = exchange(*sent, "outer")
     K, S, U, W, D = level_arrays(own, wide, lanes)
-    constants = call(middle_setup_kernel, [K, W, D, K], [], k1, *mean_halo, name="middle_setup")
+    next_half, next_lanes = wide // 2, lanes // 2
+    *constants, k2 = call(
+        middle_setup_kernel, [K, W, D, K, (own + 2 * HP, next_half, next_lanes)],
+        [((own + 2 * HP) * next_half, lanes)], k1, *mean_halo, name="middle_setup")
     message = (6, wide, lanes)
     s1, *sent = call(
         source_planes_kernel, [(planes + 2, wide, lanes), message, message], [],
         source, to_a, to_b, *row_halo, name="source_planes")
     source_halo = exchange(*sent, "outer")
-    half, next_lanes = wide // 2, lanes // 2
-    block, message = (own, half, next_lanes), (9, half, next_lanes)
-    field1, s2, k2, *sent = call(
-        middle_kernel, [(planes, rows, lanes), block, block, message, message],
-        [S, U, (2, own + 2, wide, lanes), (half * own, lanes), (half * (own + 2), lanes)],
-        s1, *source_halo, *constants, name="middle_level")
+    half = next_half
+    message = (6, half, next_lanes)
+    field1, s2, *sent = call(
+        middle_kernel, [(planes, rows, lanes), (own, half, next_lanes), message, message],
+        [S, U, (2, own + 2, wide, lanes), (half * own, lanes)],
+        s1, *source_halo, *constants, k2, name="middle_level")
 
     planes, rows, wide, lanes = own, rows // 2, half, next_lanes
     own = planes // 2

time: 62.5 us -> 62.1 us (level)
  waiting for transfers between devices: 10.4 us -> 9.74 us
    ppermute x16, waiting for transfers between devices: 10.4 us -> 9.74 us  [swapped(): return lax.ppermute(x, axis, pairs + [(j, i) for i, j in pairs])]
where the time goes in v9:
time: 62.1 us; the launch traced here: 61.6 us
  starting transfers between devices  34.7 us (56%)
  Pallas kernels  14.6 us (24%)
  waiting for transfers between devices  9.74 us (16%)
  local copies, waits for them, and re-layouts  1.64 us (3%)
  between operations  0.88 us (1%)
    ppermute x16, starting transfers between devices, swapped(): return lax.ppermute(x, axis, pairs + [(j, i) for i, j in pairs])  34.7 us
    pallas_call x10, Pallas kernels, call(): pl.pallas_call(kernel, out_shape=[jax.ShapeDtypeStruct(o, F32) if results...  14.6 us
    ppermute x16, waiting for transfers between devices, swapped(): return lax.ppermute(x, axis, pairs + [(j, i) for i, j in pairs])  9.74 us
    unnamed x6, local copies, waits for them, and re-layouts  1.64 us
  transfers between devices with their start and end apart: 16, of which 4 were waited for; matrix products, arithmetic and copies ran while one was open for 3% of the time, Pallas kernels for 16%

profile of v9, /device:TPU:1, one launch (start us, length us, event | category | flops | bytes accessed | tf_op | source)
XLA Modules:
  0.0 61.6 jit_solution(17944540842379265485)
XLA Ops:
  0.6 0.0 copy-start
  0.6 1.4 %pack_rows.1 = (f32[2,4,8,512]{3,2,1,0:T(8,128)S(1)}, f32[2,4,8,512]{3,2,1,0:T(8,128)S(1)}, f32[2,4,8,512]{3,2,1,0:T(8,128)S(1)}, f32[2,4,8,512]{3,2,1,0:T(8,128)S(1)}) custom-call(f32[16,32,512]{2,1,0:T(8,128)} %s.3, f32[16,32,512]{2,1,0:T(8,128)} %s.3, f32[16,32,512]{2,1,0:T(8,128)} %k.5, f32[16,32,512]{2,1,0:T(8,128)} %k.5), custom_call_target="tpu_custom_call" | custom-call | tf_op jit(solution)/shard_map/pack_rows/pallas_call | solution.py:644
  2.0 0.0 copy-start.1
  2.0 0.8 %collective-permute-start = (f32[2,4,8,512]{3,2,1,0:T(8,128)S(1)}, f32[2,4,8,512]{3,2,1,0:T(8,128)S(1)}, u32[]{:S(2)}, u32[]{:S(2)}) collective-permute-start(f32[2,4,8,512]{3,2,1,0:T(8,128)S(1)} %get-tuple-element.43), channel_id=1, source_target_pairs={{1,2},{2,1},{5,6},{6,5},{9,10},{10,9},{13,14},{14,13},{17,18},{18,... | collective-permute-start | bytes 393224 | tf_op jit(solution)/shard_map/ppermute | solution.py:664
  2.8 4.5 %collective-permute-start.1 = (f32[2,4,8,512]{3,2,1,0:T(8,128)S(1)}, f32[2,4,8,512]{3,2,1,0:T(8,128)S(1)}, u32[]{:S(2)}, u32[]{:S(2)}) collective-permute-start(f32[2,4,8,512]{3,2,1,0:T(8,128)S(1)} %get-tuple-element.44), channel_id=1, source_target_pairs={{0,1},{2,3},{1,0},{3,2},{4,5},{6,7},{5,4},{7,6},{8,9},{10,11},{9,8... | collective-permute-start | bytes 393224 | tf_op jit(solution)/shard_map/ppermute | solution.py:664
  7.4 0.0 copy-done
  7.4 0.5 mean.1.own_rows
  7.9 0.0 collective-permute-done.from_a.end_a
  7.9 5.1 %collective-permute-done.1.from_b.end_b = f32[2,4,8,512]{3,2,1,0:T(8,128)S(1)} collective-permute-done((f32[2,4,8,512]{3,2,1,0:T(8,128)S(1)}, f32[2,4,8,512]{3,2,1,0:T(8,128)S(1)}, u32[]{:S(2)}, u32[]{:S(2)}) %collective-permute-start.1) | collective-permute-done | bytes 131104 | tf_op jit(solution)/shard_map/ppermute | solution.py:664
  13.0 0.0 copy-done.1
  13.0 0.1 pack_planes.1
  13.2 4.6 %collective-permute-start.2 = (f32[9,32,512]{2,1,0:T(8,128)S(1)}, f32[9,32,512]{2,1,0:T(8,128)S(1)}, u32[]{:S(2)}, u32[]{:S(2)}) collective-permute-start(f32[9,32,512]{2,1,0:T(8,128)S(1)} %get-tuple-element.47), channel_id=1, source_target_pairs={{4,8},{12,16},{20,24},{8,4},{16,12},{24,20},{5,9},{13,17},{21,25},... | collective-permute-start | bytes 1769480 | tf_op jit(solution)/shard_map/ppermute | solution.py:664
  17.8 0.1 collective-permute-start.3
  17.9 0.7 %collective-permute-start.4 = (f32[2,4,8,512]{3,2,1,0:T(8,128)S(1)}, f32[2,4,8,512]{3,2,1,0:T(8,128)S(1)}, u32[]{:S(2)}, u32[]{:S(2)}) collective-permute-start(f32[2,4,8,512]{3,2,1,0:T(8,128)S(1)} %get-tuple-element.49), channel_id=1, source_target_pairs={{1,2},{2,1},{5,6},{6,5},{9,10},{10,9},{13,14},{14,13},{17,18},{18,... | collective-permute-start | bytes 393224 | tf_op jit(solution)/shard_map/ppermute | solution.py:664
  18.6 2.0 %collective-permute-start.5 = (f32[2,4,8,512]{3,2,1,0:T(8,128)S(1)}, f32[2,4,8,512]{3,2,1,0:T(8,128)S(1)}, u32[]{:S(2)}, u32[]{:S(2)}) collective-permute-start(f32[2,4,8,512]{3,2,1,0:T(8,128)S(1)} %get-tuple-element.50), channel_id=1, source_target_pairs={{0,1},{2,3},{1,0},{3,2},{4,5},{6,7},{5,4},{7,6},{8,9},{10,11},{9,8... | collective-permute-start | bytes 393224 | tf_op jit(solution)/shard_map/ppermute | solution.py:664
  20.6 0.7 %collective-permute-start.6 = (f32[8,16,256]{2,1,0:T(8,128)S(1)}, f32[8,16,256]{2,1,0:T(8,128)S(1)}, u32[]{:S(2)}, u32[]{:S(2)}) collective-permute-start(f32[8,16,256]{2,1,0:T(8,128)S(1)} %mean.1.own_rows), channel_id=1, source_target_pairs={{1,2},{2,1},{5,6},{6,5},{9,10},{10,9},{13,14},{14,13},{17,18},{18,... | collective-permute-start | bytes 393224 | tf_op jit(solution)/shard_map/ppermute | solution.py:664
  21.2 0.0 collective-permute-done.4.inner_a
  21.2 3.5 %collective-permute-start.7 = (f32[8,16,256]{2,1,0:T(8,128)S(1)}, f32[8,16,256]{2,1,0:T(8,128)S(1)}, u32[]{:S(2)}, u32[]{:S(2)}) collective-permute-start(f32[8,16,256]{2,1,0:T(8,128)S(1)} %mean.1.own_rows), channel_id=1, source_target_pairs={{0,1},{2,3},{1,0},{3,2},{4,5},{6,7},{5,4},{7,6},{8,9},{10,11},{9,8... | collective-permute-start | bytes 393224 | tf_op jit(solution)/shard_map/ppermute | solution.py:664
  24.7 1.7 %collective-permute-done.5.inner_b = f32[2,4,8,512]{3,2,1,0:T(8,128)S(1)} collective-permute-done((f32[2,4,8,512]{3,2,1,0:T(8,128)S(1)}, f32[2,4,8,512]{3,2,1,0:T(8,128)S(1)}, u32[]{:S(2)}, u32[]{:S(2)}) %collective-permute-start.5) | collective-permute-done | bytes 131104 | tf_op jit(solution)/shard_map/ppermute | solution.py:664
  26.4 2.6 %fine_prepare.1 = (f32[2,8,48,512]{3,2,1,0:T(8,128)S(1)}, f32[2,8,48,512]{3,2,1,0:T(8,128)S(1)}, f32[2,8,48,512]{3,2,1,0:T(8,128)S(1)}, f32[12,8,48,512]{3,2,1,0:T(8,128)S(1)}, f32[2,8,48,512]{3,2,1,0:T(8,128)S(1)}) custom-call(f32[16,32,512]{2,1,0:T(8,128)S(1)} %copy-done.1, f32[16,32,512]{2,1,0:T(8,128)S(1)} %copy-done, ...), custom_call_target="tpu_custom_call" | custom-call | tf_op jit(solution)/shard_map/fine_prepare/pallas_call | solution.py:644
  29.0 0.0 collective-permute-done.2.plane_a
  29.0 0.0 collective-permute-done.3.plane_b
  29.0 5.3 %fine_level.1 = (f32[16,32,512]{2,1,0:T(8,128)S(1)}, f32[10,16,256]{2,1,0:T(8,128)S(1)}, f32[10,16,256]{2,1,0:T(8,128)S(1)}, f32[10,16,256]{2,1,0:T(8,128)S(1)}) custom-call(f32[9,32,512]{2,1,0:T(8,128)S(1)} %collective-permute-done.2.plane_a, f32[9,32,512]{2,1,0:T(8,128)S(1)} %collective-permute-done.3.plane_b, f32[2,8,48,512]{3,2,1,0:T(8,128)S(1)} %get-tuple-element.51.K0, ...), custom_call_target="tpu_custom_call" | custom-call | tf_op jit(solution)/shard_map/fine_level/pallas_call | solution.py:644
  34.3 0.0 collective-permute-done.6.from_a
  34.3 0.0 collective-permute-done.7.from_b
  34.3 0.7 %collective-permute-start.8 = (f32[10,16,256]{2,1,0:T(8,128)S(1)}, f32[10,16,256]{2,1,0:T(8,128)S(1)}, u32[]{:S(2)}, u32[]{:S(2)}) collective-permute-start(f32[10,16,256]{2,1,0:T(8,128)S(1)} %get-tuple-element.61.sent_a), channel_id=1, source_target_pairs={{1,2},{2,1},{5,6},{6,5},{9,10},{10,9},{13,14},{14,13},{17,18},{18,... | collective-permute-start | bytes 491528 | tf_op jit(solution)/shard_map/ppermute | solution.py:664
  35.0 1.7 %collective-permute-start.9 = (f32[10,16,256]{2,1,0:T(8,128)S(1)}, f32[10,16,256]{2,1,0:T(8,128)S(1)}, u32[]{:S(2)}, u32[]{:S(2)}) collective-permute-start(f32[10,16,256]{2,1,0:T(8,128)S(1)} %get-tuple-element.62.sent_b), channel_id=1, source_target_pairs={{0,1},{2,3},{1,0},{3,2},{4,5},{6,7},{5,4},{7,6},{8,9},{10,11},{9,8... | collective-permute-start | bytes 491528 | tf_op jit(solution)/shard_map/ppermute | solution.py:664
  36.7 0.1 mean_planes.1
  36.8 5.9 %collective-permute-start.12 = (f32[6,48,256]{2,1,0:T(8,128)S(1)}, f32[6,48,256]{2,1,0:T(8,128)S(1)}, u32[]{:S(2)}, u32[]{:S(2)}) collective-permute-start(f32[6,48,256]{2,1,0:T(8,128)S(1)} %get-tuple-element.69), channel_id=1, source_target_pairs={{4,8},{12,16},{20,24},{8,4},{16,12},{24,20},{5,9},{13,17},{21,25},... | collective-permute-start | bytes 884744 | tf_op jit(solution)/shard_map/ppermute | solution.py:664
  42.8 0.1 collective-permute-start.13
  42.8 0.0 collective-permute-done.8.from_a
  42.8 0.0 collective-permute-done.9.from_b
  42.9 0.1 source_planes.1
  43.0 5.7 %collective-permute-start.10 = (f32[6,48,256]{2,1,0:T(8,128)S(1)}, f32[6,48,256]{2,1,0:T(8,128)S(1)}, u32[]{:S(2)}, u32[]{:S(2)}) collective-permute-start(f32[6,48,256]{2,1,0:T(8,128)S(1)} %get-tuple-element.64), channel_id=1, source_target_pairs={{4,8},{12,16},{20,24},{8,4},{16,12},{24,20},{5,9},{13,17},{21,25},... | collective-permute-start | bytes 884744 | tf_op jit(solution)/shard_map/ppermute | solution.py:664
  48.7 0.1 collective-permute-start.11
  48.8 0.0 collective-permute-done.12.from_a
  48.8 0.0 collective-permute-done.13.from_b
  48.8 1.4 %middle_setup.1 = (f32[2,10,48,256]{3,2,1,0:T(8,128)S(1)}, f32[12,10,48,256]{3,2,1,0:T(8,128)S(1)}, f32[2,10,48,256]{3,2,1,0:T(8,128)S(1)}, f32[2,10,48,256]{3,2,1,0:T(8,128)S(1)}, f32[10,24,128]{2,1,0:T(8,128)S(1)}) custom-call(f32[8,48,256]{2,1,0:T(8,128)S(1)} %get-tuple-element.68.k, f32[6,48,256]{2,1,0:T(8,128)S(1)} %collective-permute-done.12.from_a, ...), custom_call_target="tpu_custom_call" | custom-call | tf_op jit(solution)/shard_map/middle_setup/pallas_call | solution.py:644
  50.2 2.7 %collective-permute-done.10.source_a = f32[6,48,256]{2,1,0:T(8,128)S(1)} collective-permute-done((f32[6,48,256]{2,1,0:T(8,128)S(1)}, f32[6,48,256]{2,1,0:T(8,128)S(1)}, u32[]{:S(2)}, u32[]{:S(2)}) %collective-permute-start.10) | collective-permute-done | bytes 294944 | tf_op jit(solution)/shard_map/ppermute | solution.py:664
  52.9 0.0 collective-permute-done.11.source_b
  52.9 2.0 %middle_level.1 = (f32[8,16,256]{2,1,0:T(8,128)S(1)}, f32[4,24,128]{2,1,0:T(8,128)S(1)}, f32[6,24,128]{2,1,0:T(8,128)S(1)}, f32[6,24,128]{2,1,0:T(8,128)S(1)}) custom-call(f32[10,48,256]{2,1,0:T(8,128)S(1)} %get-tuple-element.63.s, f32[6,48,256]{2,1,0:T(8,128)S(1)} %collective-permute-done.10.source_a, f32[6,48,256]{2,1,0:T(8,128)S(1)} %collective-permute-done.11.source_b, ...), custom_call_target="tpu_custom_call" | custom-call | tf_op jit(solution)/shard_map/middle_level/pallas_call | solution.py:644
  54.9 3.6 %collective-permute-start.14 = (f32[6,24,128]{2,1,0:T(8,128)S(1)}, f32[6,24,128]{2,1,0:T(8,128)S(1)}, u32[]{:S(2)}, u32[]{:S(2)}) collective-permute-start(f32[6,24,128]{2,1,0:T(8,128)S(1)} %get-tuple-element.78), channel_id=1, source_target_pairs={{4,8},{12,16},{20,24},{8,4},{16,12},{24,20},{5,9},{13,17},{21,25},... | collective-permute-start | bytes 221192 | tf_op jit(solution)/shard_map/ppermute | solution.py:664
  58.6 0.1 collective-permute-start.15
  58.6 1.0 %copy.6 = f32[16,32,512]{2,1,0:T(8,128)} copy(f32[16,32,512]{2,1,0:T(8,128)S(1)} %get-tuple-element.82) | data formatting | bytes 2097152
  59.6 0.7 %copy.7 = f32[8,16,256]{2,1,0:T(8,128)} copy(f32[8,16,256]{2,1,0:T(8,128)S(1)} %get-tuple-element.83) | data formatting | bytes 262144
  60.3 0.3 collective-permute-done.14.from_a
  60.6 0.0 collective-permute-done.15.from_b
  60.6 1.0 %coarse_level.1 = (f32[4,8,128]{2,1,0:T(8,128)}, f32[4,8,128]{2,1,0:T(8,128)}) custom-call(f32[4,24,128]{2,1,0:T(8,128)S(1)} %get-tuple-element.77.s, f32[10,24,128]{2,1,0:T(8,128)S(1)} %get-tuple-element.75.k_next.k, f32[6,24,128]{2,1,0:T(8,128)S(1)} %collective-permute-done.14.from_a, f32[6,24,128]{2,1,0:T(8,128)S(1)} %collective-permute-done.15.from_b), custom_call_target="tpu_custom_call" | custom-call | tf_op jit(solution)/shard_map/coarse_level/pallas_call | solution.py:644
Async XLA Ops:
  0.6 6.8 %copy-start = (f32[16,32,512]{2,1,0:T(8,128)S(1)}, f32[16,32,512]{2,1,0:T(8,128)}, u32[]{:S(2)}) copy-start(f32[16,32,512]{2,1,0:T(8,128)} %k.5) | copy-start | bytes 3145732
  2.0 11.0 %copy-start.1 = (f32[16,32,512]{2,1,0:T(8,128)S(1)}, f32[16,32,512]{2,1,0:T(8,128)}, u32[]{:S(2)}) copy-start(f32[16,32,512]{2,1,0:T(8,128)} %s.3) | copy-start | bytes 3145732
  2.0 5.9 %collective-permute-start = (f32[2,4,8,512]{3,2,1,0:T(8,128)S(1)}, f32[2,4,8,512]{3,2,1,0:T(8,128)S(1)}, u32[]{:S(2)}, u32[]{:S(2)}) collective-permute-start(f32[2,4,8,512]{3,2,1,0:T(8,128)S(1)} %get-tuple-element.43), channel_id=1, source_target_pairs={{1,2},{2,1},{5,6},{6,5},{9,10},{10,9},{13,14},{14,13},{17,18},{18,... | collective-permute-start | bytes 393224 | tf_op jit(solution)/shard_map/ppermute | solution.py:664
  2.8 10.2 %collective-permute-start.1 = (f32[2,4,8,512]{3,2,1,0:T(8,128)S(1)}, f32[2,4,8,512]{3,2,1,0:T(8,128)S(1)}, u32[]{:S(2)}, u32[]{:S(2)}) collective-permute-start(f32[2,4,8,512]{3,2,1,0:T(8,128)S(1)} %get-tuple-element.44), channel_id=1, source_target_pairs={{0,1},{2,3},{1,0},{3,2},{4,5},{6,7},{5,4},{7,6},{8,9},{10,11},{9,8... | collective-permute-start | bytes 393224 | tf_op jit(solution)/shard_map/ppermute | solution.py:664
  13.2 15.8 %collective-permute-start.2 = (f32[9,32,512]{2,1,0:T(8,128)S(1)}, f32[9,32,512]{2,1,0:T(8,128)S(1)}, u32[]{:S(2)}, u32[]{:S(2)}) collective-permute-start(f32[9,32,512]{2,1,0:T(8,128)S(1)} %get-tuple-element.47), channel_id=1, source_target_pairs={{4,8},{12,16},{20,24},{8,4},{16,12},{24,20},{5,9},{13,17},{21,25},... | collective-permute-start | bytes 1769480 | tf_op jit(solution)/shard_map/ppermute | solution.py:664
  17.8 11.2 %collective-permute-start.3 = (f32[9,32,512]{2,1,0:T(8,128)S(1)}, f32[9,32,512]{2,1,0:T(8,128)S(1)}, u32[]{:S(2)}, u32[]{:S(2)}) collective-permute-start(f32[9,32,512]{2,1,0:T(8,128)S(1)} %get-tuple-element.48), channel_id=1, source_target_pairs={{0,4},{8,12},{16,20},{24,28},{4,0},{12,8},{20,16},{28,24},{1,5},{9... | collective-permute-start | bytes 1769480 | tf_op jit(solution)/shard_map/ppermute | solution.py:664
  17.9 3.3 %collective-permute-start.4 = (f32[2,4,8,512]{3,2,1,0:T(8,128)S(1)}, f32[2,4,8,512]{3,2,1,0:T(8,128)S(1)}, u32[]{:S(2)}, u32[]{:S(2)}) collective-permute-start(f32[2,4,8,512]{3,2,1,0:T(8,128)S(1)} %get-tuple-element.49), channel_id=1, source_target_pairs={{1,2},{2,1},{5,6},{6,5},{9,10},{10,9},{13,14},{14,13},{17,18},{18,... | collective-permute-start | bytes 393224 | tf_op jit(solution)/shard_map/ppermute | solution.py:664
  18.6 7.8 %collective-permute-start.5 = (f32[2,4,8,512]{3,2,1,0:T(8,128)S(1)}, f32[2,4,8,512]{3,2,1,0:T(8,128)S(1)}, u32[]{:S(2)}, u32[]{:S(2)}) collective-permute-start(f32[2,4,8,512]{3,2,1,0:T(8,128)S(1)} %get-tuple-element.50), channel_id=1, source_target_pairs={{0,1},{2,3},{1,0},{3,2},{4,5},{6,7},{5,4},{7,6},{8,9},{10,11},{9,8... | collective-permute-start | bytes 393224 | tf_op jit(solution)/shard_map/ppermute | solution.py:664
  20.6 13.8 %collective-permute-start.6 = (f32[8,16,256]{2,1,0:T(8,128)S(1)}, f32[8,16,256]{2,1,0:T(8,128)S(1)}, u32[]{:S(2)}, u32[]{:S(2)}) collective-permute-start(f32[8,16,256]{2,1,0:T(8,128)S(1)} %mean.1.own_rows), channel_id=1, source_target_pairs={{1,2},{2,1},{5,6},{6,5},{9,10},{10,9},{13,14},{14,13},{17,18},{18,... | collective-permute-start | bytes 393224 | tf_op jit(solution)/shard_map/ppermute | solution.py:664
  21.2 13.1 %collective-permute-start.7 = (f32[8,16,256]{2,1,0:T(8,128)S(1)}, f32[8,16,256]{2,1,0:T(8,128)S(1)}, u32[]{:S(2)}, u32[]{:S(2)}) collective-permute-start(f32[8,16,256]{2,1,0:T(8,128)S(1)} %mean.1.own_rows), channel_id=1, source_target_pairs={{0,1},{2,3},{1,0},{3,2},{4,5},{6,7},{5,4},{7,6},{8,9},{10,11},{9,8... | collective-permute-start | bytes 393224 | tf_op jit(solution)/shard_map/ppermute | solution.py:664
  34.3 8.5 %collective-permute-start.8 = (f32[10,16,256]{2,1,0:T(8,128)S(1)}, f32[10,16,256]{2,1,0:T(8,128)S(1)}, u32[]{:S(2)}, u32[]{:S(2)}) collective-permute-start(f32[10,16,256]{2,1,0:T(8,128)S(1)} %get-tuple-element.61.sent_a), channel_id=1, source_target_pairs={{1,2},{2,1},{5,6},{6,5},{9,10},{10,9},{13,14},{14,13},{17,18},{18,... | collective-permute-start | bytes 491528 | tf_op jit(solution)/shard_map/ppermute | solution.py:664
  35.0 7.8 %collective-permute-start.9 = (f32[10,16,256]{2,1,0:T(8,128)S(1)}, f32[10,16,256]{2,1,0:T(8,128)S(1)}, u32[]{:S(2)}, u32[]{:S(2)}) collective-permute-start(f32[10,16,256]{2,1,0:T(8,128)S(1)} %get-tuple-element.62.sent_b), channel_id=1, source_target_pairs={{0,1},{2,3},{1,0},{3,2},{4,5},{6,7},{5,4},{7,6},{8,9},{10,11},{9,8... | collective-permute-start | bytes 491528 | tf_op jit(solution)/shard_map/ppermute | solution.py:664
  36.8 12.0 %collective-permute-start.12 = (f32[6,48,256]{2,1,0:T(8,128)S(1)}, f32[6,48,256]{2,1,0:T(8,128)S(1)}, u32[]{:S(2)}, u32[]{:S(2)}) collective-permute-start(f32[6,48,256]{2,1,0:T(8,128)S(1)} %get-tuple-element.69), channel_id=1, source_target_pairs={{4,8},{12,16},{20,24},{8,4},{16,12},{24,20},{5,9},{13,17},{21,25},... | collective-permute-start | bytes 884744 | tf_op jit(solution)/shard_map/ppermute | solution.py:664
  42.8 6.0 %collective-permute-start.13 = (f32[6,48,256]{2,1,0:T(8,128)S(1)}, f32[6,48,256]{2,1,0:T(8,128)S(1)}, u32[]{:S(2)}, u32[]{:S(2)}) collective-permute-start(f32[6,48,256]{2,1,0:T(8,128)S(1)} %get-tuple-element.70), channel_id=1, source_target_pairs={{0,4},{8,12},{16,20},{24,28},{4,0},{12,8},{20,16},{28,24},{1,5},{9... | collective-permute-start | bytes 884744 | tf_op jit(solution)/shard_map/ppermute | solution.py:664
  43.0 9.9 %collective-permute-start.10 = (f32[6,48,256]{2,1,0:T(8,128)S(1)}, f32[6,48,256]{2,1,0:T(8,128)S(1)}, u32[]{:S(2)}, u32[]{:S(2)}) collective-permute-start(f32[6,48,256]{2,1,0:T(8,128)S(1)} %get-tuple-element.64), channel_id=1, source_target_pairs={{4,8},{12,16},{20,24},{8,4},{16,12},{24,20},{5,9},{13,17},{21,25},... | collective-permute-start | bytes 884744 | tf_op jit(solution)/shard_map/ppermute | solution.py:664
  48.7 4.2 %collective-permute-start.11 = (f32[6,48,256]{2,1,0:T(8,128)S(1)}, f32[6,48,256]{2,1,0:T(8,128)S(1)}, u32[]{:S(2)}, u32[]{:S(2)}) collective-permute-start(f32[6,48,256]{2,1,0:T(8,128)S(1)} %get-tuple-element.65), channel_id=1, source_target_pairs={{0,4},{8,12},{16,20},{24,28},{4,0},{12,8},{20,16},{28,24},{1,5},{9... | collective-permute-start | bytes 884744 | tf_op jit(solution)/shard_map/ppermute | solution.py:664
  54.9 5.7 %collective-permute-start.14 = (f32[6,24,128]{2,1,0:T(8,128)S(1)}, f32[6,24,128]{2,1,0:T(8,128)S(1)}, u32[]{:S(2)}, u32[]{:S(2)}) collective-permute-start(f32[6,24,128]{2,1,0:T(8,128)S(1)} %get-tuple-element.78), channel_id=1, source_target_pairs={{4,8},{12,16},{20,24},{8,4},{16,12},{24,20},{5,9},{13,17},{21,25},... | collective-permute-start | bytes 221192 | tf_op jit(solution)/shard_map/ppermute | solution.py:664
  58.6 2.0 %collective-permute-start.15 = (f32[6,24,128]{2,1,0:T(8,128)S(1)}, f32[6,24,128]{2,1,0:T(8,128)S(1)}, u32[]{:S(2)}, u32[]{:S(2)}) collective-permute-start(f32[6,24,128]{2,1,0:T(8,128)S(1)} %get-tuple-element.79), channel_id=1, source_target_pairs={{0,4},{8,12},{16,20},{24,28},{4,0},{12,8},{20,16},{28,24},{1,5},{9... | collective-permute-start | bytes 221192 | tf_op jit(solution)/shard_map/ppermute | solution.py:664

commit v10 on v9

--- a/solution.py
+++ b/solution.py
@@ -267,22 +267,35 @@
     return pick((m == i) | (m == i + 1), 0.125, 0.0).astype(F32).astype(jnp.bfloat16)
 
 
-def pack_rows_kernel(s_low, s_high, k_low, k_high, end_a, end_b, inner_a, inner_b):
-    planes, _, lanes = s_low.shape
-    own = planes // 2
-    even = even_mask(8, lanes)
-    ends, inner = Send(end_a, end_b, "inner"), Send(inner_a, inner_b, "inner")
+def pack_pairs(send, pairs, s_low, s_high, k_low, k_high):
     cat = lambda *parts: jnp.concatenate(parts, axis=0)
-
-    for p in range(own):
-        def pair(ref):
-            a, b = ref[2 * p], ref[2 * p + 1]
+    even = even_mask(8, s_low(0).shape[1])
+    for p in range(pairs):
+        def pair(of):
+            a, b = of(2 * p), of(2 * p + 1)
             return pick(even, a, b), pick(even, b, a)
 
         ls, lk, hs, hk = pair(s_low), pair(k_low), pair(s_high), pair(k_high)
-        send, at = (inner, p - 2) if 2 <= p < own - 2 else (ends, p if p < 2 else p - own + 4)
-        send.put((0, at), cat(lk[0][0:4], ls[0][0:4]), cat(hk[0][4:8], hs[0][4:8]))
-        send.put((1, at), cat(lk[1][0:5], ls[1][0:3]), cat(hk[1][3:8], hs[1][5:8]))
+        send.put((0, p), cat(lk[0][0:4], ls[0][0:4]), cat(hk[0][4:8], hs[0][4:8]))
+        send.put((1, p), cat(lk[1][0:5], ls[1][0:3]), cat(hk[1][3:8], hs[1][5:8]))
+
+
+def pack_ends_kernel(*refs):
+    def planes(first, last):
+        return lambda i: first[i] if i < 4 else last[i - 4]
+
+    sources = [planes(refs[2 * i], refs[2 * i + 1]) for i in range(4)]
+    pack_pairs(Send(*refs[8:], "inner"), 4, *sources)
+
+
+def pack_inner_kernel(s, k, to_a, to_b):
+    planes, rows, _ = s.shape
+
+    def plane(ref, first):
+        return lambda i: ref[4 + i, first : first + 8]
+
+    pack_pairs(Send(to_a, to_b, "inner"), planes // 2 - 4,
+               plane(s, 0), plane(s, rows - 8), plane(k, 0), plane(k, rows - 8))
 
 
 def rows_from(got, p, own):
@@ -672,14 +685,14 @@
     own = planes // 2
     wide = rows + 16
 
-    low = pl.BlockSpec((planes, 8, lanes), lambda i: (0, 0, 0))
-    high = pl.BlockSpec((planes, 8, lanes), lambda i: (0, rows // 8 - 1, 0))
+    blocks = [pl.BlockSpec((4, 8, lanes), lambda i, p=p, r=r: (p, r, 0))
+              for r in (0, rows // 8 - 1) for p in (0, planes // 4 - 1)]
     ends, inner = (2, 4, 8, lanes), (2, own - 4, 8, lanes)
-    end_a, end_b, inner_a, inner_b = call(
-        pack_rows_kernel, [ends, ends, inner, inner], [], s, s, k, k,
-        in_specs=[low, high, low, high], name="pack_rows")
-    end_halo = exchange(end_a, end_b, "inner")
-    inner_halo = exchange(inner_a, inner_b, "inner")
+    sent = call(pack_ends_kernel, [ends, ends], [], *[s] * 4, *[k] * 4,
+                in_specs=blocks * 2, name="pack_ends")
+    *end_halo, late_s, late_k = lax.optimization_barrier((*exchange(*sent, "inner"), s, k))
+    sent = call(pack_inner_kernel, [inner, inner], [], late_s, late_k, name="pack_inner")
+    inner_halo = exchange(*sent, "inner")
     half, next_lanes = rows // 2, lanes // 2
     (mean,) = call(mean_kernel, [(own, half, next_lanes)], [(half * own, lanes)], k, name="mean")
     message = (9, rows, lanes)

time: 62.1 us -> 62 us (level)
    pallas_call x10 -> x11, Pallas kernels: 14.6 us -> 14.5 us  [call(): pl.pallas_call(kernel, out_shape=[jax.ShapeDtypeStruct(o, F32) if results...]
where the time goes in v10:
time: 62 us; the launch traced here: 61.5 us
  starting transfers between devices  34.7 us (56%)
  Pallas kernels  14.5 us (23%)
  waiting for transfers between devices  9.74 us (16%)
  local copies, waits for them, and re-layouts  1.64 us (3%)
  between operations  0.89 us (1%)
    ppermute x16, starting transfers between devices, swapped(): return lax.ppermute(x, axis, pairs + [(j, i) for i, j in pairs])  34.7 us
    pallas_call x11, Pallas kernels, call(): pl.pallas_call(kernel, out_shape=[jax.ShapeDtypeStruct(o, F32) if results...  14.5 us
    ppermute x16, waiting for transfers between devices, swapped(): return lax.ppermute(x, axis, pairs + [(j, i) for i, j in pairs])  9.74 us
    unnamed x6, local copies, waits for them, and re-layouts  1.64 us
  transfers between devices with their start and end apart: 16, of which 4 were waited for; matrix products, arithmetic and copies ran while one was open for 3% of the time, Pallas kernels for 16%

profile of v10, /device:TPU:1, one launch (start us, length us, event | category | flops | bytes accessed | tf_op | source)
XLA Modules:
  0.0 61.5 jit_solution(8106219858941206676)
XLA Ops:
  0.6 1.2 %pack_ends.1 = (f32[2,4,8,512]{3,2,1,0:T(8,128)S(1)}, f32[2,4,8,512]{3,2,1,0:T(8,128)S(1)}) custom-call(f32[16,32,512]{2,1,0:T(8,128)} %s.4, f32[16,32,512]{2,1,0:T(8,128)} %s.4, f32[16,32,512]{2,1,0:T(8,128)} %s.4, f32[16,32,512]{2,1,0:T(8,128)} %s.4, f32[16,32,512]{2,1,0:T(8,128)} %k.6, f32[16,32,512]{2,1,0:T(8,128)} %k.6, f32[16,32,512]{2,1,0:T(8,128)} %k.6, ...), custom_call_target="tpu_custom_call" | custom-call | tf_op jit(solution)/shard_map/pack_ends/pallas_call | solution.py:657
  1.9 0.0 copy-start.1
  1.9 0.8 %collective-permute-start = (f32[2,4,8,512]{3,2,1,0:T(8,128)S(1)}, f32[2,4,8,512]{3,2,1,0:T(8,128)S(1)}, u32[]{:S(2)}, u32[]{:S(2)}) collective-permute-start(f32[2,4,8,512]{3,2,1,0:T(8,128)S(1)} %get-tuple-element.47), channel_id=1, source_target_pairs={{1,2},{2,1},{5,6},{6,5},{9,10},{10,9},{13,14},{14,13},{17,18},{18,... | collective-permute-start | bytes 393224 | tf_op jit(solution)/shard_map/ppermute | solution.py:677
  2.7 4.5 %collective-permute-start.1 = (f32[2,4,8,512]{3,2,1,0:T(8,128)S(1)}, f32[2,4,8,512]{3,2,1,0:T(8,128)S(1)}, u32[]{:S(2)}, u32[]{:S(2)}) collective-permute-start(f32[2,4,8,512]{3,2,1,0:T(8,128)S(1)} %get-tuple-element.48), channel_id=1, source_target_pairs={{0,1},{2,3},{1,0},{3,2},{4,5},{6,7},{5,4},{7,6},{8,9},{10,11},{9,8... | collective-permute-start | bytes 393224 | tf_op jit(solution)/shard_map/ppermute | solution.py:677
  7.2 0.0 copy-done
  7.2 0.5 mean.1.own_rows
  7.8 0.0 collective-permute-done.from_a.end_a
  7.8 5.1 %collective-permute-done.1.from_b.end_b = f32[2,4,8,512]{3,2,1,0:T(8,128)S(1)} collective-permute-done((f32[2,4,8,512]{3,2,1,0:T(8,128)S(1)}, f32[2,4,8,512]{3,2,1,0:T(8,128)S(1)}, u32[]{:S(2)}, u32[]{:S(2)}) %collective-permute-start.1) | collective-permute-done | bytes 131104 | tf_op jit(solution)/shard_map/ppermute | solution.py:677
  12.9 0.0 copy-done.1
  12.9 0.1 pack_planes.1
  13.0 4.6 %collective-permute-start.2 = (f32[9,32,512]{2,1,0:T(8,128)S(1)}, f32[9,32,512]{2,1,0:T(8,128)S(1)}, u32[]{:S(2)}, u32[]{:S(2)}) collective-permute-start(f32[9,32,512]{2,1,0:T(8,128)S(1)} %get-tuple-element.53), channel_id=1, source_target_pairs={{4,8},{12,16},{20,24},{8,4},{16,12},{24,20},{5,9},{13,17},{21,25},... | collective-permute-start | bytes 1769480 | tf_op jit(solution)/shard_map/ppermute | solution.py:677
  17.6 0.1 collective-permute-start.3
  17.7 0.1 pack_inner.1
  17.8 0.7 %collective-permute-start.4 = (f32[2,4,8,512]{3,2,1,0:T(8,128)S(1)}, f32[2,4,8,512]{3,2,1,0:T(8,128)S(1)}, u32[]{:S(2)}, u32[]{:S(2)}) collective-permute-start(f32[2,4,8,512]{3,2,1,0:T(8,128)S(1)} %get-tuple-element.57), channel_id=1, source_target_pairs={{1,2},{2,1},{5,6},{6,5},{9,10},{10,9},{13,14},{14,13},{17,18},{18,... | collective-permute-start | bytes 393224 | tf_op jit(solution)/shard_map/ppermute | solution.py:677
  18.5 2.0 %collective-permute-start.5 = (f32[2,4,8,512]{3,2,1,0:T(8,128)S(1)}, f32[2,4,8,512]{3,2,1,0:T(8,128)S(1)}, u32[]{:S(2)}, u32[]{:S(2)}) collective-permute-start(f32[2,4,8,512]{3,2,1,0:T(8,128)S(1)} %get-tuple-element.58), channel_id=1, source_target_pairs={{0,1},{2,3},{1,0},{3,2},{4,5},{6,7},{5,4},{7,6},{8,9},{10,11},{9,8... | collective-permute-start | bytes 393224 | tf_op jit(solution)/shard_map/ppermute | solution.py:677
  20.4 0.7 %collective-permute-start.6 = (f32[8,16,256]{2,1,0:T(8,128)S(1)}, f32[8,16,256]{2,1,0:T(8,128)S(1)}, u32[]{:S(2)}, u32[]{:S(2)}) collective-permute-start(f32[8,16,256]{2,1,0:T(8,128)S(1)} %mean.1.own_rows), channel_id=1, source_target_pairs={{1,2},{2,1},{5,6},{6,5},{9,10},{10,9},{13,14},{14,13},{17,18},{18,... | collective-permute-start | bytes 393224 | tf_op jit(solution)/shard_map/ppermute | solution.py:677
  21.1 0.0 collective-permute-done.4.inner_a
  21.1 3.5 %collective-permute-start.7 = (f32[8,16,256]{2,1,0:T(8,128)S(1)}, f32[8,16,256]{2,1,0:T(8,128)S(1)}, u32[]{:S(2)}, u32[]{:S(2)}) collective-permute-start(f32[8,16,256]{2,1,0:T(8,128)S(1)} %mean.1.own_rows), channel_id=1, source_target_pairs={{0,1},{2,3},{1,0},{3,2},{4,5},{6,7},{5,4},{7,6},{8,9},{10,11},{9,8... | collective-permute-start | bytes 393224 | tf_op jit(solution)/shard_map/ppermute | solution.py:677
  24.6 1.7 %collective-permute-done.5.inner_b = f32[2,4,8,512]{3,2,1,0:T(8,128)S(1)} collective-permute-done((f32[2,4,8,512]{3,2,1,0:T(8,128)S(1)}, f32[2,4,8,512]{3,2,1,0:T(8,128)S(1)}, u32[]{:S(2)}, u32[]{:S(2)}) %collective-permute-start.5) | collective-permute-done | bytes 131104 | tf_op jit(solution)/shard_map/ppermute | solution.py:677
  26.3 2.6 %fine_prepare.1 = (f32[2,8,48,512]{3,2,1,0:T(8,128)S(1)}, f32[2,8,48,512]{3,2,1,0:T(8,128)S(1)}, f32[2,8,48,512]{3,2,1,0:T(8,128)S(1)}, f32[12,8,48,512]{3,2,1,0:T(8,128)S(1)}, f32[2,8,48,512]{3,2,1,0:T(8,128)S(1)}) custom-call(f32[16,32,512]{2,1,0:T(8,128)S(1)} %copy-done.1, f32[16,32,512]{2,1,0:T(8,128)S(1)} %copy-done, ...), custom_call_target="tpu_custom_call" | custom-call | tf_op jit(solution)/shard_map/fine_prepare/pallas_call | solution.py:657
  28.9 0.0 collective-permute-done.2.plane_a
  28.9 0.0 collective-permute-done.3.plane_b
  28.9 5.3 %fine_level.1 = (f32[16,32,512]{2,1,0:T(8,128)S(1)}, f32[10,16,256]{2,1,0:T(8,128)S(1)}, f32[10,16,256]{2,1,0:T(8,128)S(1)}, f32[10,16,256]{2,1,0:T(8,128)S(1)}) custom-call(f32[9,32,512]{2,1,0:T(8,128)S(1)} %collective-permute-done.2.plane_a, f32[9,32,512]{2,1,0:T(8,128)S(1)} %collective-permute-done.3.plane_b, f32[2,8,48,512]{3,2,1,0:T(8,128)S(1)} %get-tuple-element.59.K0, ...), custom_call_target="tpu_custom_call" | custom-call | tf_op jit(solution)/shard_map/fine_level/pallas_call | solution.py:657
  34.2 0.0 collective-permute-done.6.from_a
  34.2 0.0 collective-permute-done.7.from_b
  34.2 0.7 %collective-permute-start.8 = (f32[10,16,256]{2,1,0:T(8,128)S(1)}, f32[10,16,256]{2,1,0:T(8,128)S(1)}, u32[]{:S(2)}, u32[]{:S(2)}) collective-permute-start(f32[10,16,256]{2,1,0:T(8,128)S(1)} %get-tuple-element.69.sent_a), channel_id=1, source_target_pairs={{1,2},{2,1},{5,6},{6,5},{9,10},{10,9},{13,14},{14,13},{17,18},{18,... | collective-permute-start | bytes 491528 | tf_op jit(solution)/shard_map/ppermute | solution.py:677
  34.9 1.7 %collective-permute-start.9 = (f32[10,16,256]{2,1,0:T(8,128)S(1)}, f32[10,16,256]{2,1,0:T(8,128)S(1)}, u32[]{:S(2)}, u32[]{:S(2)}) collective-permute-start(f32[10,16,256]{2,1,0:T(8,128)S(1)} %get-tuple-element.70.sent_b), channel_id=1, source_target_pairs={{0,1},{2,3},{1,0},{3,2},{4,5},{6,7},{5,4},{7,6},{8,9},{10,11},{9,8... | collective-permute-start | bytes 491528 | tf_op jit(solution)/shard_map/ppermute | solution.py:677
  36.6 0.1 mean_planes.1
  36.7 5.9 %collective-permute-start.12 = (f32[6,48,256]{2,1,0:T(8,128)S(1)}, f32[6,48,256]{2,1,0:T(8,128)S(1)}, u32[]{:S(2)}, u32[]{:S(2)}) collective-permute-start(f32[6,48,256]{2,1,0:T(8,128)S(1)} %get-tuple-element.77), channel_id=1, source_target_pairs={{4,8},{12,16},{20,24},{8,4},{16,12},{24,20},{5,9},{13,17},{21,25},... | collective-permute-start | bytes 884744 | tf_op jit(solution)/shard_map/ppermute | solution.py:677
  42.6 0.1 collective-permute-start.13
  42.7 0.0 collective-permute-done.8.from_a
  42.7 0.0 collective-permute-done.9.from_b
  42.7 0.1 source_planes.1
  42.9 5.7 %collective-permute-start.10 = (f32[6,48,256]{2,1,0:T(8,128)S(1)}, f32[6,48,256]{2,1,0:T(8,128)S(1)}, u32[]{:S(2)}, u32[]{:S(2)}) collective-permute-start(f32[6,48,256]{2,1,0:T(8,128)S(1)} %get-tuple-element.72), channel_id=1, source_target_pairs={{4,8},{12,16},{20,24},{8,4},{16,12},{24,20},{5,9},{13,17},{21,25},... | collective-permute-start | bytes 884744 | tf_op jit(solution)/shard_map/ppermute | solution.py:677
  48.6 0.1 collective-permute-start.11
  48.6 0.0 collective-permute-done.12.from_a
  48.6 0.0 collective-permute-done.13.from_b
  48.7 1.4 %middle_setup.1 = (f32[2,10,48,256]{3,2,1,0:T(8,128)S(1)}, f32[12,10,48,256]{3,2,1,0:T(8,128)S(1)}, f32[2,10,48,256]{3,2,1,0:T(8,128)S(1)}, f32[2,10,48,256]{3,2,1,0:T(8,128)S(1)}, f32[10,24,128]{2,1,0:T(8,128)S(1)}) custom-call(f32[8,48,256]{2,1,0:T(8,128)S(1)} %get-tuple-element.76.k, f32[6,48,256]{2,1,0:T(8,128)S(1)} %collective-permute-done.12.from_a, ...), custom_call_target="tpu_custom_call" | custom-call | tf_op jit(solution)/shard_map/middle_setup/pallas_call | solution.py:657
  50.1 2.7 %collective-permute-done.10.source_a = f32[6,48,256]{2,1,0:T(8,128)S(1)} collective-permute-done((f32[6,48,256]{2,1,0:T(8,128)S(1)}, f32[6,48,256]{2,1,0:T(8,128)S(1)}, u32[]{:S(2)}, u32[]{:S(2)}) %collective-permute-start.10) | collective-permute-done | bytes 294944 | tf_op jit(solution)/shard_map/ppermute | solution.py:677
  52.8 0.0 collective-permute-done.11.source_b
  52.8 2.0 %middle_level.1 = (f32[8,16,256]{2,1,0:T(8,128)S(1)}, f32[4,24,128]{2,1,0:T(8,128)S(1)}, f32[6,24,128]{2,1,0:T(8,128)S(1)}, f32[6,24,128]{2,1,0:T(8,128)S(1)}) custom-call(f32[10,48,256]{2,1,0:T(8,128)S(1)} %get-tuple-element.71.s, f32[6,48,256]{2,1,0:T(8,128)S(1)} %collective-permute-done.10.source_a, f32[6,48,256]{2,1,0:T(8,128)S(1)} %collective-permute-done.11.source_b, ...), custom_call_target="tpu_custom_call" | custom-call | tf_op jit(solution)/shard_map/middle_level/pallas_call | solution.py:657
  54.8 3.6 %collective-permute-start.14 = (f32[6,24,128]{2,1,0:T(8,128)S(1)}, f32[6,24,128]{2,1,0:T(8,128)S(1)}, u32[]{:S(2)}, u32[]{:S(2)}) collective-permute-start(f32[6,24,128]{2,1,0:T(8,128)S(1)} %get-tuple-element.86), channel_id=1, source_target_pairs={{4,8},{12,16},{20,24},{8,4},{16,12},{24,20},{5,9},{13,17},{21,25},... | collective-permute-start | bytes 221192 | tf_op jit(solution)/shard_map/ppermute | solution.py:677
  58.5 0.1 collective-permute-start.15
  58.5 1.0 %copy.6 = f32[16,32,512]{2,1,0:T(8,128)} copy(f32[16,32,512]{2,1,0:T(8,128)S(1)} %get-tuple-element.90) | data formatting | bytes 2097152
  59.5 0.7 %copy.7 = f32[8,16,256]{2,1,0:T(8,128)} copy(f32[8,16,256]{2,1,0:T(8,128)S(1)} %get-tuple-element.91) | data formatting | bytes 262144
  60.2 0.3 collective-permute-done.14.from_a
  60.5 0.0 collective-permute-done.15.from_b
  60.5 1.0 %coarse_level.1 = (f32[4,8,128]{2,1,0:T(8,128)}, f32[4,8,128]{2,1,0:T(8,128)}) custom-call(f32[4,24,128]{2,1,0:T(8,128)S(1)} %get-tuple-element.85.s, f32[10,24,128]{2,1,0:T(8,128)S(1)} %get-tuple-element.83.k_next.k, f32[6,24,128]{2,1,0:T(8,128)S(1)} %collective-permute-done.14.from_a, f32[6,24,128]{2,1,0:T(8,128)S(1)} %collective-permute-done.15.from_b), custom_call_target="tpu_custom_call" | custom-call | tf_op jit(solution)/shard_map/coarse_level/pallas_call | solution.py:657
  (1 shorter events, 0.0 us)
Async XLA Ops:
  0.6 6.6 %copy-start = (f32[16,32,512]{2,1,0:T(8,128)S(1)}, f32[16,32,512]{2,1,0:T(8,128)}, u32[]{:S(2)}) copy-start(f32[16,32,512]{2,1,0:T(8,128)} %k.6) | copy-start | bytes 3145732
  1.9 11.0 %copy-start.1 = (f32[16,32,512]{2,1,0:T(8,128)S(1)}, f32[16,32,512]{2,1,0:T(8,128)}, u32[]{:S(2)}) copy-start(f32[16,32,512]{2,1,0:T(8,128)} %s.4) | copy-start | bytes 3145732
  1.9 5.9 %collective-permute-start = (f32[2,4,8,512]{3,2,1,0:T(8,128)S(1)}, f32[2,4,8,512]{3,2,1,0:T(8,128)S(1)}, u32[]{:S(2)}, u32[]{:S(2)}) collective-permute-start(f32[2,4,8,512]{3,2,1,0:T(8,128)S(1)} %get-tuple-element.47), channel_id=1, source_target_pairs={{1,2},{2,1},{5,6},{6,5},{9,10},{10,9},{13,14},{14,13},{17,18},{18,... | collective-permute-start | bytes 393224 | tf_op jit(solution)/shard_map/ppermute | solution.py:677
  2.7 10.2 %collective-permute-start.1 = (f32[2,4,8,512]{3,2,1,0:T(8,128)S(1)}, f32[2,4,8,512]{3,2,1,0:T(8,128)S(1)}, u32[]{:S(2)}, u32[]{:S(2)}) collective-permute-start(f32[2,4,8,512]{3,2,1,0:T(8,128)S(1)} %get-tuple-element.48), channel_id=1, source_target_pairs={{0,1},{2,3},{1,0},{3,2},{4,5},{6,7},{5,4},{7,6},{8,9},{10,11},{9,8... | collective-permute-start | bytes 393224 | tf_op jit(solution)/shard_map/ppermute | solution.py:677
  13.0 15.9 %collective-permute-start.2 = (f32[9,32,512]{2,1,0:T(8,128)S(1)}, f32[9,32,512]{2,1,0:T(8,128)S(1)}, u32[]{:S(2)}, u32[]{:S(2)}) collective-permute-start(f32[9,32,512]{2,1,0:T(8,128)S(1)} %get-tuple-element.53), channel_id=1, source_target_pairs={{4,8},{12,16},{20,24},{8,4},{16,12},{24,20},{5,9},{13,17},{21,25},... | collective-permute-start | bytes 1769480 | tf_op jit(solution)/shard_map/ppermute | solution.py:677
  17.6 11.3 %collective-permute-start.3 = (f32[9,32,512]{2,1,0:T(8,128)S(1)}, f32[9,32,512]{2,1,0:T(8,128)S(1)}, u32[]{:S(2)}, u32[]{:S(2)}) collective-permute-start(f32[9,32,512]{2,1,0:T(8,128)S(1)} %get-tuple-element.54), channel_id=1, source_target_pairs={{0,4},{8,12},{16,20},{24,28},{4,0},{12,8},{20,16},{28,24},{1,5},{9... | collective-permute-start | bytes 1769480 | tf_op jit(solution)/shard_map/ppermute | solution.py:677
  17.8 3.3 %collective-permute-start.4 = (f32[2,4,8,512]{3,2,1,0:T(8,128)S(1)}, f32[2,4,8,512]{3,2,1,0:T(8,128)S(1)}, u32[]{:S(2)}, u32[]{:S(2)}) collective-permute-start(f32[2,4,8,512]{3,2,1,0:T(8,128)S(1)} %get-tuple-element.57), channel_id=1, source_target_pairs={{1,2},{2,1},{5,6},{6,5},{9,10},{10,9},{13,14},{14,13},{17,18},{18,... | collective-permute-start | bytes 393224 | tf_op jit(solution)/shard_map/ppermute | solution.py:677
  18.5 7.8 %collective-permute-start.5 = (f32[2,4,8,512]{3,2,1,0:T(8,128)S(1)}, f32[2,4,8,512]{3,2,1,0:T(8,128)S(1)}, u32[]{:S(2)}, u32[]{:S(2)}) collective-permute-start(f32[2,4,8,512]{3,2,1,0:T(8,128)S(1)} %get-tuple-element.58), channel_id=1, source_target_pairs={{0,1},{2,3},{1,0},{3,2},{4,5},{6,7},{5,4},{7,6},{8,9},{10,11},{9,8... | collective-permute-start | bytes 393224 | tf_op jit(solution)/shard_map/ppermute | solution.py:677
  20.4 13.7 %collective-permute-start.6 = (f32[8,16,256]{2,1,0:T(8,128)S(1)}, f32[8,16,256]{2,1,0:T(8,128)S(1)}, u32[]{:S(2)}, u32[]{:S(2)}) collective-permute-start(f32[8,16,256]{2,1,0:T(8,128)S(1)} %mean.1.own_rows), channel_id=1, source_target_pairs={{1,2},{2,1},{5,6},{6,5},{9,10},{10,9},{13,14},{14,13},{17,18},{18,... | collective-permute-start | bytes 393224 | tf_op jit(solution)/shard_map/ppermute | solution.py:677
  21.1 13.1 %collective-permute-start.7 = (f32[8,16,256]{2,1,0:T(8,128)S(1)}, f32[8,16,256]{2,1,0:T(8,128)S(1)}, u32[]{:S(2)}, u32[]{:S(2)}) collective-permute-start(f32[8,16,256]{2,1,0:T(8,128)S(1)} %mean.1.own_rows), channel_id=1, source_target_pairs={{0,1},{2,3},{1,0},{3,2},{4,5},{6,7},{5,4},{7,6},{8,9},{10,11},{9,8... | collective-permute-start | bytes 393224 | tf_op jit(solution)/shard_map/ppermute | solution.py:677
  34.2 8.5 %collective-permute-start.8 = (f32[10,16,256]{2,1,0:T(8,128)S(1)}, f32[10,16,256]{2,1,0:T(8,128)S(1)}, u32[]{:S(2)}, u32[]{:S(2)}) collective-permute-start(f32[10,16,256]{2,1,0:T(8,128)S(1)} %get-tuple-element.69.sent_a), channel_id=1, source_target_pairs={{1,2},{2,1},{5,6},{6,5},{9,10},{10,9},{13,14},{14,13},{17,18},{18,... | collective-permute-start | bytes 491528 | tf_op jit(solution)/shard_map/ppermute | solution.py:677
  34.9 7.8 %collective-permute-start.9 = (f32[10,16,256]{2,1,0:T(8,128)S(1)}, f32[10,16,256]{2,1,0:T(8,128)S(1)}, u32[]{:S(2)}, u32[]{:S(2)}) collective-permute-start(f32[10,16,256]{2,1,0:T(8,128)S(1)} %get-tuple-element.70.sent_b), channel_id=1, source_target_pairs={{0,1},{2,3},{1,0},{3,2},{4,5},{6,7},{5,4},{7,6},{8,9},{10,11},{9,8... | collective-permute-start | bytes 491528 | tf_op jit(solution)/shard_map/ppermute | solution.py:677
  36.7 11.9 %collective-permute-start.12 = (f32[6,48,256]{2,1,0:T(8,128)S(1)}, f32[6,48,256]{2,1,0:T(8,128)S(1)}, u32[]{:S(2)}, u32[]{:S(2)}) collective-permute-start(f32[6,48,256]{2,1,0:T(8,128)S(1)} %get-tuple-element.77), channel_id=1, source_target_pairs={{4,8},{12,16},{20,24},{8,4},{16,12},{24,20},{5,9},{13,17},{21,25},... | collective-permute-start | bytes 884744 | tf_op jit(solution)/shard_map/ppermute | solution.py:677
  42.6 6.0 %collective-permute-start.13 = (f32[6,48,256]{2,1,0:T(8,128)S(1)}, f32[6,48,256]{2,1,0:T(8,128)S(1)}, u32[]{:S(2)}, u32[]{:S(2)}) collective-permute-start(f32[6,48,256]{2,1,0:T(8,128)S(1)} %get-tuple-element.78), channel_id=1, source_target_pairs={{0,4},{8,12},{16,20},{24,28},{4,0},{12,8},{20,16},{28,24},{1,5},{9... | collective-permute-start | bytes 884744 | tf_op jit(solution)/shard_map/ppermute | solution.py:677
  42.9 9.9 %collective-permute-start.10 = (f32[6,48,256]{2,1,0:T(8,128)S(1)}, f32[6,48,256]{2,1,0:T(8,128)S(1)}, u32[]{:S(2)}, u32[]{:S(2)}) collective-permute-start(f32[6,48,256]{2,1,0:T(8,128)S(1)} %get-tuple-element.72), channel_id=1, source_target_pairs={{4,8},{12,16},{20,24},{8,4},{16,12},{24,20},{5,9},{13,17},{21,25},... | collective-permute-start | bytes 884744 | tf_op jit(solution)/shard_map/ppermute | solution.py:677
  48.6 4.2 %collective-permute-start.11 = (f32[6,48,256]{2,1,0:T(8,128)S(1)}, f32[6,48,256]{2,1,0:T(8,128)S(1)}, u32[]{:S(2)}, u32[]{:S(2)}) collective-permute-start(f32[6,48,256]{2,1,0:T(8,128)S(1)} %get-tuple-element.73), channel_id=1, source_target_pairs={{0,4},{8,12},{16,20},{24,28},{4,0},{12,8},{20,16},{28,24},{1,5},{9... | collective-permute-start | bytes 884744 | tf_op jit(solution)/shard_map/ppermute | solution.py:677
  54.8 5.7 %collective-permute-start.14 = (f32[6,24,128]{2,1,0:T(8,128)S(1)}, f32[6,24,128]{2,1,0:T(8,128)S(1)}, u32[]{:S(2)}, u32[]{:S(2)}) collective-permute-start(f32[6,24,128]{2,1,0:T(8,128)S(1)} %get-tuple-element.86), channel_id=1, source_target_pairs={{4,8},{12,16},{20,24},{8,4},{16,12},{24,20},{5,9},{13,17},{21,25},... | collective-permute-start | bytes 221192 | tf_op jit(solution)/shard_map/ppermute | solution.py:677
  58.5 2.0 %collective-permute-start.15 = (f32[6,24,128]{2,1,0:T(8,128)S(1)}, f32[6,24,128]{2,1,0:T(8,128)S(1)}, u32[]{:S(2)}, u32[]{:S(2)}) collective-permute-start(f32[6,24,128]{2,1,0:T(8,128)S(1)} %get-tuple-element.87), channel_id=1, source_target_pairs={{0,4},{8,12},{16,20},{24,28},{4,0},{12,8},{20,16},{28,24},{1,5},{9... | collective-permute-start | bytes 221192 | tf_op jit(solution)/shard_map/ppermute | solution.py:677
